TPU v7x, 32 devices: a whole 2x2x4 slice. The times are simulated.
32 devices in a mesh: seq: 8 (over z, y), tp: 4 (over x, core).
Axes of the slice: x: 2, y: 2, z: 4, core: 2. Of those that a mesh axis runs over, the one named last changes fastest.
Arguments:
- layer_input: bfloat16 [4096, 1024], P('seq'), may hold values from -6 to 6
- seq_groups: int32 [16], replicated, may hold values from 1 to 16, 64 in all
- seq_pads: int32 [16], replicated, may hold values from 0 to 7
- norm_in: bfloat16 [1024], replicated, may hold values from 0.5 to 1.5
- w_query: bfloat16 [1024, 1024], P(None, 'tp'), may hold values from -0.1875 to 0.1875
- w_key: bfloat16 [1024, 1024], P(None, 'tp'), may hold values from -0.1875 to 0.1875
- w_value: bfloat16 [1024, 1024], P(None, 'tp'), may hold values from -0.1875 to 0.1875
- conv_query: bfloat16 [4, 1024], P(None, 'tp'), may hold values from -3 to 3
- conv_key: bfloat16 [4, 1024], P(None, 'tp'), may hold values from -3 to 3
- conv_value: bfloat16 [4, 1024], P(None, 'tp'), may hold values from -3 to 3
- w_beta: bfloat16 [1024, 8], P(None, 'tp'), may hold values from -0.1875 to 0.1875
- w_gate_out: bfloat16 [1024, 1024], P(None, 'tp'), may hold values from -0.1875 to 0.1875
- norm_head: bfloat16 [128], replicated, may hold values from 0.5 to 1.5
- w_out: bfloat16 [1024, 1024], P('tp'), may hold values from -0.1875 to 0.1875
- norm_mid: bfloat16 [1024], replicated, may hold values from 0.5 to 1.5
- w_gate: bfloat16 [1024, 2816], P(None, 'tp'), may hold values from -0.1875 to 0.1875
- w_up: bfloat16 [1024, 2816], P(None, 'tp'), may hold values from -0.1875 to 0.1875
- w_down: bfloat16 [2816, 1024], P('tp'), may hold values from -0.109375 to 0.109375
- cotangent: bfloat16 [4096, 1024], P('seq'), may hold values from -6 to 6
Outputs:
- block_out: bfloat16 [4096, 1024], P('seq')
- grad_input: float32 [4096, 1024], P('seq')
- grad_norm_in: float32 [1024], P('tp')
- grad_w_query: float32 [1024, 1024], P(None, 'tp')
- grad_w_key: float32 [1024, 1024], P(None, 'tp')
- grad_w_value: float32 [1024, 1024], P(None, 'tp')
- grad_conv_query: float32 [4, 1024], P(None, 'tp')
- grad_conv_key: float32 [4, 1024], P(None, 'tp')
- grad_conv_value: float32 [4, 1024], P(None, 'tp')
- grad_w_beta: float32 [1024, 8], P(None, 'tp')
- grad_w_gate_out: float32 [1024, 1024], P(None, 'tp')
- grad_norm_head: float32 [128], P('tp')
- grad_w_out: float32 [1024, 1024], P('tp')
- grad_norm_mid: float32 [1024], P('tp')
- grad_w_gate: float32 [1024, 2816], P(None, 'tp')
- grad_w_up: float32 [1024, 2816], P(None, 'tp')
- grad_w_down: float32 [2816, 1024], P('tp')
Inputs may be any that keep to these rules, and one draw needn't show every extreme that they name: `seq_groups`: they sum to 64; the largest is exactly 16.
All inputs are finite; a program needn't handle non-finite values.
Results may differ from a plain program's by a relative error of at most 0.009.
The roundings to bfloat16 on the way count: a program that leaves them out, or rounds other values in their place, can miss the bound.
Values may be sent and summed in bfloat16 or wider, within the bound.
No kernel may reach another device: no remote copies, remote signals or barrier semaphores. Data moves between devices by JAX's collectives and lax.ppermute only.
A program may use at most 192 MiB of HBM per device.

v0:
```python
import jax
import jax.numpy as jnp
from jax import lax
from jax.sharding import PartitionSpec as P

DH = 128
KW = 4
GROUP = 64


HIGHEST = lax.Precision.HIGHEST
row_epsilon = 1e-06
head_epsilon = 1e-05
unit_epsilon = 1e-06


def shifted(value, axis, steps):
    count = lax.axis_size(axis)
    first, last = (max(0, -steps), min(count, count - steps))
    return lax.ppermute(value, axis, [(source, source + steps) for source in range(first, last)])


def entering(part, axis, combine, identity):
    place = lax.axis_index(axis)
    gathered = jax.tree.map(lambda a: lax.all_gather(a, axis), part)
    state = jax.tree.map(lambda a, e: jnp.zeros_like(a) + jnp.asarray(e, a.dtype), part, identity)

    def one(hop, state):
        return combine(
            state, jax.tree.map(lambda a: lax.dynamic_index_in_dim(a, hop, 0, False), gathered)
        )

    return lax.fori_loop(0, place, one, state)


def prefix(array, axis, combine, identity):
    devices, here = (lax.axis_size(axis), lax.axis_index(axis))
    everything = jax.tree.map(
        lambda part, kind: lax.all_gather(part.astype(kind), axis),
        array,
        (jnp.bfloat16, jnp.bfloat16),
    )
    start = jax.tree.map(
        lambda part, zero: jnp.broadcast_to(jnp.asarray(zero, part.dtype), part.shape),
        array,
        identity,
    )

    def hop(k, before):
        at = devices - 1 - k
        reached = at > here
        new = combine(
            before, jax.tree.map(lambda part, own: part[at].astype(own.dtype), everything, array)
        )
        return jax.tree.map(lambda a, b: jnp.where(reached, a, b), new, before)

    return lax.fori_loop(0, devices, hop, start)


def layout(seq_groups, seq_pads, group_count, first_group):
    seq_ends = jnp.cumsum(seq_groups, dtype=jnp.int32)
    starts = seq_ends - seq_groups
    group_ids = first_group + jnp.arange(group_count, dtype=jnp.int32)
    owner_table = (
        (group_ids[:, None] >= starts[None, :]) & (group_ids[:, None] < seq_ends[None, :])
    ).astype(jnp.int32)
    start_of = jnp.sum(owner_table * starts[None, :], axis=1, dtype=jnp.int32)
    length_of = jnp.sum(
        owner_table * (seq_groups * GROUP - seq_pads)[None, :], axis=1, dtype=jnp.int32
    )
    restart = (group_ids == start_of).astype(jnp.float32)
    position = ((group_ids - start_of) * GROUP)[:, None] + jnp.arange(GROUP, dtype=jnp.int32)[
        None, :
    ]
    live_rows = (position < length_of[:, None]).astype(jnp.float32)
    return (restart, position.reshape(-1), live_rows.reshape(-1))


def row_norm(values, gain):
    factor = lax.rsqrt(jnp.mean(values * values, axis=-1, keepdims=True) + row_epsilon)
    return values * factor * gain


def gated_norm(outputs, gain, gate_heads):
    factor = lax.rsqrt(jnp.mean(outputs * outputs, axis=-1, keepdims=True) + head_epsilon)
    return outputs * factor * gain * jax.nn.silu(gate_heads)


def causal_conv(extended, tap_table, position):
    row_count = position.shape[0]
    summed = jnp.zeros((row_count, extended.shape[1]), extended.dtype)
    for tap_number in range(KW):
        distance = KW - 1 - tap_number
        keep_mask = (position >= distance).astype(extended.dtype)[:, None]
        summed = (
            summed
            + tap_table[tap_number] * extended[tap_number : tap_number + row_count] * keep_mask
        )
    return summed


def activate(conv_out, model_width):
    acted = jax.nn.silu(conv_out)
    row_count = conv_out.shape[0]
    query_rows = acted[:, :model_width].reshape(row_count, -1, DH)
    key_rows = acted[:, model_width : 2 * model_width].reshape(row_count, -1, DH)
    value_rows = acted[:, 2 * model_width :].reshape(row_count, -1, DH)
    query_rows = query_rows * lax.rsqrt(
        jnp.sum(query_rows * query_rows, axis=-1, keepdims=True) + unit_epsilon
    )
    key_rows = key_rows * lax.rsqrt(
        jnp.sum(key_rows * key_rows, axis=-1, keepdims=True) + unit_epsilon
    )
    return (query_rows, key_rows, value_rows)


def wy_parts(key_rows, value_rows, beta_rows):
    group_len = key_rows.shape[1]
    key_dots = jnp.einsum("nihd,njhd->nhij", key_rows, key_rows, precision=HIGHEST)
    strict = jnp.tril(jnp.ones((group_len, group_len), key_rows.dtype), -1)
    beta_heads = jnp.swapaxes(beta_rows, 1, 2)
    system = jnp.eye(group_len, dtype=key_rows.dtype) + strict * beta_heads[..., None] * key_dots
    scaled_keys = jnp.swapaxes(beta_rows[..., None] * key_rows, 1, 2)
    scaled_values = jnp.swapaxes(beta_rows[..., None] * value_rows, 1, 2)
    key_mix = jax.scipy.linalg.solve_triangular(system, scaled_keys, lower=True, unit_diagonal=True)
    value_mix = jax.scipy.linalg.solve_triangular(
        system, scaled_values, lower=True, unit_diagonal=True
    )
    return (key_mix, value_mix)


def group_apply(query_rows, key_rows, key_mix, value_mix, start_states):
    group_len = key_rows.shape[1]
    inclusive = jnp.tril(jnp.ones((group_len, group_len), key_rows.dtype))
    value_new = value_mix - jnp.einsum("nhcd,nhde->nhce", key_mix, start_states, precision=HIGHEST)
    scores = jnp.einsum("nihd,njhd->nhij", query_rows, key_rows, precision=HIGHEST) * inclusive
    produced = jnp.einsum("nihd,nhde->nihe", query_rows, start_states, precision=HIGHEST)
    produced = produced + jnp.einsum("nhij,nhje->nihe", scores, value_new, precision=HIGHEST)
    final_state = start_states + jnp.einsum(
        "nihd,nhie->nhde", key_rows, value_new, precision=HIGHEST
    )
    return (produced, final_state)


def group_full(query_rows, key_rows, value_rows, beta_rows, start_states):
    key_mix, value_mix = wy_parts(key_rows, value_rows, beta_rows)
    return group_apply(query_rows, key_rows, key_mix, value_mix, start_states)


def compose(earlier_maps, later_maps):
    return (
        jnp.einsum("hij,hjk->hik", later_maps[0], earlier_maps[0], precision=HIGHEST),
        jnp.einsum("hij,hjk->hik", later_maps[0], earlier_maps[1], precision=HIGHEST)
        + later_maps[1],
    )


def link_step(carried, pieces):
    step_map, step_add = pieces
    new_map = jnp.einsum("hij,hjk->hik", step_map, carried[0], precision=HIGHEST)
    new_add = jnp.einsum("hij,hjk->hik", step_map, carried[1], precision=HIGHEST) + step_add
    return ((new_map, new_add), carried)


def mat_rows(left, right):
    return jnp.einsum("tf,df->td", left, right, preferred_element_type=jnp.float32)


def mat_weight(left, right):
    return jnp.einsum("td,tf->df", left, right, preferred_element_type=jnp.float32)


def shards(
    layer_input,
    seq_groups,
    seq_pads,
    norm_in,
    w_query,
    w_key,
    w_value,
    conv_query,
    conv_key,
    conv_value,
    w_beta,
    w_gate_out,
    norm_head,
    w_out,
    norm_mid,
    w_gate,
    w_up,
    w_down,
    cotangent,
):
    row_count, model_width = layer_input.shape
    local_width = w_query.shape[1]
    head_count = local_width // DH
    groups = row_count // GROUP
    tp_count = lax.axis_size("tp")
    tp_rank = lax.axis_index("tp")
    share = row_count // tp_count
    restart, position, live_rows = layout(
        seq_groups, seq_pads, groups, lax.axis_index("seq") * groups
    )
    live_col = live_rows[:, None]

    def own_share(values):
        return lax.dynamic_slice_in_dim(values, tp_rank * share, share, 0)

    inputs = layer_input.astype(jnp.float32)
    mid_gain = norm_mid.astype(jnp.float32)
    normed_in, in_pull = jax.vjp(row_norm, inputs, norm_in.astype(jnp.float32))
    hidden = normed_in.astype(jnp.bfloat16)
    proj_cat = jnp.concatenate([w_query, w_key, w_value], axis=1)
    projected = jnp.dot(hidden, proj_cat, preferred_element_type=jnp.float32)
    gate_raw = jnp.dot(hidden, w_gate_out, preferred_element_type=jnp.float32)
    beta_raw = jnp.dot(hidden, w_beta, preferred_element_type=jnp.float32)
    tail_rows = shifted(projected[row_count - (KW - 1) :], "seq", 1)
    tap_table = jnp.concatenate([conv_query, conv_key, conv_value], axis=1).astype(jnp.float32)
    extended = jnp.concatenate([tail_rows, projected], axis=0)
    conv_out, conv_pull = jax.vjp(
        lambda ext_rows, tap_values: causal_conv(ext_rows, tap_values, position),
        extended,
        tap_table,
    )
    (query_rows, key_rows, value_rows), act_pull = jax.vjp(
        lambda values: activate(values, local_width), conv_out
    )
    beta_sig = jax.nn.sigmoid(beta_raw)
    beta_rows = beta_sig * live_col
    q_groups = query_rows.reshape(groups, GROUP, head_count, DH)
    k_groups = key_rows.reshape(groups, GROUP, head_count, DH)
    v_groups = value_rows.reshape(groups, GROUP, head_count, DH)
    b_groups = beta_rows.reshape(groups, GROUP, head_count)
    key_mix, value_mix = wy_parts(k_groups, v_groups, b_groups)
    eye_heads = jnp.broadcast_to(jnp.eye(DH, dtype=jnp.float32), (head_count, DH, DH))
    zero_heads = jnp.zeros_like(eye_heads)
    keep_state = (1.0 - restart)[:, None, None, None]
    transit = (
        eye_heads[None] - jnp.einsum("nihd,nhie->nhde", k_groups, key_mix, precision=HIGHEST)
    ) * keep_state
    inject = jnp.einsum("nihd,nhie->nhde", k_groups, value_mix, precision=HIGHEST)
    (device_map, device_state), (prefix_maps, prefix_states) = lax.scan(
        link_step, (eye_heads, zero_heads), (transit, inject)
    )
    entry_maps = entering((device_map, device_state), "seq", compose, (eye_heads, zero_heads))
    start_states = (
        jnp.einsum("nhij,hjk->nhik", prefix_maps, entry_maps[1], precision=HIGHEST) + prefix_states
    ) * keep_state
    produced, _ = group_apply(q_groups, k_groups, key_mix, value_mix, start_states)
    heads_out = produced.reshape(row_count, head_count, DH)
    gate_heads = gate_raw.reshape(row_count, head_count, DH)
    normed, gated_pull = jax.vjp(gated_norm, heads_out, norm_head.astype(jnp.float32), gate_heads)
    attended = normed.reshape(row_count, local_width).astype(jnp.bfloat16)
    branch_terms = jnp.dot(attended, w_out, preferred_element_type=jnp.float32)
    residual = inputs + lax.psum(branch_terms, "tp")
    normed_mid, mid_pull = jax.vjp(row_norm, residual, mid_gain)
    second = normed_mid.astype(jnp.bfloat16)
    gate_val = jnp.dot(second, w_gate, preferred_element_type=jnp.float32)
    up_val = jnp.dot(second, w_up, preferred_element_type=jnp.float32)
    inner_full, ffn_pull = jax.vjp(
        lambda gate_in, up_in: jax.nn.silu(gate_in) * up_in, gate_val, up_val
    )
    inner_act = inner_full.astype(jnp.bfloat16)
    down_terms = jnp.dot(inner_act, w_down, preferred_element_type=jnp.float32)
    down_val = lax.psum(down_terms, "tp")
    block_out = ((residual + down_val) * live_col).astype(jnp.bfloat16)
    grad_y = cotangent.astype(jnp.float32) * live_col
    grad_down = grad_y.astype(jnp.bfloat16)
    grad_w_down = mat_weight(inner_act, grad_down)
    grad_inner = mat_rows(grad_down, w_down)
    grad_gate_full, grad_up_full = ffn_pull(grad_inner)
    grad_gate_val = grad_gate_full.astype(jnp.bfloat16)
    grad_up_val = grad_up_full.astype(jnp.bfloat16)
    grad_w_gate = mat_weight(second, grad_gate_val)
    grad_w_up = mat_weight(second, grad_up_val)
    mid_partial = mat_rows(grad_gate_val, w_gate) + mat_rows(grad_up_val, w_up)
    grad_second = lax.psum(mid_partial, "tp")
    grad_resid_part, _ = mid_pull(grad_second)
    _, quarter_pull = jax.vjp(row_norm, own_share(residual), mid_gain)
    mid_gain_part = quarter_pull(own_share(grad_second))[1]
    grad_residual = grad_y + grad_resid_part
    grad_branch = grad_residual.astype(jnp.bfloat16)
    grad_w_out = mat_weight(attended, grad_branch)
    grad_attended = mat_rows(grad_branch, w_out)
    grad_heads_out, grad_gain_head, grad_gate_heads = gated_pull(
        grad_attended.reshape(row_count, head_count, DH)
    )
    grad_gate_raw = grad_gate_heads.reshape(row_count, local_width).astype(jnp.bfloat16)
    grad_groups = grad_heads_out.reshape(groups, GROUP, head_count, DH)
    inclusive = jnp.tril(jnp.ones((GROUP, GROUP), jnp.float32))
    scores = jnp.einsum("nihd,njhd->nhij", q_groups, k_groups, precision=HIGHEST) * inclusive
    pushed = jnp.einsum("nhij,nihe->nhje", scores, grad_groups, precision=HIGHEST)
    direct = jnp.einsum("nihd,nihe->nhde", q_groups, grad_groups, precision=HIGHEST)
    direct = direct - jnp.einsum("nhcd,nhce->nhde", key_mix, pushed, precision=HIGHEST)
    state_flows = direct * keep_state
    (back_map, back_grad), (suffix_maps, suffix_grads) = lax.scan(
        link_step, (eye_heads, zero_heads), (jnp.swapaxes(transit, 2, 3), state_flows), reverse=True
    )
    exit_maps = prefix((back_map, back_grad), "seq", compose, (eye_heads, zero_heads))
    state_grads = (
        jnp.einsum("nhij,hjk->nhik", suffix_maps, exit_maps[1], precision=HIGHEST) + suffix_grads
    )
    _, group_pull = jax.vjp(
        lambda q_in, k_in, v_in, b_in: group_full(q_in, k_in, v_in, b_in, start_states),
        q_groups,
        k_groups,
        v_groups,
        b_groups,
    )
    grad_q, grad_k, grad_v, grad_b = group_pull((grad_groups, state_grads))
    grad_beta_raw = (
        grad_b.reshape(row_count, head_count) * live_col * beta_sig * (1.0 - beta_sig)
    ).astype(jnp.bfloat16)
    grad_conv_out = act_pull(
        (
            grad_q.reshape(row_count, head_count, DH),
            grad_k.reshape(row_count, head_count, DH),
            grad_v.reshape(row_count, head_count, DH),
        )
    )[0]
    grad_ext, grad_taps = conv_pull(grad_conv_out)
    incoming = shifted(grad_ext[: KW - 1], "seq", -1)
    grad_projected = jnp.concatenate(
        [grad_ext[KW - 1 : row_count], grad_ext[row_count:] + incoming], axis=0
    ).astype(jnp.bfloat16)
    grad_proj_cat = mat_weight(hidden, grad_projected)
    grad_w_gate_out = mat_weight(hidden, grad_gate_raw)
    grad_w_beta = mat_weight(hidden, grad_beta_raw)
    hidden_partial = (
        mat_rows(grad_projected, proj_cat)
        + mat_rows(grad_gate_raw, w_gate_out)
        + mat_rows(grad_beta_raw, w_beta)
    )
    grad_hidden, head_gain_sum, mid_gain_sum = lax.psum(
        (hidden_partial, grad_gain_head, mid_gain_part), "tp"
    )
    grad_in_part, grad_gain_in = in_pull(grad_hidden)
    grad_input = grad_residual + grad_in_part
    slice_width = model_width // tp_count
    head_slice = DH // tp_count
    in_gain_local = lax.dynamic_slice_in_dim(grad_gain_in, tp_rank * slice_width, slice_width)
    mid_gain_local = lax.dynamic_slice_in_dim(mid_gain_sum, tp_rank * slice_width, slice_width)
    head_gain_local = lax.dynamic_slice_in_dim(head_gain_sum, tp_rank * head_slice, head_slice)
    grad_q_weight = grad_proj_cat[:, :local_width]
    grad_k_weight = grad_proj_cat[:, local_width : 2 * local_width]
    grad_v_weight = grad_proj_cat[:, 2 * local_width :]
    grad_q_taps = grad_taps[:, :local_width]
    grad_k_taps = grad_taps[:, local_width : 2 * local_width]
    grad_v_taps = grad_taps[:, 2 * local_width :]
    summed_all = lax.psum(
        (
            in_gain_local,
            grad_q_weight,
            grad_k_weight,
            grad_v_weight,
            grad_q_taps,
            grad_k_taps,
            grad_v_taps,
            grad_w_beta,
            grad_w_gate_out,
            head_gain_local,
            grad_w_out,
            mid_gain_local,
            grad_w_gate,
            grad_w_up,
            grad_w_down,
        ),
        "seq",
    )
    return (
        block_out,
        grad_input,
        summed_all[0],
        summed_all[1],
        summed_all[2],
        summed_all[3],
        summed_all[4],
        summed_all[5],
        summed_all[6],
        summed_all[7],
        summed_all[8],
        summed_all[9],
        summed_all[10],
        summed_all[11],
        summed_all[12],
        summed_all[13],
        summed_all[14],
    )


def solution(mesh):
    return jax.shard_map(
        shards,
        mesh=mesh,
        in_specs=(
            P("seq", None),
            P(),
            P(),
            P(),
            P(None, "tp"),
            P(None, "tp"),
            P(None, "tp"),
            P(None, "tp"),
            P(None, "tp"),
            P(None, "tp"),
            P(None, "tp"),
            P(None, "tp"),
            P(),
            P("tp", None),
            P(),
            P(None, "tp"),
            P(None, "tp"),
            P("tp", None),
            P("seq", None),
        ),
        out_specs=(
            P("seq", None),
            P("seq", None),
            P("tp"),
            P(None, "tp"),
            P(None, "tp"),
            P(None, "tp"),
            P(None, "tp"),
            P(None, "tp"),
            P(None, "tp"),
            P(None, "tp"),
            P(None, "tp"),
            P("tp"),
            P("tp", None),
            P("tp"),
            P(None, "tp"),
            P(None, "tp"),
            P("tp", None),
        ),
        check_vma=False,
    )
```

profile of v0, /device:TPU:0, one launch (start us, length us, event | category | flops | bytes accessed | tf_op | source)
XLA Modules:
  0.0 1160.1 jit_solution(910830581205448567)
XLA Ops:
  13.9 4.9 collective-permute-start
  25.5 5.6 fusion.46
  41.2 79.4 %custom-call.13 = f32[8,2,1,64,64]{3,4,2,1,0:T(8,128)S(1)} custom-call(f32[8,2,1,64,64]{4,3,2,1,0:T(8,128)} %fusion.73), custom_call_target="InvertDiagBlocksLowerTriangular" | custom-call | tf_op jit(solution)/shard_map/jit(_solve_triangular)/vmap(vmap())/triangular_solve/custom-call.1 | solution.py:125
  124.8 3.1 fusion.84
  127.9 3.0 fusion.147
  133.5 3.0 fusion.146
  139.0 45.6 %while.67 = (s32[]{:T(128)}, f32[2,128,128]{2,1,0:T(8,128)S(1)}, f32[2,128,128]{2,1,0:T(8,128)}, f32[8,2,128,128]{3,2,1,0:T(8,128)}, f32[8,2,128,128]{2,3,1,0:T(...) while((s32[]{:T(128)}, f32[2,128,128]{2,1,0:T(8,128)S(1)}, ...), condition=%wide.region_6.8_spmd.clone, body=%wide.region_5.7_spmd.clone.sunk | while | flops 100761600 | bytes 2492027 | solution.py:242
  202.3 23.7 %all-gather.7.cloned.1.call-done = f32[16,128,128]{2,1,0:T(8,128)} async-done(((f32[2,128,128]{2,1,0:T(8,128)}), f32[16,128,128]{2,1,0:T(8,128)}) %all-gather.7.cloned.1.call-update) | async-done | bytes 1048592 | tf_op jit(solution)/shard_map/all_gather | solution.py:25
  226.0 41.6 %all-gather.9.cloned.1.call-done = f32[16,128,128]{2,1,0:T(8,128)} async-done(((f32[2,128,128]{2,1,0:T(8,128)}), f32[16,128,128]{2,1,0:T(8,128)}) %all-gather.9.cloned.1.call-update) | async-done | bytes 1048592 | tf_op jit(solution)/shard_map/all_gather | solution.py:25
  273.9 2.9 multiply_reduce_fusion.13
  287.8 58.0 %all-reduce.20.cloned.1.call-done = f32[512,1024]{1,0:T(8,128)} async-done(((f32[512,1024]{1,0:T(8,128)}), f32[512,1024]{1,0:T(8,128)}) %all-reduce.20.cloned.1.call-update) | async-done | bytes 2097168 | tf_op jit(solution)/shard_map/psum | solution.py:255
  365.2 3.4 fusion.169
  368.7 41.3 %all-reduce.22.cloned.1.call-done = f32[512,1024]{1,0:T(8,128)} async-done(((f32[512,1024]{1,0:T(8,128)}), f32[512,1024]{1,0:T(8,128)}) %all-reduce.22.cloned.1.call-update) | async-done | bytes 2097168 | tf_op jit(solution)/shard_map/psum | solution.py:277
  438.2 53.3 %while.68 = (s32[]{:T(128)}, f32[2,128,128]{2,1,0:T(8,128)S(1)}, f32[2,128,128]{2,1,0:T(8,128)}, f32[8,2,128,128]{3,2,0,1:T(8,128)}, f32[8,2,128,128]{2,3,0,1:T(...) while((s32[]{:T(128)}, f32[2,128,128]{2,1,0:T(8,128)S(1)}, ...), condition=%wide.region_18.20_spmd.clone, body=%wide.region_17.19_spmd.clone.sunk | while | flops 100761600 | bytes 3014808 | solution.py:296
  492.5 31.4 %all-gather.3 = bf16[16,128,128]{2,1,0:T(8,128)(2,1)S(1)} all-gather(bf16[2,128,128]{2,1,0:T(8,128)(2,1)S(1)} %convert_element_type.180), channel_id=5, replica_groups=mesh['seq'=8,'tp'=4] {'seq'}, dimensions={0}, use_global_device_ids=true | all-gather | bytes 589824 | tf_op jit(solution)/shard_map/all_gather | solution.py:39
  523.9 33.3 %all-gather.2 = bf16[16,128,128]{2,1,0:T(8,128)(2,1)} all-gather(bf16[2,128,128]{2,1,0:T(8,128)(2,1)S(1)} %convert_element_type.179), channel_id=4, replica_groups=mesh['seq'=8,'tp'=4] {'seq'}, dimensions={0}, use_global_device_ids=true | all-gather | bytes 589824 | tf_op jit(solution)/shard_map/all_gather | solution.py:39
  557.2 8.9 while.69
  599.4 3.1 collective-permute-done.1
  606.1 3.7 fusion.176
  622.6 7.1 all-reduce.13
  630.3 59.8 %all-reduce.26.cloned.1.call-done = (f32[512,1024]{1,0:T(8,128)}, f32[512,1024]{1,0:T(8,128)}) async-done(((f32[512,1024]{1,0:T(8,128)}, f32[512,1024]{1,0:T(8,128)}), (f32[512,1024]{1,0:T(8,128)}, f32[512,1024]{1,0:T(8,128)})) %all-reduce.26.cloned.1.call-update) | async-done | bytes 4194320 | tf_op jit(solution)/shard_map/psum | solution.py:265
  692.5 39.3 %all-reduce.11 = (f32[256]{0:T(256)}, f32[4,256]{1,0:T(4,128)}, f32[4,256]{1,0:T(4,128)}, f32[4,256]{1,0:T(4,128)}, f32[1024,2]{0,1:T(2,128)}, /*index=5*/f32[32]{0:T(128)}, f32[256]{0:T(256)}) all-reduce(f32[256]{0:T(256)S(1)} %dynamic_slice.69, f32[4,256]{1,0:T(4,128)S(1)} %get-tuple-element.653, ...), channel_id=1, replica_groups=mesh['seq'=8,'tp'=4] {'seq'}, use_global_device_ids=true, to_apply=%region_29.32 | all-reduce | flops 5664 | bytes 45312 | tf_op jit(solution)/shard_map/psum | solution.py:350
  731.8 2.9 multiply_convert_fusion
  736.6 400.9 %all-reduce.24.cloned.1.call-done = (f32[1024,256]{1,0:T(8,128)}, f32[1024,256]{1,0:T(8,128)}, f32[1024,256]{1,0:T(8,128)}, f32[1024,256]{1,0:T(8,128)}, f32[256...) async-done(((f32[1024,256]{1,0:T(8,128)}, f32[1024,256]{1,0:T(8,128)}, f32[1024,256]{1,0:T(8,128)}, f32[1024,256]{1,0:T(8,128)}, ...) | async-done | bytes 13893648 | tf_op jit(solution)/shard_map/psum | solution.py:350
  (674 shorter events, 291.5 us)
Async XLA Ops:
  7.2 345.0 %copy-start = (bf16[704,1024]{1,0:T(8,128)(2,1)S(1)}, bf16[704,1024]{1,0:T(8,128)(2,1)}, u32[]{:S(2)}) copy-start(bf16[704,1024]{1,0:T(8,128)(2,1)} %param.50) | copy-start | bytes 4325380
  7.2 218.7 %all-gather.7.cloned.1.call-start = ((), (), s32[]{:S(2)}) async-start(), calls=%async_computation.2 | async-start | bytes 1179648 | tf_op jit(solution)/shard_map/all_gather | solution.py:25
  9.5 13.2 %copy-start.134 = (f32[512]{0:T(512)}, f32[512]{0:T(512)S(1)}, u32[]{:S(2)}) copy-start(f32[512]{0:T(512)S(1)} %fusion.140) | copy-start | bytes 6148
  10.2 12.5 %copy-start.112 = (f32[1024]{0:T(1024)}, f32[1024]{0:T(1024)S(1)}, u32[]{:S(2)}) copy-start(f32[1024]{0:T(1024)S(1)} %convert_element_type.153) | copy-start | bytes 12292
  11.6 10.8 copy-start.150
  11.6 10.8 copy-start.151
  11.6 10.8 copy-start.152
  11.6 11.1 copy-start.144
  13.9 11.6 collective-permute-start
  33.3 165.7 %copy-start.2 = (f32[8,64,2,128]{3,2,1,0:T(2,128)}, f32[8,64,2,128]{3,2,1,0:T(2,128)S(1)}, u32[]{:S(2)}) copy-start(f32[8,64,2,128]{3,2,1,0:T(2,128)S(1)} %reshape.427) | copy-start | bytes 1572868
  185.4 82.2 %all-gather.9.cloned.1.call-start = ((), (), s32[]{:S(2)}) async-start(), calls=%async_computation.3 | async-start | bytes 1179648 | tf_op jit(solution)/shard_map/all_gather | solution.py:25
  186.1 159.7 %all-reduce.20.cloned.1.call-start = ((), (), s32[]{:S(2)}) async-start(), calls=%async_computation | async-start | bytes 4194304 | tf_op jit(solution)/shard_map/psum | solution.py:255
  189.3 13.0 %copy-start.18 = (f32[8,64,2,128]{3,2,1,0:T(2,128)}, f32[8,64,2,128]{3,2,1,0:T(2,128)S(1)}, u32[]{:S(2)}) copy-start(f32[8,64,2,128]{3,2,1,0:T(2,128)S(1)} %reshape.431) | copy-start | bytes 1572868
  286.6 123.4 %all-reduce.22.cloned.1.call-start = ((), (), s32[]{:S(2)}) async-start(), calls=%async_computation.1 | async-start | bytes 4194304 | tf_op jit(solution)/shard_map/psum | solution.py:277
  358.4 331.7 %all-reduce.26.cloned.1.call-start = ((), (), s32[]{:S(2)}) async-start(), calls=%async_computation.5 | async-start | bytes 8388608 | tf_op jit(solution)/shard_map/psum | solution.py:265
  368.7 43.4 %copy-start.139 = (f32[512]{0:T(512)S(1)}, f32[512]{0:T(512)}, u32[]{:S(2)}) copy-start(f32[512]{0:T(512)} %copy-done.138) | copy-start | bytes 6148
  368.7 43.4 %copy-start.51 = (bf16[512,1024]{1,0:T(8,128)(2,1)S(1)}, bf16[512,1024]{1,0:T(8,128)(2,1)}, u32[]{:S(2)}) copy-start(bf16[512,1024]{1,0:T(8,128)(2,1)} %param.51) | copy-start | bytes 3145732
  368.7 43.4 %copy-start.105 = (f32[1024]{0:T(1024)S(1)}, f32[1024]{0:T(1024)}, u32[]{:S(2)}) copy-start(f32[1024]{0:T(1024)} %convert_element_type.169) | copy-start | bytes 12292
  368.7 43.4 %copy-start.108 = (f32[512]{0:T(512)S(1)}, f32[512]{0:T(512)}, u32[]{:S(2)}) copy-start(f32[512]{0:T(512)} %copy-done.106) | copy-start | bytes 6148
  368.7 43.4 %copy-start.141 = (f32[512]{0:T(512)S(1)}, f32[512]{0:T(512)}, u32[]{:S(2)}) copy-start(f32[512]{0:T(512)} %copy-done.140) | copy-start | bytes 6148
  491.6 65.7 %copy-start.42 = (f32[2,128,128]{2,1,0:T(8,128)S(1)}, f32[2,128,128]{2,1,0:T(8,128)}, u32[]{:S(2)}) copy-start(f32[2,128,128]{2,1,0:T(8,128)} %custom-call.12) | copy-start | bytes 393220
  596.9 5.6 collective-permute-start.1
  604.9 532.6 %all-reduce.24.cloned.1.call-start = ((), (), s32[]{:S(2)}) async-start(), calls=%async_computation.4 | async-start | bytes 27787264 | tf_op jit(solution)/shard_map/psum | solution.py:350
  690.1 41.7 %copy-start.137 = (f32[512]{0:T(512)S(1)}, f32[512]{0:T(512)}, u32[]{:S(2)}) copy-start(f32[512]{0:T(512)} %copy-done.136) | copy-start | bytes 6148
  (143 other events, 384.8 us)
Sparse Core Ops, SparseCore 0:
  185.5 40.4 all-gather.6
  228.7 38.8 all-gather.8
  286.7 59.0 all-reduce.19
  358.5 51.4 all-reduce.21
  605.0 85.0 all-reduce.25
  698.3 439.1 all-reduce.23
where the time goes:
time: 1170 us; the launch traced here: 1160 us
  waiting for transfers between devices  629 us (54%)
  matrix products  148 us (13%)
  other arithmetic  127 us (11%)
  local copies, waits for them, and re-layouts  121 us (10%)
  blocking collectives  111 us (9%)
  between operations  16.3 us (1%)
    psum x1, waiting for transfers between devices, shards(): lax.psum((in_gain_local, grad_q_weight, grad_k_weight, grad_v_weight, gra...  401 us
    another operation x5, other arithmetic, wy_parts(): jax.scipy.linalg.solve_triangular(system, scaled_keys, lower=True, unit_d...  82.4 us
    all_gather x2, waiting for transfers between devices, entering(): gathered = jax.tree.map(lambda a: lax.all_gather(a, axis), part)  65.3 us
    all_gather x2, blocking collectives, prefix(): lax.all_gather(part.astype(kind), axis)  64.7 us
    psum x1, waiting for transfers between devices, shards(): down_val = lax.psum(down_terms, 'tp')  59.8 us
    psum x1, waiting for transfers between devices, shards(): residual = inputs + lax.psum(branch_terms, 'tp')  58 us
    psum x1, waiting for transfers between devices, shards(): grad_second = lax.psum(mid_partial, 'tp')  41.3 us
    psum x1, blocking collectives, shards(): lax.psum((in_gain_local, grad_q_weight, grad_k_weight, grad_v_weight, gra...  39.3 us
  transfers between devices with their start and end apart: 8, of which 7 were waited for; matrix products, arithmetic and copies ran while one was open for 5% of the time, Pallas kernels for 0%

commit v1 on v0

v1 whole, which is shorter than its diff:
```python
import jax
import jax.numpy as jnp
from jax import lax
from jax.experimental import pallas as pl
from jax.experimental.pallas import tpu as pltpu
from jax.sharding import PartitionSpec as P

DH = 128
KW = 4
GROUP = 64
TAIL = 16
LANES = 128

row_epsilon = 1e-06
head_epsilon = 1e-05
unit_epsilon = 1e-06
f32 = jnp.float32
bf16 = jnp.bfloat16


def dot(a, b, ca=1, cb=0):
    return lax.dot_general(a, b, (((ca,), (cb,)), ((), ())), preferred_element_type=f32)


def halves(a):
    high = a.astype(bf16)
    return high, (a - high.astype(f32)).astype(bf16)


def fdot(a, b, ca=1, cb=0):
    ah, al = halves(a)
    bh, bl = halves(b)
    return dot(
        jnp.concatenate([ah, al, ah], axis=ca), jnp.concatenate([bh, bh, bl], axis=cb), ca, cb
    )


def iota(shape, axis):
    return lax.broadcasted_iota(jnp.int32, shape, axis)


def rows_of(block, size):
    return pl.ds(pl.multiple_of(block * size, size), size)


def run(kernel, name, outs, args, smem=(), smem_out=(), hbm=(), scratch=(), flops=0, vmem=8):
    shapes = [jax.ShapeDtypeStruct(s, d) for s, d in outs]
    total = sum(a.size * a.dtype.itemsize for a in args)
    total += sum(s.size * s.dtype.itemsize for s in shapes)
    spaces = [
        pltpu.SMEM if i in smem else pltpu.HBM if i in hbm else pltpu.VMEM
        for i in range(len(args))
    ]
    return pl.pallas_call(
        kernel,
        name=name,
        out_shape=shapes,
        in_specs=[pl.BlockSpec(memory_space=space) for space in spaces],
        out_specs=[
            pl.BlockSpec(memory_space=pltpu.SMEM if i in smem_out else pltpu.VMEM)
            for i in range(len(outs))
        ],
        scratch_shapes=list(scratch),
        compiler_params=pltpu.CompilerParams(vmem_limit_bytes=vmem << 20),
        cost_estimate=pl.CostEstimate(flops=flops, bytes_accessed=total, transcendentals=0),
    )(*args)


def wide_gain(ref):
    return ref[...].astype(f32).reshape(1, ref.shape[0])


def live_mask(meta, block, size):
    parts = size // GROUP
    row = iota((size, 1), 0)
    limit = jnp.full((size, 1), 0, jnp.int32) + meta[1, block * parts]
    for part in range(1, parts):
        limit = jnp.where(row >= part * GROUP, meta[1, block * parts + part] + part * GROUP, limit)
    return row < limit


def rms_rows(values, gain):
    factor = lax.rsqrt(jnp.mean(values * values, axis=-1, keepdims=True) + row_epsilon)
    return values * factor * gain


def pre_kernel(first, tp, seq_groups, seq_pads, xh, coth, gain, wqh, wkh, wvh, wgh, wb, hidden, proj, gate, beta, grad_down, x_own, gd_own, meta, x, cot, wq, wk, wv, wg, sems):
    loads = [
        pltpu.make_async_copy(src, dst, sems.at[i])
        for i, (src, dst) in enumerate(
            ((xh, x), (wqh, wq), (wkh, wk), (wvh, wv), (wgh, wg), (coth, cot))
        )
    ]
    for load in loads:
        load.start()
    groups = x.shape[0] // GROUP
    for n in range(groups):
        meta[0, n] = 0
        meta[1, n] = 0

    def one(s, start):
        count = seq_groups[s]
        length = count * GROUP - seq_pads[s]
        for n in range(groups):
            gid = first[0] + n
            inside = (gid >= start) & (gid < start + count)
            here = jnp.clip(length - (gid - start) * GROUP, 0, GROUP)
            meta[0, n] = jnp.where(gid == start, 1, meta[0, n])
            meta[1, n] = jnp.where(inside, here, meta[1, n])
        return start + count

    lax.fori_loop(0, seq_groups.shape[0], one, jnp.int32(0))
    width = wq.shape[1]
    tile = 256
    share = x_own.shape[0]
    scale = wide_gain(gain)
    loads[0].wait()
    for t in range(x.shape[0] // tile):
        rows = slice(t * tile, (t + 1) * tile)
        hidden[rows] = rms_rows(x[rows].astype(f32), scale).astype(bf16)
    x_own[...] = x[rows_of(tp[0], share)]
    for t in range(x.shape[0] // tile):
        rows = slice(t * tile, (t + 1) * tile)
        beta[rows] = dot(hidden[rows], wb[...], 1, 1)
    for i, w in enumerate((wq, wk, wv, wg)):
        loads[1 + i].wait()
        for t in range(x.shape[0] // tile):
            rows = slice(t * tile, (t + 1) * tile)
            got = dot(hidden[rows], w[...])
            if i < 3:
                proj[rows, i * width : (i + 1) * width] = got
            else:
                gate[rows] = got
    loads[5].wait()
    for t in range(x.shape[0] // tile):
        rows = slice(t * tile, (t + 1) * tile)
        live = live_mask(meta, t, tile)
        grad_down[rows] = jnp.where(live, cot[rows].astype(f32), 0.0).astype(bf16)
    gd_own[...] = grad_down[rows_of(tp[0], share)]


def beta_col(beta, meta, n, h):
    raw = beta[pl.ds(pl.multiple_of(n * GROUP, GROUP), GROUP), h : h + 1]
    sig = jax.nn.sigmoid(raw)
    live = iota((GROUP, 1), 0) < meta[1, n]
    return jnp.where(live, sig, 0.0), sig, live


def unit(rows):
    return rows * lax.rsqrt(jnp.sum(rows * rows, axis=-1, keepdims=True) + unit_epsilon)


def tri_inverse(systems):
    size = systems[0].shape[0]
    eye = (iota((size, size), 0) == iota((size, size), 1)).astype(f32)
    blocks = [[eye[r : r + 8] for r in range(0, size, 8)] for _ in systems]
    lower = [[system[r : r + 8] for r in range(0, size, 8)] for system in systems]
    for j in range(size - 1):
        for low, part in zip(lower, blocks):
            line = part[j // 8][j % 8 : j % 8 + 1]
            for r in range((j + 1) // 8, size // 8):
                part[r] = part[r] - low[r][:, j : j + 1] * line
    return [jnp.concatenate(part, axis=0) for part in blocks]


def tap_table(*tables):
    values = [table[...].astype(f32) for table in tables]
    parts = values[0].shape[1] // DH
    return lambda j, c: values[c // parts][j : j + 1, (c % parts) * DH : (c % parts + 1) * DH]


def mix_kernel(meta, proj, tail, gain, wqh, wkh, wvh, cq, ck, cv, beta, ext, conv, qkv, wmix, umix, inv, score, amap, zst, dev, last, mout, oloc, badd, wq, wk, wv, sems):
    groups = proj.shape[0] // GROUP
    width = wq.shape[1]
    heads = width // DH
    loads = [
        pltpu.make_async_copy(src, dst, sems.at[i])
        for i, (src, dst) in enumerate(((wqh, wq), (wkh, wk), (wvh, wv)))
    ]
    for load in loads:
        load.start()
    ext[TAIL:] = proj[...]
    row = iota((GROUP, 1), 0)
    taps = tap_table(cq, ck, cv)
    low = rms_rows(tail[...].astype(f32), wide_gain(gain)).astype(bf16)

    def front(n):
        base = pl.multiple_of(n * GROUP, GROUP)
        for c in range(3 * heads):
            lanes = slice(c * DH, (c + 1) * DH)
            win = ext[pl.ds(pl.multiple_of(base + TAIL - 8, 8), GROUP + 8), lanes]
            acc = taps(KW - 1, c) * win[8:]
            for d in range(1, KW):
                part = jnp.where(row < meta[0, n] * d, 0.0, win[8 - d : 8 - d + GROUP])
                acc = acc + taps(KW - 1 - d, c) * part
            conv[pl.ds(base, GROUP), lanes] = acc
            acted = acc * jax.nn.sigmoid(acc)
            qkv[pl.ds(base, GROUP), lanes] = unit(acted) if c < 2 * heads else acted

    pl.loop(1, groups)(front)
    for i, w in enumerate((wq, wk, wv)):
        loads[i].wait()
        ext[0:TAIL, i * width : (i + 1) * width] = dot(low, w[...])
    front(0)
    r64 = iota((GROUP, GROUP), 0)
    c64 = iota((GROUP, GROUP), 1)
    eye = (iota((DH, DH), 0) == iota((DH, DH), 1)).astype(f32)

    def load(n, h):
        rows = pl.ds(pl.multiple_of(n * GROUP, GROUP), GROUP)
        return [qkv[rows, (i * heads + h) * DH : (i * heads + h + 1) * DH] for i in range(3)]

    def local(i, _):
        chains = [(2 * i + j, h) for j in range(2) for h in range(heads)]
        systems = []
        kept = []
        for n, h in chains:
            q, k, v = load(n, h)
            b = beta_col(beta, meta, n, h)[0]
            both = fdot(jnp.concatenate([k * b, q], axis=0), k, 1, 1)
            systems.append(jnp.where(r64 > c64, both[:GROUP], 0.0))
            score[n * heads + h] = jnp.where(r64 >= c64, both[GROUP:], 0.0)
            kept.append((k, b, v))
        inverses = tri_inverse(systems)
        for (n, h), inverse, (k, b, v) in zip(chains, inverses, kept):
            rows = pl.ds(pl.multiple_of(n * GROUP, GROUP), GROUP)
            inv[n * heads + h] = inverse
            wu = fdot(inverse, jnp.concatenate([k * b, v * b], axis=1))
            wmix[rows, h * DH : (h + 1) * DH] = wu[:, :DH]
            umix[rows, h * DH : (h + 1) * DH] = wu[:, DH:]
            kwu = fdot(k, wu, 0, 0)
            amap[n * heads + h] = eye - kwu[:, :DH]
            badd[n * heads + h] = kwu[:, DH:]
        return 0

    lax.fori_loop(0, groups // 2, local, 0)
    for h in range(heads):
        dev[h, :, :DH] = eye
        dev[h, :, DH:] = jnp.zeros((DH, DH), f32)

    def chain(n, _):
        keep = 1.0 - meta[0, n].astype(f32)
        for h in range(heads):
            start = dev[h] * keep
            zst[n * heads + h] = start
            moved = fdot(amap[n * heads + h], start)
            dev[h, :, :DH] = moved[:, :DH]
            dev[h, :, DH:] = moved[:, DH:] + badd[n * heads + h]
        return 0

    lax.fori_loop(0, groups, chain, 0)
    last[...] = dev[:, :, DH:]

    def outs(i, _):
        for n, h in [(2 * i + j, h) for j in range(2) for h in range(heads)]:
            rows = pl.ds(pl.multiple_of(n * GROUP, GROUP), GROUP)
            lanes = slice(h * DH, (h + 1) * DH)
            q = qkv[rows, lanes]
            both = fdot(jnp.concatenate([q, wmix[rows, lanes]], axis=0), zst[n * heads + h])
            lower = jnp.concatenate([-both[GROUP:, :DH], umix[rows, lanes] - both[GROUP:, DH:]], axis=1)
            made = both[:GROUP] + fdot(score[n * heads + h], lower)
            mout[rows, lanes] = made[:, :DH]
            oloc[rows, lanes] = made[:, DH:]
        return 0

    lax.fori_loop(0, groups // 2, outs, 0)


def fold_hops(hops, h):
    state = hops[-1][h]
    for hop in hops[-2::-1]:
        state = hop[h, :, DH:] + fdot(hop[h, :, :DH], state)
    return state


def out_kernel(hop_count, tp, *refs):
    hops, refs = refs[:hop_count], refs[hop_count:]
    mout, oloc, gate, nh, wo, heads_out, att, send, keep, entry = refs
    heads = gate.shape[1] // DH
    states = [fold_hops(hops, h) for h in range(heads)]
    for h in range(heads):
        entry[h] = states[h]
    share = mout.shape[0] // 4
    for rel in range(4):
        rows = rows_of(tp[0] ^ rel, share)
        lows = []
        for h in range(heads):
            lanes = slice(h * DH, (h + 1) * DH)
            o = oloc[rows, lanes] + fdot(mout[rows, lanes], states[h])
            heads_out[rows, lanes] = o
            factor = lax.rsqrt(jnp.mean(o * o, axis=-1, keepdims=True) + head_epsilon)
            g = gate[rows, lanes]
            lows.append((o * factor * wide_gain(nh) * (g * jax.nn.sigmoid(g))).astype(bf16))
        low = jnp.concatenate(lows, axis=1)
        att[rows] = low
        part = dot(low, wo[...])
        if rel % 2:
            send[rel // 2] = part.astype(bf16)
        else:
            keep[rel // 2] = part


def states_kernel(entry, zst, qkv, wmix, umix, score, states, vnew, qeff):
    groups = qkv.shape[0] // GROUP
    heads = wmix.shape[1] // DH

    def one(i, _):
        for n, h in [(2 * i + j, h) for j in range(2) for h in range(heads)]:
            rows = pl.ds(pl.multiple_of(n * GROUP, GROUP), GROUP)
            lanes = slice(h * DH, (h + 1) * DH)
            at = n * heads + h
            s = zst[at, :, DH:] + fdot(zst[at, :, :DH], entry[h])
            states[at] = s
            w = wmix[rows, lanes]
            vnew[rows, lanes] = umix[rows, lanes] - fdot(w, s)
            qeff[rows, lanes] = qkv[rows, lanes] - fdot(score[at], w)
        return 0

    lax.fori_loop(0, groups // 2, one, 0)


def mid_kernel(x, kept, got, gain, residual, second):
    total = x[...].astype(f32) + kept[...] + got[...].astype(f32)
    residual[...] = total
    second[...] = rms_rows(total, wide_gain(gain)).astype(bf16)


def ffn_kernel(tp, s0, s1, s2, s3, grad_down, wg, wu, wd, second, inner, dgate, dup, down_send, down_keep, send, keep):
    share = s0.shape[0]
    for half, pair in enumerate(((s0, s1), (s2, s3))):
        sec = jnp.concatenate([pair[0][...], pair[1][...]], axis=0)
        blocks = [rows_of(tp[0] ^ (2 * half + j), share) for j in range(2)]
        gd = jnp.concatenate([grad_down[b] for b in blocks], axis=0)
        gv = dot(sec, wg[...], 1, 1)
        uv = dot(sec, wu[...], 1, 1)
        sig = jax.nn.sigmoid(gv)
        act = gv * sig
        inn = (act * uv).astype(bf16)
        gi = dot(gd, wd[...], 1, 1)
        dg = (gi * uv * (sig * (1.0 + gv * (1.0 - sig)))).astype(bf16)
        du = (gi * act).astype(bf16)
        for j, b in enumerate(blocks):
            part = slice(j * share, (j + 1) * share)
            second[b] = sec[part]
            inner[b] = inn[part]
            dgate[b] = dg[part]
            dup[b] = du[part]
        grad = dot(dg, wg[...]) + dot(du, wu[...])
        keep[half] = grad[:share]
        send[half] = grad[share:].astype(bf16)
        down = dot(inn, wd[...])
        down_keep[half] = down[:share]
        down_send[half] = down[share:].astype(bf16)


def turn_kernel(kept, got, residual, gain, grad_y, grad_residual, branch, gain_part):
    gs = kept[...] + got[...].astype(f32)
    v = residual[...]
    g = wide_gain(gain)
    r = lax.rsqrt(jnp.mean(v * v, axis=-1, keepdims=True) + row_epsilon)
    gain_part[...] = jnp.sum(gs * v * r, axis=0, keepdims=True)
    e = gs * g
    back = r * e - v * (r * r * r) * jnp.mean(e * v, axis=-1, keepdims=True)
    total = grad_y[...].astype(f32) + back
    grad_residual[...] = total
    branch[...] = total.astype(bf16)


def flow_kernel(tp, meta, b0, b1, b2, b3, wo, heads_out, gate, nh, qeff, amap, branch, dgate, dout, rst, dev, last, nh_part, flows):
    share = b0.shape[0]
    heads = gate.shape[1] // DH
    groups = gate.shape[0] // GROUP
    gains = jnp.zeros((1, DH), f32)
    for half, pair in enumerate(((b0, b1), (b2, b3))):
        both = jnp.concatenate([pair[0][...], pair[1][...]], axis=0)
        ga = dot(both, wo[...], 1, 1)
        for j in range(2):
            rows = rows_of(tp[0] ^ (2 * half + j), share)
            branch[rows] = pair[j][...]
            for h in range(heads):
                lanes = slice(h * DH, (h + 1) * DH)
                gz = ga[j * share : (j + 1) * share, lanes]
                o = heads_out[rows, lanes]
                g = gate[rows, lanes]
                gain = wide_gain(nh)
                r = lax.rsqrt(jnp.mean(o * o, axis=-1, keepdims=True) + head_epsilon)
                sig = jax.nn.sigmoid(g)
                act = g * sig
                e = gz * gain * act
                base = gz * o * r
                gains = gains + jnp.sum(base * act, axis=0, keepdims=True)
                dgate[rows, lanes] = (base * gain * (sig * (1.0 + g * (1.0 - sig)))).astype(bf16)
                dout[rows, lanes] = r * e - o * (r * r * r) * jnp.mean(e * o, axis=-1, keepdims=True)
    nh_part[...] = gains

    def local(i, _):
        for n, h in [(2 * i + j, h) for j in range(2) for h in range(heads)]:
            rows = pl.ds(pl.multiple_of(n * GROUP, GROUP), GROUP)
            lanes = slice(h * DH, (h + 1) * DH)
            flows[n * heads + h] = fdot(qeff[rows, lanes], dout[rows, lanes], 0, 0)
        return 0

    lax.fori_loop(0, groups // 2, local, 0)
    eye = (iota((DH, DH), 0) == iota((DH, DH), 1)).astype(f32)
    for h in range(heads):
        dev[h, :, :DH] = eye
        dev[h, :, DH:] = jnp.zeros((DH, DH), f32)

    def chain(i, _):
        n = groups - 1 - i
        keep = 1.0 - meta[0, n].astype(f32)
        for h in range(heads):
            at = n * heads + h
            later = dev[h]
            rst[at] = later
            moved = fdot(amap[at], later, 0, 0)
            dev[h, :, :DH] = moved[:, :DH] * keep
            dev[h, :, DH:] = (moved[:, DH:] + flows[at]) * keep
        return 0

    lax.fori_loop(0, groups, chain, 0)
    last[...] = dev[:, :, DH:]


def side_kernel(qkv, dout, vnew, states, score, ndo, dq, dk):
    heads = dout.shape[1] // DH
    groups = dout.shape[0] // GROUP
    lower = iota((GROUP, GROUP), 0) >= iota((GROUP, GROUP), 1)

    def one(i, _):
        for n, h in [(2 * i + j, h) for j in range(2) for h in range(heads)]:
            rows = pl.ds(pl.multiple_of(n * GROUP, GROUP), GROUP)
            lanes = slice(h * DH, (h + 1) * DH)
            at = n * heads + h
            q = qkv[rows, lanes]
            k = qkv[rows, (heads + h) * DH : (heads + h + 1) * DH]
            do = dout[rows, lanes]
            ndo[rows, lanes] = fdot(score[at], do, 0, 0)
            dn = jnp.where(lower, fdot(do, vnew[rows, lanes], 1, 1), 0.0)
            dq[rows, lanes] = fdot(do, states[at], 1, 1) + fdot(dn, k)
            dk[rows, lanes] = fdot(dn, q, 0, 0)
        return 0

    lax.fori_loop(0, groups // 2, one, 0)


def unit_back(a, grad):
    r = lax.rsqrt(jnp.sum(a * a, axis=-1, keepdims=True) + unit_epsilon)
    return r * grad - a * (r * r * r) * jnp.sum(a * grad, axis=-1, keepdims=True)


def back_kernel(hop_count, meta, *refs):
    hops, refs = refs[:hop_count], refs[hop_count:]
    rst, qkv, conv, ext, cq, ck, cv, beta, inv, states, vnew, ndo, dq, dk1, gp, last, halo, dbeta, dtaps, dc = refs
    taps = tap_table(cq, ck, cv)
    heads = ndo.shape[1] // DH
    groups = ndo.shape[0] // GROUP
    total = ndo.shape[0]
    exits = [fold_hops(hops, h) for h in range(heads)]
    strict = iota((GROUP, GROUP), 0) > iota((GROUP, GROUP), 1)
    lane = iota((GROUP, LANES), 1)
    dc[total:] = jnp.zeros((8, dc.shape[1]), f32)

    def one(i, _):
        for j in range(2):
            n = 2 * i + j
            rows = pl.ds(pl.multiple_of(n * GROUP, GROUP), GROUP)
            raws = jnp.zeros((GROUP, LANES), f32)
            for h in range(heads):
                at = n * heads + h
                lanes = [slice((p * heads + h) * DH, (p * heads + h + 1) * DH) for p in range(3)]
                k = qkv[rows, lanes[1]]
                v = qkv[rows, lanes[2]]
                b, sig, live = beta_col(beta, meta, n, h)
                ds = rst[at, :, DH:] + fdot(rst[at, :, :DH], exits[h])
                dvn = ndo[rows, lanes[0]] + fdot(k, ds)
                d = fdot(inv[at], dvn, 0, 0)
                vn = vnew[rows, lanes[0]]
                dstate = fdot(d, states[at], 1, 1)
                vds = fdot(vn, ds, 1, 1)
                da = jnp.where(strict, -fdot(d, vn, 1, 1), 0.0)
                dak = fdot(da, k)
                datk = fdot(da, k * b, 0, 0)
                dk = dk1[rows, lanes[0]] + vds + b * (dak - dstate) + datk
                db = jnp.sum(d * v + (dak - dstate) * k, axis=-1, keepdims=True)
                db = jnp.where(live, db * sig * (1.0 - sig), 0.0)
                raws = jnp.where(lane == h, db, raws)
                grads = (dq[rows, lanes[0]], dk, d * b)
                for p in range(3):
                    c = conv[rows, lanes[p]]
                    s = jax.nn.sigmoid(c)
                    grad = unit_back(c * s, grads[p]) if p < 2 else grads[p]
                    dc[rows, lanes[p]] = grad * (s * (1.0 + c * (1.0 - s)))
            dbeta[rows] = raws.astype(bf16)
        return 0

    lax.fori_loop(0, groups // 2, one, 0)
    row = iota((GROUP, 1), 0)
    dtaps[...] = jnp.zeros(dtaps.shape, f32)

    def masked(win, d, here, after):
        front = jnp.where(iota((GROUP, 1), 0) < here * d, 0.0, win[:GROUP])
        if after is None:
            return front
        back = jnp.where(iota((8, 1), 0) < after * d, 0.0, win[GROUP:])
        return jnp.concatenate([front, back], axis=0)

    def taps_back(n, _):
        base = pl.multiple_of(n * GROUP, GROUP)
        here = meta[0, n]
        after = meta[0, jnp.minimum(n + 1, groups - 1)]
        for c in range(3 * heads):
            lanes = slice(c * DH, (c + 1) * DH)
            win = dc[pl.ds(base, GROUP + 8), lanes]
            old = ext[pl.ds(pl.multiple_of(base + TAIL - 8, 8), GROUP + 8), lanes]
            acc = taps(KW - 1, c) * win[:GROUP]
            dtaps[KW - 1 : KW, lanes] += jnp.sum(win[:GROUP] * old[8:], axis=0, keepdims=True)
            for d in range(1, KW):
                part = masked(win, d, here, after)
                j = KW - 1 - d
                acc = acc + taps(j, c) * part[d : d + GROUP]
                dtaps[j : j + 1, lanes] += jnp.sum(
                    part[:GROUP] * old[8 - d : 8 - d + GROUP], axis=0, keepdims=True
                )
            gp[pl.ds(base, GROUP), lanes] = acc.astype(bf16)

            @pl.when(n == groups - 1)
            def _():
                last[:, lanes] = acc[GROUP - TAIL :]

        return 0

    lax.fori_loop(0, groups, taps_back, 0)
    zero = jnp.zeros((8, DH), f32)
    for c in range(3 * heads):
        lanes = slice(c * DH, (c + 1) * DH)
        win = dc[0:8, lanes]
        acc = zero
        for d in range(1, KW):
            part = jnp.where(iota((8, 1), 0) < meta[0, 0] * d, 0.0, win)
            j = KW - 1 - d
            acc = acc + taps(j, c) * jnp.concatenate([zero, part], axis=0)[d : d + 8]
        halo[:, lanes] = acc


def hid_kernel(tp, gp_in, last, incoming, dgate, dbeta, wq, wk, wv, wg, wb, gp, send, keep):
    total = gp.shape[0]
    width = wq.shape[1]
    gp[: total - TAIL] = gp_in[: total - TAIL]
    fixed = jnp.concatenate([last[: TAIL - 8], last[TAIL - 8 :] + incoming[...]], axis=0)
    gp[total - TAIL :] = fixed.astype(bf16)
    share = total // 4
    for half in range(2):
        blocks = [rows_of(tp[0] ^ (2 * half + j), share) for j in range(2)]
        cat = lambda ref: jnp.concatenate([ref[b] for b in blocks], axis=0)
        grads = cat(gp)
        acc = dot(cat(dgate), wg[...], 1, 1)
        small = cat(dbeta).astype(f32)
        for h in range(wb.shape[0]):
            acc = acc + small[:, h : h + 1] * wb[h : h + 1].astype(f32)
        for i, w in enumerate((wq, wk, wv)):
            acc = acc + dot(grads[:, i * width : (i + 1) * width], w[...], 1, 1)
        keep[half] = acc[:share]
        send[half] = acc[share:].astype(bf16)


def in_kernel(kept, got, x, gain, grad_residual, grad_in, gain_part):
    gh = kept[...] + got[...].astype(f32)
    v = x[...].astype(f32)
    g = wide_gain(gain)
    r = lax.rsqrt(jnp.mean(v * v, axis=-1, keepdims=True) + row_epsilon)
    gain_part[...] = jnp.sum(gh * v * r, axis=0, keepdims=True)
    e = gh * g
    back = r * e - v * (r * r * r) * jnp.mean(e * v, axis=-1, keepdims=True)
    grad_in[...] = (grad_residual[...] + back).astype(bf16)


def outblock_kernel(tp, meta, kept, got, residual, out):
    total = residual[...] + kept[...] + got[...].astype(f32)
    live = live_mask(meta, tp[0], total.shape[0])
    out[...] = jnp.where(live, total, 0.0).astype(bf16)


def place_kernel(tp, a0, a1, a2, a3, out):
    for rel, part in enumerate((a0, a1, a2, a3)):
        out[rows_of(tp[0] ^ rel, part.shape[0])] = part[...].astype(out.dtype)


def swap(value, bit, axis="tp"):
    count = lax.axis_size(axis)
    return lax.ppermute(value, axis, [(i, i ^ bit) for i in range(count)])


def add_kernel(keep, got, kept, send):
    half = kept.shape[0]
    kept[...] = keep[:half] + got[:half].astype(f32)
    send[...] = (keep[half:] + got[half:].astype(f32)).astype(bf16)


def last_kernel(keep, got, own):
    own[...] = (keep[...] + got[...].astype(f32)).astype(bf16)


def pack_kernel(a, b, out):
    half = a.shape[0]
    out[:half] = a[...]
    out[half:] = b[...]


def fold(keep, got, name):
    half = (keep.shape[0] // 2, *keep.shape[1:])
    return run(add_kernel, name, [(half, f32), (half, bf16)], [keep, got])


def scatter_sum(send, keep):
    kept, send = fold(keep, swap(send, 1), "fold_tp")
    return kept[0], swap(send, 2)[0]


def spread(place, keep, send, acc, base, rows):
    blocks = 2 * keep.shape[0]
    width = blocks.bit_length() - 1
    size = rows // blocks
    for m in range(blocks):
        at = sum(((m >> (i + 1)) & 1) << (width - 2 - i) for i in range(width - 1))
        block = acc[pl.ds(pl.multiple_of((m ^ place) * size, 8), size)]
        if m & 1:
            send[at, base : base + size] = block.astype(bf16)
        else:
            keep[at, base : base + size] = block


def grads_kernel(count, place, *refs):
    pairs, (keep, send, acc) = refs[: 2 * count], refs[2 * count :]
    base = 0
    for i in range(count):
        left, right = pairs[2 * i : 2 * i + 2]
        rows = left.shape[1]
        acc[:rows] = dot(left[...], right[...], 0, 0)
        spread(place[0], keep, send, acc, base, rows)
        base += rows // (2 * keep.shape[0])


def hidden_grads_kernel(place, hidden, gp, dgate, keep, send, acc):
    wide = gp.shape[1]
    rows = hidden.shape[1]
    acc[:, :wide] = dot(hidden[...], gp[...], 0, 0)
    acc[:, wide:] = dot(hidden[...], dgate[...], 0, 0)
    spread(place[0], keep, send, acc, 0, rows)


def grads(place, pairs, blocks, name):
    size = sum(p[0].shape[1] for p in pairs) // blocks
    most = max(p[0].shape[1] for p in pairs)
    cols = pairs[0][1].shape[1]
    half = (blocks // 2, size, cols)
    args = [a for p in pairs for a in p]
    return run(
        lambda *r: grads_kernel(len(pairs), *r),
        name,
        [(half, f32), (half, bf16)],
        [place, *args],
        smem=(0,),
        scratch=[pltpu.VMEM((most, cols), f32)],
        flops=2 * pairs[0][0].shape[0] * size * blocks * cols,
        vmem=16,
    )


def sum_seq(keep, send, blocks, tag):
    count = lax.axis_size("seq")
    step = 1
    while step < blocks // 2:
        keep, send = fold(keep, swap(send, step, "seq"), tag + "_fold")
        step *= 2
    got = swap(send, step, "seq")
    (own,) = run(last_kernel, tag + "_last", [(keep.shape, bf16)], [keep, got])
    more = blocks
    while more < count:
        own = (own.astype(f32) + swap(own, more, "seq").astype(f32)).astype(bf16)
        more *= 2
    while step > 1:
        twice = (2 * own.shape[0], *own.shape[1:])
        (own,) = run(pack_kernel, tag + "_pack", [(twice, bf16)], [own, swap(own, step, "seq")])
        step //= 2
    return own, swap(own, 1, "seq")


def settle(place, near, far, outs):
    blocks = 2 * near.shape[0]
    width = blocks.bit_length() - 1
    for m in range(blocks):
        at = sum(((m >> (i + 1)) & 1) << i for i in range(width - 1))
        at = sum(((at >> i) & 1) << (width - 2 - i) for i in range(width - 1))
        source = far if m & 1 else near
        row = 0
        for out, size, lanes in outs:
            out[pl.ds(pl.multiple_of((m ^ place) * size, 8), size)] = source[
                at, row : row + size, lanes
            ].astype(f32)
            row = row + size if lanes == slice(None) else row


def settle_kernel(place, near, far, *outs):
    sizes = [out.shape[0] // (2 * near.shape[0]) for out in outs]
    settle(place[0], near, far, [(o, n, slice(None)) for o, n in zip(outs, sizes)])


def settle_cols_kernel(place, near, far, *outs):
    size = near.shape[1]
    wide = outs[0].shape[1]
    settle(
        place[0],
        near,
        far,
        [(o, size, slice(i * wide, (i + 1) * wide)) for i, o in enumerate(outs)],
    )


def gather_rel(own):
    near = swap(own, 1)
    far = swap(own, 2)
    return own, near, far, swap(far, 1)


def shift(value, steps):
    count = lax.axis_size("seq")
    pairs = [(i, i + steps) for i in range(count) if 0 <= i + steps < count]
    return lax.ppermute(value, "seq", pairs)


def hops_of(dev, last, sign, reach):
    return [shift(dev, sign * k) for k in range(1, reach)] + [shift(last, sign * reach)]


def small_kernel(dtaps, dbeta, hidden, in_part, mid_part, head_part, taps_out, gains_out):
    wide = dtaps.shape[1]
    taps_out[...] = jnp.zeros(taps_out.shape, f32)
    taps_out[0:KW, :wide] = dtaps[...]
    product = dot(dbeta[...], hidden[...], 0, 0)
    taps_out[KW : KW + 4] = product[:4]
    gains_out[...] = jnp.zeros(gains_out.shape, f32)
    gains_out[0:1] = in_part[...]
    gains_out[1:2] = mid_part[...]
    gains_out[2:3, : head_part.shape[1]] = head_part[...]


def plus_kernel(a, b, out):
    out[...] = a[...] + b[...]


def plus(a, b):
    return run(plus_kernel, "plus", [(a.shape, f32)], [a, b])[0]


def shards(
    layer_input,
    seq_groups,
    seq_pads,
    norm_in,
    w_query,
    w_key,
    w_value,
    conv_query,
    conv_key,
    conv_value,
    w_beta,
    w_gate_out,
    norm_head,
    w_out,
    norm_mid,
    w_gate,
    w_up,
    w_down,
    cotangent,
):
    total, model = layer_input.shape
    width = w_query.shape[1]
    heads = width // DH
    groups = total // GROUP
    share = total // 4
    ffw = w_gate.shape[1]
    seq_count = lax.axis_size("seq")
    reach = max(1, seq_count // 4)
    tp_rank = lax.axis_index("tp")
    tp = tp_rank.astype(jnp.int32).reshape(1)
    blocks = min(8, seq_count)
    place = (lax.axis_index("seq") % blocks).astype(jnp.int32).reshape(1)
    first = (lax.axis_index("seq") * groups).astype(jnp.int32).reshape(1)
    taps = (conv_query, conv_key, conv_value)
    wb = w_beta.T
    tail = shift(layer_input[total - TAIL :], 1)
    chains = groups * heads
    wide = (total, width)
    mats = 2 * total * model
    weight = pltpu.VMEM((model, width), bf16)
    rows = pltpu.VMEM((total, model), bf16)

    hidden, proj, gate_raw, beta_raw, grad_down, x_own, gd_own, meta = run(
        pre_kernel,
        "pre",
        [
            ((total, model), bf16),
            ((total, 3 * width), f32),
            (wide, f32),
            ((total, heads), f32),
            ((total, model), bf16),
            ((share, model), bf16),
            ((share, model), bf16),
            ((2, groups), jnp.int32),
        ],
        [first, tp, seq_groups, seq_pads, layer_input, cotangent, norm_in, w_query, w_key, w_value, w_gate_out, wb],
        smem=(0, 1, 2, 3),
        smem_out=(7,),
        hbm=(4, 5, 7, 8, 9, 10),
        scratch=[rows, rows, weight, weight, weight, weight, pltpu.SemaphoreType.DMA((6,))],
        flops=mats * 4 * width,
        vmem=12,
    )
    ext, conv, qkv, wmix, umix, inv, score, amap, zst, dev, last, mout, oloc = run(
        mix_kernel,
        "mix",
        [
            ((total + TAIL, 3 * width), f32),
            ((total, 3 * width), f32),
            ((total, 3 * width), f32),
            (wide, f32),
            (wide, f32),
            ((chains, GROUP, GROUP), f32),
            ((chains, GROUP, GROUP), f32),
            ((chains, DH, DH), f32),
            ((chains, DH, 2 * DH), f32),
            ((heads, DH, 2 * DH), f32),
            ((heads, DH, DH), f32),
            (wide, f32),
            (wide, f32),
        ],
        [meta, proj, tail, norm_in, w_query, w_key, w_value, *taps, beta_raw],
        smem=(0,),
        hbm=(4, 5, 6),
        scratch=[pltpu.VMEM((chains, DH, DH), f32), weight, weight, weight, pltpu.SemaphoreType.DMA((3,))],
        flops=6 * mats * width,
    )
    hops = hops_of(dev, last, 1, reach)
    heads_out, attended, send, keep, entry = run(
        lambda *r: out_kernel(reach, *r),
        "out",
        [(wide, f32), (wide, bf16), ((2, share, model), bf16), ((2, share, model), f32), ((heads, DH, DH), f32)],
        [tp, *hops, mout, oloc, gate_raw, norm_head, w_out],
        smem=(0,),
        flops=mats * width,
    )
    kept, got = scatter_sum(send, keep)
    states, vnew, qeff = run(
        states_kernel,
        "states",
        [((chains, DH, DH), f32), (wide, f32), (wide, f32)],
        [entry, zst, qkv, wmix, umix, score],
        flops=mats * width,
    )
    x_own, states = lax.optimization_barrier((x_own, states))
    residual, second_own = run(
        mid_kernel,
        "mid",
        [((share, model), f32), ((share, model), bf16)],
        [x_own, kept, got, norm_mid],
    )
    second, inner, dgate, dup, down_send, down_keep, send, keep = run(
        ffn_kernel,
        "ffn",
        [
            ((total, model), bf16),
            ((total, ffw), bf16),
            ((total, ffw), bf16),
            ((total, ffw), bf16),
            ((2, share, model), bf16),
            ((2, share, model), f32),
            ((2, share, model), bf16),
            ((2, share, model), f32),
        ],
        [tp, *gather_rel(second_own), grad_down, w_gate.T, w_up.T, w_down],
        smem=(0,),
        flops=6 * mats * ffw,
        vmem=16,
    )
    keep_a, send_a = grads(place, ((inner, grad_down), (dgate, second)), blocks, "grads_a")
    kept, got = scatter_sum(send, keep)
    residual, send_a = lax.optimization_barrier((residual, send_a))
    near_a, far_a = sum_seq(keep_a, send_a, blocks, "a")
    grad_residual, branch_own, mid_part = run(
        turn_kernel,
        "turn",
        [((share, model), f32), ((share, model), bf16), ((1, model), f32)],
        [kept, got, residual, norm_mid, gd_own],
    )
    branch, dgate_raw, dout, rst, dev, last, head_part = run(
        flow_kernel,
        "flow",
        [
            ((total, model), bf16),
            (wide, bf16),
            (wide, f32),
            ((chains, DH, 2 * DH), f32),
            ((heads, DH, 2 * DH), f32),
            ((heads, DH, DH), f32),
            ((1, DH), f32),
        ],
        [tp, meta, *gather_rel(branch_own), w_out, heads_out, gate_raw, norm_head, qeff, amap],
        smem=(0, 1),
        scratch=[pltpu.VMEM((chains, DH, DH), f32)],
        flops=3 * mats * width,
    )
    hops = hops_of(dev, last, -1, reach)
    ndo, dq, dk = run(
        side_kernel,
        "side",
        [(wide, f32)] * 3,
        [qkv, dout, vnew, states, score],
        flops=mats * width,
    )
    keep_b, send_b = grads(place, ((dup, second), (attended, branch)), blocks, "grads_b")
    ndo, send_b = lax.optimization_barrier((ndo, send_b))
    near_b, far_b = sum_seq(keep_b, send_b, blocks, "b")
    gp, last, halo, dbeta, dtaps = run(
        lambda *r: back_kernel(reach, *r),
        "back",
        [
            ((total, 3 * width), bf16),
            ((TAIL, 3 * width), f32),
            ((8, 3 * width), f32),
            ((total, LANES), bf16),
            ((KW, 3 * width), f32),
        ],
        [meta, *hops, rst, qkv, conv, ext, *taps, beta_raw, inv, states, vnew, ndo, dq, dk],
        smem=(0,),
        scratch=[pltpu.VMEM((total + 8, 3 * width), f32)],
        flops=3 * mats * width,
    )
    incoming = shift(halo, -1)
    gp, send, keep = run(
        hid_kernel,
        "hid",
        [((total, 3 * width), bf16), ((2, share, model), bf16), ((2, share, model), f32)],
        [tp, gp, last, incoming, dgate_raw, dbeta, w_query, w_key, w_value, w_gate_out, wb],
        smem=(0,),
        flops=mats * 4 * width,
        vmem=12,
    )
    half = (blocks // 2, model // blocks, 4 * width)
    keep_c, send_c = run(
        hidden_grads_kernel,
        "grads_c",
        [(half, f32), (half, bf16)],
        [place, hidden, gp, dgate_raw],
        smem=(0,),
        scratch=[pltpu.VMEM((model, 4 * width), f32)],
        flops=mats * 4 * width,
        vmem=16,
    )
    near_c, far_c = sum_seq(keep_c, send_c, blocks, "c")
    kept, got = scatter_sum(send, keep)
    grad_in_own, in_part = run(
        in_kernel,
        "inp",
        [((share, model), bf16), ((1, model), f32)],
        [kept, got, x_own, norm_in, grad_residual],
    )
    (grad_input,) = run(
        place_kernel,
        "place_in",
        [((total, model), f32)],
        [tp, *gather_rel(grad_in_own)],
        smem=(0,),
    )
    kept, got = scatter_sum(down_send, down_keep)
    (out_own,) = run(
        outblock_kernel,
        "outblk",
        [((share, model), bf16)],
        [tp, meta, kept, got, residual],
        smem=(0, 1),
    )
    (block_out,) = run(
        place_kernel,
        "place_out",
        [((total, model), bf16)],
        [tp, *gather_rel(out_own)],
        smem=(0,),
    )
    row8 = ((8, model), f32)
    small, gains = run(
        small_kernel, "small", [row8, row8], [dtaps, dbeta, hidden, in_part, mid_part, head_part]
    )
    for axis in ("tp", "seq"):
        step = 1
        while step < lax.axis_size(axis):
            gains = plus(gains, swap(gains, step, axis))
            if axis == "seq":
                small = plus(small, swap(small, step, axis))
            step *= 2
    grad_down_w, grad_gate_w = run(
        settle_kernel,
        "settle_a",
        [((ffw, model), f32), ((ffw, model), f32)],
        [place, near_a, far_a],
        smem=(0,),
    )
    grad_up_w, grad_out_w = run(
        settle_kernel,
        "settle_b",
        [((ffw, model), f32), ((width, model), f32)],
        [place, near_b, far_b],
        smem=(0,),
    )
    hidden_sums = run(
        settle_cols_kernel,
        "settle_c",
        [((model, width), f32)] * 4,
        [place, near_c, far_c],
        smem=(0,),
    )
    cut = model // 4
    head_cut = DH // 4
    gain_of = lambda row, size: lax.dynamic_slice(gains, (row, tp_rank * size), (1, size)).reshape(size)
    tap_of = lambda i: small[:KW, i * width : (i + 1) * width]
    return (
        block_out,
        grad_input,
        gain_of(0, cut),
        hidden_sums[0],
        hidden_sums[1],
        hidden_sums[2],
        tap_of(0),
        tap_of(1),
        tap_of(2),
        small[KW : KW + heads].T,
        hidden_sums[3],
        gain_of(2, head_cut),
        grad_out_w,
        gain_of(1, cut),
        grad_gate_w.T,
        grad_up_w.T,
        grad_down_w,
    )


def solution(mesh):
    rows = P("seq", None)
    cols = P(None, "tp")
    return jax.shard_map(
        shards,
        mesh=mesh,
        in_specs=(rows, P(), P(), P(), cols, cols, cols, cols, cols, cols, cols, cols, P(), P("tp", None), P(), cols, cols, P("tp", None), rows),
        out_specs=(rows, rows, P("tp"), cols, cols, cols, cols, cols, cols, cols, cols, P("tp"), P("tp", None), P("tp"), cols, cols, P("tp", None)),
        check_vma=False,
    )
```

time: 1170 us -> 382 us (0.33)
  waiting for transfers between devices: 629 us -> 203 us
  matrix products: 148 us -> 0 us
  other arithmetic: 127 us -> 0 us
  blocking collectives: 111 us -> 0 us
  local copies, waits for them, and re-layouts: 121 us -> 32.2 us
  Pallas kernels: 0 us -> 86.5 us
  starting transfers between devices: 6.98 us -> 57.6 us
  between operations: 16.3 us -> 1.6 us
    psum x4 -> x0, waiting for transfers between devices: 560 us -> none  [the longest x1 401 us: shards(): lax.psum((in_gain_local, grad_q_weight, grad_k_weight, grad_v_weight, gra...]
    ppermute x2 -> x52, waiting for transfers between devices: 3.05 us -> 203 us  [the longest x46 184 us: swap(): return lax.ppermute(value, axis, [(i, i ^ bit) for i in range(count)])]
    dot_general x85 -> x0, matrix products: 139 us -> none  [the longest x16 31.8 us: link_step(): jnp.einsum('hij,hjk->hik', step_map, carried[1], precision=HIGHEST)]
    pallas_call x0 -> x49, Pallas kernels: none -> 86.5 us  [run(): pl.pallas_call(kernel, name=name, out_shape=shapes, in_specs=[pl.BlockSpe...]
    another operation x10 -> x0, other arithmetic: 82.6 us -> none  [the longest x5 82.4 us: wy_parts(): jax.scipy.linalg.solve_triangular(system, scaled_keys, lower=True, unit_d...]
    all_gather x2 -> x0, waiting for transfers between devices: 65.3 us -> none  [entering(): gathered = jax.tree.map(lambda a: lax.all_gather(a, axis), part)]
    all_gather x2 -> x0, blocking collectives: 64.7 us -> none  [prefix(): lax.all_gather(part.astype(kind), axis)]
    ppermute x2 -> x52, starting transfers between devices: 6.15 us -> 57.6 us  [the longest x46 41.5 us: swap(): return lax.ppermute(value, axis, [(i, i ^ bit) for i in range(count)])]
  transfers between devices with their start and end apart: 8 -> 52, of which waited for: 7 -> 31; matrix products, arithmetic and copies ran while one was open for 5% -> 1% of each run, Pallas kernels for 0% -> 15%
where the time goes in v1:
time: 382 us; the launch traced here: 381 us
  waiting for transfers between devices  203 us (53%)
  Pallas kernels  86.5 us (23%)
  starting transfers between devices  57.6 us (15%)
  local copies, waits for them, and re-layouts  32.2 us (8%)
    ppermute x46, waiting for transfers between devices, swap(): return lax.ppermute(value, axis, [(i, i ^ bit) for i in range(count)])  184 us
    pallas_call x49, Pallas kernels, run(): pl.pallas_call(kernel, name=name, out_shape=shapes, in_specs=[pl.BlockSpe...  86.5 us
    ppermute x46, starting transfers between devices, swap(): return lax.ppermute(value, axis, [(i, i ^ bit) for i in range(count)])  41.5 us
    unnamed x164, local copies, waits for them, and re-layouts  29 us
    ppermute x6, waiting for transfers between devices, shift(): return lax.ppermute(value, 'seq', pairs)  18.8 us
    ppermute x6, starting transfers between devices, shift(): return lax.ppermute(value, 'seq', pairs)  16.1 us
  transfers between devices with their start and end apart: 52, of which 31 were waited for; matrix products, arithmetic and copies ran while one was open for 1% of the time, Pallas kernels for 15%

profile of v1, /device:TPU:0, one launch (start us, length us, event | category | flops | bytes accessed | tf_op | source)
XLA Modules:
  0.0 381.1 jit_solution(5151551768743752690)
XLA Ops:
  1.4 4.9 %collective-permute-start = (bf16[16,1024]{1,0:T(8,128)(2,1)S(1)}, bf16[16,1024]{1,0:T(8,128)(2,1)S(1)}, u32[]{:S(2)}, u32[]{:S(2)}) collective-permute-start(bf16[16,1024]{1,0:T(8,128)(2,1)S(1)} %slice.15), channel_id=1, source_target_pairs={{0,4},{4,8},{8,12},{12,16},{16,20},{20,24},{24,28},{1,5},{5,9},{9,... | collective-permute-start | bytes 98312 | tf_op jit(solution)/shard_map/ppermute | solution.py:729
  15.6 4.7 %pre.1 = (bf16[512,1024]{1,0:T(8,128)(2,1)S(1)}, f32[512,768]{1,0:T(8,128)S(1)}, f32[512,256]{1,0:T(8,128)S(1)}, f32[512,2]{1,0:T(8,128)S(1)}, bf16[512,1024]{1,...) custom-call(s32[1]{0:T(128)} %bitcast.1.first, ...), custom_call_target="tpu_custom_call" | custom-call | flops 1073741824 | bytes 8923336 | tf_op jit(solution)/shard_map/pre/pallas_call | solution.py:54
  22.1 16.6 %mix.1 = (f32[528,768]{1,0:T(8,128)S(1)}, f32[512,768]{1,0:T(8,128)S(1)}, f32[512,768]{1,0:T(8,128)S(1)}, f32[512,256]{1,0:T(8,128)S(1)}, f32[512,256]{1,0:T(8,1...) custom-call(s32[2,8]{1,0:T(2,128)S(1)} %get-tuple-element.121.meta.r, ...), custom_call_target="tpu_custom_call" | custom-call | flops 1610612736 | bytes 14118976 | tf_op jit(solution)/shard_map/mix/pallas_call | solution.py:54
  55.5 3.8 states.1
  64.1 6.0 %collective-permute-done.6.s2 = bf16[128,1024]{1,0:T(8,128)(2,1)S(1)} collective-permute-done((bf16[128,1024]{1,0:T(8,128)(2,1)S(1)}, bf16[128,1024]{1,0:T(8,128)(2,1)S(1)}, u32[]{:S(2)}, u32[]{:S(2)}) %collective-permute-start.6) | collective-permute-done | bytes 262176 | tf_op jit(solution)/shard_map/ppermute | solution.py:591
  71.7 5.6 %ffn.1 = (bf16[512,1024]{1,0:T(8,128)(2,1)S(1)}, bf16[512,704]{1,0:T(8,128)(2,1)S(1)}, bf16[512,704]{1,0:T(8,128)(2,1)S(1)}, bf16[512,704]{1,0:T(8,128)(2,1)S(1)...) custom-call(s32[1]{0:T(128)} %bitcast.tp.r_0_, ...), custom_call_target="tpu_custom_call" | custom-call | flops 4429185024 | bytes 12779524 | tf_op jit(solution)/shard_map/ffn/pallas_call | solution.py:54
  98.3 7.2 %collective-permute-done.16.b2 = bf16[128,1024]{1,0:T(8,128)(2,1)S(1)} collective-permute-done((bf16[128,1024]{1,0:T(8,128)(2,1)S(1)}, bf16[128,1024]{1,0:T(8,128)(2,1)S(1)}, u32[]{:S(2)}, u32[]{:S(2)}) %collective-permute-start.16) | collective-permute-done | bytes 262176 | tf_op jit(solution)/shard_map/ppermute | solution.py:591
  107.2 5.1 %flow.1 = (bf16[512,1024]{1,0:T(8,128)(2,1)S(1)}, bf16[512,256]{1,0:T(8,128)(2,1)S(1)}, f32[512,256]{1,0:T(8,128)S(1)}, f32[16,128,256]{2,1,0:T(8,128)S(1)}, f32...) custom-call(s32[1]{0:T(128)} %bitcast.tp.r_0_, ...), custom_call_target="tpu_custom_call" | custom-call | flops 805306368 | bytes 8520516 | tf_op jit(solution)/shard_map/flow/pallas_call | solution.py:54
  115.1 5.0 %side.1 = (f32[512,256]{1,0:T(8,128)S(1)}, f32[512,256]{1,0:T(8,128)S(1)}, f32[512,256]{1,0:T(8,128)S(1)}) custom-call(f32[512,768]{1,0:T(8,128)S(1)} %get-tuple-element.132.qkv.r_4_, f32[512,256]{1,0:T(8,128)S(1)} %get-tuple-element.171.dout, f32[512,256]{1,0:T(8,128)S(1)} %copy-done.1, f32[16,128,128]{2,1,0:T(8,128)S(1)} %get-tuple-element.169.states.r_12_, ...), custom_call_target="tpu_custom_call" | custom-call | flops 268435456 | bytes 5505024 | tf_op jit(solution)/shard_map/side/pallas_call | solution.py:54
  121.6 4.5 %collective-permute-done.19.r_2_ = f32[2,128,128]{2,1,0:T(8,128)S(1)} collective-permute-done((f32[2,128,128]{2,1,0:T(8,128)S(1)}, f32[2,128,128]{2,1,0:T(8,128)S(1)}, u32[]{:S(2)}, u32[]{:S(2)}) %collective-permute-start.19) | collective-permute-done | bytes 131104 | tf_op jit(solution)/shard_map/ppermute | solution.py:729
  126.1 7.6 %collective-permute-done.18.r_1_ = f32[2,128,256]{2,1,0:T(8,128)S(1)} collective-permute-done((f32[2,128,256]{2,1,0:T(8,128)S(1)}, f32[2,128,256]{2,1,0:T(8,128)S(1)}, u32[]{:S(2)}, u32[]{:S(2)}) %collective-permute-start.18) | collective-permute-done | bytes 262176 | tf_op jit(solution)/shard_map/ppermute | solution.py:729
  133.7 16.3 %back.1 = (bf16[512,768]{1,0:T(8,128)(2,1)S(1)}, f32[16,768]{1,0:T(8,128)S(1)}, f32[8,768]{1,0:T(8,128)S(1)}, bf16[512,128]{1,0:T(8,128)(2,1)S(1)}, f32[4,768]{1,0:T(4,128)S(1)}) custom-call(s32[2,8]{1,0:T(2,128)S(1)} %get-tuple-element.121.meta.r_0_, f32[2,128,256]{2,1,0:T(8,128)S(1)} %collective-permute-done.18.r_1_, ...), custom_call_target="tpu_custom_call" | custom-call | flops 805306368 | bytes 11679808 | tf_op jit(solution)/shard_map/back/pallas_call | solution.py:54
  151.3 4.4 %collective-permute-done.20.incoming = f32[8,768]{1,0:T(8,128)S(1)} collective-permute-done((f32[8,768]{1,0:T(8,128)S(1)}, f32[8,768]{1,0:T(8,128)S(1)}, u32[]{:S(2)}, u32[]{:S(2)}) %collective-permute-start.20) | collective-permute-done | bytes 24608 | tf_op jit(solution)/shard_map/ppermute | solution.py:729
  163.6 13.6 %collective-permute-done.47.got = bf16[2,176,1024]{2,1,0:T(8,128)(2,1)S(1)} collective-permute-done((bf16[2,176,1024]{2,1,0:T(8,128)(2,1)S(1)}, bf16[2,176,1024]{2,1,0:T(8,128)(2,1)S(1)}, u32[]{:S(2)}, u32[]{:S(2)}) %collective-permute-start.47) | collective-permute-done | bytes 720928 | tf_op jit(solution)/shard_map/ppermute | solution.py:591
  180.0 4.8 %collective-permute-done.31.got = bf16[4,128,1024]{2,1,0:T(8,128)(2,1)S(1)} collective-permute-done((bf16[4,128,1024]{2,1,0:T(8,128)(2,1)S(1)}, bf16[4,128,1024]{2,1,0:T(8,128)(2,1)S(1)}, u32[]{:S(2)}, u32[]{:S(2)}) %collective-permute-start.31) | collective-permute-done | bytes 1048608 | tf_op jit(solution)/shard_map/ppermute | solution.py:591
  187.6 6.0 %collective-permute-done.48.got = bf16[1,176,1024]{2,1,0:T(8,128)(2,1)S(1)} collective-permute-done((bf16[1,176,1024]{2,1,0:T(8,128)(2,1)S(1)}, bf16[1,176,1024]{2,1,0:T(8,128)(2,1)S(1)}, u32[]{:S(2)}, u32[]{:S(2)}) %collective-permute-start.48) | collective-permute-done | bytes 360480 | tf_op jit(solution)/shard_map/ppermute | solution.py:591
  193.8 9.7 %collective-permute-done.40.got = bf16[4,120,1024]{2,1,0:T(8,128)(2,1)S(1)} collective-permute-done((bf16[4,120,1024]{2,1,0:T(8,128)(2,1)S(1)}, bf16[4,120,1024]{2,1,0:T(8,128)(2,1)S(1)}, u32[]{:S(2)}, u32[]{:S(2)}) %collective-permute-start.40) | collective-permute-done | bytes 983072 | tf_op jit(solution)/shard_map/ppermute | solution.py:591
  208.5 4.4 %collective-permute-done.49.b = bf16[1,176,1024]{2,1,0:T(8,128)(2,1)S(1)} collective-permute-done((bf16[1,176,1024]{2,1,0:T(8,128)(2,1)S(1)}, bf16[1,176,1024]{2,1,0:T(8,128)(2,1)S(1)}, u32[]{:S(2)}, u32[]{:S(2)}) %collective-permute-start.49) | collective-permute-done | bytes 360480 | tf_op jit(solution)/shard_map/ppermute | solution.py:591
  213.1 20.1 %collective-permute-done.41.got = bf16[2,120,1024]{2,1,0:T(8,128)(2,1)S(1)} collective-permute-done((bf16[2,120,1024]{2,1,0:T(8,128)(2,1)S(1)}, bf16[2,120,1024]{2,1,0:T(8,128)(2,1)S(1)}, u32[]{:S(2)}, u32[]{:S(2)}) %collective-permute-start.41) | collective-permute-done | bytes 491552 | tf_op jit(solution)/shard_map/ppermute | solution.py:591
  236.4 16.5 %collective-permute-done.42.got = bf16[1,120,1024]{2,1,0:T(8,128)(2,1)S(1)} collective-permute-done((bf16[1,120,1024]{2,1,0:T(8,128)(2,1)S(1)}, bf16[1,120,1024]{2,1,0:T(8,128)(2,1)S(1)}, u32[]{:S(2)}, u32[]{:S(2)}) %collective-permute-start.42) | collective-permute-done | bytes 245792 | tf_op jit(solution)/shard_map/ppermute | solution.py:591
  253.0 7.1 %collective-permute-done.34.b = bf16[1,128,1024]{2,1,0:T(8,128)(2,1)S(1)} collective-permute-done((bf16[1,128,1024]{2,1,0:T(8,128)(2,1)S(1)}, bf16[1,128,1024]{2,1,0:T(8,128)(2,1)S(1)}, u32[]{:S(2)}, u32[]{:S(2)}) %collective-permute-start.34) | collective-permute-done | bytes 262176 | tf_op jit(solution)/shard_map/ppermute | solution.py:591
  263.3 6.1 %collective-permute-done.9 = bf16[1,128,1024]{2,1,0:T(8,128)(2,1)S(1)} collective-permute-done((bf16[1,128,1024]{2,1,0:T(8,128)(2,1)S(1)}, bf16[1,128,1024]{2,1,0:T(8,128)(2,1)S(1)}, u32[]{:S(2)}, u32[]{:S(2)}) %collective-permute-start.9) | collective-permute-done | bytes 262176 | tf_op jit(solution)/shard_map/ppermute | solution.py:591
  284.0 53.4 %collective-permute-done.37.b = f32[8,1024]{1,0:T(8,128)S(1)} collective-permute-done((f32[8,1024]{1,0:T(8,128)S(1)}, f32[8,1024]{1,0:T(8,128)S(1)}, u32[]{:S(2)}, u32[]{:S(2)}) %collective-permute-start.37) | collective-permute-done | bytes 32800 | tf_op jit(solution)/shard_map/ppermute | solution.py:591
  373.4 4.2 %settle_a.1 = (f32[704,1024]{1,0:T(8,128)}, f32[704,1024]{1,0:T(8,128)}) custom-call(s32[1]{0:T(128)} %bitcast.9.r_0_.place, bf16[4,176,1024]{2,1,0:T(8,128)(2,1)S(1)} %a_pack.3.near, bf16[4,176,1024]{2,1,0:T(8,128)(2,1)} %collective-permute-done.51.far), custom_call_target="tpu_custom_call" | custom-call | bytes 8650756 | tf_op jit(solution)/shard_map/settle_a/pallas_call | solution.py:54
  (298 shorter events, 141.9 us)
Async XLA Ops:
  1.4 20.6 %collective-permute-start = (bf16[16,1024]{1,0:T(8,128)(2,1)S(1)}, bf16[16,1024]{1,0:T(8,128)(2,1)S(1)}, u32[]{:S(2)}, u32[]{:S(2)}) collective-permute-start(bf16[16,1024]{1,0:T(8,128)(2,1)S(1)} %slice.15), channel_id=1, source_target_pairs={{0,4},{4,8},{8,12},{12,16},{16,20},{20,24},{24,28},{1,5},{5,9},{9,... | collective-permute-start | bytes 98312 | tf_op jit(solution)/shard_map/ppermute | solution.py:729
  92.8 67.9 %collective-permute-start.46 = (bf16[4,176,1024]{2,1,0:T(8,128)(2,1)S(1)}, bf16[4,176,1024]{2,1,0:T(8,128)(2,1)S(1)}, u32[]{:S(2)}, u32[]{:S(2)}) collective-permute-start(bf16[4,176,1024]{2,1,0:T(8,128)(2,1)S(1)} %get-tuple-element.217), channel_id=1, source_target_pairs={{0,4},{4,0},{8,12},{12,8},{16,20},{20,16},{24,28},{28,24},{1,5},{5... | collective-permute-start | bytes 4325384 | tf_op jit(solution)/shard_map/ppermute | solution.py:591
  112.2 21.4 %collective-permute-start.18 = (f32[2,128,256]{2,1,0:T(8,128)S(1)}, f32[2,128,256]{2,1,0:T(8,128)S(1)}, u32[]{:S(2)}, u32[]{:S(2)}) collective-permute-start(f32[2,128,256]{2,1,0:T(8,128)S(1)} %get-tuple-element.163), channel_id=1, source_target_pairs={{4,0},{8,4},{12,8},{16,12},{20,16},{24,20},{28,24},{5,1},{9,5},{13... | collective-permute-start | bytes 786440 | tf_op jit(solution)/shard_map/ppermute | solution.py:729
  158.7 26.2 %collective-permute-start.31 = (bf16[4,128,1024]{2,1,0:T(8,128)(2,1)S(1)}, bf16[4,128,1024]{2,1,0:T(8,128)(2,1)S(1)}, u32[]{:S(2)}, u32[]{:S(2)}) collective-permute-start(bf16[4,128,1024]{2,1,0:T(8,128)(2,1)S(1)} %get-tuple-element.199), channel_id=1, source_target_pairs={{0,4},{4,0},{8,12},{12,8},{16,20},{20,16},{24,28},{28,24},{1,5},{5... | collective-permute-start | bytes 3145736 | tf_op jit(solution)/shard_map/ppermute | solution.py:591
  160.9 16.2 %collective-permute-start.47 = (bf16[2,176,1024]{2,1,0:T(8,128)(2,1)S(1)}, bf16[2,176,1024]{2,1,0:T(8,128)(2,1)S(1)}, u32[]{:S(2)}, u32[]{:S(2)}) collective-permute-start(bf16[2,176,1024]{2,1,0:T(8,128)(2,1)S(1)} %get-tuple-element.219), channel_id=1, source_target_pairs={{0,8},{4,12},{8,0},{12,4},{16,24},{20,28},{24,16},{28,20},{1,9},{5... | collective-permute-start | bytes 2162696 | tf_op jit(solution)/shard_map/ppermute | solution.py:591
  162.6 40.9 %collective-permute-start.40 = (bf16[4,120,1024]{2,1,0:T(8,128)(2,1)S(1)}, bf16[4,120,1024]{2,1,0:T(8,128)(2,1)S(1)}, u32[]{:S(2)}, u32[]{:S(2)}) collective-permute-start(bf16[4,120,1024]{2,1,0:T(8,128)(2,1)S(1)} %get-tuple-element.210), channel_id=1, source_target_pairs={{0,4},{4,0},{8,12},{12,8},{16,20},{20,16},{24,28},{28,24},{1,5},{5... | collective-permute-start | bytes 2949128 | tf_op jit(solution)/shard_map/ppermute | solution.py:591
  177.3 16.3 %collective-permute-start.48 = (bf16[1,176,1024]{2,1,0:T(8,128)(2,1)S(1)}, bf16[1,176,1024]{2,1,0:T(8,128)(2,1)S(1)}, u32[]{:S(2)}, u32[]{:S(2)}) collective-permute-start(bf16[1,176,1024]{2,1,0:T(8,128)(2,1)S(1)} %get-tuple-element.221), channel_id=1, source_target_pairs={{0,16},{4,20},{8,24},{12,28},{16,0},{20,4},{24,8},{28,12},{1,17},{... | collective-permute-start | bytes 1081352 | tf_op jit(solution)/shard_map/ppermute | solution.py:591
  185.1 20.7 %collective-permute-start.32 = (bf16[2,128,1024]{2,1,0:T(8,128)(2,1)S(1)}, bf16[2,128,1024]{2,1,0:T(8,128)(2,1)S(1)}, u32[]{:S(2)}, u32[]{:S(2)}) collective-permute-start(bf16[2,128,1024]{2,1,0:T(8,128)(2,1)S(1)} %get-tuple-element.201), channel_id=1, source_target_pairs={{0,8},{4,12},{8,0},{12,4},{16,24},{20,28},{24,16},{28,20},{1,9},{5... | collective-permute-start | bytes 1572872 | tf_op jit(solution)/shard_map/ppermute | solution.py:591
  193.7 19.2 %collective-permute-start.49 = (bf16[1,176,1024]{2,1,0:T(8,128)(2,1)S(1)}, bf16[1,176,1024]{2,1,0:T(8,128)(2,1)S(1)}, u32[]{:S(2)}, u32[]{:S(2)}) collective-permute-start(bf16[1,176,1024]{2,1,0:T(8,128)(2,1)S(1)} %a_last.1.a), channel_id=1, source_target_pairs={{0,16},{4,20},{8,24},{12,28},{16,0},{20,4},{24,8},{28,12},{1,17},{... | collective-permute-start | bytes 1081352 | tf_op jit(solution)/shard_map/ppermute | solution.py:591
  203.7 29.5 %collective-permute-start.41 = (bf16[2,120,1024]{2,1,0:T(8,128)(2,1)S(1)}, bf16[2,120,1024]{2,1,0:T(8,128)(2,1)S(1)}, u32[]{:S(2)}, u32[]{:S(2)}) collective-permute-start(bf16[2,120,1024]{2,1,0:T(8,128)(2,1)S(1)} %get-tuple-element.212), channel_id=1, source_target_pairs={{0,8},{4,12},{8,0},{12,4},{16,24},{20,28},{24,16},{28,20},{1,9},{5... | collective-permute-start | bytes 1474568 | tf_op jit(solution)/shard_map/ppermute | solution.py:591
  205.8 27.5 %collective-permute-start.33 = (bf16[1,128,1024]{2,1,0:T(8,128)(2,1)S(1)}, bf16[1,128,1024]{2,1,0:T(8,128)(2,1)S(1)}, u32[]{:S(2)}, u32[]{:S(2)}) collective-permute-start(bf16[1,128,1024]{2,1,0:T(8,128)(2,1)S(1)} %get-tuple-element.203), channel_id=1, source_target_pairs={{0,16},{4,20},{8,24},{12,28},{16,0},{20,4},{24,8},{28,12},{1,17},{... | collective-permute-start | bytes 786440 | tf_op jit(solution)/shard_map/ppermute | solution.py:591
  212.9 50.2 %collective-permute-start.50 = (bf16[2,176,1024]{2,1,0:T(8,128)(2,1)S(1)}, bf16[2,176,1024]{2,1,0:T(8,128)(2,1)S(1)}, u32[]{:S(2)}, u32[]{:S(2)}) collective-permute-start(bf16[2,176,1024]{2,1,0:T(8,128)(2,1)S(1)} %a_pack.2.a), channel_id=1, source_target_pairs={{0,8},{4,12},{8,0},{12,4},{16,24},{20,28},{24,16},{28,20},{1,9},{5... | collective-permute-start | bytes 2162696 | tf_op jit(solution)/shard_map/ppermute | solution.py:591
  213.0 47.2 %collective-permute-start.8 = (bf16[2,128,1024]{2,1,0:T(8,128)(2,1)S(1)}, bf16[2,128,1024]{2,1,0:T(8,128)(2,1)S(1)}, u32[]{:S(2)}, u32[]{:S(2)}) collective-permute-start(bf16[2,128,1024]{2,1,0:T(8,128)(2,1)S(1)} %copy-done.70), channel_id=1, source_target_pairs={{0,1},{1,0},{2,3},{3,2},{4,5},{5,4},{6,7},{7,6},{8,9},{9,8},{10,11... | collective-permute-start | bytes 1572872 | tf_op jit(solution)/shard_map/ppermute | solution.py:591
  233.3 19.6 %collective-permute-start.42 = (bf16[1,120,1024]{2,1,0:T(8,128)(2,1)S(1)}, bf16[1,120,1024]{2,1,0:T(8,128)(2,1)S(1)}, u32[]{:S(2)}, u32[]{:S(2)}) collective-permute-start(bf16[1,120,1024]{2,1,0:T(8,128)(2,1)S(1)} %get-tuple-element.214), channel_id=1, source_target_pairs={{0,16},{4,20},{8,24},{12,28},{16,0},{20,4},{24,8},{28,12},{1,17},{... | collective-permute-start | bytes 737288 | tf_op jit(solution)/shard_map/ppermute | solution.py:591
  233.4 26.7 %collective-permute-start.34 = (bf16[1,128,1024]{2,1,0:T(8,128)(2,1)S(1)}, bf16[1,128,1024]{2,1,0:T(8,128)(2,1)S(1)}, u32[]{:S(2)}, u32[]{:S(2)}) collective-permute-start(bf16[1,128,1024]{2,1,0:T(8,128)(2,1)S(1)} %c_last.1.a), channel_id=1, source_target_pairs={{0,16},{4,20},{8,24},{12,28},{16,0},{20,4},{24,8},{28,12},{1,17},{... | collective-permute-start | bytes 786440 | tf_op jit(solution)/shard_map/ppermute | solution.py:591
  236.4 34.3 %collective-permute-start.21 = (bf16[2,128,1024]{2,1,0:T(8,128)(2,1)S(1)}, bf16[2,128,1024]{2,1,0:T(8,128)(2,1)S(1)}, u32[]{:S(2)}, u32[]{:S(2)}) collective-permute-start(bf16[2,128,1024]{2,1,0:T(8,128)(2,1)S(1)} %get-tuple-element.186), channel_id=1, source_target_pairs={{0,1},{1,0},{2,3},{3,2},{4,5},{5,4},{6,7},{7,6},{8,9},{9,8},{10,11... | collective-permute-start | bytes 1572872 | tf_op jit(solution)/shard_map/ppermute | solution.py:591
  260.2 13.5 %collective-permute-start.35 = (bf16[2,128,1024]{2,1,0:T(8,128)(2,1)S(1)}, bf16[2,128,1024]{2,1,0:T(8,128)(2,1)S(1)}, u32[]{:S(2)}, u32[]{:S(2)}) collective-permute-start(bf16[2,128,1024]{2,1,0:T(8,128)(2,1)S(1)} %c_pack.2.a), channel_id=1, source_target_pairs={{0,8},{4,12},{8,0},{12,4},{16,24},{20,28},{24,16},{28,20},{1,9},{5... | collective-permute-start | bytes 1572872 | tf_op jit(solution)/shard_map/ppermute | solution.py:591
  262.8 16.1 %collective-permute-start.44 = (bf16[2,120,1024]{2,1,0:T(8,128)(2,1)S(1)}, bf16[2,120,1024]{2,1,0:T(8,128)(2,1)S(1)}, u32[]{:S(2)}, u32[]{:S(2)}) collective-permute-start(bf16[2,120,1024]{2,1,0:T(8,128)(2,1)S(1)} %b_pack.2.a), channel_id=1, source_target_pairs={{0,8},{4,12},{8,0},{12,4},{16,24},{20,28},{24,16},{28,20},{1,9},{5... | collective-permute-start | bytes 1474568 | tf_op jit(solution)/shard_map/ppermute | solution.py:591
  263.2 110.2 %collective-permute-start.51 = (bf16[4,176,1024]{2,1,0:T(8,128)(2,1)S(1)}, bf16[4,176,1024]{2,1,0:T(8,128)(2,1)}, u32[]{:S(2)}, u32[]{:S(2)}) collective-permute-start(bf16[4,176,1024]{2,1,0:T(8,128)(2,1)S(1)} %a_pack.3.near), channel_id=1, source_target_pairs={{0,4},{4,0},{8,12},{12,8},{16,20},{20,16},{24,28},{28,24},{1,5},{5... | collective-permute-start | bytes 4325384 | tf_op jit(solution)/shard_map/ppermute | solution.py:591
  276.5 101.2 %collective-permute-start.36 = (bf16[4,128,1024]{2,1,0:T(8,128)(2,1)S(1)}, bf16[4,128,1024]{2,1,0:T(8,128)(2,1)}, u32[]{:S(2)}, u32[]{:S(2)}) collective-permute-start(bf16[4,128,1024]{2,1,0:T(8,128)(2,1)S(1)} %c_pack.3.near), channel_id=1, source_target_pairs={{0,4},{4,0},{8,12},{12,8},{16,20},{20,16},{24,28},{28,24},{1,5},{5... | collective-permute-start | bytes 3145736 | tf_op jit(solution)/shard_map/ppermute | solution.py:591
  278.9 67.8 %collective-permute-start.12 = (bf16[128,1024]{1,0:T(8,128)(2,1)S(1)}, bf16[128,1024]{1,0:T(8,128)(2,1)S(1)}, u32[]{:S(2)}, u32[]{:S(2)}) collective-permute-start(bf16[128,1024]{1,0:T(8,128)(2,1)S(1)} %collective-permute-done.11.a2), channel_id=1, source_target_pairs={{0,1},{1,0},{2,3},{3,2},{4,5},{5,4},{6,7},{7,6},{8,9},{9,8},{10,11... | collective-permute-start | bytes 786440 | tf_op jit(solution)/shard_map/ppermute | solution.py:591
  279.3 90.7 %collective-permute-start.45 = (bf16[4,120,1024]{2,1,0:T(8,128)(2,1)S(1)}, bf16[4,120,1024]{2,1,0:T(8,128)(2,1)}, u32[]{:S(2)}, u32[]{:S(2)}) collective-permute-start(bf16[4,120,1024]{2,1,0:T(8,128)(2,1)S(1)} %b_pack.3.near), channel_id=1, source_target_pairs={{0,4},{4,0},{8,12},{12,8},{16,20},{20,16},{24,28},{28,24},{1,5},{5... | collective-permute-start | bytes 2949128 | tf_op jit(solution)/shard_map/ppermute | solution.py:591
  283.0 54.4 %collective-permute-start.37 = (f32[8,1024]{1,0:T(8,128)S(1)}, f32[8,1024]{1,0:T(8,128)S(1)}, u32[]{:S(2)}, u32[]{:S(2)}) collective-permute-start(f32[8,1024]{1,0:T(8,128)S(1)} %get-tuple-element.207.a), channel_id=1, source_target_pairs={{0,4},{4,0},{8,12},{12,8},{16,20},{20,16},{24,28},{28,24},{1,5},{5... | collective-permute-start | bytes 98312 | tf_op jit(solution)/shard_map/ppermute | solution.py:591
  349.5 15.7 %collective-permute-start.24 = (bf16[128,1024]{1,0:T(8,128)(2,1)}, bf16[128,1024]{1,0:T(8,128)(2,1)}, u32[]{:S(2)}, u32[]{:S(2)}) collective-permute-start(bf16[128,1024]{1,0:T(8,128)(2,1)} %get-tuple-element.190.a0), channel_id=1, source_target_pairs={{0,2},{1,3},{2,0},{3,1},{4,6},{5,7},{6,4},{7,5},{8,10},{9,11},{10,... | collective-permute-start | bytes 786440 | tf_op jit(solution)/shard_map/ppermute | solution.py:591
  (110 other events, 925.9 us)

commit v2 on v1

--- a/solution.py
+++ b/solution.py
@@ -43,27 +43,35 @@
     return pl.ds(pl.multiple_of(block * size, size), size)
 
 
-def run(kernel, name, outs, args, smem=(), smem_out=(), hbm=(), scratch=(), flops=0, vmem=8):
-    shapes = [jax.ShapeDtypeStruct(s, d) for s, d in outs]
-    total = sum(a.size * a.dtype.itemsize for a in args)
-    total += sum(s.size * s.dtype.itemsize for s in shapes)
-    spaces = [
-        pltpu.SMEM if i in smem else pltpu.HBM if i in hbm else pltpu.VMEM
-        for i in range(len(args))
-    ]
-    return pl.pallas_call(
-        kernel,
-        name=name,
-        out_shape=shapes,
-        in_specs=[pl.BlockSpec(memory_space=space) for space in spaces],
-        out_specs=[
-            pl.BlockSpec(memory_space=pltpu.SMEM if i in smem_out else pltpu.VMEM)
-            for i in range(len(outs))
-        ],
-        scratch_shapes=list(scratch),
-        compiler_params=pltpu.CompilerParams(vmem_limit_bytes=vmem << 20),
-        cost_estimate=pl.CostEstimate(flops=flops, bytes_accessed=total, transcendentals=0),
-    )(*args)
+class Order:
+    def __init__(self):
+        self.last = None
+
+    def run(self, kernel, name, outs, args, smem=(), smem_out=(), hbm=(), hbm_out=(), pin=(), scratch=(), flops=0, vmem=8):
+        shapes = [jax.ShapeDtypeStruct(s, d) for s, d in outs]
+        total = sum(a.size * a.dtype.itemsize for a in args)
+        total += sum(s.size * s.dtype.itemsize for s in shapes)
+        args = list(args)
+        if self.last is not None:
+            at = next(i for i in range(len(args)) if i not in smem and i not in pin)
+            args[at], _ = lax.optimization_barrier((args[at], self.last))
+        for i in pin:
+            args[i] = pltpu.with_memory_space_constraint(args[i], pltpu.HBM)
+        space = lambda i, low, far: pltpu.SMEM if i in low else pltpu.HBM if i in far else pltpu.VMEM
+        made = pl.pallas_call(
+            kernel,
+            name=name,
+            out_shape=shapes,
+            in_specs=[pl.BlockSpec(memory_space=space(i, smem, hbm)) for i in range(len(args))],
+            out_specs=[
+                pl.BlockSpec(memory_space=space(i, smem_out, hbm_out)) for i in range(len(outs))
+            ],
+            scratch_shapes=list(scratch),
+            compiler_params=pltpu.CompilerParams(vmem_limit_bytes=vmem << 20),
+            cost_estimate=pl.CostEstimate(flops=flops, bytes_accessed=total, transcendentals=0),
+        )(*args)
+        self.last = next(o for i, o in enumerate(made) if i not in smem_out and i not in hbm_out)
+        return made
 
 
 def wide_gain(ref):
@@ -84,7 +92,37 @@
     return values * factor * gain
 
 
-def pre_kernel(first, tp, seq_groups, seq_pads, xh, coth, gain, wqh, wkh, wvh, wgh, wb, hidden, proj, gate, beta, grad_down, x_own, gd_own, meta, x, cot, wq, wk, wv, wg, sems):
+def beta_col(beta, meta, n, h):
+    raw = beta[pl.ds(pl.multiple_of(n * GROUP, GROUP), GROUP), h : h + 1]
+    sig = jax.nn.sigmoid(raw)
+    live = iota((GROUP, 1), 0) < meta[1, n]
+    return jnp.where(live, sig, 0.0), sig, live
+
+
+def unit(rows):
+    return rows * lax.rsqrt(jnp.sum(rows * rows, axis=-1, keepdims=True) + unit_epsilon)
+
+
+def tri_inverse(systems):
+    size = systems[0].shape[0]
+    eye = (iota((size, size), 0) == iota((size, size), 1)).astype(f32)
+    blocks = [[eye[r : r + 8] for r in range(0, size, 8)] for _ in systems]
+    lower = [[system[r : r + 8] for r in range(0, size, 8)] for system in systems]
+    for j in range(size - 1):
+        for low, part in zip(lower, blocks):
+            line = part[j // 8][j % 8 : j % 8 + 1]
+            for r in range((j + 1) // 8, size // 8):
+                part[r] = part[r] - low[r][:, j : j + 1] * line
+    return [jnp.concatenate(part, axis=0) for part in blocks]
+
+
+def tap_table(*tables):
+    values = [table[...].astype(f32) for table in tables]
+    parts = values[0].shape[1] // DH
+    return lambda j, c: values[c // parts][j : j + 1, (c % parts) * DH : (c % parts + 1) * DH]
+
+
+def front_kernel(first, tp, seq_groups, seq_pads, xh, coth, gain, wqh, wkh, wvh, wgh, wb, tail, cq, ck, cv, gate, beta, meta, qkv, wmix, umix, score, zst, dev, last, mout, oloc, hidden_h, gd_h, x_own, gd_own, ext_h, conv_h, inv_h, amap_h, x, cot, wq, wk, wv, wg, hidden, gd, ext, conv, inv, amap, badd, sems, out_sems):
     loads = [
         pltpu.make_async_copy(src, dst, sems.at[i])
         for i, (src, dst) in enumerate(
@@ -111,78 +149,47 @@
 
     lax.fori_loop(0, seq_groups.shape[0], one, jnp.int32(0))
     width = wq.shape[1]
+    heads = width // DH
     tile = 256
     share = x_own.shape[0]
     scale = wide_gain(gain)
+    own = rows_of(tp[0], share)
+    stores = []
+
+    def store(src, dst):
+        copy = pltpu.make_async_copy(src, dst, out_sems.at[len(stores)])
+        copy.start()
+        stores.append(copy)
+
     loads[0].wait()
-    for t in range(x.shape[0] // tile):
-        rows = slice(t * tile, (t + 1) * tile)
+    store(x.at[own], x_own)
+    tiles = [slice(t * tile, (t + 1) * tile) for t in range(x.shape[0] // tile)]
+    for rows in tiles:
         hidden[rows] = rms_rows(x[rows].astype(f32), scale).astype(bf16)
-    x_own[...] = x[rows_of(tp[0], share)]
-    for t in range(x.shape[0] // tile):
-        rows = slice(t * tile, (t + 1) * tile)
+    store(hidden, hidden_h)
+    low = rms_rows(tail[...].astype(f32), scale).astype(bf16)
+    for rows in tiles:
         beta[rows] = dot(hidden[rows], wb[...], 1, 1)
     for i, w in enumerate((wq, wk, wv, wg)):
         loads[1 + i].wait()
-        for t in range(x.shape[0] // tile):
-            rows = slice(t * tile, (t + 1) * tile)
+        lanes = slice(i * width, (i + 1) * width)
+        for rows in tiles:
             got = dot(hidden[rows], w[...])
             if i < 3:
-                proj[rows, i * width : (i + 1) * width] = got
+                ext[TAIL + rows.start : TAIL + rows.stop, lanes] = got
             else:
                 gate[rows] = got
+        if i < 3:
+            ext[0:TAIL, lanes] = dot(low, w[...])
+    store(ext, ext_h)
     loads[5].wait()
-    for t in range(x.shape[0] // tile):
-        rows = slice(t * tile, (t + 1) * tile)
+    for t, rows in enumerate(tiles):
         live = live_mask(meta, t, tile)
-        grad_down[rows] = jnp.where(live, cot[rows].astype(f32), 0.0).astype(bf16)
-    gd_own[...] = grad_down[rows_of(tp[0], share)]
-
-
-def beta_col(beta, meta, n, h):
-    raw = beta[pl.ds(pl.multiple_of(n * GROUP, GROUP), GROUP), h : h + 1]
-    sig = jax.nn.sigmoid(raw)
-    live = iota((GROUP, 1), 0) < meta[1, n]
-    return jnp.where(live, sig, 0.0), sig, live
-
-
-def unit(rows):
-    return rows * lax.rsqrt(jnp.sum(rows * rows, axis=-1, keepdims=True) + unit_epsilon)
-
-
-def tri_inverse(systems):
-    size = systems[0].shape[0]
-    eye = (iota((size, size), 0) == iota((size, size), 1)).astype(f32)
-    blocks = [[eye[r : r + 8] for r in range(0, size, 8)] for _ in systems]
-    lower = [[system[r : r + 8] for r in range(0, size, 8)] for system in systems]
-    for j in range(size - 1):
-        for low, part in zip(lower, blocks):
-            line = part[j // 8][j % 8 : j % 8 + 1]
-            for r in range((j + 1) // 8, size // 8):
-                part[r] = part[r] - low[r][:, j : j + 1] * line
-    return [jnp.concatenate(part, axis=0) for part in blocks]
-
-
-def tap_table(*tables):
-    values = [table[...].astype(f32) for table in tables]
-    parts = values[0].shape[1] // DH
-    return lambda j, c: values[c // parts][j : j + 1, (c % parts) * DH : (c % parts + 1) * DH]
-
-
-def mix_kernel(meta, proj, tail, gain, wqh, wkh, wvh, cq, ck, cv, beta, ext, conv, qkv, wmix, umix, inv, score, amap, zst, dev, last, mout, oloc, badd, wq, wk, wv, sems):
-    groups = proj.shape[0] // GROUP
-    width = wq.shape[1]
-    heads = width // DH
-    loads = [
-        pltpu.make_async_copy(src, dst, sems.at[i])
-        for i, (src, dst) in enumerate(((wqh, wq), (wkh, wk), (wvh, wv)))
-    ]
-    for load in loads:
-        load.start()
-    ext[TAIL:] = proj[...]
+        gd[rows] = jnp.where(live, cot[rows].astype(f32), 0.0).astype(bf16)
+    store(gd, gd_h)
+    store(gd.at[own], gd_own)
     row = iota((GROUP, 1), 0)
     taps = tap_table(cq, ck, cv)
-    low = rms_rows(tail[...].astype(f32), wide_gain(gain)).astype(bf16)
 
     def front(n):
         base = pl.multiple_of(n * GROUP, GROUP)
@@ -197,11 +204,8 @@
             acted = acc * jax.nn.sigmoid(acc)
             qkv[pl.ds(base, GROUP), lanes] = unit(acted) if c < 2 * heads else acted
 
-    pl.loop(1, groups)(front)
-    for i, w in enumerate((wq, wk, wv)):
-        loads[i].wait()
-        ext[0:TAIL, i * width : (i + 1) * width] = dot(low, w[...])
-    front(0)
+    pl.loop(0, groups)(front)
+    store(conv, conv_h)
     r64 = iota((GROUP, GROUP), 0)
     c64 = iota((GROUP, GROUP), 1)
     eye = (iota((DH, DH), 0) == iota((DH, DH), 1)).astype(f32)
@@ -234,6 +238,8 @@
         return 0
 
     lax.fori_loop(0, groups // 2, local, 0)
+    store(inv, inv_h)
+    store(amap, amap_h)
     for h in range(heads):
         dev[h, :, :DH] = eye
         dev[h, :, DH:] = jnp.zeros((DH, DH), f32)
@@ -264,6 +270,8 @@
         return 0
 
     lax.fori_loop(0, groups // 2, outs, 0)
+    for copy in stores:
+        copy.wait()
 
 
 def fold_hops(hops, h):
@@ -325,7 +333,8 @@
     second[...] = rms_rows(total, wide_gain(gain)).astype(bf16)
 
 
-def ffn_kernel(tp, s0, s1, s2, s3, grad_down, wg, wu, wd, second, inner, dgate, dup, down_send, down_keep, send, keep):
+def ffn_kernel(plans, tp, place, s0, s1, s2, s3, grad_down, wg, wu, wd, down_send, down_keep, send, keep, *refs):
+    sums, (second, inner, dgate, dup, acc) = refs[:-5], refs[-5:]
     share = s0.shape[0]
     for half, pair in enumerate(((s0, s1), (s2, s3))):
         sec = jnp.concatenate([pair[0][...], pair[1][...]], axis=0)
@@ -351,6 +360,9 @@
         down = dot(inn, wd[...])
         down_keep[half] = down[:share]
         down_send[half] = down[share:].astype(bf16)
+    for left, right, plan in ((inner, grad_down, 0), (dgate, second, 1), (dup, second, 2)):
+        acc[...] = dot(left[...], right[...], 0, 0)
+        put(acc, place[0], plans[plan], sums)
 
 
 def turn_kernel(kept, got, residual, gain, grad_y, grad_residual, branch, gain_part):
@@ -607,114 +619,124 @@
     out[half:] = b[...]
 
 
-def fold(keep, got, name):
+def fold(order, keep, got, name):
     half = (keep.shape[0] // 2, *keep.shape[1:])
-    return run(add_kernel, name, [(half, f32), (half, bf16)], [keep, got])
-
-
-def scatter_sum(send, keep):
-    kept, send = fold(keep, swap(send, 1), "fold_tp")
-    return kept[0], swap(send, 2)[0]
-
-
-def spread(place, keep, send, acc, base, rows):
-    blocks = 2 * keep.shape[0]
-    width = blocks.bit_length() - 1
-    size = rows // blocks
+    return order.run(add_kernel, name, [(half, f32), (half, bf16)], [keep, got])
+
+
+def rank_of(m, bits):
+    at = 0
+    for bit in bits:
+        at = 2 * at + ((m >> bit) & 1)
+    return at
+
+
+class Plan:
+    def __init__(self, index, bits, base, size, start=0, folds=1):
+        self.index, self.bits, self.base, self.size = index, bits, base, size
+        self.start, self.folds = start, folds
+
+
+def put(acc, place, plan, sums):
+    for part in plan if isinstance(plan, (list, tuple)) else (plan,):
+        keep, send = sums[2 * part.index : 2 * part.index + 2]
+        blocks = 1 << len(part.bits)
+        height = part.size // part.folds
+        wide = acc.shape[1]
+        for m in range(blocks):
+            at = rank_of(m, part.bits[1:])
+            low = (m >> part.bits[0]) & 1
+            for i in range(part.folds):
+                begin = part.start + (m ^ place) * part.size + i * height
+                block = acc[pl.ds(pl.multiple_of(begin, 8), height)]
+                rows = slice(part.base, part.base + height)
+                lanes = slice(i * wide, (i + 1) * wide)
+                if low:
+                    send[at, rows, lanes] = block.astype(bf16)
+                else:
+                    keep[at, rows, lanes] = block
+
+
+def take(out, place, part, bits, near, far):
+    blocks = 1 << len(bits)
+    height = part.size // part.folds
+    wide = out.shape[1]
     for m in range(blocks):
-        at = sum(((m >> (i + 1)) & 1) << (width - 2 - i) for i in range(width - 1))
-        block = acc[pl.ds(pl.multiple_of((m ^ place) * size, 8), size)]
-        if m & 1:
-            send[at, base : base + size] = block.astype(bf16)
+        source = far if (m >> bits[-1]) & 1 else near
+        at = rank_of(m, bits[-2::-1])
+        for i in range(part.folds):
+            begin = part.start + (m ^ place) * part.size + i * height
+            out[pl.ds(pl.multiple_of(begin, 8), height)] = source[
+                at, part.base : part.base + height, i * wide : (i + 1) * wide
+            ].astype(f32)
+
+
+class Sum:
+    def __init__(self, order, keep, send, scatter, gather, tag):
+        self.order, self.tag, self.gather = order, tag, gather
+        self.keep, self.left = keep, list(scatter)
+        self.swap(send)
+        self.own = self.near = None
+
+    def swap(self, send):
+        self.got = swap(send, 1 << self.left.pop(0), "seq")
+
+    def step(self):
+        order, tag = self.order, self.tag
+        if self.own is None and self.left:
+            self.keep, send = fold(order, self.keep, self.got, tag + "_fold")
+            self.swap(send)
+            return
+        if self.own is None:
+            (self.own,) = order.run(
+                last_kernel, tag + "_last", [(self.keep.shape, bf16)], [self.keep, self.got]
+            )
+            more = 1 << len(self.gather)
+            while more < lax.axis_size("seq"):
+                other = swap(self.own, more, "seq")
+                self.own = (self.own.astype(f32) + other.astype(f32)).astype(bf16)
+                more *= 2
+            self.left = list(self.gather)
         else:
-            keep[at, base : base + size] = block
-
-
-def grads_kernel(count, place, *refs):
-    pairs, (keep, send, acc) = refs[: 2 * count], refs[2 * count :]
-    base = 0
-    for i in range(count):
-        left, right = pairs[2 * i : 2 * i + 2]
-        rows = left.shape[1]
-        acc[:rows] = dot(left[...], right[...], 0, 0)
-        spread(place[0], keep, send, acc, base, rows)
-        base += rows // (2 * keep.shape[0])
-
-
-def hidden_grads_kernel(place, hidden, gp, dgate, keep, send, acc):
-    wide = gp.shape[1]
-    rows = hidden.shape[1]
-    acc[:, :wide] = dot(hidden[...], gp[...], 0, 0)
-    acc[:, wide:] = dot(hidden[...], dgate[...], 0, 0)
-    spread(place[0], keep, send, acc, 0, rows)
-
-
-def grads(place, pairs, blocks, name):
-    size = sum(p[0].shape[1] for p in pairs) // blocks
-    most = max(p[0].shape[1] for p in pairs)
-    cols = pairs[0][1].shape[1]
-    half = (blocks // 2, size, cols)
-    args = [a for p in pairs for a in p]
-    return run(
-        lambda *r: grads_kernel(len(pairs), *r),
-        name,
-        [(half, f32), (half, bf16)],
-        [place, *args],
-        smem=(0,),
-        scratch=[pltpu.VMEM((most, cols), f32)],
-        flops=2 * pairs[0][0].shape[0] * size * blocks * cols,
-        vmem=16,
-    )
-
-
-def sum_seq(keep, send, blocks, tag):
-    count = lax.axis_size("seq")
-    step = 1
-    while step < blocks // 2:
-        keep, send = fold(keep, swap(send, step, "seq"), tag + "_fold")
-        step *= 2
-    got = swap(send, step, "seq")
-    (own,) = run(last_kernel, tag + "_last", [(keep.shape, bf16)], [keep, got])
-    more = blocks
-    while more < count:
-        own = (own.astype(f32) + swap(own, more, "seq").astype(f32)).astype(bf16)
-        more *= 2
-    while step > 1:
-        twice = (2 * own.shape[0], *own.shape[1:])
-        (own,) = run(pack_kernel, tag + "_pack", [(twice, bf16)], [own, swap(own, step, "seq")])
-        step //= 2
-    return own, swap(own, 1, "seq")
-
-
-def settle(place, near, far, outs):
-    blocks = 2 * near.shape[0]
-    width = blocks.bit_length() - 1
-    for m in range(blocks):
-        at = sum(((m >> (i + 1)) & 1) << i for i in range(width - 1))
-        at = sum(((at >> i) & 1) << (width - 2 - i) for i in range(width - 1))
-        source = far if m & 1 else near
-        row = 0
-        for out, size, lanes in outs:
-            out[pl.ds(pl.multiple_of((m ^ place) * size, 8), size)] = source[
-                at, row : row + size, lanes
-            ].astype(f32)
-            row = row + size if lanes == slice(None) else row
-
-
-def settle_kernel(place, near, far, *outs):
-    sizes = [out.shape[0] // (2 * near.shape[0]) for out in outs]
-    settle(place[0], near, far, [(o, n, slice(None)) for o, n in zip(outs, sizes)])
-
-
-def settle_cols_kernel(place, near, far, *outs):
-    size = near.shape[1]
-    wide = outs[0].shape[1]
-    settle(
-        place[0],
-        near,
-        far,
-        [(o, size, slice(i * wide, (i + 1) * wide)) for i, o in enumerate(outs)],
-    )
+            twice = (2 * self.own.shape[0], *self.own.shape[1:])
+            (self.own,) = order.run(
+                pack_kernel, tag + "_pack", [(twice, bf16)], [self.own, self.got]
+            )
+        self.swap(self.own)
+
+    def settle(self, plans, outs, name):
+        count = len(outs)
+
+        def kernel(place, near, far, *refs):
+            for part, out in zip(plans, refs):
+                take(out, place[0], part, self.gather, near, far)
+
+        return self.order.run(
+            kernel, name, [(o, f32) for o in outs], [self.place, self.own, self.got], smem=(0,)
+        )
+
+
+def scatter_first(order, keep, send):
+    return fold(order, keep, swap(send, 1), "fold_tp")
+
+
+def grads_b_kernel(plans, place, attended, branch, hidden, dgate, *refs):
+    sums, (acc, acc2) = refs[:-2], refs[-2:]
+    acc[...] = dot(attended[...], branch[...], 0, 0)
+    put(acc, place[0], plans[0], sums)
+    acc2[...] = dot(hidden[...], dgate[...], 0, 0)
+    put(acc2, place[0], plans[1], sums)
+
+
+def grads_c_kernel(plans, place, hidden, gp, *refs):
+    sums, acc = refs[:-1], refs[-1]
+    acc[...] = dot(hidden[...], gp[...], 0, 0)
+    for plan in plans:
+        put(acc, place[0], plan, sums)
+
+
+def sum_shapes(blocks, rows, cols):
+    return [((blocks // 2, rows, cols), f32), ((blocks // 2, rows, cols), bf16)]
 
 
 def gather_rel(own):
@@ -749,8 +771,8 @@
     out[...] = a[...] + b[...]
 
 
-def plus(a, b):
-    return run(plus_kernel, "plus", [(a.shape, f32)], [a, b])[0]
+def plus(order, a, b):
+    return order.run(plus_kernel, "plus", [(a.shape, f32)], [a, b])[0]
 
 
 def shards(
@@ -784,7 +806,7 @@
     reach = max(1, seq_count // 4)
     tp_rank = lax.axis_index("tp")
     tp = tp_rank.astype(jnp.int32).reshape(1)
-    blocks = min(8, seq_count)
+    blocks = 8
     place = (lax.axis_index("seq") % blocks).astype(jnp.int32).reshape(1)
     first = (lax.axis_index("seq") * groups).astype(jnp.int32).reshape(1)
     taps = (conv_query, conv_key, conv_value)
@@ -793,53 +815,66 @@
     chains = groups * heads
     wide = (total, width)
     mats = 2 * total * model
+    order = Order()
+    run = order.run
+
+    def begin(keep, send, scatter, gather, tag):
+        made = Sum(order, keep, send, scatter, gather, tag)
+        made.place = place
+        return made
+
     weight = pltpu.VMEM((model, width), bf16)
     rows = pltpu.VMEM((total, model), bf16)
-
-    hidden, proj, gate_raw, beta_raw, grad_down, x_own, gd_own, meta = run(
-        pre_kernel,
-        "pre",
+    ext_shape = (total + TAIL, 3 * width)
+    conv_shape = (total, 3 * width)
+    inv_shape = (chains, GROUP, GROUP)
+    map_shape = (chains, DH, DH)
+    (
+        gate_raw, beta_raw, meta, qkv, wmix, umix, score, zst, dev, last, mout, oloc,
+        hidden, grad_down, x_own, gd_own, ext, conv, inv, amap,
+    ) = run(
+        front_kernel,
+        "front",
         [
-            ((total, model), bf16),
-            ((total, 3 * width), f32),
             (wide, f32),
             ((total, heads), f32),
-            ((total, model), bf16),
-            ((share, model), bf16),
-            ((share, model), bf16),
             ((2, groups), jnp.int32),
-        ],
-        [first, tp, seq_groups, seq_pads, layer_input, cotangent, norm_in, w_query, w_key, w_value, w_gate_out, wb],
-        smem=(0, 1, 2, 3),
-        smem_out=(7,),
-        hbm=(4, 5, 7, 8, 9, 10),
-        scratch=[rows, rows, weight, weight, weight, weight, pltpu.SemaphoreType.DMA((6,))],
-        flops=mats * 4 * width,
-        vmem=12,
-    )
-    ext, conv, qkv, wmix, umix, inv, score, amap, zst, dev, last, mout, oloc = run(
-        mix_kernel,
-        "mix",
-        [
-            ((total + TAIL, 3 * width), f32),
-            ((total, 3 * width), f32),
-            ((total, 3 * width), f32),
+            (conv_shape, f32),
             (wide, f32),
             (wide, f32),
-            ((chains, GROUP, GROUP), f32),
-            ((chains, GROUP, GROUP), f32),
-            ((chains, DH, DH), f32),
+            (inv_shape, f32),
             ((chains, DH, 2 * DH), f32),
             ((heads, DH, 2 * DH), f32),
             ((heads, DH, DH), f32),
             (wide, f32),
             (wide, f32),
+            ((total, model), bf16),
+            ((total, model), bf16),
+            ((share, model), bf16),
+            ((share, model), bf16),
+            (ext_shape, f32),
+            (conv_shape, f32),
+            (inv_shape, f32),
+            (map_shape, f32),
         ],
-        [meta, proj, tail, norm_in, w_query, w_key, w_value, *taps, beta_raw],
-        smem=(0,),
-        hbm=(4, 5, 6),
-        scratch=[pltpu.VMEM((chains, DH, DH), f32), weight, weight, weight, pltpu.SemaphoreType.DMA((3,))],
-        flops=6 * mats * width,
+        [first, tp, seq_groups, seq_pads, layer_input, cotangent, norm_in, w_query, w_key, w_value, w_gate_out, wb, tail, *taps],
+        smem=(0, 1, 2, 3),
+        smem_out=(2,),
+        hbm=(4, 5, 7, 8, 9, 10),
+        hbm_out=tuple(range(12, 20)),
+        pin=(2, 3, 4, 5, 6, 7, 8, 9, 10, 11, 13, 14, 15),
+        scratch=[
+            rows, rows, weight, weight, weight, weight, rows, rows,
+            pltpu.VMEM(ext_shape, f32),
+            pltpu.VMEM(conv_shape, f32),
+            pltpu.VMEM(inv_shape, f32),
+            pltpu.VMEM(map_shape, f32),
+            pltpu.VMEM(map_shape, f32),
+            pltpu.SemaphoreType.DMA((6,)),
+            pltpu.SemaphoreType.DMA((8,)),
+        ],
+        flops=mats * 10 * width,
+        vmem=20,
     )
     hops = hops_of(dev, last, 1, reach)
     heads_out, attended, send, keep, entry = run(
@@ -850,49 +885,65 @@
         smem=(0,),
         flops=mats * width,
     )
-    kept, got = scatter_sum(send, keep)
+    kept, far = scatter_first(order, keep, send)
+    got = swap(far, 2)
     states, vnew, qeff = run(
         states_kernel,
         "states",
-        [((chains, DH, DH), f32), (wide, f32), (wide, f32)],
+        [(map_shape, f32), (wide, f32), (wide, f32)],
         [entry, zst, qkv, wmix, umix, score],
         flops=mats * width,
     )
-    x_own, states = lax.optimization_barrier((x_own, states))
     residual, second_own = run(
         mid_kernel,
         "mid",
         [((share, model), f32), ((share, model), bf16)],
-        [x_own, kept, got, norm_mid],
-    )
-    second, inner, dgate, dup, down_send, down_keep, send, keep = run(
-        ffn_kernel,
+        [x_own, kept[0], got[0], norm_mid],
+    )
+    size = ffw // blocks
+    bits = [(0, 1, 2), (1, 0, 2), (0, 1, 2), (0, 1, 2), (1, 0, 2)]
+    gathers = [(2, 1, 0), (2, 0, 1), (2, 1, 0), (2, 1, 0), (2, 0, 1)]
+    cut_rows = ffw // 2
+    plans_a = [
+        Plan(0, bits[0], 0, size),
+        Plan(1, bits[1], 0, size),
+        Plan(2, bits[2], 0, size),
+    ]
+    down_send, down_keep, send, keep, *sums = run(
+        lambda *r: ffn_kernel(plans_a, *r),
         "ffn",
         [
-            ((total, model), bf16),
-            ((total, ffw), bf16),
-            ((total, ffw), bf16),
-            ((total, ffw), bf16),
             ((2, share, model), bf16),
             ((2, share, model), f32),
             ((2, share, model), bf16),
             ((2, share, model), f32),
+            *(sum_shapes(blocks, size, model) * 3),
         ],
-        [tp, *gather_rel(second_own), grad_down, w_gate.T, w_up.T, w_down],
-        smem=(0,),
-        flops=6 * mats * ffw,
-        vmem=16,
-    )
-    keep_a, send_a = grads(place, ((inner, grad_down), (dgate, second)), blocks, "grads_a")
-    kept, got = scatter_sum(send, keep)
-    residual, send_a = lax.optimization_barrier((residual, send_a))
-    near_a, far_a = sum_seq(keep_a, send_a, blocks, "a")
+        [tp, place, *gather_rel(second_own), grad_down, w_gate.T, w_up.T, w_down],
+        smem=(0, 1),
+        scratch=[
+            rows,
+            pltpu.VMEM((total, ffw), bf16),
+            pltpu.VMEM((total, ffw), bf16),
+            pltpu.VMEM((total, ffw), bf16),
+            pltpu.VMEM((ffw, model), f32),
+        ],
+        flops=9 * mats * ffw,
+        vmem=24,
+    )
+    near = swap(send, 1)
+    a1 = begin(sums[0], sums[1], bits[0], gathers[0], "a1")
+    a2 = begin(sums[2], sums[3], bits[1], gathers[1], "a2")
+    kept, far = fold(order, keep, near, "fold_tp")
+    got = swap(far, 2)
     grad_residual, branch_own, mid_part = run(
         turn_kernel,
         "turn",
         [((share, model), f32), ((share, model), bf16), ((1, model), f32)],
-        [kept, got, residual, norm_mid, gd_own],
-    )
+        [kept[0], got[0], residual, norm_mid, gd_own],
+    )
+    branch_all = gather_rel(branch_own)
+    a3 = begin(sums[4], sums[5], bits[2], gathers[2], "a3")
     branch, dgate_raw, dout, rst, dev, last, head_part = run(
         flow_kernel,
         "flow",
@@ -905,9 +956,9 @@
             ((heads, DH, DH), f32),
             ((1, DH), f32),
         ],
-        [tp, meta, *gather_rel(branch_own), w_out, heads_out, gate_raw, norm_head, qeff, amap],
+        [tp, meta, *branch_all, w_out, heads_out, gate_raw, norm_head, qeff, amap],
         smem=(0, 1),
-        scratch=[pltpu.VMEM((chains, DH, DH), f32)],
+        scratch=[pltpu.VMEM(map_shape, f32)],
         flops=3 * mats * width,
     )
     hops = hops_of(dev, last, -1, reach)
@@ -918,14 +969,27 @@
         [qkv, dout, vnew, states, score],
         flops=mats * width,
     )
-    keep_b, send_b = grads(place, ((dup, second), (attended, branch)), blocks, "grads_b")
-    ndo, send_b = lax.optimization_barrier((ndo, send_b))
-    near_b, far_b = sum_seq(keep_b, send_b, blocks, "b")
+    a1.step()
+    a2.step()
+    plans_b = [
+        Plan(0, bits[3], 0, width // blocks),
+        Plan(0, bits[3], width // blocks, model // blocks, folds=model // width),
+    ]
+    sums = run(
+        lambda *r: grads_b_kernel(plans_b, *r),
+        "grads_b",
+        sum_shapes(blocks, 2 * width // blocks, model),
+        [place, attended, branch, hidden, dgate_raw],
+        smem=(0,),
+        scratch=[pltpu.VMEM((width, model), f32), pltpu.VMEM((model, width), f32)],
+        flops=2 * mats * width,
+    )
+    b1 = begin(*sums, bits[3], gathers[3], "b1")
     gp, last, halo, dbeta, dtaps = run(
         lambda *r: back_kernel(reach, *r),
         "back",
         [
-            ((total, 3 * width), bf16),
+            (conv_shape, bf16),
             ((TAIL, 3 * width), f32),
             ((8, 3 * width), f32),
             ((total, LANES), bf16),
@@ -937,91 +1001,137 @@
         flops=3 * mats * width,
     )
     incoming = shift(halo, -1)
+    a1.step()
+    a2.step()
+    a3.step()
     gp, send, keep = run(
         hid_kernel,
         "hid",
-        [((total, 3 * width), bf16), ((2, share, model), bf16), ((2, share, model), f32)],
+        [(conv_shape, bf16), ((2, share, model), bf16), ((2, share, model), f32)],
         [tp, gp, last, incoming, dgate_raw, dbeta, w_query, w_key, w_value, w_gate_out, wb],
         smem=(0,),
         flops=mats * 4 * width,
         vmem=12,
     )
-    half = (blocks // 2, model // blocks, 4 * width)
-    keep_c, send_c = run(
-        hidden_grads_kernel,
+    near = swap(send, 1)
+    half = model // 2
+    plans_c = [
+        Plan(0, bits[3], 0, half // blocks),
+        Plan(1, bits[4], 0, half // blocks, start=half),
+    ]
+    sums = run(
+        lambda *r: grads_c_kernel(plans_c, *r),
         "grads_c",
-        [(half, f32), (half, bf16)],
-        [place, hidden, gp, dgate_raw],
+        sum_shapes(blocks, half // blocks, 3 * width) * 2,
+        [place, hidden, gp],
         smem=(0,),
-        scratch=[pltpu.VMEM((model, 4 * width), f32)],
-        flops=mats * 4 * width,
+        scratch=[pltpu.VMEM((model, 3 * width), f32)],
+        flops=mats * 3 * width,
         vmem=16,
     )
-    near_c, far_c = sum_seq(keep_c, send_c, blocks, "c")
-    kept, got = scatter_sum(send, keep)
+    c1 = begin(sums[0], sums[1], bits[3], gathers[3], "c1")
+    c2 = begin(sums[2], sums[3], bits[4], gathers[4], "c2")
+    kept, far = fold(order, keep, near, "fold_tp")
+    got = swap(far, 2)
+    b1.step()
+    a1.step()
+    a2.step()
     grad_in_own, in_part = run(
         in_kernel,
         "inp",
         [((share, model), bf16), ((1, model), f32)],
-        [kept, got, x_own, norm_in, grad_residual],
-    )
+        [kept[0], got[0], x_own, norm_in, grad_residual],
+    )
+    grad_in_all = gather_rel(grad_in_own)
+    row8 = ((8, model), f32)
+    small, gains = run(
+        small_kernel, "small", [row8, row8], [dtaps, dbeta, hidden, in_part, mid_part, head_part]
+    )
+    down_near = swap(down_send, 1)
+    a3.step()
+    b1.step()
+    c1.step()
+    c2.step()
+    kept, far = fold(order, down_keep, down_near, "fold_tp")
+    got = swap(far, 2)
+    a1.step()
+    a2.step()
     (grad_input,) = run(
         place_kernel,
         "place_in",
         [((total, model), f32)],
-        [tp, *gather_rel(grad_in_own)],
+        [tp, *grad_in_all],
         smem=(0,),
     )
-    kept, got = scatter_sum(down_send, down_keep)
     (out_own,) = run(
         outblock_kernel,
         "outblk",
         [((share, model), bf16)],
-        [tp, meta, kept, got, residual],
+        [tp, meta, kept[0], got[0], residual],
         smem=(0, 1),
     )
+    out_all = gather_rel(out_own)
+    a3.step()
+    b1.step()
+    c1.step()
+    c2.step()
+    a1.step()
+    a2.step()
+    gains = plus(order, gains, swap(gains, 1))
+    a3.step()
+    b1.step()
+    c1.step()
+    c2.step()
+    gains = plus(order, gains, swap(gains, 2))
+    step = 1
+    small = jnp.concatenate([small, gains], axis=0)
     (block_out,) = run(
         place_kernel,
         "place_out",
         [((total, model), bf16)],
-        [tp, *gather_rel(out_own)],
+        [tp, *out_all],
         smem=(0,),
     )
-    row8 = ((8, model), f32)
-    small, gains = run(
-        small_kernel, "small", [row8, row8], [dtaps, dbeta, hidden, in_part, mid_part, head_part]
-    )
-    for axis in ("tp", "seq"):
-        step = 1
-        while step < lax.axis_size(axis):
-            gains = plus(gains, swap(gains, step, axis))
-            if axis == "seq":
-                small = plus(small, swap(small, step, axis))
-            step *= 2
-    grad_down_w, grad_gate_w = run(
-        settle_kernel,
-        "settle_a",
-        [((ffw, model), f32), ((ffw, model), f32)],
-        [place, near_a, far_a],
-        smem=(0,),
-    )
-    grad_up_w, grad_out_w = run(
-        settle_kernel,
-        "settle_b",
-        [((ffw, model), f32), ((width, model), f32)],
-        [place, near_b, far_b],
-        smem=(0,),
-    )
+    a3.step()
+    b1.step()
+    c1.step()
+    c2.step()
+    while step < seq_count:
+        small = plus(order, small, swap(small, step, "seq"))
+        step *= 2
+    c1.step()
+    c2.step()
+    (grad_down_w,) = a1.settle([plans_a[0]], [(ffw, model)], "settle_a1")
+    (grad_gate_w,) = a2.settle([plans_a[1]], [(ffw, model)], "settle_a2")
+    (grad_up_w,) = a3.settle([plans_a[2]], [(ffw, model)], "settle_a3")
+    grad_out_w, grad_gate_out_w = b1.settle(
+        plans_b, [(width, model), (model, width)], "settle_b1"
+    )
+
+    def settle_c(place, near1, far1, near2, far2, *outs):
+        for plan, gather, near, far in (
+            (plans_c[0], gathers[3], near1, far1),
+            (plans_c[1], gathers[4], near2, far2),
+        ):
+            for m in range(blocks):
+                source = far if (m >> gather[-1]) & 1 else near
+                at = rank_of(m, gather[-2::-1])
+                begin = plan.start + (m ^ place[0]) * plan.size
+                for i, out in enumerate(outs):
+                    out[pl.ds(pl.multiple_of(begin, 8), plan.size)] = source[
+                        at, :, i * width : (i + 1) * width
+                    ].astype(f32)
+
     hidden_sums = run(
-        settle_cols_kernel,
+        settle_c,
         "settle_c",
-        [((model, width), f32)] * 4,
-        [place, near_c, far_c],
+        [((model, width), f32)] * 3,
+        [place, c1.own, c1.got, c2.own, c2.got],
         smem=(0,),
     )
     cut = model // 4
     head_cut = DH // 4
-    gain_of = lambda row, size: lax.dynamic_slice(gains, (row, tp_rank * size), (1, size)).reshape(size)
+    gain_of = lambda row, size: lax.dynamic_slice(small, (8 + row, tp_rank * size), (1, size)).reshape(size)
     tap_of = lambda i: small[:KW, i * width : (i + 1) * width]
     return (
         block_out,
@@ -1034,7 +1144,7 @@
         tap_of(1),
         tap_of(2),
         small[KW : KW + heads].T,
-        hidden_sums[3],
+        grad_gate_out_w,
         gain_of(2, head_cut),
         grad_out_w,
         gain_of(1, cut),

time: 382 us -> 329 us (0.86)
  waiting for transfers between devices: 203 us -> 145 us
  starting transfers between devices: 57.6 us -> 79.1 us
  local copies, waits for them, and re-layouts: 32.2 us -> 17 us
    ppermute x46 -> x61, waiting for transfers between devices: 184 us -> 130 us  [swap(): return lax.ppermute(value, axis, [(i, i ^ bit) for i in range(count)])]
    ppermute x46 -> x61, starting transfers between devices: 41.5 us -> 62.3 us  [swap(): return lax.ppermute(value, axis, [(i, i ^ bit) for i in range(count)])]
    unnamed x164 -> x88, local copies, waits for them, and re-layouts: 29 us -> 13.8 us
    pallas_call x49 -> x61, Pallas kernels: 86.5 us -> 85.7 us  [run(): pl.pallas_call(kernel, name=name, out_shape=shapes, in_specs=[pl.BlockSpe...]
  transfers between devices with their start and end apart: 52 -> 67, of which waited for: 31 -> 33; matrix products, arithmetic and copies ran while one was open for 1% -> 1% of each run, Pallas kernels for 15% -> 15%
where the time goes in v2:
time: 329 us
  waiting for transfers between devices  145 us (44%)
  Pallas kernels  85.7 us (26%)
  starting transfers between devices  79.1 us (24%)
  local copies, waits for them, and re-layouts  17 us (5%)
    ppermute x61, waiting for transfers between devices, swap(): return lax.ppermute(value, axis, [(i, i ^ bit) for i in range(count)])  130 us
    pallas_call x61, Pallas kernels, run(): pl.pallas_call(kernel, name=name, out_shape=shapes, in_specs=[pl.BlockSpe...  85.7 us
    ppermute x61, starting transfers between devices, swap(): return lax.ppermute(value, axis, [(i, i ^ bit) for i in range(count)])  62.3 us
    ppermute x6, starting transfers between devices, shift(): return lax.ppermute(value, 'seq', pairs)  16.8 us
    ppermute x6, waiting for transfers between devices, shift(): return lax.ppermute(value, 'seq', pairs)  15.4 us
    unnamed x88, local copies, waits for them, and re-layouts  13.8 us
  transfers between devices with their start and end apart: 67, of which 33 were waited for; matrix products, arithmetic and copies ran while one was open for 1% of the time, Pallas kernels for 15%

profile of v2, /device:TPU:0, one launch (start us, length us, event | category | flops | bytes accessed | tf_op | source)
XLA Modules:
  0.0 328.8 jit_solution(1214611879144712780)
XLA Ops:
  1.4 4.9 %collective-permute-start = (bf16[16,1024]{1,0:T(8,128)(2,1)S(1)}, bf16[16,1024]{1,0:T(8,128)(2,1)S(1)}, u32[]{:S(2)}, u32[]{:S(2)}) collective-permute-start(bf16[16,1024]{1,0:T(8,128)(2,1)S(1)} %slice.15), channel_id=1, source_target_pairs={{0,4},{4,8},{8,12},{12,16},{16,20},{20,24},{24,28},{1,5},{5,9},{9,... | collective-permute-start | bytes 98312 | tf_op jit(solution)/shard_map/ppermute | solution.py:751
  7.9 21.8 %front.1 = (f32[512,256]{1,0:T(8,128)S(1)}, f32[512,2]{1,0:T(8,128)S(1)}, s32[2,8]{1,0:T(2,128)S(1)}, f32[512,768]{1,0:T(8,128)S(1)}, f32[512,256]{1,0:T(8,128)S...) custom-call(s32[1]{0:T(128)} %bitcast.1.first, ...), custom_call_target="tpu_custom_call" | custom-call | flops 2684354560 | bytes 18317512 | tf_op jit(solution)/shard_map/front/pallas_call | solution.py:61
  34.0 4.2 %collective-permute-start.1 = (f32[2,128,256]{2,1,0:T(8,128)S(1)}, f32[2,128,256]{2,1,0:T(8,128)S(1)}, u32[]{:S(2)}, u32[]{:S(2)}) collective-permute-start(f32[2,128,256]{2,1,0:T(8,128)S(1)} %get-tuple-element.187), channel_id=1, source_target_pairs={{0,4},{4,8},{8,12},{12,16},{16,20},{20,24},{24,28},{1,5},{5,9},{9,... | collective-permute-start | bytes 786440 | tf_op jit(solution)/shard_map/ppermute | solution.py:751
  38.3 3.7 %collective-permute-start.2 = (f32[2,128,128]{2,1,0:T(8,128)S(1)}, f32[2,128,128]{2,1,0:T(8,128)S(1)}, u32[]{:S(2)}, u32[]{:S(2)}) collective-permute-start(f32[2,128,128]{2,1,0:T(8,128)S(1)} %get-tuple-element.190), channel_id=1, source_target_pairs={{0,8},{4,12},{8,16},{12,20},{16,24},{20,28},{1,9},{5,13},{9,17},{1... | collective-permute-start | bytes 393224 | tf_op jit(solution)/shard_map/ppermute | solution.py:751
  51.1 3.8 %states.1 = (f32[16,128,128]{2,1,0:T(8,128)S(1)}, f32[512,256]{1,0:T(8,128)S(1)}, f32[512,256]{1,0:T(8,128)S(1)}) custom-call(f32[2,128,128]{2,1,0:T(8,128)S(1)} %get-tuple-element.199.entry, f32[16,128,256]{2,1,0:T(8,128)S(1)} %get-tuple-element.200.zst, f32[512,768]{1,0:T(8,128)S(1)} %get-tuple-element.232.qkv.r_4_, ...), custom_call_target="tpu_custom_call" | custom-call | flops 268435456 | bytes 7208960 | tf_op jit(solution)/shard_map/states/pallas_call | solution.py:61
  60.3 6.4 %collective-permute-done.6.r_4_ = bf16[128,1024]{1,0:T(8,128)(2,1)} collective-permute-done((bf16[128,1024]{1,0:T(8,128)(2,1)}, bf16[128,1024]{1,0:T(8,128)(2,1)}, u32[]{:S(2)}, u32[]{:S(2)}) %collective-permute-start.6) | collective-permute-done | bytes 262176 | tf_op jit(solution)/shard_map/ppermute | solution.py:603
  73.9 9.6 %ffn.1 = (bf16[2,128,1024]{2,1,0:T(8,128)(2,1)S(1)}, f32[2,128,1024]{2,1,0:T(8,128)S(1)}, bf16[2,128,1024]{2,1,0:T(8,128)(2,1)S(1)}, f32[2,128,1024]{2,1,0:T(8,1...) custom-call(s32[1]{0:T(128)} %bitcast.tp.r_0_, ...), custom_call_target="tpu_custom_call" | custom-call | flops 6643777536 | bytes 16056328 | tf_op jit(solution)/shard_map/ffn/pallas_call | solution.py:61
  95.8 6.1 %collective-permute-done.11.b2 = bf16[128,1024]{1,0:T(8,128)(2,1)S(1)} collective-permute-done((bf16[128,1024]{1,0:T(8,128)(2,1)S(1)}, bf16[128,1024]{1,0:T(8,128)(2,1)S(1)}, u32[]{:S(2)}, u32[]{:S(2)}) %collective-permute-start.11) | collective-permute-done | bytes 262176 | tf_op jit(solution)/shard_map/ppermute | solution.py:603
  105.7 5.0 %flow.1 = (bf16[512,1024]{1,0:T(8,128)(2,1)S(1)}, bf16[512,256]{1,0:T(8,128)(2,1)S(1)}, f32[512,256]{1,0:T(8,128)S(1)}, f32[16,128,256]{2,1,0:T(8,128)S(1)}, f32...) custom-call(s32[1]{0:T(128)} %bitcast.tp.r_0_, ...), custom_call_target="tpu_custom_call" | custom-call | flops 805306368 | bytes 8520516 | tf_op jit(solution)/shard_map/flow/pallas_call | solution.py:61
  112.3 5.0 %side.1 = (f32[512,256]{1,0:T(8,128)S(1)}, f32[512,256]{1,0:T(8,128)S(1)}, f32[512,256]{1,0:T(8,128)S(1)}) custom-call(f32[512,768]{1,0:T(8,128)S(1)} %get-tuple-element.232.qkv.r_4_, f32[512,256]{1,0:T(8,128)S(1)} %get-tuple-element.233.dout, f32[512,256]{1,0:T(8,128)S(1)} %copy-done.3, f32[16,128,128]{2,1,0:T(8,128)S(1)} %copy-done.1, ...), custom_call_target="tpu_custom_call" | custom-call | flops 268435456 | bytes 5505024 | tf_op jit(solution)/shard_map/side/pallas_call | solution.py:61
  128.2 4.3 %collective-permute-done.16.r_2_ = f32[2,128,128]{2,1,0:T(8,128)S(1)} collective-permute-done((f32[2,128,128]{2,1,0:T(8,128)S(1)}, f32[2,128,128]{2,1,0:T(8,128)S(1)}, u32[]{:S(2)}, u32[]{:S(2)}) %collective-permute-start.16) | collective-permute-done | bytes 131104 | tf_op jit(solution)/shard_map/ppermute | solution.py:751
  132.5 16.3 %back.1 = (bf16[512,768]{1,0:T(8,128)(2,1)S(1)}, f32[16,768]{1,0:T(8,128)S(1)}, f32[8,768]{1,0:T(8,128)S(1)}, bf16[512,128]{1,0:T(8,128)(2,1)S(1)}, f32[4,768]{1,0:T(4,128)S(1)}) custom-call(s32[2,8]{1,0:T(2,128)S(1)} %get-tuple-element.185.meta.r_0_, f32[2,128,256]{2,1,0:T(8,128)S(1)} %collective-permute-done.13.r_1_, ...), custom_call_target="tpu_custom_call" | custom-call | flops 805306368 | bytes 11679808 | tf_op jit(solution)/shard_map/back/pallas_call | solution.py:61
  150.6 4.0 %collective-permute-done.20.incoming = f32[8,768]{1,0:T(8,128)S(1)} collective-permute-done((f32[8,768]{1,0:T(8,128)S(1)}, f32[8,768]{1,0:T(8,128)S(1)}, u32[]{:S(2)}, u32[]{:S(2)}) %collective-permute-start.20) | collective-permute-done | bytes 24608 | tf_op jit(solution)/shard_map/ppermute | solution.py:751
  165.4 5.5 %collective-permute-done.22.got = bf16[4,64,1024]{2,1,0:T(8,128)(2,1)S(1)} collective-permute-done((bf16[4,64,1024]{2,1,0:T(8,128)(2,1)S(1)}, bf16[4,64,1024]{2,1,0:T(8,128)(2,1)S(1)}, u32[]{:S(2)}, u32[]{:S(2)}) %collective-permute-start.22) | collective-permute-done | bytes 524320 | tf_op jit(solution)/shard_map/ppermute | solution.py:603
  185.4 13.6 %collective-permute-done.27.got = bf16[2,64,1024]{2,1,0:T(8,128)(2,1)S(1)} collective-permute-done((bf16[2,64,1024]{2,1,0:T(8,128)(2,1)S(1)}, bf16[2,64,1024]{2,1,0:T(8,128)(2,1)S(1)}, u32[]{:S(2)}, u32[]{:S(2)}) %collective-permute-start.27) | collective-permute-done | bytes 262176 | tf_op jit(solution)/shard_map/ppermute | solution.py:603
  203.5 10.4 %collective-permute-done.32.b = bf16[1,88,1024]{2,1,0:T(8,128)(2,1)S(1)} collective-permute-done((bf16[1,88,1024]{2,1,0:T(8,128)(2,1)S(1)}, bf16[1,88,1024]{2,1,0:T(8,128)(2,1)S(1)}, u32[]{:S(2)}, u32[]{:S(2)}) %collective-permute-start.32) | collective-permute-done | bytes 180256 | tf_op jit(solution)/shard_map/ppermute | solution.py:603
  213.9 6.6 %collective-permute-done.38.got = bf16[1,64,1024]{2,1,0:T(8,128)(2,1)S(1)} collective-permute-done((bf16[1,64,1024]{2,1,0:T(8,128)(2,1)S(1)}, bf16[1,64,1024]{2,1,0:T(8,128)(2,1)S(1)}, u32[]{:S(2)}, u32[]{:S(2)}) %collective-permute-start.38) | collective-permute-done | bytes 131104 | tf_op jit(solution)/shard_map/ppermute | solution.py:603
  228.3 7.9 %collective-permute-done.39.got = bf16[2,64,768]{2,1,0:T(8,128)(2,1)S(1)} collective-permute-done((bf16[2,64,768]{2,1,0:T(8,128)(2,1)S(1)}, bf16[2,64,768]{2,1,0:T(8,128)(2,1)S(1)}, u32[]{:S(2)}, u32[]{:S(2)}) %collective-permute-start.39) | collective-permute-done | bytes 196640 | tf_op jit(solution)/shard_map/ppermute | solution.py:603
  242.1 9.4 %collective-permute-done.44.b = bf16[1,88,1024]{2,1,0:T(8,128)(2,1)S(1)} collective-permute-done((bf16[1,88,1024]{2,1,0:T(8,128)(2,1)S(1)}, bf16[1,88,1024]{2,1,0:T(8,128)(2,1)S(1)}, u32[]{:S(2)}, u32[]{:S(2)}) %collective-permute-start.44) | collective-permute-done | bytes 180256 | tf_op jit(solution)/shard_map/ppermute | solution.py:603
  256.4 5.9 %collective-permute-done.47.got = bf16[1,64,768]{2,1,0:T(8,128)(2,1)S(1)} collective-permute-done((bf16[1,64,768]{2,1,0:T(8,128)(2,1)S(1)}, bf16[1,64,768]{2,1,0:T(8,128)(2,1)S(1)}, u32[]{:S(2)}, u32[]{:S(2)}) %collective-permute-start.47) | collective-permute-done | bytes 98336 | tf_op jit(solution)/shard_map/ppermute | solution.py:603
  269.7 6.2 %collective-permute-done.53.b = bf16[2,64,1024]{2,1,0:T(8,128)(2,1)S(1)} collective-permute-done((bf16[2,64,1024]{2,1,0:T(8,128)(2,1)S(1)}, bf16[2,64,1024]{2,1,0:T(8,128)(2,1)S(1)}, u32[]{:S(2)}, u32[]{:S(2)}) %collective-permute-start.53) | collective-permute-done | bytes 262176 | tf_op jit(solution)/shard_map/ppermute | solution.py:603
  278.2 5.3 %collective-permute-done.57.b = f32[16,1024]{1,0:T(8,128)S(1)} collective-permute-done((f32[16,1024]{1,0:T(8,128)S(1)}, f32[16,1024]{1,0:T(8,128)S(1)}, u32[]{:S(2)}, u32[]{:S(2)}) %collective-permute-start.57) | collective-permute-done | bytes 65568 | tf_op jit(solution)/shard_map/ppermute | solution.py:603
  292.2 17.9 %collective-permute-done.60.b = bf16[2,64,768]{2,1,0:T(8,128)(2,1)S(1)} collective-permute-done((bf16[2,64,768]{2,1,0:T(8,128)(2,1)S(1)}, bf16[2,64,768]{2,1,0:T(8,128)(2,1)S(1)}, u32[]{:S(2)}, u32[]{:S(2)}) %collective-permute-start.60) | collective-permute-done | bytes 196640 | tf_op jit(solution)/shard_map/ppermute | solution.py:603
  322.8 4.2 %collective-permute-done.65.far1 = bf16[4,64,768]{2,1,0:T(8,128)(2,1)S(1)} collective-permute-done((bf16[4,64,768]{2,1,0:T(8,128)(2,1)S(1)}, bf16[4,64,768]{2,1,0:T(8,128)(2,1)S(1)}, u32[]{:S(2)}, u32[]{:S(2)}) %collective-permute-start.65) | collective-permute-done | bytes 393248 | tf_op jit(solution)/shard_map/ppermute | solution.py:603
  (265 shorter events, 139.2 us)
Async XLA Ops:
  87.1 30.2 %collective-permute-start.14 = (bf16[4,88,1024]{2,1,0:T(8,128)(2,1)S(1)}, bf16[4,88,1024]{2,1,0:T(8,128)(2,1)S(1)}, u32[]{:S(2)}, u32[]{:S(2)}) collective-permute-start(bf16[4,88,1024]{2,1,0:T(8,128)(2,1)S(1)} %get-tuple-element.237), channel_id=1, source_target_pairs={{0,4},{4,0},{8,12},{12,8},{16,20},{20,16},{24,28},{28,24},{1,5},{5... | collective-permute-start | bytes 2162696 | tf_op jit(solution)/shard_map/ppermute | solution.py:603
  90.7 30.3 %collective-permute-start.15 = (bf16[4,88,1024]{2,1,0:T(8,128)(2,1)S(1)}, bf16[4,88,1024]{2,1,0:T(8,128)(2,1)S(1)}, u32[]{:S(2)}, u32[]{:S(2)}) collective-permute-start(bf16[4,88,1024]{2,1,0:T(8,128)(2,1)S(1)} %get-tuple-element.240), channel_id=1, source_target_pairs={{0,8},{4,12},{8,0},{12,4},{16,24},{20,28},{24,16},{28,20},{1,9},{5... | collective-permute-start | bytes 2162696 | tf_op jit(solution)/shard_map/ppermute | solution.py:603
  101.9 48.5 %collective-permute-start.19 = (bf16[4,88,1024]{2,1,0:T(8,128)(2,1)S(1)}, bf16[4,88,1024]{2,1,0:T(8,128)(2,1)S(1)}, u32[]{:S(2)}, u32[]{:S(2)}) collective-permute-start(bf16[4,88,1024]{2,1,0:T(8,128)(2,1)S(1)} %get-tuple-element.263), channel_id=1, source_target_pairs={{0,4},{4,0},{8,12},{12,8},{16,20},{20,16},{24,28},{28,24},{1,5},{5... | collective-permute-start | bytes 2162696 | tf_op jit(solution)/shard_map/ppermute | solution.py:603
  110.7 17.5 %collective-permute-start.13 = (f32[2,128,256]{2,1,0:T(8,128)S(1)}, f32[2,128,256]{2,1,0:T(8,128)S(1)}, u32[]{:S(2)}, u32[]{:S(2)}) collective-permute-start(f32[2,128,256]{2,1,0:T(8,128)S(1)} %get-tuple-element.227), channel_id=1, source_target_pairs={{4,0},{8,4},{12,8},{16,12},{20,16},{24,20},{28,24},{5,1},{9,5},{13... | collective-permute-start | bytes 786440 | tf_op jit(solution)/shard_map/ppermute | solution.py:751
  117.4 32.8 %collective-permute-start.17 = (bf16[2,88,1024]{2,1,0:T(8,128)(2,1)S(1)}, bf16[2,88,1024]{2,1,0:T(8,128)(2,1)S(1)}, u32[]{:S(2)}, u32[]{:S(2)}) collective-permute-start(bf16[2,88,1024]{2,1,0:T(8,128)(2,1)S(1)} %get-tuple-element.257), channel_id=1, source_target_pairs={{0,8},{4,12},{8,0},{12,4},{16,24},{20,28},{24,16},{28,20},{1,9},{5... | collective-permute-start | bytes 1081352 | tf_op jit(solution)/shard_map/ppermute | solution.py:603
  121.2 29.1 %collective-permute-start.18 = (bf16[2,88,1024]{2,1,0:T(8,128)(2,1)S(1)}, bf16[2,88,1024]{2,1,0:T(8,128)(2,1)S(1)}, u32[]{:S(2)}, u32[]{:S(2)}) collective-permute-start(bf16[2,88,1024]{2,1,0:T(8,128)(2,1)S(1)} %get-tuple-element.260), channel_id=1, source_target_pairs={{0,4},{4,0},{8,12},{12,8},{16,20},{20,16},{24,28},{28,24},{1,5},{5... | collective-permute-start | bytes 1081352 | tf_op jit(solution)/shard_map/ppermute | solution.py:603
  164.3 18.1 %collective-permute-start.26 = (bf16[2,88,1024]{2,1,0:T(8,128)(2,1)S(1)}, bf16[2,88,1024]{2,1,0:T(8,128)(2,1)S(1)}, u32[]{:S(2)}, u32[]{:S(2)}) collective-permute-start(bf16[2,88,1024]{2,1,0:T(8,128)(2,1)S(1)} %get-tuple-element.294), channel_id=1, source_target_pairs={{0,8},{4,12},{8,0},{12,4},{16,24},{20,28},{24,16},{28,20},{1,9},{5... | collective-permute-start | bytes 1081352 | tf_op jit(solution)/shard_map/ppermute | solution.py:603
  171.0 28.8 %collective-permute-start.30 = (bf16[2,128,1024]{2,1,0:T(8,128)(2,1)S(1)}, bf16[2,128,1024]{2,1,0:T(8,128)(2,1)S(1)}, u32[]{:S(2)}, u32[]{:S(2)}) collective-permute-start(bf16[2,128,1024]{2,1,0:T(8,128)(2,1)S(1)} %get-tuple-element.215), channel_id=1, source_target_pairs={{0,1},{1,0},{2,3},{3,2},{4,5},{5,4},{6,7},{7,6},{8,9},{9,8},{10,11... | collective-permute-start | bytes 1572872 | tf_op jit(solution)/shard_map/ppermute | solution.py:603
  177.8 21.9 %collective-permute-start.29 = (bf16[4,64,768]{2,1,0:T(8,128)(2,1)S(1)}, bf16[4,64,768]{2,1,0:T(8,128)(2,1)S(1)}, u32[]{:S(2)}, u32[]{:S(2)}) collective-permute-start(bf16[4,64,768]{2,1,0:T(8,128)(2,1)S(1)} %get-tuple-element.303), channel_id=1, source_target_pairs={{0,8},{4,12},{8,0},{12,4},{16,24},{20,28},{24,16},{28,20},{1,9},{5... | collective-permute-start | bytes 1179656 | tf_op jit(solution)/shard_map/ppermute | solution.py:603
  177.9 21.2 %collective-permute-start.27 = (bf16[2,64,1024]{2,1,0:T(8,128)(2,1)S(1)}, bf16[2,64,1024]{2,1,0:T(8,128)(2,1)S(1)}, u32[]{:S(2)}, u32[]{:S(2)}) collective-permute-start(bf16[2,64,1024]{2,1,0:T(8,128)(2,1)S(1)} %get-tuple-element.297), channel_id=1, source_target_pairs={{0,8},{4,12},{8,0},{12,4},{16,24},{20,28},{24,16},{28,20},{1,9},{5... | collective-permute-start | bytes 786440 | tf_op jit(solution)/shard_map/ppermute | solution.py:603
  182.4 21.1 %collective-permute-start.34 = (bf16[128,1024]{1,0:T(8,128)(2,1)S(1)}, bf16[128,1024]{1,0:T(8,128)(2,1)S(1)}, u32[]{:S(2)}, u32[]{:S(2)}) collective-permute-start(bf16[128,1024]{1,0:T(8,128)(2,1)S(1)} %get-tuple-element.309.a0), channel_id=1, source_target_pairs={{0,2},{1,3},{2,0},{3,1},{4,6},{5,7},{6,4},{7,5},{8,10},{9,11},{10,... | collective-permute-start | bytes 786440 | tf_op jit(solution)/shard_map/ppermute | solution.py:603
  199.1 21.5 %collective-permute-start.33 = (bf16[128,1024]{1,0:T(8,128)(2,1)S(1)}, bf16[128,1024]{1,0:T(8,128)(2,1)S(1)}, u32[]{:S(2)}, u32[]{:S(2)}) collective-permute-start(bf16[128,1024]{1,0:T(8,128)(2,1)S(1)} %get-tuple-element.309.a0), channel_id=1, source_target_pairs={{0,1},{1,0},{2,3},{3,2},{4,5},{5,4},{6,7},{7,6},{8,9},{9,8},{10,11... | collective-permute-start | bytes 786440 | tf_op jit(solution)/shard_map/ppermute | solution.py:603
  199.9 20.8 %collective-permute-start.36 = (bf16[1,128,1024]{2,1,0:T(8,128)(2,1)S(1)}, bf16[1,128,1024]{2,1,0:T(8,128)(2,1)S(1)}, u32[]{:S(2)}, u32[]{:S(2)}) collective-permute-start(bf16[1,128,1024]{2,1,0:T(8,128)(2,1)S(1)} %get-tuple-element.311), channel_id=1, source_target_pairs={{0,2},{1,3},{2,0},{3,1},{4,6},{5,7},{6,4},{7,5},{8,10},{9,11},{10,... | collective-permute-start | bytes 786440 | tf_op jit(solution)/shard_map/ppermute | solution.py:603
  200.6 20.0 %collective-permute-start.38 = (bf16[1,64,1024]{2,1,0:T(8,128)(2,1)S(1)}, bf16[1,64,1024]{2,1,0:T(8,128)(2,1)S(1)}, u32[]{:S(2)}, u32[]{:S(2)}) collective-permute-start(bf16[1,64,1024]{2,1,0:T(8,128)(2,1)S(1)} %get-tuple-element.316), channel_id=1, source_target_pairs={{0,16},{4,20},{8,24},{12,28},{16,0},{20,4},{24,8},{28,12},{1,17},{... | collective-permute-start | bytes 393224 | tf_op jit(solution)/shard_map/ppermute | solution.py:603
  203.5 19.3 %collective-permute-start.35 = (bf16[128,1024]{1,0:T(8,128)(2,1)S(1)}, bf16[128,1024]{1,0:T(8,128)(2,1)S(1)}, u32[]{:S(2)}, u32[]{:S(2)}) collective-permute-start(bf16[128,1024]{1,0:T(8,128)(2,1)S(1)} %collective-permute-done.34.a2), channel_id=1, source_target_pairs={{0,1},{1,0},{2,3},{3,2},{4,5},{5,4},{6,7},{7,6},{8,9},{9,8},{10,11... | collective-permute-start | bytes 786440 | tf_op jit(solution)/shard_map/ppermute | solution.py:603
  220.5 18.8 %collective-permute-start.41 = (bf16[2,88,1024]{2,1,0:T(8,128)(2,1)S(1)}, bf16[2,88,1024]{2,1,0:T(8,128)(2,1)S(1)}, u32[]{:S(2)}, u32[]{:S(2)}) collective-permute-start(bf16[2,88,1024]{2,1,0:T(8,128)(2,1)S(1)} %a1_pack.2.a), channel_id=1, source_target_pairs={{0,8},{4,12},{8,0},{12,4},{16,24},{20,28},{24,16},{28,20},{1,9},{5... | collective-permute-start | bytes 1081352 | tf_op jit(solution)/shard_map/ppermute | solution.py:603
  220.6 18.9 %collective-permute-start.42 = (bf16[2,88,1024]{2,1,0:T(8,128)(2,1)S(1)}, bf16[2,88,1024]{2,1,0:T(8,128)(2,1)S(1)}, u32[]{:S(2)}, u32[]{:S(2)}) collective-permute-start(bf16[2,88,1024]{2,1,0:T(8,128)(2,1)S(1)} %a2_pack.2.a), channel_id=1, source_target_pairs={{0,4},{4,0},{8,12},{12,8},{16,20},{20,16},{24,28},{28,24},{1,5},{5... | collective-permute-start | bytes 1081352 | tf_op jit(solution)/shard_map/ppermute | solution.py:603
  226.8 24.7 %collective-permute-start.50 = (bf16[128,1024]{1,0:T(8,128)(2,1)S(1)}, bf16[128,1024]{1,0:T(8,128)(2,1)S(1)}, u32[]{:S(2)}, u32[]{:S(2)}) collective-permute-start(bf16[128,1024]{1,0:T(8,128)(2,1)S(1)} %outblk.1.a0), channel_id=1, source_target_pairs={{0,2},{1,3},{2,0},{3,1},{4,6},{5,7},{6,4},{7,5},{8,10},{9,11},{10,... | collective-permute-start | bytes 786440 | tf_op jit(solution)/shard_map/ppermute | solution.py:603
  252.0 17.6 %collective-permute-start.52 = (bf16[2,88,1024]{2,1,0:T(8,128)(2,1)S(1)}, bf16[2,88,1024]{2,1,0:T(8,128)(2,1)S(1)}, u32[]{:S(2)}, u32[]{:S(2)}) collective-permute-start(bf16[2,88,1024]{2,1,0:T(8,128)(2,1)S(1)} %a3_pack.2.a), channel_id=1, source_target_pairs={{0,8},{4,12},{8,0},{12,4},{16,24},{20,28},{24,16},{28,20},{1,9},{5... | collective-permute-start | bytes 1081352 | tf_op jit(solution)/shard_map/ppermute | solution.py:603
  256.4 53.7 %collective-permute-start.61 = (bf16[4,88,1024]{2,1,0:T(8,128)(2,1)S(1)}, bf16[4,88,1024]{2,1,0:T(8,128)(2,1)}, u32[]{:S(2)}, u32[]{:S(2)}) collective-permute-start(bf16[4,88,1024]{2,1,0:T(8,128)(2,1)S(1)} %a1_pack.3.near), channel_id=1, source_target_pairs={{0,4},{4,0},{8,12},{12,8},{16,20},{20,16},{24,28},{28,24},{1,5},{5... | collective-permute-start | bytes 2162696 | tf_op jit(solution)/shard_map/ppermute | solution.py:603
  285.1 30.1 %collective-permute-start.62 = (bf16[4,88,1024]{2,1,0:T(8,128)(2,1)S(1)}, bf16[4,88,1024]{2,1,0:T(8,128)(2,1)}, u32[]{:S(2)}, u32[]{:S(2)}) collective-permute-start(bf16[4,88,1024]{2,1,0:T(8,128)(2,1)S(1)} %a2_pack.3.near), channel_id=1, source_target_pairs={{0,8},{4,12},{8,0},{12,4},{16,24},{20,28},{24,16},{28,20},{1,9},{5... | collective-permute-start | bytes 2162696 | tf_op jit(solution)/shard_map/ppermute | solution.py:603
  286.8 31.3 %collective-permute-start.63 = (bf16[4,88,1024]{2,1,0:T(8,128)(2,1)S(1)}, bf16[4,88,1024]{2,1,0:T(8,128)(2,1)}, u32[]{:S(2)}, u32[]{:S(2)}) collective-permute-start(bf16[4,88,1024]{2,1,0:T(8,128)(2,1)S(1)} %a3_pack.3.near), channel_id=1, source_target_pairs={{0,4},{4,0},{8,12},{12,8},{16,20},{20,16},{24,28},{28,24},{1,5},{5... | collective-permute-start | bytes 2162696 | tf_op jit(solution)/shard_map/ppermute | solution.py:603
  289.5 20.6 %collective-permute-start.60 = (bf16[2,64,768]{2,1,0:T(8,128)(2,1)S(1)}, bf16[2,64,768]{2,1,0:T(8,128)(2,1)S(1)}, u32[]{:S(2)}, u32[]{:S(2)}) collective-permute-start(bf16[2,64,768]{2,1,0:T(8,128)(2,1)S(1)} %c2_pack.2.a), channel_id=1, source_target_pairs={{0,4},{4,0},{8,12},{12,8},{16,20},{20,16},{24,28},{28,24},{1,5},{5... | collective-permute-start | bytes 589832 | tf_op jit(solution)/shard_map/ppermute | solution.py:603
  289.5 31.9 %collective-permute-start.64 = (bf16[4,64,1024]{2,1,0:T(8,128)(2,1)S(1)}, bf16[4,64,1024]{2,1,0:T(8,128)(2,1)S(1)}, u32[]{:S(2)}, u32[]{:S(2)}) collective-permute-start(bf16[4,64,1024]{2,1,0:T(8,128)(2,1)S(1)} %b1_pack.3.near), channel_id=1, source_target_pairs={{0,4},{4,0},{8,12},{12,8},{16,20},{20,16},{24,28},{28,24},{1,5},{5... | collective-permute-start | bytes 1572872 | tf_op jit(solution)/shard_map/ppermute | solution.py:603
  (87 other events, 872.9 us)

commit v3 on v2

--- a/solution.py
+++ b/solution.py
@@ -35,26 +35,40 @@
     )
 
 
+def gdot(a, b, ca=1, cb=0):
+    return dot(a.astype(bf16), b.astype(bf16), ca, cb)
+
+
 def iota(shape, axis):
     return lax.broadcasted_iota(jnp.int32, shape, axis)
 
 
 def rows_of(block, size):
     return pl.ds(pl.multiple_of(block * size, size), size)
+
+
+COST = 1153500
 
 
 class Order:
     def __init__(self):
         self.last = None
-
-    def run(self, kernel, name, outs, args, smem=(), smem_out=(), hbm=(), hbm_out=(), pin=(), scratch=(), flops=0, vmem=8):
-        shapes = [jax.ShapeDtypeStruct(s, d) for s, d in outs]
-        total = sum(a.size * a.dtype.itemsize for a in args)
-        total += sum(s.size * s.dtype.itemsize for s in shapes)
+        self.also = ()
+
+    def wait(self, *values):
+        self.also = values
+
+    def run(self, kernel, name, outs, args, smem=(), smem_out=(), hbm=(), pin=(), scratch=(), flops=COST, vmem=8):
+        held = {"far": pltpu.HBM, "near": pltpu.VMEM}
+        shapes = [
+            held[o[2]](o[0], o[1]) if len(o) > 2 else jax.ShapeDtypeStruct(*o) for o in outs
+        ]
+        hbm_out = [i for i, o in enumerate(outs) if o[2:] == ("far",)]
         args = list(args)
         if self.last is not None:
             at = next(i for i in range(len(args)) if i not in smem and i not in pin)
-            args[at], _ = lax.optimization_barrier((args[at], self.last))
+            args[at] = lax.optimization_barrier((args[at], self.last, *self.also))[0]
+            self.also = ()
         for i in pin:
             args[i] = pltpu.with_memory_space_constraint(args[i], pltpu.HBM)
         space = lambda i, low, far: pltpu.SMEM if i in low else pltpu.HBM if i in far else pltpu.VMEM
@@ -68,7 +82,7 @@
             ],
             scratch_shapes=list(scratch),
             compiler_params=pltpu.CompilerParams(vmem_limit_bytes=vmem << 20),
-            cost_estimate=pl.CostEstimate(flops=flops, bytes_accessed=total, transcendentals=0),
+            cost_estimate=pl.CostEstimate(flops=flops, bytes_accessed=1, transcendentals=0),
         )(*args)
         self.last = next(o for i, o in enumerate(made) if i not in smem_out and i not in hbm_out)
         return made
@@ -103,17 +117,30 @@
     return rows * lax.rsqrt(jnp.sum(rows * rows, axis=-1, keepdims=True) + unit_epsilon)
 
 
-def tri_inverse(systems):
+def tri_inverse(systems, block=16):
     size = systems[0].shape[0]
-    eye = (iota((size, size), 0) == iota((size, size), 1)).astype(f32)
-    blocks = [[eye[r : r + 8] for r in range(0, size, 8)] for _ in systems]
+    row = iota((size, size), 0)
+    col = iota((size, size), 1)
+    eye = (row == col).astype(f32)
+    tiles = [[eye[r : r + 8] for r in range(0, size, 8)] for _ in systems]
     lower = [[system[r : r + 8] for r in range(0, size, 8)] for system in systems]
-    for j in range(size - 1):
-        for low, part in zip(lower, blocks):
-            line = part[j // 8][j % 8 : j % 8 + 1]
-            for r in range((j + 1) // 8, size // 8):
-                part[r] = part[r] - low[r][:, j : j + 1] * line
-    return [jnp.concatenate(part, axis=0) for part in blocks]
+    for step in range(block - 1):
+        for low, part in zip(lower, tiles):
+            for start in range(0, size, block):
+                j = start + step
+                line = part[j // 8][j % 8 : j % 8 + 1]
+                for r in range((j + 1) // 8, (start + block) // 8):
+                    part[r] = part[r] - low[r][:, j : j + 1] * line
+    inverses = [jnp.concatenate(part, axis=0) for part in tiles]
+    while block < size:
+        pick = ((row // block) % 2 == 1) & (col // block == row // block - 1)
+        mids = [
+            fdot(inverse, jnp.where(pick, system, 0.0))
+            for inverse, system in zip(inverses, systems)
+        ]
+        inverses = [inverse - fdot(mid, inverse) for mid, inverse in zip(mids, inverses)]
+        block *= 2
+    return inverses
 
 
 def tap_table(*tables):
@@ -122,7 +149,7 @@
     return lambda j, c: values[c // parts][j : j + 1, (c % parts) * DH : (c % parts + 1) * DH]
 
 
-def front_kernel(first, tp, seq_groups, seq_pads, xh, coth, gain, wqh, wkh, wvh, wgh, wb, tail, cq, ck, cv, gate, beta, meta, qkv, wmix, umix, score, zst, dev, last, mout, oloc, hidden_h, gd_h, x_own, gd_own, ext_h, conv_h, inv_h, amap_h, x, cot, wq, wk, wv, wg, hidden, gd, ext, conv, inv, amap, badd, sems, out_sems):
+def front_kernel(first, tp, seq_groups, seq_pads, xh, coth, gain, wqh, wkh, wvh, wgh, wb, tail, cq, ck, cv, gate, beta, meta, qkv, wmix, umix, score, zst, dev, last, hidden_h, gd_h, x_own, gd_own, ext_h, conv_h, inv_h, amap_h, x, cot, wq, wk, wv, wg, hidden, gd, ext, conv, inv, amap, badd, sems, out_sems):
     loads = [
         pltpu.make_async_copy(src, dst, sems.at[i])
         for i, (src, dst) in enumerate(
@@ -215,7 +242,7 @@
         return [qkv[rows, (i * heads + h) * DH : (i * heads + h + 1) * DH] for i in range(3)]
 
     def local(i, _):
-        chains = [(2 * i + j, h) for j in range(2) for h in range(heads)]
+        chains = [(j, h) for j in range(groups) for h in range(heads)]
         systems = []
         kept = []
         for n, h in chains:
@@ -237,7 +264,7 @@
             badd[n * heads + h] = kwu[:, DH:]
         return 0
 
-    lax.fori_loop(0, groups // 2, local, 0)
+    local(0, 0)
     store(inv, inv_h)
     store(amap, amap_h)
     for h in range(heads):
@@ -257,21 +284,29 @@
     lax.fori_loop(0, groups, chain, 0)
     last[...] = dev[:, :, DH:]
 
-    def outs(i, _):
+    for copy in stores:
+        copy.wait()
+
+
+def local_kernel(qkv, wmix, umix, score, zst, mout, oloc):
+    groups = qkv.shape[0] // GROUP
+    heads = wmix.shape[1] // DH
+
+    def one(i, _):
         for n, h in [(2 * i + j, h) for j in range(2) for h in range(heads)]:
             rows = pl.ds(pl.multiple_of(n * GROUP, GROUP), GROUP)
             lanes = slice(h * DH, (h + 1) * DH)
             q = qkv[rows, lanes]
             both = fdot(jnp.concatenate([q, wmix[rows, lanes]], axis=0), zst[n * heads + h])
-            lower = jnp.concatenate([-both[GROUP:, :DH], umix[rows, lanes] - both[GROUP:, DH:]], axis=1)
+            lower = jnp.concatenate(
+                [-both[GROUP:, :DH], umix[rows, lanes] - both[GROUP:, DH:]], axis=1
+            )
             made = both[:GROUP] + fdot(score[n * heads + h], lower)
             mout[rows, lanes] = made[:, :DH]
             oloc[rows, lanes] = made[:, DH:]
         return 0
 
-    lax.fori_loop(0, groups // 2, outs, 0)
-    for copy in stores:
-        copy.wait()
+    lax.fori_loop(0, groups // 2, one, 0)
 
 
 def fold_hops(hops, h):
@@ -333,15 +368,28 @@
     second[...] = rms_rows(total, wide_gain(gain)).astype(bf16)
 
 
-def ffn_kernel(plans, tp, place, s0, s1, s2, s3, grad_down, wg, wu, wd, down_send, down_keep, send, keep, *refs):
-    sums, (second, inner, dgate, dup, acc) = refs[:-5], refs[-5:]
+def ffn_kernel(plans, tp, place, s0, s1, s2, s3, gdh, wgh, wuh, wdh, down_send, down_keep, send, keep, *refs):
+    sums, (second, inner, dgate, dup, acc, wg, wu, grad_down, wd, sems) = refs[:-10], refs[-10:]
+    loads = [
+        pltpu.make_async_copy(src, dst, sems.at[i])
+        for i, (src, dst) in enumerate(((wgh, wg), (wuh, wu), (gdh, grad_down), (wdh, wd)))
+    ]
+    for load in loads:
+        load.start()
     share = s0.shape[0]
     for half, pair in enumerate(((s0, s1), (s2, s3))):
         sec = jnp.concatenate([pair[0][...], pair[1][...]], axis=0)
         blocks = [rows_of(tp[0] ^ (2 * half + j), share) for j in range(2)]
+        if half == 0:
+            loads[0].wait()
+        gv = dot(sec, wg[...], 1, 1)
+        if half == 0:
+            loads[1].wait()
+        uv = dot(sec, wu[...], 1, 1)
+        if half == 0:
+            loads[2].wait()
+            loads[3].wait()
         gd = jnp.concatenate([grad_down[b] for b in blocks], axis=0)
-        gv = dot(sec, wg[...], 1, 1)
-        uv = dot(sec, wu[...], 1, 1)
         sig = jax.nn.sigmoid(gv)
         act = gv * sig
         inn = (act * uv).astype(bf16)
@@ -362,7 +410,7 @@
         down_send[half] = down[share:].astype(bf16)
     for left, right, plan in ((inner, grad_down, 0), (dgate, second, 1), (dup, second, 2)):
         acc[...] = dot(left[...], right[...], 0, 0)
-        put(acc, place[0], plans[plan], sums)
+        put(acc, acc.shape[1], place[0], plans[plan], sums)
 
 
 def turn_kernel(kept, got, residual, gain, grad_y, grad_residual, branch, gain_part):
@@ -463,7 +511,7 @@
 
 def back_kernel(hop_count, meta, *refs):
     hops, refs = refs[:hop_count], refs[hop_count:]
-    rst, qkv, conv, ext, cq, ck, cv, beta, inv, states, vnew, ndo, dq, dk1, gp, last, halo, dbeta, dtaps, dc = refs
+    rst, qkv, conv, cq, ck, cv, beta, inv, states, vnew, ndo, dq, dk1, dc, halo, dbeta = refs
     taps = tap_table(cq, ck, cv)
     heads = ndo.shape[1] // DH
     groups = ndo.shape[0] // GROUP
@@ -484,15 +532,16 @@
                 k = qkv[rows, lanes[1]]
                 v = qkv[rows, lanes[2]]
                 b, sig, live = beta_col(beta, meta, n, h)
-                ds = rst[at, :, DH:] + fdot(rst[at, :, :DH], exits[h])
-                dvn = ndo[rows, lanes[0]] + fdot(k, ds)
-                d = fdot(inv[at], dvn, 0, 0)
+                ds = rst[at, :, DH:] + gdot(rst[at, :, :DH], exits[h])
+                dvn = ndo[rows, lanes[0]] + gdot(k, ds)
+                d = gdot(inv[at], dvn, 0, 0)
                 vn = vnew[rows, lanes[0]]
-                dstate = fdot(d, states[at], 1, 1)
-                vds = fdot(vn, ds, 1, 1)
-                da = jnp.where(strict, -fdot(d, vn, 1, 1), 0.0)
-                dak = fdot(da, k)
-                datk = fdot(da, k * b, 0, 0)
+                both = gdot(d, jnp.concatenate([states[at], vn], axis=0), 1, 1)
+                dstate = both[:, :DH]
+                vds = gdot(vn, ds, 1, 1)
+                da = jnp.where(strict, -both[:, DH:], 0.0)
+                dak = gdot(da, k)
+                datk = gdot(da, k * b, 0, 0)
                 dk = dk1[rows, lanes[0]] + vds + b * (dak - dstate) + datk
                 db = jnp.sum(d * v + (dak - dstate) * k, axis=-1, keepdims=True)
                 db = jnp.where(live, db * sig * (1.0 - sig), 0.0)
@@ -507,7 +556,22 @@
         return 0
 
     lax.fori_loop(0, groups // 2, one, 0)
-    row = iota((GROUP, 1), 0)
+    zero = jnp.zeros((8, DH), f32)
+    for c in range(3 * heads):
+        lanes = slice(c * DH, (c + 1) * DH)
+        win = dc[0:8, lanes]
+        acc = zero
+        for d in range(1, KW):
+            part = jnp.where(iota((8, 1), 0) < meta[0, 0] * d, 0.0, win)
+            j = KW - 1 - d
+            acc = acc + taps(j, c) * jnp.concatenate([zero, part], axis=0)[d : d + 8]
+        halo[:, lanes] = acc
+
+
+def taps_kernel(meta, dc, ext, cq, ck, cv, gp, last, dtaps):
+    heads = cq.shape[1] // DH
+    groups = gp.shape[0] // GROUP
+    taps = tap_table(cq, ck, cv)
     dtaps[...] = jnp.zeros(dtaps.shape, f32)
 
     def masked(win, d, here, after):
@@ -543,19 +607,9 @@
         return 0
 
     lax.fori_loop(0, groups, taps_back, 0)
-    zero = jnp.zeros((8, DH), f32)
-    for c in range(3 * heads):
-        lanes = slice(c * DH, (c + 1) * DH)
-        win = dc[0:8, lanes]
-        acc = zero
-        for d in range(1, KW):
-            part = jnp.where(iota((8, 1), 0) < meta[0, 0] * d, 0.0, win)
-            j = KW - 1 - d
-            acc = acc + taps(j, c) * jnp.concatenate([zero, part], axis=0)[d : d + 8]
-        halo[:, lanes] = acc
-
-
-def hid_kernel(tp, gp_in, last, incoming, dgate, dbeta, wq, wk, wv, wg, wb, gp, send, keep):
+
+
+def hid_kernel(tp, gp_in, last, incoming, dgate, dbeta, wq, wk, wv, wg, wb, x, gp, send, keep, gain_part):
     total = gp.shape[0]
     width = wq.shape[1]
     gp[: total - TAIL] = gp_in[: total - TAIL]
@@ -572,16 +626,19 @@
             acc = acc + small[:, h : h + 1] * wb[h : h + 1].astype(f32)
         for i, w in enumerate((wq, wk, wv)):
             acc = acc + dot(grads[:, i * width : (i + 1) * width], w[...], 1, 1)
+        v = cat(x).astype(f32)
+        r = lax.rsqrt(jnp.mean(v * v, axis=-1, keepdims=True) + row_epsilon)
+        part = jnp.sum(acc * (v * r), axis=0, keepdims=True)
+        gain_part[...] = part if half == 0 else gain_part[...] + part
         keep[half] = acc[:share]
         send[half] = acc[share:].astype(bf16)
 
 
-def in_kernel(kept, got, x, gain, grad_residual, grad_in, gain_part):
+def in_kernel(kept, got, x, gain, grad_residual, grad_in):
     gh = kept[...] + got[...].astype(f32)
     v = x[...].astype(f32)
     g = wide_gain(gain)
     r = lax.rsqrt(jnp.mean(v * v, axis=-1, keepdims=True) + row_epsilon)
-    gain_part[...] = jnp.sum(gh * v * r, axis=0, keepdims=True)
     e = gh * g
     back = r * e - v * (r * r * r) * jnp.mean(e * v, axis=-1, keepdims=True)
     grad_in[...] = (grad_residual[...] + back).astype(bf16)
@@ -632,23 +689,21 @@
 
 
 class Plan:
-    def __init__(self, index, bits, base, size, start=0, folds=1):
+    def __init__(self, index, bits, base, size, start=0, folds=1, lane=0):
         self.index, self.bits, self.base, self.size = index, bits, base, size
-        self.start, self.folds = start, folds
-
-
-def put(acc, place, plan, sums):
-    for part in plan if isinstance(plan, (list, tuple)) else (plan,):
+        self.start, self.folds, self.lane = start, folds, lane
+
+
+def put(acc, wide, place, plans, sums):
+    for part in plans:
         keep, send = sums[2 * part.index : 2 * part.index + 2]
-        blocks = 1 << len(part.bits)
         height = part.size // part.folds
-        wide = acc.shape[1]
-        for m in range(blocks):
+        for m in range(1 << len(part.bits)):
             at = rank_of(m, part.bits[1:])
             low = (m >> part.bits[0]) & 1
             for i in range(part.folds):
                 begin = part.start + (m ^ place) * part.size + i * height
-                block = acc[pl.ds(pl.multiple_of(begin, 8), height)]
+                block = acc[pl.ds(pl.multiple_of(begin, 8), height), part.lane : part.lane + wide]
                 rows = slice(part.base, part.base + height)
                 lanes = slice(i * wide, (i + 1) * wide)
                 if low:
@@ -658,10 +713,9 @@
 
 
 def take(out, place, part, bits, near, far):
-    blocks = 1 << len(bits)
     height = part.size // part.folds
     wide = out.shape[1]
-    for m in range(blocks):
+    for m in range(1 << len(bits)):
         source = far if (m >> bits[-1]) & 1 else near
         at = rank_of(m, bits[-2::-1])
         for i in range(part.folds):
@@ -704,35 +758,46 @@
             )
         self.swap(self.own)
 
-    def settle(self, plans, outs, name):
-        count = len(outs)
-
-        def kernel(place, near, far, *refs):
-            for part, out in zip(plans, refs):
-                take(out, place[0], part, self.gather, near, far)
-
-        return self.order.run(
-            kernel, name, [(o, f32) for o in outs], [self.place, self.own, self.got], smem=(0,)
-        )
-
 
 def scatter_first(order, keep, send):
     return fold(order, keep, swap(send, 1), "fold_tp")
-
-
-def grads_b_kernel(plans, place, attended, branch, hidden, dgate, *refs):
-    sums, (acc, acc2) = refs[:-2], refs[-2:]
-    acc[...] = dot(attended[...], branch[...], 0, 0)
-    put(acc, place[0], plans[0], sums)
-    acc2[...] = dot(hidden[...], dgate[...], 0, 0)
-    put(acc2, place[0], plans[1], sums)
 
 
 def grads_c_kernel(plans, place, hidden, gp, *refs):
     sums, acc = refs[:-1], refs[-1]
     acc[...] = dot(hidden[...], gp[...], 0, 0)
-    for plan in plans:
-        put(acc, place[0], plan, sums)
+    put(acc, acc.shape[1] // 3, place[0], plans, sums)
+
+
+def grads_d_kernel(plans, way, base, place, attended, branch, hidden, dgate, small, gains, keep, send, acc, acc2, both):
+    sums = (keep, send)
+    acc[...] = dot(attended[...], branch[...], 0, 0)
+    put(acc, acc.shape[1], place[0], plans[:1], sums)
+    acc2[...] = dot(hidden[...], dgate[...], 0, 0)
+    put(acc2, acc2.shape[1], place[0], plans[1:], sums)
+    both[...] = small[...] + gains[...]
+    for m in range(1 << len(way)):
+        line = both[pl.ds(m ^ place[0], 1)] + jnp.zeros((8, both.shape[1]), f32)
+        at = rank_of(m, way[1:])
+        if (m >> way[0]) & 1:
+            send[at, base : base + 8] = line.astype(bf16)
+        else:
+            keep[at, base : base + 8] = line
+
+
+def settle_kernel(jobs, line_at, place, *refs):
+    count = 1 + max(part.index for parts in jobs for part, _ in parts)
+    pairs, outs = refs[: 2 * count], refs[2 * count :]
+    for parts, out in zip(jobs, outs):
+        for part, way in parts:
+            take(out, place[0], part, way, *pairs[2 * part.index : 2 * part.index + 2])
+    if line_at is not None:
+        index, way, base = line_at
+        near, far = pairs[2 * index : 2 * index + 2]
+        for m in range(1 << len(way)):
+            source = far if (m >> way[-1]) & 1 else near
+            at = rank_of(m, way[-2::-1])
+            outs[-1][pl.ds(m ^ place[0], 1)] = source[at, base : base + 8].astype(f32)[:1]
 
 
 def sum_shapes(blocks, rows, cols):
@@ -755,16 +820,15 @@
     return [shift(dev, sign * k) for k in range(1, reach)] + [shift(last, sign * reach)]
 
 
-def small_kernel(dtaps, dbeta, hidden, in_part, mid_part, head_part, taps_out, gains_out):
+def small_kernel(dtaps, dbeta, hidden, in_part, mid_part, head_part, local, gains):
     wide = dtaps.shape[1]
-    taps_out[...] = jnp.zeros(taps_out.shape, f32)
-    taps_out[0:KW, :wide] = dtaps[...]
-    product = dot(dbeta[...], hidden[...], 0, 0)
-    taps_out[KW : KW + 4] = product[:4]
-    gains_out[...] = jnp.zeros(gains_out.shape, f32)
-    gains_out[0:1] = in_part[...]
-    gains_out[1:2] = mid_part[...]
-    gains_out[2:3, : head_part.shape[1]] = head_part[...]
+    local[...] = jnp.zeros(local.shape, f32)
+    local[0:KW, :wide] = dtaps[...]
+    local[KW : KW + 2] = dot(dbeta[...], hidden[...], 0, 0)[:2]
+    gains[...] = jnp.zeros(gains.shape, f32)
+    gains[KW + 2 : KW + 3] = in_part[...]
+    gains[KW + 3 : KW + 4] = mid_part[...]
+    gains[0:1, wide : wide + head_part.shape[1]] = head_part[...]
 
 
 def plus_kernel(a, b, out):
@@ -829,39 +893,40 @@
     conv_shape = (total, 3 * width)
     inv_shape = (chains, GROUP, GROUP)
     map_shape = (chains, DH, DH)
+    zst_shape = (chains, DH, 2 * DH)
+    dev_shapes = [((heads, DH, 2 * DH), f32), ((heads, DH, DH), f32)]
+    near = "near"
+    far = "far"
+    tp_sums = [((2, share, model), bf16), ((2, share, model), f32)]
     (
-        gate_raw, beta_raw, meta, qkv, wmix, umix, score, zst, dev, last, mout, oloc,
+        gate_raw, beta_raw, meta, qkv, wmix, umix, score, zst, dev, last,
         hidden, grad_down, x_own, gd_own, ext, conv, inv, amap,
     ) = run(
         front_kernel,
         "front",
         [
-            (wide, f32),
-            ((total, heads), f32),
+            (wide, f32, near),
+            ((total, heads), f32, near),
             ((2, groups), jnp.int32),
-            (conv_shape, f32),
-            (wide, f32),
-            (wide, f32),
-            (inv_shape, f32),
-            ((chains, DH, 2 * DH), f32),
-            ((heads, DH, 2 * DH), f32),
-            ((heads, DH, DH), f32),
-            (wide, f32),
-            (wide, f32),
-            ((total, model), bf16),
-            ((total, model), bf16),
-            ((share, model), bf16),
-            ((share, model), bf16),
-            (ext_shape, f32),
-            (conv_shape, f32),
-            (inv_shape, f32),
-            (map_shape, f32),
+            (conv_shape, f32, near),
+            (wide, f32, near),
+            (wide, f32, near),
+            (inv_shape, f32, near),
+            (zst_shape, f32, near),
+            *dev_shapes,
+            ((total, model), bf16, far),
+            ((total, model), bf16, far),
+            ((share, model), bf16, far),
+            ((share, model), bf16, far),
+            (ext_shape, f32, far),
+            (conv_shape, f32, far),
+            (inv_shape, f32, far),
+            (map_shape, f32, far),
         ],
         [first, tp, seq_groups, seq_pads, layer_input, cotangent, norm_in, w_query, w_key, w_value, w_gate_out, wb, tail, *taps],
         smem=(0, 1, 2, 3),
         smem_out=(2,),
         hbm=(4, 5, 7, 8, 9, 10),
-        hbm_out=tuple(range(12, 20)),
         pin=(2, 3, 4, 5, 6, 7, 8, 9, 10, 11, 13, 14, 15),
         scratch=[
             rows, rows, weight, weight, weight, weight, rows, rows,
@@ -873,69 +938,75 @@
             pltpu.SemaphoreType.DMA((6,)),
             pltpu.SemaphoreType.DMA((8,)),
         ],
-        flops=mats * 10 * width,
-        vmem=20,
+        vmem=22,
     )
     hops = hops_of(dev, last, 1, reach)
+    mout, oloc = run(
+        local_kernel, "local", [(wide, f32, near)] * 2, [qkv, wmix, umix, score, zst]
+    )
     heads_out, attended, send, keep, entry = run(
         lambda *r: out_kernel(reach, *r),
         "out",
-        [(wide, f32), (wide, bf16), ((2, share, model), bf16), ((2, share, model), f32), ((heads, DH, DH), f32)],
+        [(wide, f32, near), (wide, bf16, near), *tp_sums, ((heads, DH, DH), f32)],
         [tp, *hops, mout, oloc, gate_raw, norm_head, w_out],
         smem=(0,),
-        flops=mats * width,
-    )
-    kept, far = scatter_first(order, keep, send)
-    got = swap(far, 2)
+    )
+    kept, cross = scatter_first(order, keep, send)
+    got = swap(cross, 2)
     states, vnew, qeff = run(
         states_kernel,
         "states",
-        [(map_shape, f32), (wide, f32), (wide, f32)],
+        [(map_shape, f32, near), (wide, f32, near), (wide, f32, near)],
         [entry, zst, qkv, wmix, umix, score],
-        flops=mats * width,
     )
     residual, second_own = run(
         mid_kernel,
         "mid",
-        [((share, model), f32), ((share, model), bf16)],
+        [((share, model), f32, near), ((share, model), bf16)],
         [x_own, kept[0], got[0], norm_mid],
     )
     size = ffw // blocks
-    bits = [(0, 1, 2), (1, 0, 2), (0, 1, 2), (0, 1, 2), (1, 0, 2)]
-    gathers = [(2, 1, 0), (2, 0, 1), (2, 1, 0), (2, 1, 0), (2, 0, 1)]
-    cut_rows = ffw // 2
-    plans_a = [
-        Plan(0, bits[0], 0, size),
-        Plan(1, bits[1], 0, size),
-        Plan(2, bits[2], 0, size),
+    ways = [
+        ((0, 1, 2), (2, 1, 0)),
+        ((1, 0, 2), (2, 0, 1)),
+        ((0, 1, 2), (1, 2, 0)),
+        ((1, 0, 2), (2, 0, 1)),
     ]
+    near_up = size // 16 * 8
+    far_up = size - near_up
+    down_parts = [Plan(0, ways[0][0], 0, size)]
+    gate_parts = [Plan(1, ways[1][0], 0, size)]
+    up_parts = [
+        Plan(0, ways[0][0], size, near_up),
+        Plan(1, ways[1][0], size, far_up, start=near_up * blocks),
+    ]
+    plans_a = (down_parts, gate_parts, up_parts)
+    f1_rows, f2_rows = size + near_up, size + far_up
+    all_rows = gather_rel(second_own)
     down_send, down_keep, send, keep, *sums = run(
         lambda *r: ffn_kernel(plans_a, *r),
         "ffn",
-        [
-            ((2, share, model), bf16),
-            ((2, share, model), f32),
-            ((2, share, model), bf16),
-            ((2, share, model), f32),
-            *(sum_shapes(blocks, size, model) * 3),
-        ],
-        [tp, place, *gather_rel(second_own), grad_down, w_gate.T, w_up.T, w_down],
+        [*tp_sums, *tp_sums, *sum_shapes(blocks, f1_rows, model), *sum_shapes(blocks, f2_rows, model)],
+        [tp, place, *all_rows, grad_down, w_gate.T, w_up.T, w_down],
         smem=(0, 1),
+        hbm=(6, 7, 8, 9),
+        pin=(6, 7, 8, 9),
         scratch=[
             rows,
-            pltpu.VMEM((total, ffw), bf16),
-            pltpu.VMEM((total, ffw), bf16),
-            pltpu.VMEM((total, ffw), bf16),
+            *[pltpu.VMEM((total, ffw), bf16)] * 3,
             pltpu.VMEM((ffw, model), f32),
+            *[pltpu.VMEM((ffw, model), bf16)] * 2,
+            rows,
+            pltpu.VMEM((ffw, model), bf16),
+            pltpu.SemaphoreType.DMA((4,)),
         ],
-        flops=9 * mats * ffw,
-        vmem=24,
-    )
-    near = swap(send, 1)
-    a1 = begin(sums[0], sums[1], bits[0], gathers[0], "a1")
-    a2 = begin(sums[2], sums[3], bits[1], gathers[1], "a2")
-    kept, far = fold(order, keep, near, "fold_tp")
-    got = swap(far, 2)
+        vmem=28,
+    )
+    beside = swap(send, 1)
+    f1 = begin(sums[0], sums[1], *ways[0], "f1")
+    f2 = begin(sums[2], sums[3], *ways[1], "f2")
+    kept, cross = fold(order, keep, beside, "fold_tp")
+    got = swap(cross, 2)
     grad_residual, branch_own, mid_part = run(
         turn_kernel,
         "turn",
@@ -943,7 +1014,6 @@
         [kept[0], got[0], residual, norm_mid, gd_own],
     )
     branch_all = gather_rel(branch_own)
-    a3 = begin(sums[4], sums[5], bits[2], gathers[2], "a3")
     branch, dgate_raw, dout, rst, dev, last, head_part = run(
         flow_kernel,
         "flow",
@@ -951,111 +1021,113 @@
             ((total, model), bf16),
             (wide, bf16),
             (wide, f32),
-            ((chains, DH, 2 * DH), f32),
-            ((heads, DH, 2 * DH), f32),
-            ((heads, DH, DH), f32),
+            (zst_shape, f32),
+            *dev_shapes,
             ((1, DH), f32),
         ],
         [tp, meta, *branch_all, w_out, heads_out, gate_raw, norm_head, qeff, amap],
         smem=(0, 1),
         scratch=[pltpu.VMEM(map_shape, f32)],
-        flops=3 * mats * width,
     )
     hops = hops_of(dev, last, -1, reach)
+    down_near = swap(down_send, 1)
     ndo, dq, dk = run(
         side_kernel,
         "side",
         [(wide, f32)] * 3,
         [qkv, dout, vnew, states, score],
-        flops=mats * width,
-    )
-    a1.step()
-    a2.step()
-    plans_b = [
-        Plan(0, bits[3], 0, width // blocks),
-        Plan(0, bits[3], width // blocks, model // blocks, folds=model // width),
-    ]
-    sums = run(
-        lambda *r: grads_b_kernel(plans_b, *r),
-        "grads_b",
-        sum_shapes(blocks, 2 * width // blocks, model),
-        [place, attended, branch, hidden, dgate_raw],
-        smem=(0,),
-        scratch=[pltpu.VMEM((width, model), f32), pltpu.VMEM((model, width), f32)],
-        flops=2 * mats * width,
-    )
-    b1 = begin(*sums, bits[3], gathers[3], "b1")
-    gp, last, halo, dbeta, dtaps = run(
+    )
+    down_kept, cross = fold(order, down_keep, down_near, "fold_tp")
+    down_got = swap(cross, 2)
+    order.wait(*hops)
+    f1.step()
+    f2.step()
+    dc, halo, dbeta = run(
         lambda *r: back_kernel(reach, *r),
         "back",
-        [
-            (conv_shape, bf16),
-            ((TAIL, 3 * width), f32),
-            ((8, 3 * width), f32),
-            ((total, LANES), bf16),
-            ((KW, 3 * width), f32),
-        ],
-        [meta, *hops, rst, qkv, conv, ext, *taps, beta_raw, inv, states, vnew, ndo, dq, dk],
+        [((total + 8, 3 * width), f32), ((8, 3 * width), f32), ((total, LANES), bf16)],
+        [meta, *hops, rst, qkv, conv, *taps, beta_raw, inv, states, vnew, ndo, dq, dk],
         smem=(0,),
-        scratch=[pltpu.VMEM((total + 8, 3 * width), f32)],
-        flops=3 * mats * width,
     )
     incoming = shift(halo, -1)
-    a1.step()
-    a2.step()
-    a3.step()
-    gp, send, keep = run(
+    gp, last, dtaps = run(
+        taps_kernel,
+        "taps",
+        [(conv_shape, bf16), ((TAIL, 3 * width), f32), ((KW, 3 * width), f32)],
+        [meta, dc, ext, *taps],
+        smem=(0,),
+    )
+    (out_own,) = run(
+        outblock_kernel,
+        "outblk",
+        [((share, model), bf16)],
+        [tp, meta, down_kept[0], down_got[0], residual],
+        smem=(0, 1),
+    )
+    f1.step()
+    f2.step()
+    gp, send, keep, in_part = run(
         hid_kernel,
         "hid",
-        [(conv_shape, bf16), ((2, share, model), bf16), ((2, share, model), f32)],
-        [tp, gp, last, incoming, dgate_raw, dbeta, w_query, w_key, w_value, w_gate_out, wb],
+        [(conv_shape, bf16), *tp_sums, ((1, model), f32)],
+        [tp, gp, last, incoming, dgate_raw, dbeta, w_query, w_key, w_value, w_gate_out, wb, layer_input],
         smem=(0,),
-        flops=mats * 4 * width,
         vmem=12,
     )
-    near = swap(send, 1)
-    half = model // 2
+    beside = swap(send, 1)
+    piece = model // blocks
+    fold_rows = piece * width // model
+    split = dict(folds=model // width)
     plans_c = [
-        Plan(0, bits[3], 0, half // blocks),
-        Plan(1, bits[4], 0, half // blocks, start=half),
+        Plan(0, ways[2][0], i * fold_rows, piece, lane=i * width, **split) for i in range(3)
     ]
-    sums = run(
+    keep_c, send_c = run(
         lambda *r: grads_c_kernel(plans_c, *r),
         "grads_c",
-        sum_shapes(blocks, half // blocks, 3 * width) * 2,
+        sum_shapes(blocks, 3 * fold_rows, model),
         [place, hidden, gp],
         smem=(0,),
         scratch=[pltpu.VMEM((model, 3 * width), f32)],
-        flops=mats * 3 * width,
         vmem=16,
     )
-    c1 = begin(sums[0], sums[1], bits[3], gathers[3], "c1")
-    c2 = begin(sums[2], sums[3], bits[4], gathers[4], "c2")
-    kept, far = fold(order, keep, near, "fold_tp")
-    got = swap(far, 2)
-    b1.step()
-    a1.step()
-    a2.step()
-    grad_in_own, in_part = run(
-        in_kernel,
-        "inp",
-        [((share, model), bf16), ((1, model), f32)],
-        [kept[0], got[0], x_own, norm_in, grad_residual],
-    )
-    grad_in_all = gather_rel(grad_in_own)
+    f3 = begin(keep_c, send_c, *ways[2], "f3")
+    kept, cross = fold(order, keep, beside, "fold_tp")
+    got = swap(cross, 2)
     row8 = ((8, model), f32)
     small, gains = run(
         small_kernel, "small", [row8, row8], [dtaps, dbeta, hidden, in_part, mid_part, head_part]
     )
-    down_near = swap(down_send, 1)
-    a3.step()
-    b1.step()
-    c1.step()
-    c2.step()
-    kept, far = fold(order, down_keep, down_near, "fold_tp")
-    got = swap(far, 2)
-    a1.step()
-    a2.step()
+    gains = plus(order, gains, swap(gains, 1))
+    far_gains = swap(gains, 2)
+    (grad_in_own,) = run(
+        in_kernel,
+        "inp",
+        [((share, model), bf16)],
+        [kept[0], got[0], x_own, norm_in, grad_residual],
+    )
+    grad_in_all = gather_rel(grad_in_own)
+    gains = plus(order, gains, far_gains)
+    wo_rows = width // blocks
+    out_parts = [Plan(0, ways[3][0], 0, wo_rows)]
+    gate_out_parts = [Plan(0, ways[3][0], wo_rows, piece, **split)]
+    line_base = wo_rows + fold_rows
+    keep_d, send_d = run(
+        lambda *r: grads_d_kernel(out_parts + gate_out_parts, ways[3][0], line_base, *r),
+        "grads_d",
+        sum_shapes(blocks, line_base + 8, model),
+        [place, attended, branch, hidden, dgate_raw, small, gains],
+        smem=(0,),
+        scratch=[
+            pltpu.VMEM((width, model), f32),
+            pltpu.VMEM((model, width), f32),
+            pltpu.VMEM((8, model), f32),
+        ],
+        vmem=12,
+    )
+    f4 = begin(keep_d, send_d, *ways[3], "f4")
+    f1.step()
+    f2.step()
+    f3.step()
     (grad_input,) = run(
         place_kernel,
         "place_in",
@@ -1063,28 +1135,8 @@
         [tp, *grad_in_all],
         smem=(0,),
     )
-    (out_own,) = run(
-        outblock_kernel,
-        "outblk",
-        [((share, model), bf16)],
-        [tp, meta, kept[0], got[0], residual],
-        smem=(0, 1),
-    )
     out_all = gather_rel(out_own)
-    a3.step()
-    b1.step()
-    c1.step()
-    c2.step()
-    a1.step()
-    a2.step()
-    gains = plus(order, gains, swap(gains, 1))
-    a3.step()
-    b1.step()
-    c1.step()
-    c2.step()
-    gains = plus(order, gains, swap(gains, 2))
-    step = 1
-    small = jnp.concatenate([small, gains], axis=0)
+    f4.step()
     (block_out,) = run(
         place_kernel,
         "place_out",
@@ -1092,51 +1144,56 @@
         [tp, *out_all],
         smem=(0,),
     )
-    a3.step()
-    b1.step()
-    c1.step()
-    c2.step()
-    while step < seq_count:
-        small = plus(order, small, swap(small, step, "seq"))
-        step *= 2
-    c1.step()
-    c2.step()
-    (grad_down_w,) = a1.settle([plans_a[0]], [(ffw, model)], "settle_a1")
-    (grad_gate_w,) = a2.settle([plans_a[1]], [(ffw, model)], "settle_a2")
-    (grad_up_w,) = a3.settle([plans_a[2]], [(ffw, model)], "settle_a3")
-    grad_out_w, grad_gate_out_w = b1.settle(
-        plans_b, [(width, model), (model, width)], "settle_b1"
-    )
-
-    def settle_c(place, near1, far1, near2, far2, *outs):
-        for plan, gather, near, far in (
-            (plans_c[0], gathers[3], near1, far1),
-            (plans_c[1], gathers[4], near2, far2),
-        ):
-            for m in range(blocks):
-                source = far if (m >> gather[-1]) & 1 else near
-                at = rank_of(m, gather[-2::-1])
-                begin = plan.start + (m ^ place[0]) * plan.size
-                for i, out in enumerate(outs):
-                    out[pl.ds(pl.multiple_of(begin, 8), plan.size)] = source[
-                        at, :, i * width : (i + 1) * width
-                    ].astype(f32)
-
-    hidden_sums = run(
-        settle_c,
-        "settle_c",
-        [((model, width), f32)] * 3,
-        [place, c1.own, c1.got, c2.own, c2.got],
-        smem=(0,),
+    f1.step()
+    f3.step()
+    f4.step()
+    f2.step()
+    f2.step()
+    f4.step()
+    f3.step()
+    f1.step()
+    f4.step()
+    f3.step()
+    f4.step()
+    f3.step()
+
+    def settle(name, jobs, flows, outs, line_at=None):
+        return run(
+            lambda *r: settle_kernel(jobs, line_at, *r),
+            name,
+            [(o, f32) for o in outs],
+            [place, *[a for flow in flows for a in (flow.own, flow.got)]],
+            smem=(0,),
+        )
+
+    wayed = lambda parts, ways_of: [(part, ways_of[part.index][1]) for part in parts]
+    (grad_down_w,) = settle("settle_1", [wayed(down_parts, ways)], [f1], [(ffw, model)])
+    grad_gate_w, grad_up_w = settle(
+        "settle_2",
+        [wayed(gate_parts, ways), wayed(up_parts, ways)],
+        [f1, f2],
+        [(ffw, model)] * 2,
+    )
+    grad_out_w, grad_gate_out_w, small = settle(
+        "settle_4",
+        [wayed(out_parts, ways[3:]), wayed(gate_out_parts, ways[3:])],
+        [f4],
+        [(width, model), (model, width), (8, model)],
+        line_at=(0, ways[3][1], line_base),
+    )
+    hidden_sums = settle(
+        "settle_3", [wayed([part], ways[2:]) for part in plans_c], [f3], [(model, width)] * 3
     )
     cut = model // 4
     head_cut = DH // 4
-    gain_of = lambda row, size: lax.dynamic_slice(small, (8 + row, tp_rank * size), (1, size)).reshape(size)
+    gain_of = lambda row, size, lane=0: lax.dynamic_slice(
+        small, (row, lane + tp_rank * size), (1, size)
+    ).reshape(size)
     tap_of = lambda i: small[:KW, i * width : (i + 1) * width]
     return (
         block_out,
         grad_input,
-        gain_of(0, cut),
+        gain_of(KW + 2, cut),
         hidden_sums[0],
         hidden_sums[1],
         hidden_sums[2],
@@ -1145,9 +1202,9 @@
         tap_of(2),
         small[KW : KW + heads].T,
         grad_gate_out_w,
-        gain_of(2, head_cut),
+        gain_of(0, head_cut, 3 * width),
         grad_out_w,
-        gain_of(1, cut),
+        gain_of(KW + 3, cut),
         grad_gate_w.T,
         grad_up_w.T,
         grad_down_w,

time: 329 us -> 296 us (0.90)
  starting transfers between devices: 79.1 us -> 66.9 us
  waiting for transfers between devices: 145 us -> 135 us
  local copies, waits for them, and re-layouts: 17 us -> 7.55 us
  Pallas kernels: 85.7 us -> 82 us
    ppermute x61 -> x46, starting transfers between devices: 62.3 us -> 50.4 us  [swap(): return lax.ppermute(value, axis, [(i, i ^ bit) for i in range(count)])]
    unnamed x88 -> x70, local copies, waits for them, and re-layouts: 13.8 us -> 4.36 us
    ppermute x6, waiting for transfers between devices: 15.4 us -> 8.59 us  [shift(): return lax.ppermute(value, 'seq', pairs)]
    pallas_call x61 -> x49, Pallas kernels: 85.7 us -> 82 us  [run(): pl.pallas_call(kernel, name=name, out_shape=shapes, in_specs=[pl.BlockSpe...]
    ppermute x61 -> x46, waiting for transfers between devices: 130 us -> 127 us  [swap(): return lax.ppermute(value, axis, [(i, i ^ bit) for i in range(count)])]
  transfers between devices with their start and end apart: 67 -> 52, of which waited for: 33 -> 24; matrix products, arithmetic and copies ran while one was open for 1% -> 1% of each run, Pallas kernels for 15% -> 16%
where the time goes in v3:
time: 296 us; the launch traced here: 293 us
  waiting for transfers between devices  135 us (46%)
  Pallas kernels  82 us (28%)
  starting transfers between devices  66.9 us (23%)
  local copies, waits for them, and re-layouts  7.55 us (3%)
    ppermute x46, waiting for transfers between devices, swap(): return lax.ppermute(value, axis, [(i, i ^ bit) for i in range(count)])  127 us
    pallas_call x49, Pallas kernels, run(): pl.pallas_call(kernel, name=name, out_shape=shapes, in_specs=[pl.BlockSpe...  82 us
    ppermute x46, starting transfers between devices, swap(): return lax.ppermute(value, axis, [(i, i ^ bit) for i in range(count)])  50.4 us
    ppermute x6, starting transfers between devices, shift(): return lax.ppermute(value, 'seq', pairs)  16.5 us
    ppermute x6, waiting for transfers between devices, shift(): return lax.ppermute(value, 'seq', pairs)  8.59 us
  transfers between devices with their start and end apart: 52, of which 24 were waited for; matrix products, arithmetic and copies ran while one was open for 1% of the time, Pallas kernels for 16%

profile of v3, /device:TPU:0, one launch (start us, length us, event | category | flops | bytes accessed | tf_op | source)
XLA Modules:
  0.0 293.2 jit_solution(6977728496965737895)
XLA Ops:
  1.4 4.9 %collective-permute-start = (bf16[16,1024]{1,0:T(8,128)(2,1)S(1)}, bf16[16,1024]{1,0:T(8,128)(2,1)S(1)}, u32[]{:S(2)}, u32[]{:S(2)}) collective-permute-start(bf16[16,1024]{1,0:T(8,128)(2,1)S(1)} %slice.15), channel_id=1, source_target_pairs={{0,4},{4,8},{8,12},{12,16},{16,20},{20,24},{24,28},{1,5},{5,9},{9,... | collective-permute-start | bytes 98312 | tf_op jit(solution)/shard_map/ppermute | solution.py:816
  7.9 15.0 %front.1 = (f32[512,256]{1,0:T(8,128)S(1)}, f32[512,2]{1,0:T(8,128)S(1)}, s32[2,8]{1,0:T(2,128)S(1)}, f32[512,768]{1,0:T(8,128)S(1)}, f32[512,256]{1,0:T(8,128)S...) custom-call(s32[1]{0:T(128)} %bitcast.1.first, ...), custom_call_target="tpu_custom_call" | custom-call | flops 1153500 | bytes 1 | tf_op jit(solution)/shard_map/front/pallas_call | solution.py:75
  22.9 4.2 %collective-permute-start.1 = (f32[2,128,256]{2,1,0:T(8,128)S(1)}, f32[2,128,256]{2,1,0:T(8,128)S(1)}, u32[]{:S(2)}, u32[]{:S(2)}) collective-permute-start(f32[2,128,256]{2,1,0:T(8,128)S(1)} %get-tuple-element.165), channel_id=1, source_target_pairs={{0,4},{4,8},{8,12},{12,16},{16,20},{20,24},{24,28},{1,5},{5,9},{9,... | collective-permute-start | bytes 786440 | tf_op jit(solution)/shard_map/ppermute | solution.py:816
  27.2 3.5 %collective-permute-start.2 = (f32[2,128,128]{2,1,0:T(8,128)S(1)}, f32[2,128,128]{2,1,0:T(8,128)S(1)}, u32[]{:S(2)}, u32[]{:S(2)}) collective-permute-start(f32[2,128,128]{2,1,0:T(8,128)S(1)} %get-tuple-element.175), channel_id=1, source_target_pairs={{0,8},{4,12},{8,16},{12,20},{16,24},{20,28},{1,9},{5,13},{9,17},{1... | collective-permute-start | bytes 393224 | tf_op jit(solution)/shard_map/ppermute | solution.py:816
  39.6 4.0 %states.1 = (f32[16,128,128]{2,1,0:T(8,128)S(1)}, f32[512,256]{1,0:T(8,128)S(1)}, f32[512,256]{1,0:T(8,128)S(1)}) custom-call(f32[2,128,128]{2,1,0:T(8,128)S(1)} %get-tuple-element.183.entry, f32[16,128,256]{2,1,0:T(8,128)S(1)} %get-tuple-element.172.zst, f32[512,768]{1,0:T(8,128)S(1)} %get-tuple-element.206.qkv.r_4_, ...), custom_call_target="tpu_custom_call" | custom-call | flops 1153500 | bytes 1 | tf_op jit(solution)/shard_map/states/pallas_call | solution.py:75
  49.6 6.3 %collective-permute-done.6.r_4_ = bf16[128,1024]{1,0:T(8,128)(2,1)} collective-permute-done((bf16[128,1024]{1,0:T(8,128)(2,1)}, bf16[128,1024]{1,0:T(8,128)(2,1)}, u32[]{:S(2)}, u32[]{:S(2)}) %collective-permute-start.6) | collective-permute-done | bytes 262176 | tf_op jit(solution)/shard_map/ppermute | solution.py:660
  57.8 11.5 %ffn.1 = (bf16[2,128,1024]{2,1,0:T(8,128)(2,1)S(1)}, f32[2,128,1024]{2,1,0:T(8,128)S(1)}, bf16[2,128,1024]{2,1,0:T(8,128)(2,1)S(1)}, f32[2,128,1024]{2,1,0:T(8,1...) custom-call(s32[1]{0:T(128)} %bitcast.tp.r_0_, ...), custom_call_target="tpu_custom_call" | custom-call | flops 1153500 | bytes 1 | tf_op jit(solution)/shard_map/ffn/pallas_call | solution.py:75
  69.6 3.9 %collective-permute-start.17 = (bf16[4,136,1024]{2,1,0:T(8,128)(2,1)S(1)}, bf16[4,136,1024]{2,1,0:T(8,128)(2,1)S(1)}, u32[]{:S(2)}, u32[]{:S(2)}) collective-permute-start(bf16[4,136,1024]{2,1,0:T(8,128)(2,1)S(1)} %get-tuple-element.220), channel_id=1, source_target_pairs={{0,8},{4,12},{8,0},{12,4},{16,24},{20,28},{24,16},{28,20},{1,9},{5... | collective-permute-start | bytes 3342344 | tf_op jit(solution)/shard_map/ppermute | solution.py:660
  77.1 4.8 %collective-permute-done.9 = bf16[1,128,1024]{2,1,0:T(8,128)(2,1)S(1)} collective-permute-done((bf16[1,128,1024]{2,1,0:T(8,128)(2,1)S(1)}, bf16[1,128,1024]{2,1,0:T(8,128)(2,1)S(1)}, u32[]{:S(2)}, u32[]{:S(2)}) %collective-permute-start.9) | collective-permute-done | bytes 262176 | tf_op jit(solution)/shard_map/ppermute | solution.py:660
  83.9 6.0 %collective-permute-done.11.b2 = bf16[128,1024]{1,0:T(8,128)(2,1)S(1)} collective-permute-done((bf16[128,1024]{1,0:T(8,128)(2,1)S(1)}, bf16[128,1024]{1,0:T(8,128)(2,1)S(1)}, u32[]{:S(2)}, u32[]{:S(2)}) %collective-permute-start.11) | collective-permute-done | bytes 262176 | tf_op jit(solution)/shard_map/ppermute | solution.py:660
  91.4 5.0 %flow.1 = (bf16[512,1024]{1,0:T(8,128)(2,1)S(1)}, bf16[512,256]{1,0:T(8,128)(2,1)S(1)}, f32[512,256]{1,0:T(8,128)S(1)}, f32[16,128,256]{2,1,0:T(8,128)S(1)}, f32...) custom-call(s32[1]{0:T(128)} %bitcast.tp.r_0_, ...), custom_call_target="tpu_custom_call" | custom-call | flops 1153500 | bytes 1 | tf_op jit(solution)/shard_map/flow/pallas_call | solution.py:75
  99.1 5.2 %side.1 = (f32[512,256]{1,0:T(8,128)S(1)}, f32[512,256]{1,0:T(8,128)S(1)}, f32[512,256]{1,0:T(8,128)S(1)}) custom-call(f32[512,768]{1,0:T(8,128)S(1)} %get-tuple-element.206.qkv.r_4_, f32[512,256]{1,0:T(8,128)S(1)} %get-tuple-element.207.dout, f32[512,256]{1,0:T(8,128)S(1)} %copy-done.9, f32[16,128,128]{2,1,0:T(8,128)S(1)} %get-tuple-element.184.states.r_11_, ...), custom_call_target="tpu_custom_call" | custom-call | flops 1153500 | bytes 1 | tf_op jit(solution)/shard_map/side/pallas_call | solution.py:75
  104.4 6.5 %collective-permute-done.15.r_2_ = f32[2,128,128]{2,1,0:T(8,128)S(1)} collective-permute-done((f32[2,128,128]{2,1,0:T(8,128)S(1)}, f32[2,128,128]{2,1,0:T(8,128)S(1)}, u32[]{:S(2)}, u32[]{:S(2)}) %collective-permute-start.15) | collective-permute-done | bytes 131104 | tf_op jit(solution)/shard_map/ppermute | solution.py:816
  115.0 9.6 %back.1 = (f32[520,768]{1,0:T(8,128)S(1)}, f32[8,768]{1,0:T(8,128)S(1)}, bf16[512,128]{1,0:T(8,128)(2,1)S(1)}) custom-call(s32[2,8]{1,0:T(2,128)S(1)} %get-tuple-element.163.meta.r_0_, f32[2,128,256]{2,1,0:T(8,128)S(1)} %collective-permute-done.14.r_1_, f32[2,128,128]{2,1,0:T(8,128)S(1)} %collective-permute-done.15.r_2_, ...), custom_call_target="tpu_custom_call" | custom-call | flops 1153500 | bytes 1 | tf_op jit(solution)/shard_map/back/pallas_call | solution.py:75
  142.4 3.6 %collective-permute-done.24 = bf16[1,128,1024]{2,1,0:T(8,128)(2,1)S(1)} collective-permute-done((bf16[1,128,1024]{2,1,0:T(8,128)(2,1)S(1)}, bf16[1,128,1024]{2,1,0:T(8,128)(2,1)S(1)}, u32[]{:S(2)}, u32[]{:S(2)}) %collective-permute-start.24) | collective-permute-done | bytes 262176 | tf_op jit(solution)/shard_map/ppermute | solution.py:660
  150.9 5.8 %collective-permute-done.26.got = bf16[1,128,1024]{2,1,0:T(8,128)(2,1)S(1)} collective-permute-done((bf16[1,128,1024]{2,1,0:T(8,128)(2,1)S(1)}, bf16[1,128,1024]{2,1,0:T(8,128)(2,1)S(1)}, u32[]{:S(2)}, u32[]{:S(2)}) %collective-permute-start.26) | collective-permute-done | bytes 262176 | tf_op jit(solution)/shard_map/ppermute | solution.py:660
  157.2 10.0 %collective-permute-done.27.got = bf16[1,136,1024]{2,1,0:T(8,128)(2,1)S(1)} collective-permute-done((bf16[1,136,1024]{2,1,0:T(8,128)(2,1)S(1)}, bf16[1,136,1024]{2,1,0:T(8,128)(2,1)S(1)}, u32[]{:S(2)}, u32[]{:S(2)}) %collective-permute-start.27) | collective-permute-done | bytes 278560 | tf_op jit(solution)/shard_map/ppermute | solution.py:660
  178.9 22.2 %collective-permute-done.36.b = bf16[1,128,1024]{2,1,0:T(8,128)(2,1)S(1)} collective-permute-done((bf16[1,128,1024]{2,1,0:T(8,128)(2,1)S(1)}, bf16[1,128,1024]{2,1,0:T(8,128)(2,1)S(1)}, u32[]{:S(2)}, u32[]{:S(2)}) %collective-permute-start.36) | collective-permute-done | bytes 262176 | tf_op jit(solution)/shard_map/ppermute | solution.py:660
  204.9 10.2 %collective-permute-done.40.b = bf16[2,136,1024]{2,1,0:T(8,128)(2,1)S(1)} collective-permute-done((bf16[2,136,1024]{2,1,0:T(8,128)(2,1)S(1)}, bf16[2,136,1024]{2,1,0:T(8,128)(2,1)S(1)}, u32[]{:S(2)}, u32[]{:S(2)}) %collective-permute-start.40) | collective-permute-done | bytes 557088 | tf_op jit(solution)/shard_map/ppermute | solution.py:660
  215.3 6.5 %collective-permute-done.41.got = bf16[1,72,1024]{2,1,0:T(8,128)(2,1)S(1)} collective-permute-done((bf16[1,72,1024]{2,1,0:T(8,128)(2,1)S(1)}, bf16[1,72,1024]{2,1,0:T(8,128)(2,1)S(1)}, u32[]{:S(2)}, u32[]{:S(2)}) %collective-permute-start.41) | collective-permute-done | bytes 147488 | tf_op jit(solution)/shard_map/ppermute | solution.py:660
  226.8 20.0 %collective-permute-done.44.b = bf16[1,72,1024]{2,1,0:T(8,128)(2,1)S(1)} collective-permute-done((bf16[1,72,1024]{2,1,0:T(8,128)(2,1)S(1)}, bf16[1,72,1024]{2,1,0:T(8,128)(2,1)S(1)}, u32[]{:S(2)}, u32[]{:S(2)}) %collective-permute-start.44) | collective-permute-done | bytes 147488 | tf_op jit(solution)/shard_map/ppermute | solution.py:660
  250.2 4.9 %collective-permute-done.45.b = bf16[1,96,1024]{2,1,0:T(8,128)(2,1)S(1)} collective-permute-done((bf16[1,96,1024]{2,1,0:T(8,128)(2,1)S(1)}, bf16[1,96,1024]{2,1,0:T(8,128)(2,1)S(1)}, u32[]{:S(2)}, u32[]{:S(2)}) %collective-permute-start.45) | collective-permute-done | bytes 196640 | tf_op jit(solution)/shard_map/ppermute | solution.py:660
  260.1 14.4 %collective-permute-done.47.b = bf16[2,96,1024]{2,1,0:T(8,128)(2,1)S(1)} collective-permute-done((bf16[2,96,1024]{2,1,0:T(8,128)(2,1)S(1)}, bf16[2,96,1024]{2,1,0:T(8,128)(2,1)S(1)}, u32[]{:S(2)}, u32[]{:S(2)}) %collective-permute-start.47) | collective-permute-done | bytes 393248 | tf_op jit(solution)/shard_map/ppermute | solution.py:660
  277.8 4.1 %settle_2.1 = (f32[704,1024]{1,0:T(8,128)}, f32[704,1024]{1,0:T(8,128)}) custom-call(s32[1]{0:T(128)} %bitcast.3.r_1_.r_0_, bf16[4,128,1024]{2,1,0:T(8,128)(2,1)S(1)} %f1_pack.3.r_1_, bf16[4,128,1024]{2,1,0:T(8,128)(2,1)S(1)} %collective-permute-done.48.r_2_, bf16[4,136,1024]{2,1,0:T(8,128)(2,1)S(1)} %f2_pack.3.r_3_, ...), custom_call_target="tpu_custom_call" | custom-call | flops 1153500 | bytes 1 | tf_op jit(solution)/shard_map/settle_2/pallas_call | solution.py:75
  (204 shorter events, 99.7 us)
Async XLA Ops:
  69.6 41.6 %collective-permute-start.17 = (bf16[4,136,1024]{2,1,0:T(8,128)(2,1)S(1)}, bf16[4,136,1024]{2,1,0:T(8,128)(2,1)S(1)}, u32[]{:S(2)}, u32[]{:S(2)}) collective-permute-start(bf16[4,136,1024]{2,1,0:T(8,128)(2,1)S(1)} %get-tuple-element.220), channel_id=1, source_target_pairs={{0,8},{4,12},{8,0},{12,4},{16,24},{20,28},{24,16},{28,20},{1,9},{5... | collective-permute-start | bytes 3342344 | tf_op jit(solution)/shard_map/ppermute | solution.py:660
  75.2 35.8 %collective-permute-start.16 = (bf16[4,128,1024]{2,1,0:T(8,128)(2,1)S(1)}, bf16[4,128,1024]{2,1,0:T(8,128)(2,1)S(1)}, u32[]{:S(2)}, u32[]{:S(2)}) collective-permute-start(bf16[4,128,1024]{2,1,0:T(8,128)(2,1)S(1)} %get-tuple-element.217), channel_id=1, source_target_pairs={{0,4},{4,0},{8,12},{12,8},{16,20},{20,16},{24,28},{28,24},{1,5},{5... | collective-permute-start | bytes 3145736 | tf_op jit(solution)/shard_map/ppermute | solution.py:660
  96.5 14.4 %collective-permute-start.14 = (f32[2,128,256]{2,1,0:T(8,128)S(1)}, f32[2,128,256]{2,1,0:T(8,128)S(1)}, u32[]{:S(2)}, u32[]{:S(2)}) collective-permute-start(f32[2,128,256]{2,1,0:T(8,128)S(1)} %get-tuple-element.212), channel_id=1, source_target_pairs={{4,0},{8,4},{12,8},{16,12},{20,16},{24,20},{28,24},{5,1},{9,5},{13... | collective-permute-start | bytes 786440 | tf_op jit(solution)/shard_map/ppermute | solution.py:816
  111.5 18.2 %collective-permute-start.20 = (bf16[2,136,1024]{2,1,0:T(8,128)(2,1)S(1)}, bf16[2,136,1024]{2,1,0:T(8,128)(2,1)S(1)}, u32[]{:S(2)}, u32[]{:S(2)}) collective-permute-start(bf16[2,136,1024]{2,1,0:T(8,128)(2,1)S(1)} %get-tuple-element.240), channel_id=1, source_target_pairs={{0,4},{4,0},{8,12},{12,8},{16,20},{20,16},{24,28},{28,24},{1,5},{5... | collective-permute-start | bytes 1671176 | tf_op jit(solution)/shard_map/ppermute | solution.py:660
  111.6 18.0 %collective-permute-start.19 = (bf16[2,128,1024]{2,1,0:T(8,128)(2,1)S(1)}, bf16[2,128,1024]{2,1,0:T(8,128)(2,1)S(1)}, u32[]{:S(2)}, u32[]{:S(2)}) collective-permute-start(bf16[2,128,1024]{2,1,0:T(8,128)(2,1)S(1)} %get-tuple-element.237), channel_id=1, source_target_pairs={{0,8},{4,12},{8,0},{12,4},{16,24},{20,28},{24,16},{28,20},{1,9},{5... | collective-permute-start | bytes 1572872 | tf_op jit(solution)/shard_map/ppermute | solution.py:660
  113.5 15.3 %collective-permute-start.18 = (bf16[1,128,1024]{2,1,0:T(8,128)(2,1)S(1)}, bf16[1,128,1024]{2,1,0:T(8,128)(2,1)S(1)}, u32[]{:S(2)}, u32[]{:S(2)}) collective-permute-start(bf16[1,128,1024]{2,1,0:T(8,128)(2,1)S(1)} %get-tuple-element.233), channel_id=1, source_target_pairs={{0,2},{1,3},{2,0},{3,1},{4,6},{5,7},{6,4},{7,5},{8,10},{9,11},{10,... | collective-permute-start | bytes 786440 | tf_op jit(solution)/shard_map/ppermute | solution.py:660
  134.3 33.4 %collective-permute-start.28 = (bf16[4,96,1024]{2,1,0:T(8,128)(2,1)S(1)}, bf16[4,96,1024]{2,1,0:T(8,128)(2,1)S(1)}, u32[]{:S(2)}, u32[]{:S(2)}) collective-permute-start(bf16[4,96,1024]{2,1,0:T(8,128)(2,1)S(1)} %get-tuple-element.272), channel_id=1, source_target_pairs={{0,4},{4,0},{8,12},{12,8},{16,20},{20,16},{24,28},{28,24},{1,5},{5... | collective-permute-start | bytes 2359304 | tf_op jit(solution)/shard_map/ppermute | solution.py:660
  140.9 15.8 %collective-permute-start.26 = (bf16[1,128,1024]{2,1,0:T(8,128)(2,1)S(1)}, bf16[1,128,1024]{2,1,0:T(8,128)(2,1)S(1)}, u32[]{:S(2)}, u32[]{:S(2)}) collective-permute-start(bf16[1,128,1024]{2,1,0:T(8,128)(2,1)S(1)} %get-tuple-element.268), channel_id=1, source_target_pairs={{0,16},{4,20},{8,24},{12,28},{16,0},{20,4},{24,8},{28,12},{1,17},{... | collective-permute-start | bytes 786440 | tf_op jit(solution)/shard_map/ppermute | solution.py:660
  147.2 25.5 %collective-permute-start.32 = (bf16[4,72,1024]{2,1,0:T(8,128)(2,1)S(1)}, bf16[4,72,1024]{2,1,0:T(8,128)(2,1)S(1)}, u32[]{:S(2)}, u32[]{:S(2)}) collective-permute-start(bf16[4,72,1024]{2,1,0:T(8,128)(2,1)S(1)} %get-tuple-element.276), channel_id=1, source_target_pairs={{0,8},{4,12},{8,0},{12,4},{16,24},{20,28},{24,16},{28,20},{1,9},{5... | collective-permute-start | bytes 1769480 | tf_op jit(solution)/shard_map/ppermute | solution.py:660
  149.7 17.5 %collective-permute-start.27 = (bf16[1,136,1024]{2,1,0:T(8,128)(2,1)S(1)}, bf16[1,136,1024]{2,1,0:T(8,128)(2,1)S(1)}, u32[]{:S(2)}, u32[]{:S(2)}) collective-permute-start(bf16[1,136,1024]{2,1,0:T(8,128)(2,1)S(1)} %get-tuple-element.270), channel_id=1, source_target_pairs={{0,16},{4,20},{8,24},{12,28},{16,0},{20,4},{24,8},{28,12},{1,17},{... | collective-permute-start | bytes 835592 | tf_op jit(solution)/shard_map/ppermute | solution.py:660
  156.7 14.7 %collective-permute-start.31 = (bf16[128,1024]{1,0:T(8,128)(2,1)S(1)}, bf16[128,1024]{1,0:T(8,128)(2,1)S(1)}, u32[]{:S(2)}, u32[]{:S(2)}) collective-permute-start(bf16[128,1024]{1,0:T(8,128)(2,1)S(1)} %collective-permute-done.30.a2), channel_id=1, source_target_pairs={{0,1},{1,0},{2,3},{3,2},{4,5},{5,4},{6,7},{7,6},{8,9},{9,8},{10,11... | collective-permute-start | bytes 786440 | tf_op jit(solution)/shard_map/ppermute | solution.py:660
  168.0 33.1 %collective-permute-start.37 = (bf16[2,96,1024]{2,1,0:T(8,128)(2,1)S(1)}, bf16[2,96,1024]{2,1,0:T(8,128)(2,1)S(1)}, u32[]{:S(2)}, u32[]{:S(2)}) collective-permute-start(bf16[2,96,1024]{2,1,0:T(8,128)(2,1)S(1)} %get-tuple-element.281), channel_id=1, source_target_pairs={{0,8},{4,12},{8,0},{12,4},{16,24},{20,28},{24,16},{28,20},{1,9},{5... | collective-permute-start | bytes 1179656 | tf_op jit(solution)/shard_map/ppermute | solution.py:660
  172.9 28.3 %collective-permute-start.38 = (bf16[2,72,1024]{2,1,0:T(8,128)(2,1)S(1)}, bf16[2,72,1024]{2,1,0:T(8,128)(2,1)S(1)}, u32[]{:S(2)}, u32[]{:S(2)}) collective-permute-start(bf16[2,72,1024]{2,1,0:T(8,128)(2,1)S(1)} %get-tuple-element.284), channel_id=1, source_target_pairs={{0,4},{4,0},{8,12},{12,8},{16,20},{20,16},{24,28},{28,24},{1,5},{5... | collective-permute-start | bytes 884744 | tf_op jit(solution)/shard_map/ppermute | solution.py:660
  174.4 26.9 %collective-permute-start.39 = (bf16[1,136,1024]{2,1,0:T(8,128)(2,1)S(1)}, bf16[1,136,1024]{2,1,0:T(8,128)(2,1)S(1)}, u32[]{:S(2)}, u32[]{:S(2)}) collective-permute-start(bf16[1,136,1024]{2,1,0:T(8,128)(2,1)S(1)} %f2_last.1.a), channel_id=1, source_target_pairs={{0,16},{4,20},{8,24},{12,28},{16,0},{20,4},{24,8},{28,12},{1,17},{... | collective-permute-start | bytes 835592 | tf_op jit(solution)/shard_map/ppermute | solution.py:660
  176.4 24.7 %collective-permute-start.36 = (bf16[1,128,1024]{2,1,0:T(8,128)(2,1)S(1)}, bf16[1,128,1024]{2,1,0:T(8,128)(2,1)S(1)}, u32[]{:S(2)}, u32[]{:S(2)}) collective-permute-start(bf16[1,128,1024]{2,1,0:T(8,128)(2,1)S(1)} %f1_last.1.a), channel_id=1, source_target_pairs={{0,16},{4,20},{8,24},{12,28},{16,0},{20,4},{24,8},{28,12},{1,17},{... | collective-permute-start | bytes 786440 | tf_op jit(solution)/shard_map/ppermute | solution.py:660
  202.0 21.1 %collective-permute-start.43 = (bf16[2,128,1024]{2,1,0:T(8,128)(2,1)S(1)}, bf16[2,128,1024]{2,1,0:T(8,128)(2,1)S(1)}, u32[]{:S(2)}, u32[]{:S(2)}) collective-permute-start(bf16[2,128,1024]{2,1,0:T(8,128)(2,1)S(1)} %f1_pack.2.a), channel_id=1, source_target_pairs={{0,8},{4,12},{8,0},{12,4},{16,24},{20,28},{24,16},{28,20},{1,9},{5... | collective-permute-start | bytes 1572872 | tf_op jit(solution)/shard_map/ppermute | solution.py:660
  202.0 19.8 %collective-permute-start.42 = (bf16[1,96,1024]{2,1,0:T(8,128)(2,1)S(1)}, bf16[1,96,1024]{2,1,0:T(8,128)(2,1)S(1)}, u32[]{:S(2)}, u32[]{:S(2)}) collective-permute-start(bf16[1,96,1024]{2,1,0:T(8,128)(2,1)S(1)} %get-tuple-element.291), channel_id=1, source_target_pairs={{0,16},{4,20},{8,24},{12,28},{16,0},{20,4},{24,8},{28,12},{1,17},{... | collective-permute-start | bytes 589832 | tf_op jit(solution)/shard_map/ppermute | solution.py:660
  204.7 17.0 %collective-permute-start.41 = (bf16[1,72,1024]{2,1,0:T(8,128)(2,1)S(1)}, bf16[1,72,1024]{2,1,0:T(8,128)(2,1)S(1)}, u32[]{:S(2)}, u32[]{:S(2)}) collective-permute-start(bf16[1,72,1024]{2,1,0:T(8,128)(2,1)S(1)} %get-tuple-element.289), channel_id=1, source_target_pairs={{0,16},{4,20},{8,24},{12,28},{16,0},{20,4},{24,8},{28,12},{1,17},{... | collective-permute-start | bytes 442376 | tf_op jit(solution)/shard_map/ppermute | solution.py:660
  215.2 62.6 %collective-permute-start.49 = (bf16[4,136,1024]{2,1,0:T(8,128)(2,1)S(1)}, bf16[4,136,1024]{2,1,0:T(8,128)(2,1)}, u32[]{:S(2)}, u32[]{:S(2)}) collective-permute-start(bf16[4,136,1024]{2,1,0:T(8,128)(2,1)S(1)} %f2_pack.3.r_3_), channel_id=1, source_target_pairs={{0,8},{4,12},{8,0},{12,4},{16,24},{20,28},{24,16},{28,20},{1,9},{5... | collective-permute-start | bytes 3342344 | tf_op jit(solution)/shard_map/ppermute | solution.py:660
  223.2 52.8 %collective-permute-start.48 = (bf16[4,128,1024]{2,1,0:T(8,128)(2,1)S(1)}, bf16[4,128,1024]{2,1,0:T(8,128)(2,1)S(1)}, u32[]{:S(2)}, u32[]{:S(2)}) collective-permute-start(bf16[4,128,1024]{2,1,0:T(8,128)(2,1)S(1)} %f1_pack.3.r_1_), channel_id=1, source_target_pairs={{0,4},{4,0},{8,12},{12,8},{16,20},{20,16},{24,28},{28,24},{1,5},{5... | collective-permute-start | bytes 3145736 | tf_op jit(solution)/shard_map/ppermute | solution.py:660
  224.7 22.2 %collective-permute-start.44 = (bf16[1,72,1024]{2,1,0:T(8,128)(2,1)S(1)}, bf16[1,72,1024]{2,1,0:T(8,128)(2,1)S(1)}, u32[]{:S(2)}, u32[]{:S(2)}) collective-permute-start(bf16[1,72,1024]{2,1,0:T(8,128)(2,1)S(1)} %f4_last.1.a), channel_id=1, source_target_pairs={{0,16},{4,20},{8,24},{12,28},{16,0},{20,4},{24,8},{28,12},{1,17},{... | collective-permute-start | bytes 442376 | tf_op jit(solution)/shard_map/ppermute | solution.py:660
  256.0 25.9 %collective-permute-start.50 = (bf16[4,72,1024]{2,1,0:T(8,128)(2,1)}, bf16[4,72,1024]{2,1,0:T(8,128)(2,1)}, u32[]{:S(2)}, u32[]{:S(2)}) collective-permute-start(bf16[4,72,1024]{2,1,0:T(8,128)(2,1)} %f4_pack.3.r_1_), channel_id=1, source_target_pairs={{0,8},{4,12},{8,0},{12,4},{16,24},{20,28},{24,16},{28,20},{1,9},{5... | collective-permute-start | bytes 1769480 | tf_op jit(solution)/shard_map/ppermute | solution.py:660
  257.3 17.2 %collective-permute-start.47 = (bf16[2,96,1024]{2,1,0:T(8,128)(2,1)S(1)}, bf16[2,96,1024]{2,1,0:T(8,128)(2,1)S(1)}, u32[]{:S(2)}, u32[]{:S(2)}) collective-permute-start(bf16[2,96,1024]{2,1,0:T(8,128)(2,1)S(1)} %f3_pack.2.a), channel_id=1, source_target_pairs={{0,16},{4,20},{8,24},{12,28},{16,0},{20,4},{24,8},{28,12},{1,17},{... | collective-permute-start | bytes 1179656 | tf_op jit(solution)/shard_map/ppermute | solution.py:660
  275.4 14.6 %collective-permute-start.51 = (bf16[4,96,1024]{2,1,0:T(8,128)(2,1)}, bf16[4,96,1024]{2,1,0:T(8,128)(2,1)}, u32[]{:S(2)}, u32[]{:S(2)}) collective-permute-start(bf16[4,96,1024]{2,1,0:T(8,128)(2,1)} %f3_pack.3.r_1_), channel_id=1, source_target_pairs={{0,4},{4,0},{8,12},{12,8},{16,20},{20,16},{24,28},{28,24},{1,5},{5... | collective-permute-start | bytes 2359304 | tf_op jit(solution)/shard_map/ppermute | solution.py:660
  (63 other events, 463.2 us)

commit v4 on v3

--- a/solution.py
+++ b/solution.py
@@ -48,6 +48,8 @@
 
 
 COST = 1153500
+STEPS = {'hops': ['f2', 'f1'], 'back': [], 'taps': ['f1', 'f2'], 'hid': [], 'x': [], 'tail': ['f3', 'f1', 'f2', 'in', 'f4', 'out', 'f1', 'f3', 'f4', 'f2', 'f2', 'f3', 'f1', 'f4', 'f4', 'f3', 'f3', 'f4', 's1', 's2', 's4', 's3']}
+WAYS = {'f1': ((0, 1, 2), (2, 1, 0)), 'f2': ((1, 0, 2), (2, 0, 1)), 'f3': ((0, 1, 2), (1, 2, 0)), 'f4': ((1, 0, 2), (2, 0, 1))}
 
 
 class Order:
@@ -66,7 +68,8 @@
         hbm_out = [i for i, o in enumerate(outs) if o[2:] == ("far",)]
         args = list(args)
         if self.last is not None:
-            at = next(i for i in range(len(args)) if i not in smem and i not in pin)
+            free = [i for i in range(len(args)) if i not in smem]
+            at = min(free, key=lambda i: (i in pin, i))
             args[at] = lax.optimization_barrier((args[at], self.last, *self.also))[0]
             self.also = ()
         for i in pin:
@@ -167,7 +170,7 @@
         count = seq_groups[s]
         length = count * GROUP - seq_pads[s]
         for n in range(groups):
-            gid = first[0] + n
+            gid = first[0] * groups + n
             inside = (gid >= start) & (gid < start + count)
             here = jnp.clip(length - (gid - start) * GROUP, 0, GROUP)
             meta[0, n] = jnp.where(gid == start, 1, meta[0, n])
@@ -368,49 +371,64 @@
     second[...] = rms_rows(total, wide_gain(gain)).astype(bf16)
 
 
-def ffn_kernel(plans, tp, place, s0, s1, s2, s3, gdh, wgh, wuh, wdh, down_send, down_keep, send, keep, *refs):
-    sums, (second, inner, dgate, dup, acc, wg, wu, grad_down, wd, sems) = refs[:-10], refs[-10:]
+def warm_kernel(wgh, wuh, wdh, gdh, wg, wu, wd, gd, grad_inner, sems):
     loads = [
         pltpu.make_async_copy(src, dst, sems.at[i])
-        for i, (src, dst) in enumerate(((wgh, wg), (wuh, wu), (gdh, grad_down), (wdh, wd)))
+        for i, (src, dst) in enumerate(((wdh, wd), (gdh, gd), (wgh, wg), (wuh, wu)))
     ]
     for load in loads:
         load.start()
-    share = s0.shape[0]
-    for half, pair in enumerate(((s0, s1), (s2, s3))):
-        sec = jnp.concatenate([pair[0][...], pair[1][...]], axis=0)
-        blocks = [rows_of(tp[0] ^ (2 * half + j), share) for j in range(2)]
-        if half == 0:
-            loads[0].wait()
-        gv = dot(sec, wg[...], 1, 1)
-        if half == 0:
-            loads[1].wait()
-        uv = dot(sec, wu[...], 1, 1)
-        if half == 0:
-            loads[2].wait()
-            loads[3].wait()
-        gd = jnp.concatenate([grad_down[b] for b in blocks], axis=0)
-        sig = jax.nn.sigmoid(gv)
-        act = gv * sig
-        inn = (act * uv).astype(bf16)
-        gi = dot(gd, wd[...], 1, 1)
-        dg = (gi * uv * (sig * (1.0 + gv * (1.0 - sig)))).astype(bf16)
-        du = (gi * act).astype(bf16)
-        for j, b in enumerate(blocks):
-            part = slice(j * share, (j + 1) * share)
-            second[b] = sec[part]
-            inner[b] = inn[part]
-            dgate[b] = dg[part]
-            dup[b] = du[part]
-        grad = dot(dg, wg[...]) + dot(du, wu[...])
-        keep[half] = grad[:share]
-        send[half] = grad[share:].astype(bf16)
-        down = dot(inn, wd[...])
-        down_keep[half] = down[:share]
-        down_send[half] = down[share:].astype(bf16)
-    for left, right, plan in ((inner, grad_down, 0), (dgate, second, 1), (dup, second, 2)):
-        acc[...] = dot(left[...], right[...], 0, 0)
-        put(acc, acc.shape[1], place[0], plans[plan], sums)
+    loads[0].wait()
+    loads[1].wait()
+    tile = 256
+    for t in range(gd.shape[0] // tile):
+        rows = slice(t * tile, (t + 1) * tile)
+        grad_inner[rows] = dot(gd[rows], wd[...], 1, 1)
+    loads[2].wait()
+    loads[3].wait()
+
+
+def ffn_half(tp, half, sa, sb, wg, wu, wd, grad_inner, sec, inner, dgate, dup, down_keep, down_send, keep, send):
+    share = sa.shape[0]
+    sec[:share] = sa[...]
+    sec[share:] = sb[...]
+    gv = dot(sec[...], wg[...], 1, 1)
+    uv = dot(sec[...], wu[...], 1, 1)
+    sig = jax.nn.sigmoid(gv)
+    act = gv * sig
+    inn = (act * uv).astype(bf16)
+    gi = jnp.concatenate(
+        [grad_inner[rows_of(tp[0] ^ (2 * half + j), share)] for j in range(2)], axis=0
+    )
+    dg = (gi * uv * (sig * (1.0 + gv * (1.0 - sig)))).astype(bf16)
+    du = (gi * act).astype(bf16)
+    inner[...] = inn
+    dgate[...] = dg
+    dup[...] = du
+    grad = dot(dg, wg[...]) + dot(du, wu[...])
+    keep[0] = grad[:share]
+    send[0] = grad[share:].astype(bf16)
+    down = dot(inn, wd[...])
+    down_keep[0] = down[:share]
+    down_send[0] = down[share:].astype(bf16)
+
+
+def ffn_a_kernel(tp, sa, sb, wg, wu, wd, grad_inner, *outs):
+    ffn_half(tp, 0, sa, sb, wg, wu, wd, grad_inner, *outs)
+
+
+def ffn_b_kernel(plans, tp, place, sa, sb, wg, wu, wd, grad_inner, gd, sec_a, inner_a, dgate_a, dup_a, down_keep, down_send, keep, send, *refs):
+    sums, (sec, inner, dgate, dup, acc) = refs[:-5], refs[-5:]
+    share = sa.shape[0]
+    ffn_half(tp, 1, sa, sb, wg, wu, wd, grad_inner, sec, inner, dgate, dup, down_keep, down_send, keep, send)
+    near = [jnp.concatenate([gd[rows_of(tp[0] ^ (2 * i + j), share)] for j in range(2)], axis=0) for i in range(2)]
+    for pair, plan in (
+        (((inner_a[...], near[0]), (inner[...], near[1])), 0),
+        (((dgate_a[...], sec_a[...]), (dgate[...], sec[...])), 1),
+        (((dup_a[...], sec_a[...]), (dup[...], sec[...])), 2),
+    ):
+        acc[...] = dot(*pair[0], 0, 0) + dot(*pair[1], 0, 0)
+        put(acc, acc.shape[1], (place[0] & 7), plans[plan], sums)
 
 
 def turn_kernel(kept, got, residual, gain, grad_y, grad_residual, branch, gain_part):
@@ -693,6 +711,9 @@
         self.index, self.bits, self.base, self.size = index, bits, base, size
         self.start, self.folds, self.lane = start, folds, lane
 
+    def rest(self):
+        return self.bits, self.base, self.size, self.start, self.folds, self.lane
+
 
 def put(acc, wide, place, plans, sums):
     for part in plans:
@@ -759,6 +780,18 @@
         self.swap(self.own)
 
 
+def pair_kernel(keep_a, got_a, keep_b, got_b, kept, send):
+    kept[...] = keep_a[...] + got_a[...].astype(f32)
+    send[...] = (keep_b[...] + got_b[...].astype(f32)).astype(bf16)
+
+
+def fold_pair(order, keep_a, got_a, keep_b, got_b):
+    shape = keep_a.shape
+    return order.run(
+        pair_kernel, "fold_tp", [(shape, f32), (shape, bf16)], [keep_a, got_a, keep_b, got_b]
+    )
+
+
 def scatter_first(order, keep, send):
     return fold(order, keep, swap(send, 1), "fold_tp")
 
@@ -766,18 +799,18 @@
 def grads_c_kernel(plans, place, hidden, gp, *refs):
     sums, acc = refs[:-1], refs[-1]
     acc[...] = dot(hidden[...], gp[...], 0, 0)
-    put(acc, acc.shape[1] // 3, place[0], plans, sums)
+    put(acc, acc.shape[1] // 3, (place[0] & 7), plans, sums)
 
 
 def grads_d_kernel(plans, way, base, place, attended, branch, hidden, dgate, small, gains, keep, send, acc, acc2, both):
     sums = (keep, send)
     acc[...] = dot(attended[...], branch[...], 0, 0)
-    put(acc, acc.shape[1], place[0], plans[:1], sums)
+    put(acc, acc.shape[1], (place[0] & 7), plans[:1], sums)
     acc2[...] = dot(hidden[...], dgate[...], 0, 0)
-    put(acc2, acc2.shape[1], place[0], plans[1:], sums)
+    put(acc2, acc2.shape[1], (place[0] & 7), plans[1:], sums)
     both[...] = small[...] + gains[...]
     for m in range(1 << len(way)):
-        line = both[pl.ds(m ^ place[0], 1)] + jnp.zeros((8, both.shape[1]), f32)
+        line = both[pl.ds(m ^ (place[0] & 7), 1)] + jnp.zeros((8, both.shape[1]), f32)
         at = rank_of(m, way[1:])
         if (m >> way[0]) & 1:
             send[at, base : base + 8] = line.astype(bf16)
@@ -785,19 +818,18 @@
             keep[at, base : base + 8] = line
 
 
-def settle_kernel(jobs, line_at, place, *refs):
-    count = 1 + max(part.index for parts in jobs for part, _ in parts)
+def settle_kernel(count, jobs, line_at, place, *refs):
     pairs, outs = refs[: 2 * count], refs[2 * count :]
     for parts, out in zip(jobs, outs):
         for part, way in parts:
-            take(out, place[0], part, way, *pairs[2 * part.index : 2 * part.index + 2])
+            take(out, (place[0] & 7), part, way, *pairs[2 * part.index : 2 * part.index + 2])
     if line_at is not None:
         index, way, base = line_at
         near, far = pairs[2 * index : 2 * index + 2]
         for m in range(1 << len(way)):
             source = far if (m >> way[-1]) & 1 else near
             at = rank_of(m, way[-2::-1])
-            outs[-1][pl.ds(m ^ place[0], 1)] = source[at, base : base + 8].astype(f32)[:1]
+            outs[-1][pl.ds(m ^ (place[0] & 7), 1)] = source[at, base : base + 8].astype(f32)[:1]
 
 
 def sum_shapes(blocks, rows, cols):
@@ -871,8 +903,7 @@
     tp_rank = lax.axis_index("tp")
     tp = tp_rank.astype(jnp.int32).reshape(1)
     blocks = 8
-    place = (lax.axis_index("seq") % blocks).astype(jnp.int32).reshape(1)
-    first = (lax.axis_index("seq") * groups).astype(jnp.int32).reshape(1)
+    place = lax.axis_index("seq").astype(jnp.int32).reshape(1)
     taps = (conv_query, conv_key, conv_value)
     wb = w_beta.T
     tail = shift(layer_input[total - TAIL :], 1)
@@ -923,7 +954,7 @@
             (inv_shape, f32, far),
             (map_shape, f32, far),
         ],
-        [first, tp, seq_groups, seq_pads, layer_input, cotangent, norm_in, w_query, w_key, w_value, w_gate_out, wb, tail, *taps],
+        [place, tp, seq_groups, seq_pads, layer_input, cotangent, norm_in, w_query, w_key, w_value, w_gate_out, wb, tail, *taps],
         smem=(0, 1, 2, 3),
         smem_out=(2,),
         hbm=(4, 5, 7, 8, 9, 10),
@@ -966,12 +997,13 @@
         [x_own, kept[0], got[0], norm_mid],
     )
     size = ffw // blocks
-    ways = [
-        ((0, 1, 2), (2, 1, 0)),
-        ((1, 0, 2), (2, 0, 1)),
-        ((0, 1, 2), (1, 2, 0)),
-        ((1, 0, 2), (2, 0, 1)),
-    ]
+    ways = [WAYS[name] for name in ("f1", "f2", "f3", "f4")]
+    flows = {}
+
+    def go(slot):
+        for name in STEPS[slot]:
+            flows[name].step()
+
     near_up = size // 16 * 8
     far_up = size - near_up
     down_parts = [Plan(0, ways[0][0], 0, size)]
@@ -982,30 +1014,55 @@
     ]
     plans_a = (down_parts, gate_parts, up_parts)
     f1_rows, f2_rows = size + near_up, size + far_up
-    all_rows = gather_rel(second_own)
-    down_send, down_keep, send, keep, *sums = run(
-        lambda *r: ffn_kernel(plans_a, *r),
-        "ffn",
-        [*tp_sums, *tp_sums, *sum_shapes(blocks, f1_rows, model), *sum_shapes(blocks, f2_rows, model)],
-        [tp, place, *all_rows, grad_down, w_gate.T, w_up.T, w_down],
+    own_rows, beside_rows = second_own, swap(second_own, 1)
+    far_rows = swap(second_own, 2)
+    w_shape = (ffw, model)
+    wg, wu, wd, gd, grad_inner = run(
+        warm_kernel,
+        "warm",
+        [
+            (w_shape, bf16, near),
+            (w_shape, bf16, near),
+            (w_shape, bf16, near),
+            ((total, model), bf16, near),
+            ((total, ffw), f32, near),
+        ],
+        [w_gate.T, w_up.T, w_down, grad_down],
+        hbm=(0, 1, 2, 3),
+        pin=(0, 1, 2, 3),
+        scratch=[pltpu.SemaphoreType.DMA((4,))],
+    )
+    part = (1, share, model)
+    half_ffn = ((2 * share, ffw), bf16)
+    half_outs = [(part, f32), (part, bf16)] * 2
+    sec_a, inner_a, dgate_a, dup_a, down_keep_a, down_send_a, keep_a, send_a = run(
+        ffn_a_kernel,
+        "ffn_a",
+        [((2 * share, model), bf16), half_ffn, half_ffn, half_ffn, *half_outs],
+        [tp, own_rows, beside_rows, wg, wu, wd, grad_inner],
+        smem=(0,),
+        vmem=12,
+    )
+    far_rows, sec_a = lax.optimization_barrier((far_rows, sec_a))
+    near_a = swap(send_a, 1)
+    down_near_a = swap(down_send_a, 1)
+    down_keep_b, down_send_b, keep_b, send_b, *sums = run(
+        lambda *r: ffn_b_kernel(plans_a, *r),
+        "ffn_b",
+        [*half_outs, *sum_shapes(blocks, f1_rows, model), *sum_shapes(blocks, f2_rows, model)],
+        [tp, place, far_rows, swap(far_rows, 1), wg, wu, wd, grad_inner, gd, sec_a, inner_a, dgate_a, dup_a],
         smem=(0, 1),
-        hbm=(6, 7, 8, 9),
-        pin=(6, 7, 8, 9),
         scratch=[
-            rows,
-            *[pltpu.VMEM((total, ffw), bf16)] * 3,
+            pltpu.VMEM((2 * share, model), bf16),
+            *[pltpu.VMEM((2 * share, ffw), bf16)] * 3,
             pltpu.VMEM((ffw, model), f32),
-            *[pltpu.VMEM((ffw, model), bf16)] * 2,
-            rows,
-            pltpu.VMEM((ffw, model), bf16),
-            pltpu.SemaphoreType.DMA((4,)),
         ],
-        vmem=28,
-    )
-    beside = swap(send, 1)
-    f1 = begin(sums[0], sums[1], *ways[0], "f1")
-    f2 = begin(sums[2], sums[3], *ways[1], "f2")
-    kept, cross = fold(order, keep, beside, "fold_tp")
+        vmem=16,
+    )
+    near_b = swap(send_b, 1)
+    flows["f1"] = begin(sums[0], sums[1], *ways[0], "f1")
+    flows["f2"] = begin(sums[2], sums[3], *ways[1], "f2")
+    kept, cross = fold_pair(order, keep_a, near_a, keep_b, near_b)
     got = swap(cross, 2)
     grad_residual, branch_own, mid_part = run(
         turn_kernel,
@@ -1030,18 +1087,17 @@
         scratch=[pltpu.VMEM(map_shape, f32)],
     )
     hops = hops_of(dev, last, -1, reach)
-    down_near = swap(down_send, 1)
+    down_near_b = swap(down_send_b, 1)
     ndo, dq, dk = run(
         side_kernel,
         "side",
         [(wide, f32)] * 3,
         [qkv, dout, vnew, states, score],
     )
-    down_kept, cross = fold(order, down_keep, down_near, "fold_tp")
+    down_kept, cross = fold_pair(order, down_keep_a, down_near_a, down_keep_b, down_near_b)
     down_got = swap(cross, 2)
     order.wait(*hops)
-    f1.step()
-    f2.step()
+    go("hops")
     dc, halo, dbeta = run(
         lambda *r: back_kernel(reach, *r),
         "back",
@@ -1050,6 +1106,7 @@
         smem=(0,),
     )
     incoming = shift(halo, -1)
+    go("back")
     gp, last, dtaps = run(
         taps_kernel,
         "taps",
@@ -1064,8 +1121,7 @@
         [tp, meta, down_kept[0], down_got[0], residual],
         smem=(0, 1),
     )
-    f1.step()
-    f2.step()
+    go("taps")
     gp, send, keep, in_part = run(
         hid_kernel,
         "hid",
@@ -1090,7 +1146,8 @@
         scratch=[pltpu.VMEM((model, 3 * width), f32)],
         vmem=16,
     )
-    f3 = begin(keep_c, send_c, *ways[2], "f3")
+    flows["f3"] = begin(keep_c, send_c, *ways[2], "f3")
+    go("hid")
     kept, cross = fold(order, keep, beside, "fold_tp")
     got = swap(cross, 2)
     row8 = ((8, model), f32)
@@ -1099,6 +1156,7 @@
     )
     gains = plus(order, gains, swap(gains, 1))
     far_gains = swap(gains, 2)
+    go("x")
     (grad_in_own,) = run(
         in_kernel,
         "inp",
@@ -1124,66 +1182,64 @@
         ],
         vmem=12,
     )
-    f4 = begin(keep_d, send_d, *ways[3], "f4")
-    f1.step()
-    f2.step()
-    f3.step()
-    (grad_input,) = run(
-        place_kernel,
-        "place_in",
-        [((total, model), f32)],
-        [tp, *grad_in_all],
-        smem=(0,),
-    )
+    flows["f4"] = begin(keep_d, send_d, *ways[3], "f4")
     out_all = gather_rel(out_own)
-    f4.step()
-    (block_out,) = run(
-        place_kernel,
-        "place_out",
-        [((total, model), bf16)],
-        [tp, *out_all],
-        smem=(0,),
-    )
-    f1.step()
-    f3.step()
-    f4.step()
-    f2.step()
-    f2.step()
-    f4.step()
-    f3.step()
-    f1.step()
-    f4.step()
-    f3.step()
-    f4.step()
-    f3.step()
-
-    def settle(name, jobs, flows, outs, line_at=None):
+    results = {}
+
+    def settle(name, jobs, used, outs, line_at=None):
         return run(
-            lambda *r: settle_kernel(jobs, line_at, *r),
+            lambda *r: settle_kernel(len(used), jobs, line_at, *r),
             name,
             [(o, f32) for o in outs],
-            [place, *[a for flow in flows for a in (flow.own, flow.got)]],
+            [place, *[a for flow in used for a in (flows[flow].own, flows[flow].got)]],
             smem=(0,),
         )
 
-    wayed = lambda parts, ways_of: [(part, ways_of[part.index][1]) for part in parts]
-    (grad_down_w,) = settle("settle_1", [wayed(down_parts, ways)], [f1], [(ffw, model)])
-    grad_gate_w, grad_up_w = settle(
-        "settle_2",
-        [wayed(gate_parts, ways), wayed(up_parts, ways)],
-        [f1, f2],
-        [(ffw, model)] * 2,
-    )
-    grad_out_w, grad_gate_out_w, small = settle(
-        "settle_4",
-        [wayed(out_parts, ways[3:]), wayed(gate_out_parts, ways[3:])],
-        [f4],
-        [(width, model), (model, width), (8, model)],
-        line_at=(0, ways[3][1], line_base),
-    )
-    hidden_sums = settle(
-        "settle_3", [wayed([part], ways[2:]) for part in plans_c], [f3], [(model, width)] * 3
-    )
+    def wayed(parts, first_flow=0):
+        moved = [Plan(p.index - first_flow, *p.rest()) for p in parts]
+        return [(m, ways[p.index][1]) for m, p in zip(moved, parts)]
+
+    def late(parts, flow):
+        return [(part, ways[flow][1]) for part in parts]
+
+    for name in STEPS["tail"]:
+        if name in flows:
+            flows[name].step()
+        elif name in ("in", "out"):
+            results[name] = run(
+                place_kernel,
+                "place_" + name,
+                [((total, model), f32 if name == "in" else bf16)],
+                [tp, *(grad_in_all if name == "in" else out_all)],
+                smem=(0,),
+            )
+        elif name == "s1":
+            results[name] = settle(
+                "settle_1",
+                [wayed(down_parts), wayed(up_parts)],
+                ["f1", "f2"],
+                [(ffw, model)] * 2,
+            )
+        elif name == "s2":
+            results[name] = settle("settle_2", [wayed(gate_parts, 1)], ["f2"], [(ffw, model)])
+        elif name == "s3":
+            results[name] = settle(
+                "settle_3", [late([part], 2) for part in plans_c], ["f3"], [(model, width)] * 3
+            )
+        else:
+            results[name] = settle(
+                "settle_4",
+                [late(out_parts, 3), late(gate_out_parts, 3)],
+                ["f4"],
+                [(width, model), (model, width), (8, model)],
+                line_at=(0, ways[3][1], line_base),
+            )
+    (grad_input,) = results["in"]
+    (block_out,) = results["out"]
+    grad_down_w, grad_up_w = results["s1"]
+    (grad_gate_w,) = results["s2"]
+    hidden_sums = results["s3"]
+    grad_out_w, grad_gate_out_w, small = results["s4"]
     cut = model // 4
     head_cut = DH // 4
     gain_of = lambda row, size, lane=0: lax.dynamic_slice(

time: 296 us -> 276 us (0.932)
  waiting for transfers between devices: 135 us -> 120 us
  local copies, waits for them, and re-layouts: 7.55 us -> 4.31 us
    ppermute x46 -> x48, waiting for transfers between devices: 127 us -> 111 us  [swap(): return lax.ppermute(value, axis, [(i, i ^ bit) for i in range(count)])]
    unnamed x70 -> x40, local copies, waits for them, and re-layouts: 4.36 us -> 1.12 us
    ppermute x46 -> x48, starting transfers between devices: 50.4 us -> 52.7 us  [swap(): return lax.ppermute(value, axis, [(i, i ^ bit) for i in range(count)])]
    pallas_call x49 -> x51, Pallas kernels: 82 us -> 80.3 us  [run(): pl.pallas_call(kernel, name=name, out_shape=shapes, in_specs=[pl.BlockSpe...]
  transfers between devices with their start and end apart: 52 -> 54, of which waited for: 24 -> 25; matrix products, arithmetic and copies ran while one was open for 1% -> 1% of each run, Pallas kernels for 16% -> 21%
where the time goes in v4:
time: 276 us; the launch traced here: 275 us
  waiting for transfers between devices  120 us (43%)
  Pallas kernels  80.3 us (29%)
  starting transfers between devices  69.2 us (25%)
  local copies, waits for them, and re-layouts  4.31 us (2%)
    ppermute x48, waiting for transfers between devices, swap(): return lax.ppermute(value, axis, [(i, i ^ bit) for i in range(count)])  111 us
    pallas_call x51, Pallas kernels, run(): pl.pallas_call(kernel, name=name, out_shape=shapes, in_specs=[pl.BlockSpe...  80.3 us
    ppermute x48, starting transfers between devices, swap(): return lax.ppermute(value, axis, [(i, i ^ bit) for i in range(count)])  52.7 us
    ppermute x6, starting transfers between devices, shift(): return lax.ppermute(value, 'seq', pairs)  16.5 us
    ppermute x6, waiting for transfers between devices, shift(): return lax.ppermute(value, 'seq', pairs)  8.83 us
  transfers between devices with their start and end apart: 54, of which 25 were waited for; matrix products, arithmetic and copies ran while one was open for 1% of the time, Pallas kernels for 21%

profile of v4, /device:TPU:0, one launch (start us, length us, event | category | flops | bytes accessed | tf_op | source)
XLA Modules:
  0.0 275.3 jit_solution(10826592468732262545)
XLA Ops:
  1.4 4.9 %collective-permute-start = (bf16[16,1024]{1,0:T(8,128)(2,1)S(1)}, bf16[16,1024]{1,0:T(8,128)(2,1)S(1)}, u32[]{:S(2)}, u32[]{:S(2)}) collective-permute-start(bf16[16,1024]{1,0:T(8,128)(2,1)S(1)} %slice.15), channel_id=1, source_target_pairs={{0,4},{4,8},{8,12},{12,16},{16,20},{20,24},{24,28},{1,5},{5,9},{9,... | collective-permute-start | bytes 98312 | tf_op jit(solution)/shard_map/ppermute | solution.py:848
  7.9 15.1 %front.1 = (f32[512,256]{1,0:T(8,128)S(1)}, f32[512,2]{1,0:T(8,128)S(1)}, s32[2,8]{1,0:T(2,128)S(1)}, f32[512,768]{1,0:T(8,128)S(1)}, f32[512,256]{1,0:T(8,128)S...) custom-call(s32[1]{0:T(128)} %bitcast.1.first.r_1_.r_0_, ...), custom_call_target="tpu_custom_call" | custom-call | flops 1153500 | bytes 1 | tf_op jit(solution)/shard_map/front/pallas_call | solution.py:78
  23.0 4.2 %collective-permute-start.1 = (f32[2,128,256]{2,1,0:T(8,128)S(1)}, f32[2,128,256]{2,1,0:T(8,128)S(1)}, u32[]{:S(2)}, u32[]{:S(2)}) collective-permute-start(f32[2,128,256]{2,1,0:T(8,128)S(1)} %get-tuple-element.182), channel_id=1, source_target_pairs={{0,4},{4,8},{8,12},{12,16},{16,20},{20,24},{24,28},{1,5},{5,9},{9,... | collective-permute-start | bytes 786440 | tf_op jit(solution)/shard_map/ppermute | solution.py:848
  27.2 3.5 %collective-permute-start.2 = (f32[2,128,128]{2,1,0:T(8,128)S(1)}, f32[2,128,128]{2,1,0:T(8,128)S(1)}, u32[]{:S(2)}, u32[]{:S(2)}) collective-permute-start(f32[2,128,128]{2,1,0:T(8,128)S(1)} %get-tuple-element.192), channel_id=1, source_target_pairs={{0,8},{4,12},{8,16},{12,20},{16,24},{20,28},{1,9},{5,13},{9,17},{1... | collective-permute-start | bytes 393224 | tf_op jit(solution)/shard_map/ppermute | solution.py:848
  38.9 3.8 %states.1 = (f32[16,128,128]{2,1,0:T(8,128)S(1)}, f32[512,256]{1,0:T(8,128)S(1)}, f32[512,256]{1,0:T(8,128)S(1)}) custom-call(f32[2,128,128]{2,1,0:T(8,128)S(1)} %get-tuple-element.200.entry, f32[16,128,256]{2,1,0:T(8,128)S(1)} %get-tuple-element.189.zst, f32[512,768]{1,0:T(8,128)S(1)} %get-tuple-element.238.qkv.r_4_, ...), custom_call_target="tpu_custom_call" | custom-call | flops 1153500 | bytes 1 | tf_op jit(solution)/shard_map/states/pallas_call | solution.py:78
  56.4 5.2 %ffn_b.1 = (f32[1,128,1024]{2,1,0:T(8,128)S(1)}, bf16[1,128,1024]{2,1,0:T(8,128)(2,1)S(1)}, f32[1,128,1024]{2,1,0:T(8,128)S(1)}, bf16[1,128,1024]{2,1,0:T(8,128)...) custom-call(s32[1]{0:T(128)} %bitcast.tp.r_0_, ...), custom_call_target="tpu_custom_call" | custom-call | flops 1153500 | bytes 1 | tf_op jit(solution)/shard_map/ffn_b/pallas_call | solution.py:78
  61.8 3.7 %collective-permute-start.18 = (bf16[4,136,1024]{2,1,0:T(8,128)(2,1)S(1)}, bf16[4,136,1024]{2,1,0:T(8,128)(2,1)S(1)}, u32[]{:S(2)}, u32[]{:S(2)}) collective-permute-start(bf16[4,136,1024]{2,1,0:T(8,128)(2,1)S(1)} %get-tuple-element.251), channel_id=1, source_target_pairs={{0,8},{4,12},{8,0},{12,4},{16,24},{20,28},{24,16},{28,20},{1,9},{5... | collective-permute-start | bytes 3342344 | tf_op jit(solution)/shard_map/ppermute | solution.py:678
  69.2 4.8 %collective-permute-done.10 = bf16[1,128,1024]{2,1,0:T(8,128)(2,1)S(1)} collective-permute-done((bf16[1,128,1024]{2,1,0:T(8,128)(2,1)S(1)}, bf16[1,128,1024]{2,1,0:T(8,128)(2,1)S(1)}, u32[]{:S(2)}, u32[]{:S(2)}) %collective-permute-start.10) | collective-permute-done | bytes 262176 | tf_op jit(solution)/shard_map/ppermute | solution.py:678
  75.9 6.0 %collective-permute-done.12.b2 = bf16[128,1024]{1,0:T(8,128)(2,1)S(1)} collective-permute-done((bf16[128,1024]{1,0:T(8,128)(2,1)S(1)}, bf16[128,1024]{1,0:T(8,128)(2,1)S(1)}, u32[]{:S(2)}, u32[]{:S(2)}) %collective-permute-start.12) | collective-permute-done | bytes 262176 | tf_op jit(solution)/shard_map/ppermute | solution.py:678
  83.4 5.2 %flow.1 = (bf16[512,1024]{1,0:T(8,128)(2,1)S(1)}, bf16[512,256]{1,0:T(8,128)(2,1)S(1)}, f32[512,256]{1,0:T(8,128)S(1)}, f32[16,128,256]{2,1,0:T(8,128)S(1)}, f32...) custom-call(s32[1]{0:T(128)} %bitcast.tp.r_0_, ...), custom_call_target="tpu_custom_call" | custom-call | flops 1153500 | bytes 1 | tf_op jit(solution)/shard_map/flow/pallas_call | solution.py:78
  91.3 5.0 %side.1 = (f32[512,256]{1,0:T(8,128)S(1)}, f32[512,256]{1,0:T(8,128)S(1)}, f32[512,256]{1,0:T(8,128)S(1)}) custom-call(f32[512,768]{1,0:T(8,128)S(1)} %get-tuple-element.238.qkv.r_4_, f32[512,256]{1,0:T(8,128)S(1)} %get-tuple-element.239.dout, f32[512,256]{1,0:T(8,128)S(1)} %get-tuple-element.240.vnew.r_12_, ...), custom_call_target="tpu_custom_call" | custom-call | flops 1153500 | bytes 1 | tf_op jit(solution)/shard_map/side/pallas_call | solution.py:78
  96.4 6.7 %collective-permute-done.17.r_2_ = f32[2,128,128]{2,1,0:T(8,128)S(1)} collective-permute-done((f32[2,128,128]{2,1,0:T(8,128)S(1)}, f32[2,128,128]{2,1,0:T(8,128)S(1)}, u32[]{:S(2)}, u32[]{:S(2)}) %collective-permute-start.17) | collective-permute-done | bytes 131104 | tf_op jit(solution)/shard_map/ppermute | solution.py:848
  106.7 9.6 %back.1 = (f32[520,768]{1,0:T(8,128)S(1)}, f32[8,768]{1,0:T(8,128)S(1)}, bf16[512,128]{1,0:T(8,128)(2,1)S(1)}) custom-call(s32[2,8]{1,0:T(2,128)S(1)} %get-tuple-element.180.meta.r_0_, f32[2,128,256]{2,1,0:T(8,128)S(1)} %collective-permute-done.16.r_1_, f32[2,128,128]{2,1,0:T(8,128)S(1)} %collective-permute-done.17.r_2_, ...), custom_call_target="tpu_custom_call" | custom-call | flops 1153500 | bytes 1 | tf_op jit(solution)/shard_map/back/pallas_call | solution.py:78
  134.5 3.2 %collective-permute-done.26 = bf16[1,128,1024]{2,1,0:T(8,128)(2,1)S(1)} collective-permute-done((bf16[1,128,1024]{2,1,0:T(8,128)(2,1)S(1)}, bf16[1,128,1024]{2,1,0:T(8,128)(2,1)S(1)}, u32[]{:S(2)}, u32[]{:S(2)}) %collective-permute-start.26) | collective-permute-done | bytes 262176 | tf_op jit(solution)/shard_map/ppermute | solution.py:678
  143.3 5.1 %collective-permute-done.29.got = bf16[1,128,1024]{2,1,0:T(8,128)(2,1)S(1)} collective-permute-done((bf16[1,128,1024]{2,1,0:T(8,128)(2,1)S(1)}, bf16[1,128,1024]{2,1,0:T(8,128)(2,1)S(1)}, u32[]{:S(2)}, u32[]{:S(2)}) %collective-permute-start.29) | collective-permute-done | bytes 262176 | tf_op jit(solution)/shard_map/ppermute | solution.py:678
  148.9 10.1 %collective-permute-done.30.got = bf16[1,136,1024]{2,1,0:T(8,128)(2,1)S(1)} collective-permute-done((bf16[1,136,1024]{2,1,0:T(8,128)(2,1)S(1)}, bf16[1,136,1024]{2,1,0:T(8,128)(2,1)S(1)}, u32[]{:S(2)}, u32[]{:S(2)}) %collective-permute-start.30) | collective-permute-done | bytes 278560 | tf_op jit(solution)/shard_map/ppermute | solution.py:678
  159.7 3.3 %collective-permute-start.39 = (bf16[2,96,1024]{2,1,0:T(8,128)(2,1)S(1)}, bf16[2,96,1024]{2,1,0:T(8,128)(2,1)S(1)}, u32[]{:S(2)}, u32[]{:S(2)}) collective-permute-start(bf16[2,96,1024]{2,1,0:T(8,128)(2,1)S(1)} %get-tuple-element.315), channel_id=1, source_target_pairs={{0,8},{4,12},{8,0},{12,4},{16,24},{20,28},{24,16},{28,20},{1,9},{5... | collective-permute-start | bytes 1179656 | tf_op jit(solution)/shard_map/ppermute | solution.py:678
  170.9 22.0 %collective-permute-done.38.b = bf16[1,128,1024]{2,1,0:T(8,128)(2,1)S(1)} collective-permute-done((bf16[1,128,1024]{2,1,0:T(8,128)(2,1)S(1)}, bf16[1,128,1024]{2,1,0:T(8,128)(2,1)S(1)}, u32[]{:S(2)}, u32[]{:S(2)}) %collective-permute-start.38) | collective-permute-done | bytes 262176 | tf_op jit(solution)/shard_map/ppermute | solution.py:678
  196.7 10.2 %collective-permute-done.42.b = bf16[2,136,1024]{2,1,0:T(8,128)(2,1)S(1)} collective-permute-done((bf16[2,136,1024]{2,1,0:T(8,128)(2,1)S(1)}, bf16[2,136,1024]{2,1,0:T(8,128)(2,1)S(1)}, u32[]{:S(2)}, u32[]{:S(2)}) %collective-permute-start.42) | collective-permute-done | bytes 557088 | tf_op jit(solution)/shard_map/ppermute | solution.py:678
  207.0 3.4 %collective-permute-done.43.got = bf16[1,96,1024]{2,1,0:T(8,128)(2,1)S(1)} collective-permute-done((bf16[1,96,1024]{2,1,0:T(8,128)(2,1)S(1)}, bf16[1,96,1024]{2,1,0:T(8,128)(2,1)S(1)}, u32[]{:S(2)}, u32[]{:S(2)}) %collective-permute-start.43) | collective-permute-done | bytes 196640 | tf_op jit(solution)/shard_map/ppermute | solution.py:678
  226.3 25.0 %collective-permute-done.48.b = bf16[2,96,1024]{2,1,0:T(8,128)(2,1)S(1)} collective-permute-done((bf16[2,96,1024]{2,1,0:T(8,128)(2,1)S(1)}, bf16[2,96,1024]{2,1,0:T(8,128)(2,1)S(1)}, u32[]{:S(2)}, u32[]{:S(2)}) %collective-permute-start.48) | collective-permute-done | bytes 393248 | tf_op jit(solution)/shard_map/ppermute | solution.py:678
  257.0 4.1 %settle_1.1 = (f32[704,1024]{1,0:T(8,128)}, f32[704,1024]{1,0:T(8,128)}) custom-call(s32[1]{0:T(128)} %bitcast.1.first.r_1_.r_0_, bf16[4,128,1024]{2,1,0:T(8,128)(2,1)S(1)} %f1_pack.3.r_1_, bf16[4,128,1024]{2,1,0:T(8,128)(2,1)} %collective-permute-done.50.r_2_, bf16[4,136,1024]{2,1,0:T(8,128)(2,1)S(1)} %f2_pack.3.r_3_.r_1_, ...), custom_call_target="tpu_custom_call" | custom-call | flops 1153500 | bytes 1 | tf_op jit(solution)/shard_map/settle_1/pallas_call | solution.py:78
  262.9 3.6 %collective-permute-done.52.r_2_ = bf16[4,72,1024]{2,1,0:T(8,128)(2,1)} collective-permute-done((bf16[4,72,1024]{2,1,0:T(8,128)(2,1)}, bf16[4,72,1024]{2,1,0:T(8,128)(2,1)}, u32[]{:S(2)}, u32[]{:S(2)}) %collective-permute-start.52) | collective-permute-done | bytes 589856 | tf_op jit(solution)/shard_map/ppermute | solution.py:678
  272.0 3.3 %settle_3.1 = (f32[1024,256]{1,0:T(8,128)}, f32[1024,256]{1,0:T(8,128)}, f32[1024,256]{1,0:T(8,128)}) custom-call(s32[1]{0:T(128)} %bitcast.1.first.r_1_.r_0_, bf16[4,96,1024]{2,1,0:T(8,128)(2,1)} %f3_pack.3.r_1_, bf16[4,96,1024]{2,1,0:T(8,128)(2,1)} %collective-permute-done.53.r_2_), custom_call_target="tpu_custom_call" | custom-call | flops 1153500 | bytes 1 | tf_op jit(solution)/shard_map/settle_3/pallas_call | solution.py:78
  (180 shorter events, 102.9 us)
Async XLA Ops:
  61.8 41.3 %collective-permute-start.18 = (bf16[4,136,1024]{2,1,0:T(8,128)(2,1)S(1)}, bf16[4,136,1024]{2,1,0:T(8,128)(2,1)S(1)}, u32[]{:S(2)}, u32[]{:S(2)}) collective-permute-start(bf16[4,136,1024]{2,1,0:T(8,128)(2,1)S(1)} %get-tuple-element.251), channel_id=1, source_target_pairs={{0,8},{4,12},{8,0},{12,4},{16,24},{20,28},{24,16},{28,20},{1,9},{5... | collective-permute-start | bytes 3342344 | tf_op jit(solution)/shard_map/ppermute | solution.py:678
  67.2 36.2 %collective-permute-start.19 = (bf16[4,128,1024]{2,1,0:T(8,128)(2,1)S(1)}, bf16[4,128,1024]{2,1,0:T(8,128)(2,1)S(1)}, u32[]{:S(2)}, u32[]{:S(2)}) collective-permute-start(bf16[4,128,1024]{2,1,0:T(8,128)(2,1)S(1)} %get-tuple-element.254), channel_id=1, source_target_pairs={{0,4},{4,0},{8,12},{12,8},{16,20},{20,16},{24,28},{28,24},{1,5},{5... | collective-permute-start | bytes 3145736 | tf_op jit(solution)/shard_map/ppermute | solution.py:678
  82.4 13.9 %collective-permute-start.15 = (bf16[1,128,1024]{2,1,0:T(8,128)(2,1)S(1)}, bf16[1,128,1024]{2,1,0:T(8,128)(2,1)S(1)}, u32[]{:S(2)}, u32[]{:S(2)}) collective-permute-start(bf16[1,128,1024]{2,1,0:T(8,128)(2,1)S(1)} %get-tuple-element.244), channel_id=1, source_target_pairs={{0,1},{1,0},{2,3},{3,2},{4,5},{5,4},{6,7},{7,6},{8,9},{9,8},{10,11... | collective-permute-start | bytes 786440 | tf_op jit(solution)/shard_map/ppermute | solution.py:678
  88.7 14.4 %collective-permute-start.16 = (f32[2,128,256]{2,1,0:T(8,128)S(1)}, f32[2,128,256]{2,1,0:T(8,128)S(1)}, u32[]{:S(2)}, u32[]{:S(2)}) collective-permute-start(f32[2,128,256]{2,1,0:T(8,128)S(1)} %get-tuple-element.246), channel_id=1, source_target_pairs={{4,0},{8,4},{12,8},{16,12},{20,16},{24,20},{28,24},{5,1},{9,5},{13... | collective-permute-start | bytes 786440 | tf_op jit(solution)/shard_map/ppermute | solution.py:848
  103.3 18.1 %collective-permute-start.22 = (bf16[2,136,1024]{2,1,0:T(8,128)(2,1)S(1)}, bf16[2,136,1024]{2,1,0:T(8,128)(2,1)S(1)}, u32[]{:S(2)}, u32[]{:S(2)}) collective-permute-start(bf16[2,136,1024]{2,1,0:T(8,128)(2,1)S(1)} %get-tuple-element.274), channel_id=1, source_target_pairs={{0,4},{4,0},{8,12},{12,8},{16,20},{20,16},{24,28},{28,24},{1,5},{5... | collective-permute-start | bytes 1671176 | tf_op jit(solution)/shard_map/ppermute | solution.py:678
  103.6 17.7 %collective-permute-start.21 = (bf16[2,128,1024]{2,1,0:T(8,128)(2,1)S(1)}, bf16[2,128,1024]{2,1,0:T(8,128)(2,1)S(1)}, u32[]{:S(2)}, u32[]{:S(2)}) collective-permute-start(bf16[2,128,1024]{2,1,0:T(8,128)(2,1)S(1)} %get-tuple-element.271), channel_id=1, source_target_pairs={{0,8},{4,12},{8,0},{12,4},{16,24},{20,28},{24,16},{28,20},{1,9},{5... | collective-permute-start | bytes 1572872 | tf_op jit(solution)/shard_map/ppermute | solution.py:678
  105.2 15.4 %collective-permute-start.20 = (bf16[1,128,1024]{2,1,0:T(8,128)(2,1)S(1)}, bf16[1,128,1024]{2,1,0:T(8,128)(2,1)S(1)}, u32[]{:S(2)}, u32[]{:S(2)}) collective-permute-start(bf16[1,128,1024]{2,1,0:T(8,128)(2,1)S(1)} %get-tuple-element.267), channel_id=1, source_target_pairs={{0,2},{1,3},{2,0},{3,1},{4,6},{5,7},{6,4},{7,5},{8,10},{9,11},{10,... | collective-permute-start | bytes 786440 | tf_op jit(solution)/shard_map/ppermute | solution.py:678
  126.1 33.5 %collective-permute-start.28 = (bf16[4,96,1024]{2,1,0:T(8,128)(2,1)S(1)}, bf16[4,96,1024]{2,1,0:T(8,128)(2,1)S(1)}, u32[]{:S(2)}, u32[]{:S(2)}) collective-permute-start(bf16[4,96,1024]{2,1,0:T(8,128)(2,1)S(1)} %get-tuple-element.302), channel_id=1, source_target_pairs={{0,4},{4,0},{8,12},{12,8},{16,20},{20,16},{24,28},{28,24},{1,5},{5... | collective-permute-start | bytes 2359304 | tf_op jit(solution)/shard_map/ppermute | solution.py:678
  132.6 15.8 %collective-permute-start.29 = (bf16[1,128,1024]{2,1,0:T(8,128)(2,1)S(1)}, bf16[1,128,1024]{2,1,0:T(8,128)(2,1)S(1)}, u32[]{:S(2)}, u32[]{:S(2)}) collective-permute-start(bf16[1,128,1024]{2,1,0:T(8,128)(2,1)S(1)} %get-tuple-element.305), channel_id=1, source_target_pairs={{0,16},{4,20},{8,24},{12,28},{16,0},{20,4},{24,8},{28,12},{1,17},{... | collective-permute-start | bytes 786440 | tf_op jit(solution)/shard_map/ppermute | solution.py:678
  139.0 25.6 %collective-permute-start.34 = (bf16[4,72,1024]{2,1,0:T(8,128)(2,1)S(1)}, bf16[4,72,1024]{2,1,0:T(8,128)(2,1)S(1)}, u32[]{:S(2)}, u32[]{:S(2)}) collective-permute-start(bf16[4,72,1024]{2,1,0:T(8,128)(2,1)S(1)} %get-tuple-element.310), channel_id=1, source_target_pairs={{0,8},{4,12},{8,0},{12,4},{16,24},{20,28},{24,16},{28,20},{1,9},{5... | collective-permute-start | bytes 1769480 | tf_op jit(solution)/shard_map/ppermute | solution.py:678
  141.5 17.5 %collective-permute-start.30 = (bf16[1,136,1024]{2,1,0:T(8,128)(2,1)S(1)}, bf16[1,136,1024]{2,1,0:T(8,128)(2,1)S(1)}, u32[]{:S(2)}, u32[]{:S(2)}) collective-permute-start(bf16[1,136,1024]{2,1,0:T(8,128)(2,1)S(1)} %get-tuple-element.307), channel_id=1, source_target_pairs={{0,16},{4,20},{8,24},{12,28},{16,0},{20,4},{24,8},{28,12},{1,17},{... | collective-permute-start | bytes 835592 | tf_op jit(solution)/shard_map/ppermute | solution.py:678
  148.4 14.7 %collective-permute-start.33 = (bf16[128,1024]{1,0:T(8,128)(2,1)S(1)}, bf16[128,1024]{1,0:T(8,128)(2,1)S(1)}, u32[]{:S(2)}, u32[]{:S(2)}) collective-permute-start(bf16[128,1024]{1,0:T(8,128)(2,1)S(1)} %collective-permute-done.32.a2), channel_id=1, source_target_pairs={{0,1},{1,0},{2,3},{3,2},{4,5},{5,4},{6,7},{7,6},{8,9},{9,8},{10,11... | collective-permute-start | bytes 786440 | tf_op jit(solution)/shard_map/ppermute | solution.py:678
  159.7 33.2 %collective-permute-start.39 = (bf16[2,96,1024]{2,1,0:T(8,128)(2,1)S(1)}, bf16[2,96,1024]{2,1,0:T(8,128)(2,1)S(1)}, u32[]{:S(2)}, u32[]{:S(2)}) collective-permute-start(bf16[2,96,1024]{2,1,0:T(8,128)(2,1)S(1)} %get-tuple-element.315), channel_id=1, source_target_pairs={{0,8},{4,12},{8,0},{12,4},{16,24},{20,28},{24,16},{28,20},{1,9},{5... | collective-permute-start | bytes 1179656 | tf_op jit(solution)/shard_map/ppermute | solution.py:678
  164.7 28.4 %collective-permute-start.40 = (bf16[2,72,1024]{2,1,0:T(8,128)(2,1)S(1)}, bf16[2,72,1024]{2,1,0:T(8,128)(2,1)S(1)}, u32[]{:S(2)}, u32[]{:S(2)}) collective-permute-start(bf16[2,72,1024]{2,1,0:T(8,128)(2,1)S(1)} %get-tuple-element.318), channel_id=1, source_target_pairs={{0,4},{4,0},{8,12},{12,8},{16,20},{20,16},{24,28},{28,24},{1,5},{5... | collective-permute-start | bytes 884744 | tf_op jit(solution)/shard_map/ppermute | solution.py:678
  166.2 26.9 %collective-permute-start.41 = (bf16[1,136,1024]{2,1,0:T(8,128)(2,1)S(1)}, bf16[1,136,1024]{2,1,0:T(8,128)(2,1)S(1)}, u32[]{:S(2)}, u32[]{:S(2)}) collective-permute-start(bf16[1,136,1024]{2,1,0:T(8,128)(2,1)S(1)} %f2_last.1.a), channel_id=1, source_target_pairs={{0,16},{4,20},{8,24},{12,28},{16,0},{20,4},{24,8},{28,12},{1,17},{... | collective-permute-start | bytes 835592 | tf_op jit(solution)/shard_map/ppermute | solution.py:678
  168.3 24.6 %collective-permute-start.38 = (bf16[1,128,1024]{2,1,0:T(8,128)(2,1)S(1)}, bf16[1,128,1024]{2,1,0:T(8,128)(2,1)S(1)}, u32[]{:S(2)}, u32[]{:S(2)}) collective-permute-start(bf16[1,128,1024]{2,1,0:T(8,128)(2,1)S(1)} %f1_last.1.a), channel_id=1, source_target_pairs={{0,16},{4,20},{8,24},{12,28},{16,0},{20,4},{24,8},{28,12},{1,17},{... | collective-permute-start | bytes 786440 | tf_op jit(solution)/shard_map/ppermute | solution.py:678
  193.8 21.1 %collective-permute-start.44 = (bf16[2,128,1024]{2,1,0:T(8,128)(2,1)S(1)}, bf16[2,128,1024]{2,1,0:T(8,128)(2,1)S(1)}, u32[]{:S(2)}, u32[]{:S(2)}) collective-permute-start(bf16[2,128,1024]{2,1,0:T(8,128)(2,1)S(1)} %f1_pack.2.a), channel_id=1, source_target_pairs={{0,8},{4,12},{8,0},{12,4},{16,24},{20,28},{24,16},{28,20},{1,9},{5... | collective-permute-start | bytes 1572872 | tf_op jit(solution)/shard_map/ppermute | solution.py:678
  193.8 16.6 %collective-permute-start.43 = (bf16[1,96,1024]{2,1,0:T(8,128)(2,1)S(1)}, bf16[1,96,1024]{2,1,0:T(8,128)(2,1)S(1)}, u32[]{:S(2)}, u32[]{:S(2)}) collective-permute-start(bf16[1,96,1024]{2,1,0:T(8,128)(2,1)S(1)} %get-tuple-element.323), channel_id=1, source_target_pairs={{0,16},{4,20},{8,24},{12,28},{16,0},{20,4},{24,8},{28,12},{1,17},{... | collective-permute-start | bytes 589832 | tf_op jit(solution)/shard_map/ppermute | solution.py:678
  196.2 18.7 %collective-permute-start.45 = (bf16[1,72,1024]{2,1,0:T(8,128)(2,1)S(1)}, bf16[1,72,1024]{2,1,0:T(8,128)(2,1)S(1)}, u32[]{:S(2)}, u32[]{:S(2)}) collective-permute-start(bf16[1,72,1024]{2,1,0:T(8,128)(2,1)S(1)} %get-tuple-element.326), channel_id=1, source_target_pairs={{0,16},{4,20},{8,24},{12,28},{16,0},{20,4},{24,8},{28,12},{1,17},{... | collective-permute-start | bytes 442376 | tf_op jit(solution)/shard_map/ppermute | solution.py:678
  217.0 40.0 %collective-permute-start.51 = (bf16[4,136,1024]{2,1,0:T(8,128)(2,1)S(1)}, bf16[4,136,1024]{2,1,0:T(8,128)(2,1)S(1)}, u32[]{:S(2)}, u32[]{:S(2)}) collective-permute-start(bf16[4,136,1024]{2,1,0:T(8,128)(2,1)S(1)} %f2_pack.3.r_3_.r_1_), channel_id=1, source_target_pairs={{0,8},{4,12},{8,0},{12,4},{16,24},{20,28},{24,16},{28,20},{1,9},{5... | collective-permute-start | bytes 3342344 | tf_op jit(solution)/shard_map/ppermute | solution.py:678
  217.0 40.0 %collective-permute-start.50 = (bf16[4,128,1024]{2,1,0:T(8,128)(2,1)S(1)}, bf16[4,128,1024]{2,1,0:T(8,128)(2,1)}, u32[]{:S(2)}, u32[]{:S(2)}) collective-permute-start(bf16[4,128,1024]{2,1,0:T(8,128)(2,1)S(1)} %f1_pack.3.r_1_), channel_id=1, source_target_pairs={{0,4},{4,0},{8,12},{12,8},{16,20},{20,16},{24,28},{28,24},{1,5},{5... | collective-permute-start | bytes 3145736 | tf_op jit(solution)/shard_map/ppermute | solution.py:678
  222.3 29.0 %collective-permute-start.48 = (bf16[2,96,1024]{2,1,0:T(8,128)(2,1)S(1)}, bf16[2,96,1024]{2,1,0:T(8,128)(2,1)S(1)}, u32[]{:S(2)}, u32[]{:S(2)}) collective-permute-start(bf16[2,96,1024]{2,1,0:T(8,128)(2,1)S(1)} %f3_pack.2.a), channel_id=1, source_target_pairs={{0,16},{4,20},{8,24},{12,28},{16,0},{20,4},{24,8},{28,12},{1,17},{... | collective-permute-start | bytes 1179656 | tf_op jit(solution)/shard_map/ppermute | solution.py:678
  224.8 27.4 %collective-permute-start.49 = (bf16[2,72,1024]{2,1,0:T(8,128)(2,1)S(1)}, bf16[2,72,1024]{2,1,0:T(8,128)(2,1)S(1)}, u32[]{:S(2)}, u32[]{:S(2)}) collective-permute-start(bf16[2,72,1024]{2,1,0:T(8,128)(2,1)S(1)} %f4_pack.2.a), channel_id=1, source_target_pairs={{0,4},{4,0},{8,12},{12,8},{16,20},{20,16},{24,28},{28,24},{1,5},{5... | collective-permute-start | bytes 884744 | tf_op jit(solution)/shard_map/ppermute | solution.py:678
  255.5 16.5 %collective-permute-start.53 = (bf16[4,96,1024]{2,1,0:T(8,128)(2,1)}, bf16[4,96,1024]{2,1,0:T(8,128)(2,1)}, u32[]{:S(2)}, u32[]{:S(2)}) collective-permute-start(bf16[4,96,1024]{2,1,0:T(8,128)(2,1)} %f3_pack.3.r_1_), channel_id=1, source_target_pairs={{0,4},{4,0},{8,12},{12,8},{16,20},{20,16},{24,28},{28,24},{1,5},{5... | collective-permute-start | bytes 2359304 | tf_op jit(solution)/shard_map/ppermute | solution.py:678
  (50 other events, 319.0 us)

commit v5 on v4

--- a/solution.py
+++ b/solution.py
@@ -48,7 +48,7 @@
 
 
 COST = 1153500
-STEPS = {'hops': ['f2', 'f1'], 'back': [], 'taps': ['f1', 'f2'], 'hid': [], 'x': [], 'tail': ['f3', 'f1', 'f2', 'in', 'f4', 'out', 'f1', 'f3', 'f4', 'f2', 'f2', 'f3', 'f1', 'f4', 'f4', 'f3', 'f3', 'f4', 's1', 's2', 's4', 's3']}
+STEPS = {'hops': ['f2', 'f1'], 'back': ['f1', 'f2'], 'taps': ['f2'], 'hid': [], 'x': ['f1'], 'tail': ['f3', 'in', 'f4', 'out', 'f1', 'f3', 'f4', 'f2', 'f2', 'f3', 'f1', 'f4', 'f4', 'f3', 'f3', 'f4', 's1', 's2', 's4', 's3']}
 WAYS = {'f1': ((0, 1, 2), (2, 1, 0)), 'f2': ((1, 0, 2), (2, 0, 1)), 'f3': ((0, 1, 2), (1, 2, 0)), 'f4': ((1, 0, 2), (2, 0, 1))}
 
 
@@ -87,7 +87,8 @@
             compiler_params=pltpu.CompilerParams(vmem_limit_bytes=vmem << 20),
             cost_estimate=pl.CostEstimate(flops=flops, bytes_accessed=1, transcendentals=0),
         )(*args)
-        self.last = next(o for i, o in enumerate(made) if i not in smem_out and i not in hbm_out)
+        kept = [i for i in range(len(made)) if i not in smem_out]
+        self.last = made[min(kept, key=lambda i: (i in hbm_out, i))]
         return made
 
 
@@ -313,9 +314,9 @@
 
 
 def fold_hops(hops, h):
-    state = hops[-1][h]
+    state = hops[-1][h].astype(f32)
     for hop in hops[-2::-1]:
-        state = hop[h, :, DH:] + fdot(hop[h, :, :DH], state)
+        state = hop[h, :, DH:].astype(f32) + fdot(hop[h, :, :DH].astype(f32), state)
     return state
 
 
@@ -444,7 +445,7 @@
     branch[...] = total.astype(bf16)
 
 
-def flow_kernel(tp, meta, b0, b1, b2, b3, wo, heads_out, gate, nh, qeff, amap, branch, dgate, dout, rst, dev, last, nh_part, flows):
+def flow_kernel(tp, meta, b0, b1, b2, b3, wo, heads_out, gate, nh, qeff, amap, branch, dgate, dout, rst, dev_low, last, nh_part, flows, dev):
     share = b0.shape[0]
     heads = gate.shape[1] // DH
     groups = gate.shape[0] // GROUP
@@ -497,7 +498,8 @@
         return 0
 
     lax.fori_loop(0, groups, chain, 0)
-    last[...] = dev[:, :, DH:]
+    dev_low[...] = dev[...].astype(bf16)
+    last[...] = dev[:, :, DH:].astype(bf16)
 
 
 def side_kernel(qkv, dout, vnew, states, score, ndo, dq, dk):
@@ -733,17 +735,19 @@
                     keep[at, rows, lanes] = block
 
 
-def take(out, place, part, bits, near, far):
+def take(out, place, part, bits, near, far, send=None):
     height = part.size // part.folds
     wide = out.shape[1]
     for m in range(1 << len(bits)):
         source = far if (m >> bits[-1]) & 1 else near
         at = rank_of(m, bits[-2::-1])
+        start = part.start + (m ^ place) * part.size
         for i in range(part.folds):
-            begin = part.start + (m ^ place) * part.size + i * height
-            out[pl.ds(pl.multiple_of(begin, 8), height)] = source[
+            out[pl.ds(pl.multiple_of(start + i * height, 8), height)] = source[
                 at, part.base : part.base + height, i * wide : (i + 1) * wide
             ].astype(f32)
+        if send is not None:
+            send(pl.ds(pl.multiple_of(start, 8), part.size))
 
 
 class Sum:
@@ -819,10 +823,26 @@
 
 
 def settle_kernel(count, jobs, line_at, place, *refs):
-    pairs, outs = refs[: 2 * count], refs[2 * count :]
-    for parts, out in zip(jobs, outs):
+    pairs, refs = refs[: 2 * count], refs[2 * count :]
+    size = len(jobs)
+    outs, (staged, sem) = refs[: len(refs) - size - 1], (refs[len(refs) - size - 1 : -1], refs[-1])
+    copies = []
+    for parts, out, stage in zip(jobs, outs, staged):
+
+        def send(rows):
+            copy = pltpu.make_async_copy(stage.at[rows], out.at[rows], sem.at[len(copies)])
+            copy.start()
+            copies.append(copy)
+
         for part, way in parts:
-            take(out, (place[0] & 7), part, way, *pairs[2 * part.index : 2 * part.index + 2])
+            take(
+                stage,
+                (place[0] & 7),
+                part,
+                way,
+                *pairs[2 * part.index : 2 * part.index + 2],
+                send,
+            )
     if line_at is not None:
         index, way, base = line_at
         near, far = pairs[2 * index : 2 * index + 2]
@@ -830,6 +850,8 @@
             source = far if (m >> way[-1]) & 1 else near
             at = rank_of(m, way[-2::-1])
             outs[-1][pl.ds(m ^ (place[0] & 7), 1)] = source[at, base : base + 8].astype(f32)[:1]
+    for copy in copies:
+        copy.wait()
 
 
 def sum_shapes(blocks, rows, cols):
@@ -1079,12 +1101,12 @@
             (wide, bf16),
             (wide, f32),
             (zst_shape, f32),
-            *dev_shapes,
+            *[(shape, bf16) for shape, _ in dev_shapes],
             ((1, DH), f32),
         ],
         [tp, meta, *branch_all, w_out, heads_out, gate_raw, norm_head, qeff, amap],
         smem=(0, 1),
-        scratch=[pltpu.VMEM(map_shape, f32)],
+        scratch=[pltpu.VMEM(map_shape, f32), pltpu.VMEM(dev_shapes[0][0], f32)],
     )
     hops = hops_of(dev, last, -1, reach)
     down_near_b = swap(down_send_b, 1)
@@ -1190,9 +1212,13 @@
         return run(
             lambda *r: settle_kernel(len(used), jobs, line_at, *r),
             name,
-            [(o, f32) for o in outs],
+            [(o, f32, far) for o in outs[: len(jobs)]] + [(o, f32) for o in outs[len(jobs) :]],
             [place, *[a for flow in used for a in (flows[flow].own, flows[flow].got)]],
             smem=(0,),
+            scratch=[
+                *[pltpu.VMEM(o, f32) for o in outs[: len(jobs)]],
+                pltpu.SemaphoreType.DMA((blocks * sum(len(parts) for parts in jobs),)),
+            ],
         )
 
     def wayed(parts, first_flow=0):

time: 276 us -> 272 us (0.986)
    ppermute x6, waiting for transfers between devices: 8.83 us -> 2.67 us  [shift(): return lax.ppermute(value, 'seq', pairs)]
    ppermute x48, waiting for transfers between devices: 111 us -> 116 us  [swap(): return lax.ppermute(value, axis, [(i, i ^ bit) for i in range(count)])]
  transfers between devices with their start and end apart: 54 -> 54, of which waited for: 25 -> 23; matrix products, arithmetic and copies ran while one was open for 1% -> 1% of each run, Pallas kernels for 21% -> 21%
where the time goes in v5:
time: 272 us
  waiting for transfers between devices  119 us (44%)
  Pallas kernels  80 us (29%)
  starting transfers between devices  68.6 us (25%)
  local copies, waits for them, and re-layouts  3.3 us (1%)
    ppermute x48, waiting for transfers between devices, swap(): return lax.ppermute(value, axis, [(i, i ^ bit) for i in range(count)])  116 us
    pallas_call x51, Pallas kernels, run(): pl.pallas_call(kernel, name=name, out_shape=shapes, in_specs=[pl.BlockSpe...  80 us
    ppermute x48, starting transfers between devices, swap(): return lax.ppermute(value, axis, [(i, i ^ bit) for i in range(count)])  52.2 us
    ppermute x6, starting transfers between devices, shift(): return lax.ppermute(value, 'seq', pairs)  16.4 us
  transfers between devices with their start and end apart: 54, of which 23 were waited for; matrix products, arithmetic and copies ran while one was open for 1% of the time, Pallas kernels for 21%

profile of v5, /device:TPU:0, one launch (start us, length us, event | category | flops | bytes accessed | tf_op | source)
XLA Modules:
  0.0 272.0 jit_solution(7306310660282677514)
XLA Ops:
  1.4 4.9 %collective-permute-start = (bf16[16,1024]{1,0:T(8,128)(2,1)S(1)}, bf16[16,1024]{1,0:T(8,128)(2,1)S(1)}, u32[]{:S(2)}, u32[]{:S(2)}) collective-permute-start(bf16[16,1024]{1,0:T(8,128)(2,1)S(1)} %slice.15), channel_id=1, source_target_pairs={{0,4},{4,8},{8,12},{12,16},{16,20},{20,24},{24,28},{1,5},{5,9},{9,... | collective-permute-start | bytes 98312 | tf_op jit(solution)/shard_map/ppermute | solution.py:870
  7.9 15.1 %front.1 = (f32[512,256]{1,0:T(8,128)S(1)}, f32[512,2]{1,0:T(8,128)S(1)}, s32[2,8]{1,0:T(2,128)S(1)}, f32[512,768]{1,0:T(8,128)S(1)}, f32[512,256]{1,0:T(8,128)S...) custom-call(s32[1]{0:T(128)} %bitcast.1.first.r_1_.r_0_, ...), custom_call_target="tpu_custom_call" | custom-call | flops 1153500 | bytes 1 | tf_op jit(solution)/shard_map/front/pallas_call | solution.py:78
  23.0 4.2 %collective-permute-start.1 = (f32[2,128,256]{2,1,0:T(8,128)S(1)}, f32[2,128,256]{2,1,0:T(8,128)S(1)}, u32[]{:S(2)}, u32[]{:S(2)}) collective-permute-start(f32[2,128,256]{2,1,0:T(8,128)S(1)} %get-tuple-element.183), channel_id=1, source_target_pairs={{0,4},{4,8},{8,12},{12,16},{16,20},{20,24},{24,28},{1,5},{5,9},{9,... | collective-permute-start | bytes 786440 | tf_op jit(solution)/shard_map/ppermute | solution.py:870
  27.2 3.5 %collective-permute-start.2 = (f32[2,128,128]{2,1,0:T(8,128)S(1)}, f32[2,128,128]{2,1,0:T(8,128)S(1)}, u32[]{:S(2)}, u32[]{:S(2)}) collective-permute-start(f32[2,128,128]{2,1,0:T(8,128)S(1)} %get-tuple-element.193), channel_id=1, source_target_pairs={{0,8},{4,12},{8,16},{12,20},{16,24},{20,28},{1,9},{5,13},{9,17},{1... | collective-permute-start | bytes 393224 | tf_op jit(solution)/shard_map/ppermute | solution.py:870
  38.9 3.8 %states.1 = (f32[16,128,128]{2,1,0:T(8,128)S(1)}, f32[512,256]{1,0:T(8,128)S(1)}, f32[512,256]{1,0:T(8,128)S(1)}) custom-call(f32[2,128,128]{2,1,0:T(8,128)S(1)} %get-tuple-element.201.entry, f32[16,128,256]{2,1,0:T(8,128)S(1)} %get-tuple-element.190.zst, f32[512,768]{1,0:T(8,128)S(1)} %get-tuple-element.239.qkv.r_4_, ...), custom_call_target="tpu_custom_call" | custom-call | flops 1153500 | bytes 1 | tf_op jit(solution)/shard_map/states/pallas_call | solution.py:78
  56.3 5.2 %ffn_b.1 = (f32[1,128,1024]{2,1,0:T(8,128)S(1)}, bf16[1,128,1024]{2,1,0:T(8,128)(2,1)S(1)}, f32[1,128,1024]{2,1,0:T(8,128)S(1)}, bf16[1,128,1024]{2,1,0:T(8,128)...) custom-call(s32[1]{0:T(128)} %bitcast.tp.r_0_, ...), custom_call_target="tpu_custom_call" | custom-call | flops 1153500 | bytes 1 | tf_op jit(solution)/shard_map/ffn_b/pallas_call | solution.py:78
  61.8 3.7 %collective-permute-start.18 = (bf16[4,136,1024]{2,1,0:T(8,128)(2,1)S(1)}, bf16[4,136,1024]{2,1,0:T(8,128)(2,1)S(1)}, u32[]{:S(2)}, u32[]{:S(2)}) collective-permute-start(bf16[4,136,1024]{2,1,0:T(8,128)(2,1)S(1)} %get-tuple-element.252), channel_id=1, source_target_pairs={{0,8},{4,12},{8,0},{12,4},{16,24},{20,28},{24,16},{28,20},{1,9},{5... | collective-permute-start | bytes 3342344 | tf_op jit(solution)/shard_map/ppermute | solution.py:680
  69.2 6.5 %collective-permute-done.10 = bf16[1,128,1024]{2,1,0:T(8,128)(2,1)S(1)} collective-permute-done((bf16[1,128,1024]{2,1,0:T(8,128)(2,1)S(1)}, bf16[1,128,1024]{2,1,0:T(8,128)(2,1)S(1)}, u32[]{:S(2)}, u32[]{:S(2)}) %collective-permute-start.10) | collective-permute-done | bytes 262176 | tf_op jit(solution)/shard_map/ppermute | solution.py:680
  77.6 5.6 %collective-permute-done.12.b2 = bf16[128,1024]{1,0:T(8,128)(2,1)S(1)} collective-permute-done((bf16[128,1024]{1,0:T(8,128)(2,1)S(1)}, bf16[128,1024]{1,0:T(8,128)(2,1)S(1)}, u32[]{:S(2)}, u32[]{:S(2)}) %collective-permute-start.12) | collective-permute-done | bytes 262176 | tf_op jit(solution)/shard_map/ppermute | solution.py:680
  84.7 5.2 %flow.1 = (bf16[512,1024]{1,0:T(8,128)(2,1)S(1)}, bf16[512,256]{1,0:T(8,128)(2,1)S(1)}, f32[512,256]{1,0:T(8,128)S(1)}, f32[16,128,256]{2,1,0:T(8,128)S(1)}, bf1...) custom-call(s32[1]{0:T(128)} %bitcast.tp.r_0_, ...), custom_call_target="tpu_custom_call" | custom-call | flops 1153500 | bytes 1 | tf_op jit(solution)/shard_map/flow/pallas_call | solution.py:78
  92.5 5.0 %side.1 = (f32[512,256]{1,0:T(8,128)S(1)}, f32[512,256]{1,0:T(8,128)S(1)}, f32[512,256]{1,0:T(8,128)S(1)}) custom-call(f32[512,768]{1,0:T(8,128)S(1)} %get-tuple-element.239.qkv.r_4_, f32[512,256]{1,0:T(8,128)S(1)} %get-tuple-element.240.dout, f32[512,256]{1,0:T(8,128)S(1)} %get-tuple-element.241.vnew.r_12_, ...), custom_call_target="tpu_custom_call" | custom-call | flops 1153500 | bytes 1 | tf_op jit(solution)/shard_map/side/pallas_call | solution.py:78
  103.5 9.6 %back.1 = (f32[520,768]{1,0:T(8,128)S(1)}, f32[8,768]{1,0:T(8,128)S(1)}, bf16[512,128]{1,0:T(8,128)(2,1)S(1)}) custom-call(s32[2,8]{1,0:T(2,128)S(1)} %get-tuple-element.181.meta.r_0_, bf16[2,128,256]{2,1,0:T(8,128)(2,1)S(1)} %collective-permute-done.16.r_1_, bf16[2,128,128]{2,1,0:T(8,128)(2,1)S(1)} %collective-permute-done.17.r_2_, ...), custom_call_target="tpu_custom_call" | custom-call | flops 1153500 | bytes 1 | tf_op jit(solution)/shard_map/back/pallas_call | solution.py:78
  125.1 4.5 %collective-permute-done.23.got = bf16[1,136,1024]{2,1,0:T(8,128)(2,1)S(1)} collective-permute-done((bf16[1,136,1024]{2,1,0:T(8,128)(2,1)S(1)}, bf16[1,136,1024]{2,1,0:T(8,128)(2,1)S(1)}, u32[]{:S(2)}, u32[]{:S(2)}) %collective-permute-start.23) | collective-permute-done | bytes 278560 | tf_op jit(solution)/shard_map/ppermute | solution.py:680
  137.2 11.1 %collective-permute-done.27.got = bf16[1,128,1024]{2,1,0:T(8,128)(2,1)S(1)} collective-permute-done((bf16[1,128,1024]{2,1,0:T(8,128)(2,1)S(1)}, bf16[1,128,1024]{2,1,0:T(8,128)(2,1)S(1)}, u32[]{:S(2)}, u32[]{:S(2)}) %collective-permute-start.27) | collective-permute-done | bytes 262176 | tf_op jit(solution)/shard_map/ppermute | solution.py:680
  151.3 6.1 %collective-permute-done.32.a2 = bf16[128,1024]{1,0:T(8,128)(2,1)S(1)} collective-permute-done((bf16[128,1024]{1,0:T(8,128)(2,1)S(1)}, bf16[128,1024]{1,0:T(8,128)(2,1)S(1)}, u32[]{:S(2)}, u32[]{:S(2)}) %collective-permute-start.32) | collective-permute-done | bytes 262176 | tf_op jit(solution)/shard_map/ppermute | solution.py:680
  162.5 3.5 %collective-permute-done.34.got = bf16[4,72,1024]{2,1,0:T(8,128)(2,1)S(1)} collective-permute-done((bf16[4,72,1024]{2,1,0:T(8,128)(2,1)S(1)}, bf16[4,72,1024]{2,1,0:T(8,128)(2,1)S(1)}, u32[]{:S(2)}, u32[]{:S(2)}) %collective-permute-start.34) | collective-permute-done | bytes 589856 | tf_op jit(solution)/shard_map/ppermute | solution.py:680
  171.7 20.4 %collective-permute-done.38.b = bf16[1,128,1024]{2,1,0:T(8,128)(2,1)S(1)} collective-permute-done((bf16[1,128,1024]{2,1,0:T(8,128)(2,1)S(1)}, bf16[1,128,1024]{2,1,0:T(8,128)(2,1)S(1)}, u32[]{:S(2)}, u32[]{:S(2)}) %collective-permute-start.38) | collective-permute-done | bytes 262176 | tf_op jit(solution)/shard_map/ppermute | solution.py:680
  196.0 8.0 %collective-permute-done.42.b = bf16[2,136,1024]{2,1,0:T(8,128)(2,1)S(1)} collective-permute-done((bf16[2,136,1024]{2,1,0:T(8,128)(2,1)S(1)}, bf16[2,136,1024]{2,1,0:T(8,128)(2,1)S(1)}, u32[]{:S(2)}, u32[]{:S(2)}) %collective-permute-start.42) | collective-permute-done | bytes 557088 | tf_op jit(solution)/shard_map/ppermute | solution.py:680
  204.0 5.2 %collective-permute-done.43.got = bf16[1,96,1024]{2,1,0:T(8,128)(2,1)S(1)} collective-permute-done((bf16[1,96,1024]{2,1,0:T(8,128)(2,1)S(1)}, bf16[1,96,1024]{2,1,0:T(8,128)(2,1)S(1)}, u32[]{:S(2)}, u32[]{:S(2)}) %collective-permute-start.43) | collective-permute-done | bytes 196640 | tf_op jit(solution)/shard_map/ppermute | solution.py:680
  216.4 4.2 %collective-permute-done.46.b = bf16[1,72,1024]{2,1,0:T(8,128)(2,1)S(1)} collective-permute-done((bf16[1,72,1024]{2,1,0:T(8,128)(2,1)S(1)}, bf16[1,72,1024]{2,1,0:T(8,128)(2,1)S(1)}, u32[]{:S(2)}, u32[]{:S(2)}) %collective-permute-start.46) | collective-permute-done | bytes 147488 | tf_op jit(solution)/shard_map/ppermute | solution.py:680
  225.6 22.8 %collective-permute-done.48.b = bf16[2,96,1024]{2,1,0:T(8,128)(2,1)S(1)} collective-permute-done((bf16[2,96,1024]{2,1,0:T(8,128)(2,1)S(1)}, bf16[2,96,1024]{2,1,0:T(8,128)(2,1)S(1)}, u32[]{:S(2)}, u32[]{:S(2)}) %collective-permute-start.48) | collective-permute-done | bytes 393248 | tf_op jit(solution)/shard_map/ppermute | solution.py:680
  254.6 3.9 %settle_1.1 = (f32[704,1024]{1,0:T(8,128)}, f32[704,1024]{1,0:T(8,128)}) custom-call(s32[1]{0:T(128)} %bitcast.1.first.r_1_.r_0_, bf16[4,128,1024]{2,1,0:T(8,128)(2,1)S(1)} %f1_pack.3.r_1_, bf16[4,128,1024]{2,1,0:T(8,128)(2,1)} %collective-permute-done.50.r_2_, bf16[4,136,1024]{2,1,0:T(8,128)(2,1)S(1)} %f2_pack.3.r_3_.r_1_, ...), custom_call_target="tpu_custom_call" | custom-call | flops 1153500 | bytes 1 | tf_op jit(solution)/shard_map/settle_1/pallas_call | solution.py:78
  260.3 3.1 %collective-permute-done.52.r_2_ = bf16[4,72,1024]{2,1,0:T(8,128)(2,1)} collective-permute-done((bf16[4,72,1024]{2,1,0:T(8,128)(2,1)}, bf16[4,72,1024]{2,1,0:T(8,128)(2,1)}, u32[]{:S(2)}, u32[]{:S(2)}) %collective-permute-start.52) | collective-permute-done | bytes 589856 | tf_op jit(solution)/shard_map/ppermute | solution.py:680
  268.5 3.3 %settle_3.1 = (f32[1024,256]{1,0:T(8,128)}, f32[1024,256]{1,0:T(8,128)}, f32[1024,256]{1,0:T(8,128)}) custom-call(s32[1]{0:T(128)} %bitcast.1.first.r_1_.r_0_, bf16[4,96,1024]{2,1,0:T(8,128)(2,1)} %f3_pack.3.r_1_, bf16[4,96,1024]{2,1,0:T(8,128)(2,1)} %collective-permute-done.53.r_2_), custom_call_target="tpu_custom_call" | custom-call | flops 1153500 | bytes 1 | tf_op jit(solution)/shard_map/settle_3/pallas_call | solution.py:78
  (180 shorter events, 101.9 us)
Async XLA Ops:
  61.8 37.0 %collective-permute-start.18 = (bf16[4,136,1024]{2,1,0:T(8,128)(2,1)S(1)}, bf16[4,136,1024]{2,1,0:T(8,128)(2,1)S(1)}, u32[]{:S(2)}, u32[]{:S(2)}) collective-permute-start(bf16[4,136,1024]{2,1,0:T(8,128)(2,1)S(1)} %get-tuple-element.252), channel_id=1, source_target_pairs={{0,8},{4,12},{8,0},{12,4},{16,24},{20,28},{24,16},{28,20},{1,9},{5... | collective-permute-start | bytes 3342344 | tf_op jit(solution)/shard_map/ppermute | solution.py:680
  65.5 35.1 %collective-permute-start.19 = (bf16[4,128,1024]{2,1,0:T(8,128)(2,1)S(1)}, bf16[4,128,1024]{2,1,0:T(8,128)(2,1)S(1)}, u32[]{:S(2)}, u32[]{:S(2)}) collective-permute-start(bf16[4,128,1024]{2,1,0:T(8,128)(2,1)S(1)} %get-tuple-element.255), channel_id=1, source_target_pairs={{0,4},{4,0},{8,12},{12,8},{16,20},{20,16},{24,28},{28,24},{1,5},{5... | collective-permute-start | bytes 3145736 | tf_op jit(solution)/shard_map/ppermute | solution.py:680
  83.7 13.8 %collective-permute-start.15 = (bf16[1,128,1024]{2,1,0:T(8,128)(2,1)S(1)}, bf16[1,128,1024]{2,1,0:T(8,128)(2,1)S(1)}, u32[]{:S(2)}, u32[]{:S(2)}) collective-permute-start(bf16[1,128,1024]{2,1,0:T(8,128)(2,1)S(1)} %get-tuple-element.245), channel_id=1, source_target_pairs={{0,1},{1,0},{2,3},{3,2},{4,5},{5,4},{6,7},{7,6},{8,9},{9,8},{10,11... | collective-permute-start | bytes 786440 | tf_op jit(solution)/shard_map/ppermute | solution.py:680
  98.9 16.1 %collective-permute-start.21 = (bf16[2,136,1024]{2,1,0:T(8,128)(2,1)S(1)}, bf16[2,136,1024]{2,1,0:T(8,128)(2,1)S(1)}, u32[]{:S(2)}, u32[]{:S(2)}) collective-permute-start(bf16[2,136,1024]{2,1,0:T(8,128)(2,1)S(1)} %get-tuple-element.269), channel_id=1, source_target_pairs={{0,4},{4,0},{8,12},{12,8},{16,20},{20,16},{24,28},{28,24},{1,5},{5... | collective-permute-start | bytes 1671176 | tf_op jit(solution)/shard_map/ppermute | solution.py:680
  100.8 14.1 %collective-permute-start.20 = (bf16[2,128,1024]{2,1,0:T(8,128)(2,1)S(1)}, bf16[2,128,1024]{2,1,0:T(8,128)(2,1)S(1)}, u32[]{:S(2)}, u32[]{:S(2)}) collective-permute-start(bf16[2,128,1024]{2,1,0:T(8,128)(2,1)S(1)} %get-tuple-element.266), channel_id=1, source_target_pairs={{0,8},{4,12},{8,0},{12,4},{16,24},{20,28},{24,16},{28,20},{1,9},{5... | collective-permute-start | bytes 1572872 | tf_op jit(solution)/shard_map/ppermute | solution.py:680
  115.1 14.5 %collective-permute-start.23 = (bf16[1,136,1024]{2,1,0:T(8,128)(2,1)S(1)}, bf16[1,136,1024]{2,1,0:T(8,128)(2,1)S(1)}, u32[]{:S(2)}, u32[]{:S(2)}) collective-permute-start(bf16[1,136,1024]{2,1,0:T(8,128)(2,1)S(1)} %get-tuple-element.279), channel_id=1, source_target_pairs={{0,16},{4,20},{8,24},{12,28},{16,0},{20,4},{24,8},{28,12},{1,17},{... | collective-permute-start | bytes 835592 | tf_op jit(solution)/shard_map/ppermute | solution.py:680
  132.8 26.1 %collective-permute-start.30 = (bf16[4,96,1024]{2,1,0:T(8,128)(2,1)S(1)}, bf16[4,96,1024]{2,1,0:T(8,128)(2,1)S(1)}, u32[]{:S(2)}, u32[]{:S(2)}) collective-permute-start(bf16[4,96,1024]{2,1,0:T(8,128)(2,1)S(1)} %get-tuple-element.308), channel_id=1, source_target_pairs={{0,4},{4,0},{8,12},{12,8},{16,20},{20,16},{24,28},{28,24},{1,5},{5... | collective-permute-start | bytes 2359304 | tf_op jit(solution)/shard_map/ppermute | solution.py:680
  133.4 14.9 %collective-permute-start.27 = (bf16[1,128,1024]{2,1,0:T(8,128)(2,1)S(1)}, bf16[1,128,1024]{2,1,0:T(8,128)(2,1)S(1)}, u32[]{:S(2)}, u32[]{:S(2)}) collective-permute-start(bf16[1,128,1024]{2,1,0:T(8,128)(2,1)S(1)} %get-tuple-element.301), channel_id=1, source_target_pairs={{0,16},{4,20},{8,24},{12,28},{16,0},{20,4},{24,8},{28,12},{1,17},{... | collective-permute-start | bytes 786440 | tf_op jit(solution)/shard_map/ppermute | solution.py:680
  133.5 14.9 %collective-permute-start.28 = (bf16[1,128,1024]{2,1,0:T(8,128)(2,1)S(1)}, bf16[1,128,1024]{2,1,0:T(8,128)(2,1)S(1)}, u32[]{:S(2)}, u32[]{:S(2)}) collective-permute-start(bf16[1,128,1024]{2,1,0:T(8,128)(2,1)S(1)} %get-tuple-element.303), channel_id=1, source_target_pairs={{0,2},{1,3},{2,0},{3,1},{4,6},{5,7},{6,4},{7,5},{8,10},{9,11},{10,... | collective-permute-start | bytes 786440 | tf_op jit(solution)/shard_map/ppermute | solution.py:680
  149.7 16.3 %collective-permute-start.34 = (bf16[4,72,1024]{2,1,0:T(8,128)(2,1)S(1)}, bf16[4,72,1024]{2,1,0:T(8,128)(2,1)S(1)}, u32[]{:S(2)}, u32[]{:S(2)}) collective-permute-start(bf16[4,72,1024]{2,1,0:T(8,128)(2,1)S(1)} %get-tuple-element.312), channel_id=1, source_target_pairs={{0,8},{4,12},{8,0},{12,4},{16,24},{20,28},{24,16},{28,20},{1,9},{5... | collective-permute-start | bytes 1769480 | tf_op jit(solution)/shard_map/ppermute | solution.py:680
  159.3 32.8 %collective-permute-start.39 = (bf16[2,96,1024]{2,1,0:T(8,128)(2,1)S(1)}, bf16[2,96,1024]{2,1,0:T(8,128)(2,1)S(1)}, u32[]{:S(2)}, u32[]{:S(2)}) collective-permute-start(bf16[2,96,1024]{2,1,0:T(8,128)(2,1)S(1)} %get-tuple-element.317), channel_id=1, source_target_pairs={{0,8},{4,12},{8,0},{12,4},{16,24},{20,28},{24,16},{28,20},{1,9},{5... | collective-permute-start | bytes 1179656 | tf_op jit(solution)/shard_map/ppermute | solution.py:680
  166.1 26.2 %collective-permute-start.40 = (bf16[2,72,1024]{2,1,0:T(8,128)(2,1)S(1)}, bf16[2,72,1024]{2,1,0:T(8,128)(2,1)S(1)}, u32[]{:S(2)}, u32[]{:S(2)}) collective-permute-start(bf16[2,72,1024]{2,1,0:T(8,128)(2,1)S(1)} %get-tuple-element.320), channel_id=1, source_target_pairs={{0,4},{4,0},{8,12},{12,8},{16,20},{20,16},{24,28},{28,24},{1,5},{5... | collective-permute-start | bytes 884744 | tf_op jit(solution)/shard_map/ppermute | solution.py:680
  167.6 24.7 %collective-permute-start.41 = (bf16[1,136,1024]{2,1,0:T(8,128)(2,1)S(1)}, bf16[1,136,1024]{2,1,0:T(8,128)(2,1)S(1)}, u32[]{:S(2)}, u32[]{:S(2)}) collective-permute-start(bf16[1,136,1024]{2,1,0:T(8,128)(2,1)S(1)} %f2_last.1.a), channel_id=1, source_target_pairs={{0,16},{4,20},{8,24},{12,28},{16,0},{20,4},{24,8},{28,12},{1,17},{... | collective-permute-start | bytes 835592 | tf_op jit(solution)/shard_map/ppermute | solution.py:680
  167.7 24.5 %collective-permute-start.38 = (bf16[1,128,1024]{2,1,0:T(8,128)(2,1)S(1)}, bf16[1,128,1024]{2,1,0:T(8,128)(2,1)S(1)}, u32[]{:S(2)}, u32[]{:S(2)}) collective-permute-start(bf16[1,128,1024]{2,1,0:T(8,128)(2,1)S(1)} %f1_last.1.a), channel_id=1, source_target_pairs={{0,16},{4,20},{8,24},{12,28},{16,0},{20,4},{24,8},{28,12},{1,17},{... | collective-permute-start | bytes 786440 | tf_op jit(solution)/shard_map/ppermute | solution.py:680
  193.1 19.0 %collective-permute-start.44 = (bf16[2,128,1024]{2,1,0:T(8,128)(2,1)S(1)}, bf16[2,128,1024]{2,1,0:T(8,128)(2,1)S(1)}, u32[]{:S(2)}, u32[]{:S(2)}) collective-permute-start(bf16[2,128,1024]{2,1,0:T(8,128)(2,1)S(1)} %f1_pack.2.a), channel_id=1, source_target_pairs={{0,8},{4,12},{8,0},{12,4},{16,24},{20,28},{24,16},{28,20},{1,9},{5... | collective-permute-start | bytes 1572872 | tf_op jit(solution)/shard_map/ppermute | solution.py:680
  193.1 16.2 %collective-permute-start.43 = (bf16[1,96,1024]{2,1,0:T(8,128)(2,1)S(1)}, bf16[1,96,1024]{2,1,0:T(8,128)(2,1)S(1)}, u32[]{:S(2)}, u32[]{:S(2)}) collective-permute-start(bf16[1,96,1024]{2,1,0:T(8,128)(2,1)S(1)} %get-tuple-element.325), channel_id=1, source_target_pairs={{0,16},{4,20},{8,24},{12,28},{16,0},{20,4},{24,8},{28,12},{1,17},{... | collective-permute-start | bytes 589832 | tf_op jit(solution)/shard_map/ppermute | solution.py:680
  194.9 17.2 %collective-permute-start.45 = (bf16[1,72,1024]{2,1,0:T(8,128)(2,1)S(1)}, bf16[1,72,1024]{2,1,0:T(8,128)(2,1)S(1)}, u32[]{:S(2)}, u32[]{:S(2)}) collective-permute-start(bf16[1,72,1024]{2,1,0:T(8,128)(2,1)S(1)} %get-tuple-element.328), channel_id=1, source_target_pairs={{0,16},{4,20},{8,24},{12,28},{16,0},{20,4},{24,8},{28,12},{1,17},{... | collective-permute-start | bytes 442376 | tf_op jit(solution)/shard_map/ppermute | solution.py:680
  209.3 13.3 %collective-permute-start.47 = (bf16[1,96,1024]{2,1,0:T(8,128)(2,1)S(1)}, bf16[1,96,1024]{2,1,0:T(8,128)(2,1)S(1)}, u32[]{:S(2)}, u32[]{:S(2)}) collective-permute-start(bf16[1,96,1024]{2,1,0:T(8,128)(2,1)S(1)} %f3_last.1.a), channel_id=1, source_target_pairs={{0,8},{4,12},{8,0},{12,4},{16,24},{20,28},{24,16},{28,20},{1,9},{5... | collective-permute-start | bytes 589832 | tf_op jit(solution)/shard_map/ppermute | solution.py:680
  214.5 40.1 %collective-permute-start.51 = (bf16[4,136,1024]{2,1,0:T(8,128)(2,1)S(1)}, bf16[4,136,1024]{2,1,0:T(8,128)(2,1)S(1)}, u32[]{:S(2)}, u32[]{:S(2)}) collective-permute-start(bf16[4,136,1024]{2,1,0:T(8,128)(2,1)S(1)} %f2_pack.3.r_3_.r_1_), channel_id=1, source_target_pairs={{0,8},{4,12},{8,0},{12,4},{16,24},{20,28},{24,16},{28,20},{1,9},{5... | collective-permute-start | bytes 3342344 | tf_op jit(solution)/shard_map/ppermute | solution.py:680
  215.0 39.7 %collective-permute-start.50 = (bf16[4,128,1024]{2,1,0:T(8,128)(2,1)S(1)}, bf16[4,128,1024]{2,1,0:T(8,128)(2,1)}, u32[]{:S(2)}, u32[]{:S(2)}) collective-permute-start(bf16[4,128,1024]{2,1,0:T(8,128)(2,1)S(1)} %f1_pack.3.r_1_), channel_id=1, source_target_pairs={{0,4},{4,0},{8,12},{12,8},{16,20},{20,16},{24,28},{28,24},{1,5},{5... | collective-permute-start | bytes 3145736 | tf_op jit(solution)/shard_map/ppermute | solution.py:680
  222.6 25.8 %collective-permute-start.48 = (bf16[2,96,1024]{2,1,0:T(8,128)(2,1)S(1)}, bf16[2,96,1024]{2,1,0:T(8,128)(2,1)S(1)}, u32[]{:S(2)}, u32[]{:S(2)}) collective-permute-start(bf16[2,96,1024]{2,1,0:T(8,128)(2,1)S(1)} %f3_pack.2.a), channel_id=1, source_target_pairs={{0,16},{4,20},{8,24},{12,28},{16,0},{20,4},{24,8},{28,12},{1,17},{... | collective-permute-start | bytes 1179656 | tf_op jit(solution)/shard_map/ppermute | solution.py:680
  224.1 25.2 %collective-permute-start.49 = (bf16[2,72,1024]{2,1,0:T(8,128)(2,1)S(1)}, bf16[2,72,1024]{2,1,0:T(8,128)(2,1)S(1)}, u32[]{:S(2)}, u32[]{:S(2)}) collective-permute-start(bf16[2,72,1024]{2,1,0:T(8,128)(2,1)S(1)} %f4_pack.2.a), channel_id=1, source_target_pairs={{0,4},{4,0},{8,12},{12,8},{16,20},{20,16},{24,28},{28,24},{1,5},{5... | collective-permute-start | bytes 884744 | tf_op jit(solution)/shard_map/ppermute | solution.py:680
  250.2 13.1 %collective-permute-start.52 = (bf16[4,72,1024]{2,1,0:T(8,128)(2,1)}, bf16[4,72,1024]{2,1,0:T(8,128)(2,1)}, u32[]{:S(2)}, u32[]{:S(2)}) collective-permute-start(bf16[4,72,1024]{2,1,0:T(8,128)(2,1)} %f4_pack.3.r_1_), channel_id=1, source_target_pairs={{0,8},{4,12},{8,0},{12,4},{16,24},{20,28},{24,16},{28,20},{1,9},{5... | collective-permute-start | bytes 1769480 | tf_op jit(solution)/shard_map/ppermute | solution.py:680
  253.2 15.3 %collective-permute-start.53 = (bf16[4,96,1024]{2,1,0:T(8,128)(2,1)}, bf16[4,96,1024]{2,1,0:T(8,128)(2,1)}, u32[]{:S(2)}, u32[]{:S(2)}) collective-permute-start(bf16[4,96,1024]{2,1,0:T(8,128)(2,1)} %f3_pack.3.r_1_), channel_id=1, source_target_pairs={{0,4},{4,0},{8,12},{12,8},{16,20},{20,16},{24,28},{28,24},{1,5},{5... | collective-permute-start | bytes 2359304 | tf_op jit(solution)/shard_map/ppermute | solution.py:680
  (50 other events, 337.0 us)

commit v6 on v5

--- a/solution.py
+++ b/solution.py
@@ -48,7 +48,7 @@
 
 
 COST = 1153500
-STEPS = {'hops': ['f2', 'f1'], 'back': ['f1', 'f2'], 'taps': ['f2'], 'hid': [], 'x': ['f1'], 'tail': ['f3', 'in', 'f4', 'out', 'f1', 'f3', 'f4', 'f2', 'f2', 'f3', 'f1', 'f4', 'f4', 'f3', 'f3', 'f4', 's1', 's2', 's4', 's3']}
+STEPS = {'hops': ['f2', 'f1'], 'back': ['f1', 'f2'], 'taps': ['f1'], 'hid': [], 'x': ['f2'], 'tail': ['f3', 'in', 'f4', 'out', 'f1', 'f4', 'f3', 'f2', 'f2', 'f4', 'f3', 'f1', 'f4', 'f3', 'f3', 'f4', 's1', 's2', 's4', 's3']}
 WAYS = {'f1': ((0, 1, 2), (2, 1, 0)), 'f2': ((1, 0, 2), (2, 0, 1)), 'f3': ((0, 1, 2), (1, 2, 0)), 'f4': ((1, 0, 2), (2, 0, 1))}
 
 
@@ -153,7 +153,7 @@
     return lambda j, c: values[c // parts][j : j + 1, (c % parts) * DH : (c % parts + 1) * DH]
 
 
-def front_kernel(first, tp, seq_groups, seq_pads, xh, coth, gain, wqh, wkh, wvh, wgh, wb, tail, cq, ck, cv, gate, beta, meta, qkv, wmix, umix, score, zst, dev, last, hidden_h, gd_h, x_own, gd_own, ext_h, conv_h, inv_h, amap_h, x, cot, wq, wk, wv, wg, hidden, gd, ext, conv, inv, amap, badd, sems, out_sems):
+def front_kernel(first, tp, seq_groups, seq_pads, xh, coth, gain, wqh, wkh, wvh, wgh, wb, tail, cq, ck, cv, gate, beta, meta, qkv, wmix, umix, score, zst, dev_low, last, hidden_h, gd_h, x_own, gd_own, ext_h, conv_h, inv_h, amap_h, x, cot, wq, wk, wv, wg, hidden, gd, ext, conv, inv, amap, badd, dev, sems, out_sems):
     loads = [
         pltpu.make_async_copy(src, dst, sems.at[i])
         for i, (src, dst) in enumerate(
@@ -286,7 +286,8 @@
         return 0
 
     lax.fori_loop(0, groups, chain, 0)
-    last[...] = dev[:, :, DH:]
+    dev_low[...] = dev[...].astype(bf16)
+    last[...] = dev[:, :, DH:].astype(bf16)
 
     for copy in stores:
         copy.wait()
@@ -966,7 +967,7 @@
             (wide, f32, near),
             (inv_shape, f32, near),
             (zst_shape, f32, near),
-            *dev_shapes,
+            *[(shape, bf16) for shape, _ in dev_shapes],
             ((total, model), bf16, far),
             ((total, model), bf16, far),
             ((share, model), bf16, far),
@@ -988,6 +989,7 @@
             pltpu.VMEM(inv_shape, f32),
             pltpu.VMEM(map_shape, f32),
             pltpu.VMEM(map_shape, f32),
+            pltpu.VMEM(dev_shapes[0][0], f32),
             pltpu.SemaphoreType.DMA((6,)),
             pltpu.SemaphoreType.DMA((8,)),
         ],

time: 272 us -> 270 us (level)
  transfers between devices with their start and end apart: 54 -> 54, of which waited for: 23 -> 21; matrix products, arithmetic and copies ran while one was open for 1% -> 1% of each run, Pallas kernels for 21% -> 21%
where the time goes in v6:
time: 270 us
  waiting for transfers between devices  118 us (44%)
  Pallas kernels  79.8 us (30%)
  starting transfers between devices  67.3 us (25%)
  local copies, waits for them, and re-layouts  3.31 us (1%)
    ppermute x48, waiting for transfers between devices, swap(): return lax.ppermute(value, axis, [(i, i ^ bit) for i in range(count)])  115 us
    pallas_call x51, Pallas kernels, run(): pl.pallas_call(kernel, name=name, out_shape=shapes, in_specs=[pl.BlockSpe...  79.8 us
    ppermute x48, starting transfers between devices, swap(): return lax.ppermute(value, axis, [(i, i ^ bit) for i in range(count)])  50.7 us
    ppermute x6, starting transfers between devices, shift(): return lax.ppermute(value, 'seq', pairs)  16.6 us
  transfers between devices with their start and end apart: 54, of which 21 were waited for; matrix products, arithmetic and copies ran while one was open for 1% of the time, Pallas kernels for 21%

profile of v6, /device:TPU:0, one launch (start us, length us, event | category | flops | bytes accessed | tf_op | source)
XLA Modules:
  0.0 269.9 jit_solution(1387168331503087958)
XLA Ops:
  1.4 4.9 %collective-permute-start = (bf16[16,1024]{1,0:T(8,128)(2,1)S(1)}, bf16[16,1024]{1,0:T(8,128)(2,1)S(1)}, u32[]{:S(2)}, u32[]{:S(2)}) collective-permute-start(bf16[16,1024]{1,0:T(8,128)(2,1)S(1)} %slice.15), channel_id=1, source_target_pairs={{0,4},{4,8},{8,12},{12,16},{16,20},{20,24},{24,28},{1,5},{5,9},{9,... | collective-permute-start | bytes 98312 | tf_op jit(solution)/shard_map/ppermute | solution.py:871
  7.9 15.1 %front.1 = (f32[512,256]{1,0:T(8,128)S(1)}, f32[512,2]{1,0:T(8,128)S(1)}, s32[2,8]{1,0:T(2,128)S(1)}, f32[512,768]{1,0:T(8,128)S(1)}, f32[512,256]{1,0:T(8,128)S...) custom-call(s32[1]{0:T(128)} %bitcast.1.first.r_1_.r_0_, ...), custom_call_target="tpu_custom_call" | custom-call | flops 1153500 | bytes 1 | tf_op jit(solution)/shard_map/front/pallas_call | solution.py:78
  22.9 4.2 %collective-permute-start.1 = (bf16[2,128,256]{2,1,0:T(8,128)(2,1)S(1)}, bf16[2,128,256]{2,1,0:T(8,128)(2,1)S(1)}, u32[]{:S(2)}, u32[]{:S(2)}) collective-permute-start(bf16[2,128,256]{2,1,0:T(8,128)(2,1)S(1)} %get-tuple-element.183), channel_id=1, source_target_pairs={{0,4},{4,8},{8,12},{12,16},{16,20},{20,24},{24,28},{1,5},{5,9},{9,... | collective-permute-start | bytes 393224 | tf_op jit(solution)/shard_map/ppermute | solution.py:871
  27.2 3.7 %collective-permute-start.2 = (bf16[2,128,128]{2,1,0:T(8,128)(2,1)S(1)}, bf16[2,128,128]{2,1,0:T(8,128)(2,1)S(1)}, u32[]{:S(2)}, u32[]{:S(2)}) collective-permute-start(bf16[2,128,128]{2,1,0:T(8,128)(2,1)S(1)} %get-tuple-element.193), channel_id=1, source_target_pairs={{0,8},{4,12},{8,16},{12,20},{16,24},{20,28},{1,9},{5,13},{9,17},{1... | collective-permute-start | bytes 196616 | tf_op jit(solution)/shard_map/ppermute | solution.py:871
  38.9 3.8 %states.1 = (f32[16,128,128]{2,1,0:T(8,128)S(1)}, f32[512,256]{1,0:T(8,128)S(1)}, f32[512,256]{1,0:T(8,128)S(1)}) custom-call(f32[2,128,128]{2,1,0:T(8,128)S(1)} %get-tuple-element.201.entry, f32[16,128,256]{2,1,0:T(8,128)S(1)} %get-tuple-element.190.zst, f32[512,768]{1,0:T(8,128)S(1)} %get-tuple-element.239.qkv.r_4_, ...), custom_call_target="tpu_custom_call" | custom-call | flops 1153500 | bytes 1 | tf_op jit(solution)/shard_map/states/pallas_call | solution.py:78
  42.7 3.0 %collective-permute-done.4 = bf16[1,128,1024]{2,1,0:T(8,128)(2,1)S(1)} collective-permute-done((bf16[1,128,1024]{2,1,0:T(8,128)(2,1)S(1)}, bf16[1,128,1024]{2,1,0:T(8,128)(2,1)S(1)}, u32[]{:S(2)}, u32[]{:S(2)}) %collective-permute-start.4) | collective-permute-done | bytes 262176 | tf_op jit(solution)/shard_map/ppermute | solution.py:681
  56.3 5.2 %ffn_b.1 = (f32[1,128,1024]{2,1,0:T(8,128)S(1)}, bf16[1,128,1024]{2,1,0:T(8,128)(2,1)S(1)}, f32[1,128,1024]{2,1,0:T(8,128)S(1)}, bf16[1,128,1024]{2,1,0:T(8,128)...) custom-call(s32[1]{0:T(128)} %bitcast.tp.r_0_, ...), custom_call_target="tpu_custom_call" | custom-call | flops 1153500 | bytes 1 | tf_op jit(solution)/shard_map/ffn_b/pallas_call | solution.py:78
  67.5 6.5 %collective-permute-done.10 = bf16[1,128,1024]{2,1,0:T(8,128)(2,1)S(1)} collective-permute-done((bf16[1,128,1024]{2,1,0:T(8,128)(2,1)S(1)}, bf16[1,128,1024]{2,1,0:T(8,128)(2,1)S(1)}, u32[]{:S(2)}, u32[]{:S(2)}) %collective-permute-start.10) | collective-permute-done | bytes 262176 | tf_op jit(solution)/shard_map/ppermute | solution.py:681
  75.9 5.6 %collective-permute-done.12.b2 = bf16[128,1024]{1,0:T(8,128)(2,1)S(1)} collective-permute-done((bf16[128,1024]{1,0:T(8,128)(2,1)S(1)}, bf16[128,1024]{1,0:T(8,128)(2,1)S(1)}, u32[]{:S(2)}, u32[]{:S(2)}) %collective-permute-start.12) | collective-permute-done | bytes 262176 | tf_op jit(solution)/shard_map/ppermute | solution.py:681
  83.0 5.2 %flow.1 = (bf16[512,1024]{1,0:T(8,128)(2,1)S(1)}, bf16[512,256]{1,0:T(8,128)(2,1)S(1)}, f32[512,256]{1,0:T(8,128)S(1)}, f32[16,128,256]{2,1,0:T(8,128)S(1)}, bf1...) custom-call(s32[1]{0:T(128)} %bitcast.tp.r_0_, ...), custom_call_target="tpu_custom_call" | custom-call | flops 1153500 | bytes 1 | tf_op jit(solution)/shard_map/flow/pallas_call | solution.py:78
  90.9 5.0 %side.1 = (f32[512,256]{1,0:T(8,128)S(1)}, f32[512,256]{1,0:T(8,128)S(1)}, f32[512,256]{1,0:T(8,128)S(1)}) custom-call(f32[512,768]{1,0:T(8,128)S(1)} %get-tuple-element.239.qkv.r_4_, f32[512,256]{1,0:T(8,128)S(1)} %get-tuple-element.240.dout, f32[512,256]{1,0:T(8,128)S(1)} %get-tuple-element.241.vnew.r_12_, ...), custom_call_target="tpu_custom_call" | custom-call | flops 1153500 | bytes 1 | tf_op jit(solution)/shard_map/side/pallas_call | solution.py:78
  103.3 9.6 %back.1 = (f32[520,768]{1,0:T(8,128)S(1)}, f32[8,768]{1,0:T(8,128)S(1)}, bf16[512,128]{1,0:T(8,128)(2,1)S(1)}) custom-call(s32[2,8]{1,0:T(2,128)S(1)} %get-tuple-element.181.meta.r_0_, bf16[2,128,256]{2,1,0:T(8,128)(2,1)S(1)} %collective-permute-done.16.r_1_, bf16[2,128,128]{2,1,0:T(8,128)(2,1)S(1)} %collective-permute-done.17.r_2_, ...), custom_call_target="tpu_custom_call" | custom-call | flops 1153500 | bytes 1 | tf_op jit(solution)/shard_map/back/pallas_call | solution.py:78
  120.0 6.9 %collective-permute-done.23.got = bf16[1,128,1024]{2,1,0:T(8,128)(2,1)S(1)} collective-permute-done((bf16[1,128,1024]{2,1,0:T(8,128)(2,1)S(1)}, bf16[1,128,1024]{2,1,0:T(8,128)(2,1)S(1)}, u32[]{:S(2)}, u32[]{:S(2)}) %collective-permute-start.23) | collective-permute-done | bytes 262176 | tf_op jit(solution)/shard_map/ppermute | solution.py:681
  134.4 11.8 %collective-permute-done.27.got = bf16[1,136,1024]{2,1,0:T(8,128)(2,1)S(1)} collective-permute-done((bf16[1,136,1024]{2,1,0:T(8,128)(2,1)S(1)}, bf16[1,136,1024]{2,1,0:T(8,128)(2,1)S(1)}, u32[]{:S(2)}, u32[]{:S(2)}) %collective-permute-start.27) | collective-permute-done | bytes 278560 | tf_op jit(solution)/shard_map/ppermute | solution.py:681
  149.2 6.1 %collective-permute-done.32.a2 = bf16[128,1024]{1,0:T(8,128)(2,1)S(1)} collective-permute-done((bf16[128,1024]{1,0:T(8,128)(2,1)S(1)}, bf16[128,1024]{1,0:T(8,128)(2,1)S(1)}, u32[]{:S(2)}, u32[]{:S(2)}) %collective-permute-start.32) | collective-permute-done | bytes 262176 | tf_op jit(solution)/shard_map/ppermute | solution.py:681
  160.6 3.3 %collective-permute-done.34.got = bf16[4,72,1024]{2,1,0:T(8,128)(2,1)S(1)} collective-permute-done((bf16[4,72,1024]{2,1,0:T(8,128)(2,1)S(1)}, bf16[4,72,1024]{2,1,0:T(8,128)(2,1)S(1)}, u32[]{:S(2)}, u32[]{:S(2)}) %collective-permute-start.34) | collective-permute-done | bytes 589856 | tf_op jit(solution)/shard_map/ppermute | solution.py:681
  169.5 20.7 %collective-permute-done.38.b = bf16[1,128,1024]{2,1,0:T(8,128)(2,1)S(1)} collective-permute-done((bf16[1,128,1024]{2,1,0:T(8,128)(2,1)S(1)}, bf16[1,128,1024]{2,1,0:T(8,128)(2,1)S(1)}, u32[]{:S(2)}, u32[]{:S(2)}) %collective-permute-start.38) | collective-permute-done | bytes 262176 | tf_op jit(solution)/shard_map/ppermute | solution.py:681
  193.8 8.3 %collective-permute-done.42.b = bf16[2,136,1024]{2,1,0:T(8,128)(2,1)S(1)} collective-permute-done((bf16[2,136,1024]{2,1,0:T(8,128)(2,1)S(1)}, bf16[2,136,1024]{2,1,0:T(8,128)(2,1)S(1)}, u32[]{:S(2)}, u32[]{:S(2)}) %collective-permute-start.42) | collective-permute-done | bytes 557088 | tf_op jit(solution)/shard_map/ppermute | solution.py:681
  202.2 4.8 %collective-permute-done.43.got = bf16[1,72,1024]{2,1,0:T(8,128)(2,1)S(1)} collective-permute-done((bf16[1,72,1024]{2,1,0:T(8,128)(2,1)S(1)}, bf16[1,72,1024]{2,1,0:T(8,128)(2,1)S(1)}, u32[]{:S(2)}, u32[]{:S(2)}) %collective-permute-start.43) | collective-permute-done | bytes 147488 | tf_op jit(solution)/shard_map/ppermute | solution.py:681
  207.1 3.3 %collective-permute-start.47 = (bf16[1,96,1024]{2,1,0:T(8,128)(2,1)S(1)}, bf16[1,96,1024]{2,1,0:T(8,128)(2,1)S(1)}, u32[]{:S(2)}, u32[]{:S(2)}) collective-permute-start(bf16[1,96,1024]{2,1,0:T(8,128)(2,1)S(1)} %f3_last.1.a), channel_id=1, source_target_pairs={{0,8},{4,12},{8,0},{12,4},{16,24},{20,28},{24,16},{28,20},{1,9},{5... | collective-permute-start | bytes 589832 | tf_op jit(solution)/shard_map/ppermute | solution.py:681
  214.2 4.7 %collective-permute-done.46.b = bf16[1,72,1024]{2,1,0:T(8,128)(2,1)S(1)} collective-permute-done((bf16[1,72,1024]{2,1,0:T(8,128)(2,1)S(1)}, bf16[1,72,1024]{2,1,0:T(8,128)(2,1)S(1)}, u32[]{:S(2)}, u32[]{:S(2)}) %collective-permute-start.46) | collective-permute-done | bytes 147488 | tf_op jit(solution)/shard_map/ppermute | solution.py:681
  224.1 22.3 %collective-permute-done.48.b = bf16[2,96,1024]{2,1,0:T(8,128)(2,1)S(1)} collective-permute-done((bf16[2,96,1024]{2,1,0:T(8,128)(2,1)S(1)}, bf16[2,96,1024]{2,1,0:T(8,128)(2,1)S(1)}, u32[]{:S(2)}, u32[]{:S(2)}) %collective-permute-start.48) | collective-permute-done | bytes 393248 | tf_op jit(solution)/shard_map/ppermute | solution.py:681
  252.7 3.9 %settle_1.1 = (f32[704,1024]{1,0:T(8,128)}, f32[704,1024]{1,0:T(8,128)}) custom-call(s32[1]{0:T(128)} %bitcast.1.first.r_1_.r_0_, bf16[4,128,1024]{2,1,0:T(8,128)(2,1)S(1)} %f1_pack.3.r_1_, bf16[4,128,1024]{2,1,0:T(8,128)(2,1)} %collective-permute-done.50.r_2_, bf16[4,136,1024]{2,1,0:T(8,128)(2,1)S(1)} %f2_pack.3.r_3_.r_1_, ...), custom_call_target="tpu_custom_call" | custom-call | flops 1153500 | bytes 1 | tf_op jit(solution)/shard_map/settle_1/pallas_call | solution.py:78
  266.5 3.3 %settle_3.1 = (f32[1024,256]{1,0:T(8,128)}, f32[1024,256]{1,0:T(8,128)}, f32[1024,256]{1,0:T(8,128)}) custom-call(s32[1]{0:T(128)} %bitcast.1.first.r_1_.r_0_, bf16[4,96,1024]{2,1,0:T(8,128)(2,1)} %f3_pack.3.r_1_, bf16[4,96,1024]{2,1,0:T(8,128)(2,1)} %collective-permute-done.53.r_2_), custom_call_target="tpu_custom_call" | custom-call | flops 1153500 | bytes 1 | tf_op jit(solution)/shard_map/settle_3/pallas_call | solution.py:78
  (180 shorter events, 97.1 us)
Async XLA Ops:
  61.8 35.3 %collective-permute-start.18 = (bf16[4,136,1024]{2,1,0:T(8,128)(2,1)S(1)}, bf16[4,136,1024]{2,1,0:T(8,128)(2,1)S(1)}, u32[]{:S(2)}, u32[]{:S(2)}) collective-permute-start(bf16[4,136,1024]{2,1,0:T(8,128)(2,1)S(1)} %get-tuple-element.252), channel_id=1, source_target_pairs={{0,8},{4,12},{8,0},{12,4},{16,24},{20,28},{24,16},{28,20},{1,9},{5... | collective-permute-start | bytes 3342344 | tf_op jit(solution)/shard_map/ppermute | solution.py:681
  63.4 34.0 %collective-permute-start.19 = (bf16[4,128,1024]{2,1,0:T(8,128)(2,1)S(1)}, bf16[4,128,1024]{2,1,0:T(8,128)(2,1)S(1)}, u32[]{:S(2)}, u32[]{:S(2)}) collective-permute-start(bf16[4,128,1024]{2,1,0:T(8,128)(2,1)S(1)} %get-tuple-element.255), channel_id=1, source_target_pairs={{0,4},{4,0},{8,12},{12,8},{16,20},{20,16},{24,28},{28,24},{1,5},{5... | collective-permute-start | bytes 3145736 | tf_op jit(solution)/shard_map/ppermute | solution.py:681
  82.0 13.8 %collective-permute-start.15 = (bf16[1,128,1024]{2,1,0:T(8,128)(2,1)S(1)}, bf16[1,128,1024]{2,1,0:T(8,128)(2,1)S(1)}, u32[]{:S(2)}, u32[]{:S(2)}) collective-permute-start(bf16[1,128,1024]{2,1,0:T(8,128)(2,1)S(1)} %get-tuple-element.245), channel_id=1, source_target_pairs={{0,1},{1,0},{2,3},{3,2},{4,5},{5,4},{6,7},{7,6},{8,9},{9,8},{10,11... | collective-permute-start | bytes 786440 | tf_op jit(solution)/shard_map/ppermute | solution.py:681
  97.6 15.3 %collective-permute-start.20 = (bf16[2,128,1024]{2,1,0:T(8,128)(2,1)S(1)}, bf16[2,128,1024]{2,1,0:T(8,128)(2,1)S(1)}, u32[]{:S(2)}, u32[]{:S(2)}) collective-permute-start(bf16[2,128,1024]{2,1,0:T(8,128)(2,1)S(1)} %get-tuple-element.266), channel_id=1, source_target_pairs={{0,8},{4,12},{8,0},{12,4},{16,24},{20,28},{24,16},{28,20},{1,9},{5... | collective-permute-start | bytes 1572872 | tf_op jit(solution)/shard_map/ppermute | solution.py:681
  99.8 16.3 %collective-permute-start.21 = (bf16[2,136,1024]{2,1,0:T(8,128)(2,1)S(1)}, bf16[2,136,1024]{2,1,0:T(8,128)(2,1)S(1)}, u32[]{:S(2)}, u32[]{:S(2)}) collective-permute-start(bf16[2,136,1024]{2,1,0:T(8,128)(2,1)S(1)} %get-tuple-element.269), channel_id=1, source_target_pairs={{0,4},{4,0},{8,12},{12,8},{16,20},{20,16},{24,28},{28,24},{1,5},{5... | collective-permute-start | bytes 1671176 | tf_op jit(solution)/shard_map/ppermute | solution.py:681
  101.8 17.5 %collective-permute-start.22 = (bf16[1,128,1024]{2,1,0:T(8,128)(2,1)S(1)}, bf16[1,128,1024]{2,1,0:T(8,128)(2,1)S(1)}, u32[]{:S(2)}, u32[]{:S(2)}) collective-permute-start(bf16[1,128,1024]{2,1,0:T(8,128)(2,1)S(1)} %get-tuple-element.275), channel_id=1, source_target_pairs={{0,2},{1,3},{2,0},{3,1},{4,6},{5,7},{6,4},{7,5},{8,10},{9,11},{10,... | collective-permute-start | bytes 786440 | tf_op jit(solution)/shard_map/ppermute | solution.py:681
  113.1 13.8 %collective-permute-start.23 = (bf16[1,128,1024]{2,1,0:T(8,128)(2,1)S(1)}, bf16[1,128,1024]{2,1,0:T(8,128)(2,1)S(1)}, u32[]{:S(2)}, u32[]{:S(2)}) collective-permute-start(bf16[1,128,1024]{2,1,0:T(8,128)(2,1)S(1)} %get-tuple-element.279), channel_id=1, source_target_pairs={{0,16},{4,20},{8,24},{12,28},{16,0},{20,4},{24,8},{28,12},{1,17},{... | collective-permute-start | bytes 786440 | tf_op jit(solution)/shard_map/ppermute | solution.py:681
  130.0 27.0 %collective-permute-start.30 = (bf16[4,96,1024]{2,1,0:T(8,128)(2,1)S(1)}, bf16[4,96,1024]{2,1,0:T(8,128)(2,1)S(1)}, u32[]{:S(2)}, u32[]{:S(2)}) collective-permute-start(bf16[4,96,1024]{2,1,0:T(8,128)(2,1)S(1)} %get-tuple-element.308), channel_id=1, source_target_pairs={{0,4},{4,0},{8,12},{12,8},{16,20},{20,16},{24,28},{28,24},{1,5},{5... | collective-permute-start | bytes 2359304 | tf_op jit(solution)/shard_map/ppermute | solution.py:681
  130.6 15.6 %collective-permute-start.27 = (bf16[1,136,1024]{2,1,0:T(8,128)(2,1)S(1)}, bf16[1,136,1024]{2,1,0:T(8,128)(2,1)S(1)}, u32[]{:S(2)}, u32[]{:S(2)}) collective-permute-start(bf16[1,136,1024]{2,1,0:T(8,128)(2,1)S(1)} %get-tuple-element.301), channel_id=1, source_target_pairs={{0,16},{4,20},{8,24},{12,28},{16,0},{20,4},{24,8},{28,12},{1,17},{... | collective-permute-start | bytes 835592 | tf_op jit(solution)/shard_map/ppermute | solution.py:681
  130.7 15.6 %collective-permute-start.28 = (bf16[1,128,1024]{2,1,0:T(8,128)(2,1)S(1)}, bf16[1,128,1024]{2,1,0:T(8,128)(2,1)S(1)}, u32[]{:S(2)}, u32[]{:S(2)}) collective-permute-start(bf16[1,128,1024]{2,1,0:T(8,128)(2,1)S(1)} %get-tuple-element.303), channel_id=1, source_target_pairs={{0,2},{1,3},{2,0},{3,1},{4,6},{5,7},{6,4},{7,5},{8,10},{9,11},{10,... | collective-permute-start | bytes 786440 | tf_op jit(solution)/shard_map/ppermute | solution.py:681
  147.6 16.3 %collective-permute-start.34 = (bf16[4,72,1024]{2,1,0:T(8,128)(2,1)S(1)}, bf16[4,72,1024]{2,1,0:T(8,128)(2,1)S(1)}, u32[]{:S(2)}, u32[]{:S(2)}) collective-permute-start(bf16[4,72,1024]{2,1,0:T(8,128)(2,1)S(1)} %get-tuple-element.312), channel_id=1, source_target_pairs={{0,8},{4,12},{8,0},{12,4},{16,24},{20,28},{24,16},{28,20},{1,9},{5... | collective-permute-start | bytes 1769480 | tf_op jit(solution)/shard_map/ppermute | solution.py:681
  157.4 32.9 %collective-permute-start.40 = (bf16[2,96,1024]{2,1,0:T(8,128)(2,1)S(1)}, bf16[2,96,1024]{2,1,0:T(8,128)(2,1)S(1)}, u32[]{:S(2)}, u32[]{:S(2)}) collective-permute-start(bf16[2,96,1024]{2,1,0:T(8,128)(2,1)S(1)} %get-tuple-element.320), channel_id=1, source_target_pairs={{0,8},{4,12},{8,0},{12,4},{16,24},{20,28},{24,16},{28,20},{1,9},{5... | collective-permute-start | bytes 1179656 | tf_op jit(solution)/shard_map/ppermute | solution.py:681
  164.0 26.2 %collective-permute-start.39 = (bf16[2,72,1024]{2,1,0:T(8,128)(2,1)S(1)}, bf16[2,72,1024]{2,1,0:T(8,128)(2,1)S(1)}, u32[]{:S(2)}, u32[]{:S(2)}) collective-permute-start(bf16[2,72,1024]{2,1,0:T(8,128)(2,1)S(1)} %get-tuple-element.317), channel_id=1, source_target_pairs={{0,4},{4,0},{8,12},{12,8},{16,20},{20,16},{24,28},{28,24},{1,5},{5... | collective-permute-start | bytes 884744 | tf_op jit(solution)/shard_map/ppermute | solution.py:681
  165.5 24.9 %collective-permute-start.41 = (bf16[1,136,1024]{2,1,0:T(8,128)(2,1)S(1)}, bf16[1,136,1024]{2,1,0:T(8,128)(2,1)S(1)}, u32[]{:S(2)}, u32[]{:S(2)}) collective-permute-start(bf16[1,136,1024]{2,1,0:T(8,128)(2,1)S(1)} %f2_last.1.a), channel_id=1, source_target_pairs={{0,16},{4,20},{8,24},{12,28},{16,0},{20,4},{24,8},{28,12},{1,17},{... | collective-permute-start | bytes 835592 | tf_op jit(solution)/shard_map/ppermute | solution.py:681
  165.5 24.7 %collective-permute-start.38 = (bf16[1,128,1024]{2,1,0:T(8,128)(2,1)S(1)}, bf16[1,128,1024]{2,1,0:T(8,128)(2,1)S(1)}, u32[]{:S(2)}, u32[]{:S(2)}) collective-permute-start(bf16[1,128,1024]{2,1,0:T(8,128)(2,1)S(1)} %f1_last.1.a), channel_id=1, source_target_pairs={{0,16},{4,20},{8,24},{12,28},{16,0},{20,4},{24,8},{28,12},{1,17},{... | collective-permute-start | bytes 786440 | tf_op jit(solution)/shard_map/ppermute | solution.py:681
  190.9 21.6 %collective-permute-start.45 = (bf16[2,128,1024]{2,1,0:T(8,128)(2,1)S(1)}, bf16[2,128,1024]{2,1,0:T(8,128)(2,1)S(1)}, u32[]{:S(2)}, u32[]{:S(2)}) collective-permute-start(bf16[2,128,1024]{2,1,0:T(8,128)(2,1)S(1)} %f1_pack.2.a), channel_id=1, source_target_pairs={{0,8},{4,12},{8,0},{12,4},{16,24},{20,28},{24,16},{28,20},{1,9},{5... | collective-permute-start | bytes 1572872 | tf_op jit(solution)/shard_map/ppermute | solution.py:681
  190.9 16.1 %collective-permute-start.44 = (bf16[1,96,1024]{2,1,0:T(8,128)(2,1)S(1)}, bf16[1,96,1024]{2,1,0:T(8,128)(2,1)S(1)}, u32[]{:S(2)}, u32[]{:S(2)}) collective-permute-start(bf16[1,96,1024]{2,1,0:T(8,128)(2,1)S(1)} %get-tuple-element.327), channel_id=1, source_target_pairs={{0,16},{4,20},{8,24},{12,28},{16,0},{20,4},{24,8},{28,12},{1,17},{... | collective-permute-start | bytes 589832 | tf_op jit(solution)/shard_map/ppermute | solution.py:681
  192.8 14.2 %collective-permute-start.43 = (bf16[1,72,1024]{2,1,0:T(8,128)(2,1)S(1)}, bf16[1,72,1024]{2,1,0:T(8,128)(2,1)S(1)}, u32[]{:S(2)}, u32[]{:S(2)}) collective-permute-start(bf16[1,72,1024]{2,1,0:T(8,128)(2,1)S(1)} %get-tuple-element.325), channel_id=1, source_target_pairs={{0,16},{4,20},{8,24},{12,28},{16,0},{20,4},{24,8},{28,12},{1,17},{... | collective-permute-start | bytes 442376 | tf_op jit(solution)/shard_map/ppermute | solution.py:681
  210.6 42.1 %collective-permute-start.51 = (bf16[4,136,1024]{2,1,0:T(8,128)(2,1)S(1)}, bf16[4,136,1024]{2,1,0:T(8,128)(2,1)S(1)}, u32[]{:S(2)}, u32[]{:S(2)}) collective-permute-start(bf16[4,136,1024]{2,1,0:T(8,128)(2,1)S(1)} %f2_pack.3.r_3_.r_1_), channel_id=1, source_target_pairs={{0,8},{4,12},{8,0},{12,4},{16,24},{20,28},{24,16},{28,20},{1,9},{5... | collective-permute-start | bytes 3342344 | tf_op jit(solution)/shard_map/ppermute | solution.py:681
  212.6 40.1 %collective-permute-start.50 = (bf16[4,128,1024]{2,1,0:T(8,128)(2,1)S(1)}, bf16[4,128,1024]{2,1,0:T(8,128)(2,1)}, u32[]{:S(2)}, u32[]{:S(2)}) collective-permute-start(bf16[4,128,1024]{2,1,0:T(8,128)(2,1)S(1)} %f1_pack.3.r_1_), channel_id=1, source_target_pairs={{0,4},{4,0},{8,12},{12,8},{16,20},{20,16},{24,28},{28,24},{1,5},{5... | collective-permute-start | bytes 3145736 | tf_op jit(solution)/shard_map/ppermute | solution.py:681
  220.0 26.4 %collective-permute-start.48 = (bf16[2,96,1024]{2,1,0:T(8,128)(2,1)S(1)}, bf16[2,96,1024]{2,1,0:T(8,128)(2,1)S(1)}, u32[]{:S(2)}, u32[]{:S(2)}) collective-permute-start(bf16[2,96,1024]{2,1,0:T(8,128)(2,1)S(1)} %f3_pack.2.a), channel_id=1, source_target_pairs={{0,16},{4,20},{8,24},{12,28},{16,0},{20,4},{24,8},{28,12},{1,17},{... | collective-permute-start | bytes 1179656 | tf_op jit(solution)/shard_map/ppermute | solution.py:681
  222.4 24.9 %collective-permute-start.49 = (bf16[2,72,1024]{2,1,0:T(8,128)(2,1)S(1)}, bf16[2,72,1024]{2,1,0:T(8,128)(2,1)S(1)}, u32[]{:S(2)}, u32[]{:S(2)}) collective-permute-start(bf16[2,72,1024]{2,1,0:T(8,128)(2,1)S(1)} %f4_pack.2.a), channel_id=1, source_target_pairs={{0,4},{4,0},{8,12},{12,8},{16,20},{20,16},{24,28},{28,24},{1,5},{5... | collective-permute-start | bytes 884744 | tf_op jit(solution)/shard_map/ppermute | solution.py:681
  248.2 13.1 %collective-permute-start.52 = (bf16[4,72,1024]{2,1,0:T(8,128)(2,1)}, bf16[4,72,1024]{2,1,0:T(8,128)(2,1)}, u32[]{:S(2)}, u32[]{:S(2)}) collective-permute-start(bf16[4,72,1024]{2,1,0:T(8,128)(2,1)} %f4_pack.3.r_1_), channel_id=1, source_target_pairs={{0,8},{4,12},{8,0},{12,4},{16,24},{20,28},{24,16},{28,20},{1,9},{5... | collective-permute-start | bytes 1769480 | tf_op jit(solution)/shard_map/ppermute | solution.py:681
  251.0 15.4 %collective-permute-start.53 = (bf16[4,96,1024]{2,1,0:T(8,128)(2,1)}, bf16[4,96,1024]{2,1,0:T(8,128)(2,1)}, u32[]{:S(2)}, u32[]{:S(2)}) collective-permute-start(bf16[4,96,1024]{2,1,0:T(8,128)(2,1)} %f3_pack.3.r_1_), channel_id=1, source_target_pairs={{0,4},{4,0},{8,12},{12,8},{16,20},{20,16},{24,28},{28,24},{1,5},{5... | collective-permute-start | bytes 2359304 | tf_op jit(solution)/shard_map/ppermute | solution.py:681
  (50 other events, 362.0 us)

commit v7 on v6

--- a/solution.py
+++ b/solution.py
@@ -477,7 +477,7 @@
         for n, h in [(2 * i + j, h) for j in range(2) for h in range(heads)]:
             rows = pl.ds(pl.multiple_of(n * GROUP, GROUP), GROUP)
             lanes = slice(h * DH, (h + 1) * DH)
-            flows[n * heads + h] = fdot(qeff[rows, lanes], dout[rows, lanes], 0, 0)
+            flows[n * heads + h] = gdot(qeff[rows, lanes], dout[rows, lanes], 0, 0)
         return 0
 
     lax.fori_loop(0, groups // 2, local, 0)
@@ -493,7 +493,7 @@
             at = n * heads + h
             later = dev[h]
             rst[at] = later
-            moved = fdot(amap[at], later, 0, 0)
+            moved = gdot(amap[at], later, 0, 0)
             dev[h, :, :DH] = moved[:, :DH] * keep
             dev[h, :, DH:] = (moved[:, DH:] + flows[at]) * keep
         return 0
@@ -516,10 +516,10 @@
             q = qkv[rows, lanes]
             k = qkv[rows, (heads + h) * DH : (heads + h + 1) * DH]
             do = dout[rows, lanes]
-            ndo[rows, lanes] = fdot(score[at], do, 0, 0)
-            dn = jnp.where(lower, fdot(do, vnew[rows, lanes], 1, 1), 0.0)
-            dq[rows, lanes] = fdot(do, states[at], 1, 1) + fdot(dn, k)
-            dk[rows, lanes] = fdot(dn, q, 0, 0)
+            ndo[rows, lanes] = gdot(score[at], do, 0, 0)
+            dn = jnp.where(lower, gdot(do, vnew[rows, lanes], 1, 1), 0.0)
+            dq[rows, lanes] = gdot(do, states[at], 1, 1) + gdot(dn, k)
+            dk[rows, lanes] = gdot(dn, q, 0, 0)
         return 0
 
     lax.fori_loop(0, groups // 2, one, 0)

time: 270 us -> 268 us (level)
  transfers between devices with their start and end apart: 54 -> 54, of which waited for: 21 -> 22; matrix products, arithmetic and copies ran while one was open for 1% -> 1% of each run, Pallas kernels for 21% -> 21%
where the time goes in v7:
time: 268 us
  waiting for transfers between devices  120 us (45%)
  Pallas kernels  77.6 us (29%)
  starting transfers between devices  65.6 us (24%)
  local copies, waits for them, and re-layouts  3.31 us (1%)
    ppermute x48, waiting for transfers between devices, swap(): return lax.ppermute(value, axis, [(i, i ^ bit) for i in range(count)])  115 us
    pallas_call x51, Pallas kernels, run(): pl.pallas_call(kernel, name=name, out_shape=shapes, in_specs=[pl.BlockSpe...  77.6 us
    ppermute x48, starting transfers between devices, swap(): return lax.ppermute(value, axis, [(i, i ^ bit) for i in range(count)])  49 us
    ppermute x6, starting transfers between devices, shift(): return lax.ppermute(value, 'seq', pairs)  16.6 us
  transfers between devices with their start and end apart: 54, of which 22 were waited for; matrix products, arithmetic and copies ran while one was open for 1% of the time, Pallas kernels for 21%

profile of v7, /device:TPU:0, one launch (start us, length us, event | category | flops | bytes accessed | tf_op | source)
XLA Modules:
  0.0 267.8 jit_solution(14929641647021640968)
XLA Ops:
  1.4 4.9 %collective-permute-start = (bf16[16,1024]{1,0:T(8,128)(2,1)S(1)}, bf16[16,1024]{1,0:T(8,128)(2,1)S(1)}, u32[]{:S(2)}, u32[]{:S(2)}) collective-permute-start(bf16[16,1024]{1,0:T(8,128)(2,1)S(1)} %slice.15), channel_id=1, source_target_pairs={{0,4},{4,8},{8,12},{12,16},{16,20},{20,24},{24,28},{1,5},{5,9},{9,... | collective-permute-start | bytes 98312 | tf_op jit(solution)/shard_map/ppermute | solution.py:871
  7.9 15.1 %front.1 = (f32[512,256]{1,0:T(8,128)S(1)}, f32[512,2]{1,0:T(8,128)S(1)}, s32[2,8]{1,0:T(2,128)S(1)}, f32[512,768]{1,0:T(8,128)S(1)}, f32[512,256]{1,0:T(8,128)S...) custom-call(s32[1]{0:T(128)} %bitcast.1.first.r_1_.r_0_, ...), custom_call_target="tpu_custom_call" | custom-call | flops 1153500 | bytes 1 | tf_op jit(solution)/shard_map/front/pallas_call | solution.py:78
  22.9 4.2 %collective-permute-start.1 = (bf16[2,128,256]{2,1,0:T(8,128)(2,1)S(1)}, bf16[2,128,256]{2,1,0:T(8,128)(2,1)S(1)}, u32[]{:S(2)}, u32[]{:S(2)}) collective-permute-start(bf16[2,128,256]{2,1,0:T(8,128)(2,1)S(1)} %get-tuple-element.183), channel_id=1, source_target_pairs={{0,4},{4,8},{8,12},{12,16},{16,20},{20,24},{24,28},{1,5},{5,9},{9,... | collective-permute-start | bytes 393224 | tf_op jit(solution)/shard_map/ppermute | solution.py:871
  27.2 3.7 %collective-permute-start.2 = (bf16[2,128,128]{2,1,0:T(8,128)(2,1)S(1)}, bf16[2,128,128]{2,1,0:T(8,128)(2,1)S(1)}, u32[]{:S(2)}, u32[]{:S(2)}) collective-permute-start(bf16[2,128,128]{2,1,0:T(8,128)(2,1)S(1)} %get-tuple-element.193), channel_id=1, source_target_pairs={{0,8},{4,12},{8,16},{12,20},{16,24},{20,28},{1,9},{5,13},{9,17},{1... | collective-permute-start | bytes 196616 | tf_op jit(solution)/shard_map/ppermute | solution.py:871
  38.9 3.8 %states.1 = (f32[16,128,128]{2,1,0:T(8,128)S(1)}, f32[512,256]{1,0:T(8,128)S(1)}, f32[512,256]{1,0:T(8,128)S(1)}) custom-call(f32[2,128,128]{2,1,0:T(8,128)S(1)} %get-tuple-element.201.entry, f32[16,128,256]{2,1,0:T(8,128)S(1)} %get-tuple-element.190.zst, f32[512,768]{1,0:T(8,128)S(1)} %get-tuple-element.239.qkv.r_4_, ...), custom_call_target="tpu_custom_call" | custom-call | flops 1153500 | bytes 1 | tf_op jit(solution)/shard_map/states/pallas_call | solution.py:78
  56.3 5.2 %ffn_b.1 = (f32[1,128,1024]{2,1,0:T(8,128)S(1)}, bf16[1,128,1024]{2,1,0:T(8,128)(2,1)S(1)}, f32[1,128,1024]{2,1,0:T(8,128)S(1)}, bf16[1,128,1024]{2,1,0:T(8,128)...) custom-call(s32[1]{0:T(128)} %bitcast.tp.r_0_, ...), custom_call_target="tpu_custom_call" | custom-call | flops 1153500 | bytes 1 | tf_op jit(solution)/shard_map/ffn_b/pallas_call | solution.py:78
  67.5 6.5 %collective-permute-done.10 = bf16[1,128,1024]{2,1,0:T(8,128)(2,1)S(1)} collective-permute-done((bf16[1,128,1024]{2,1,0:T(8,128)(2,1)S(1)}, bf16[1,128,1024]{2,1,0:T(8,128)(2,1)S(1)}, u32[]{:S(2)}, u32[]{:S(2)}) %collective-permute-start.10) | collective-permute-done | bytes 262176 | tf_op jit(solution)/shard_map/ppermute | solution.py:681
  75.9 5.6 %collective-permute-done.12.b2 = bf16[128,1024]{1,0:T(8,128)(2,1)S(1)} collective-permute-done((bf16[128,1024]{1,0:T(8,128)(2,1)S(1)}, bf16[128,1024]{1,0:T(8,128)(2,1)S(1)}, u32[]{:S(2)}, u32[]{:S(2)}) %collective-permute-start.12) | collective-permute-done | bytes 262176 | tf_op jit(solution)/shard_map/ppermute | solution.py:681
  83.0 4.4 %flow.1 = (bf16[512,1024]{1,0:T(8,128)(2,1)S(1)}, bf16[512,256]{1,0:T(8,128)(2,1)S(1)}, f32[512,256]{1,0:T(8,128)S(1)}, f32[16,128,256]{2,1,0:T(8,128)S(1)}, bf1...) custom-call(s32[1]{0:T(128)} %bitcast.tp.r_0_, ...), custom_call_target="tpu_custom_call" | custom-call | flops 1153500 | bytes 1 | tf_op jit(solution)/shard_map/flow/pallas_call | solution.py:78
  90.1 3.6 %side.1 = (f32[512,256]{1,0:T(8,128)S(1)}, f32[512,256]{1,0:T(8,128)S(1)}, f32[512,256]{1,0:T(8,128)S(1)}) custom-call(f32[512,768]{1,0:T(8,128)S(1)} %get-tuple-element.239.qkv.r_4_, f32[512,256]{1,0:T(8,128)S(1)} %get-tuple-element.240.dout, f32[512,256]{1,0:T(8,128)S(1)} %get-tuple-element.241.vnew.r_12_, ...), custom_call_target="tpu_custom_call" | custom-call | flops 1153500 | bytes 1 | tf_op jit(solution)/shard_map/side/pallas_call | solution.py:78
  101.1 9.6 %back.1 = (f32[520,768]{1,0:T(8,128)S(1)}, f32[8,768]{1,0:T(8,128)S(1)}, bf16[512,128]{1,0:T(8,128)(2,1)S(1)}) custom-call(s32[2,8]{1,0:T(2,128)S(1)} %get-tuple-element.181.meta.r_0_, bf16[2,128,256]{2,1,0:T(8,128)(2,1)S(1)} %collective-permute-done.16.r_1_, bf16[2,128,128]{2,1,0:T(8,128)(2,1)S(1)} %collective-permute-done.17.r_2_, ...), custom_call_target="tpu_custom_call" | custom-call | flops 1153500 | bytes 1 | tf_op jit(solution)/shard_map/back/pallas_call | solution.py:78
  117.8 6.9 %collective-permute-done.23.got = bf16[1,128,1024]{2,1,0:T(8,128)(2,1)S(1)} collective-permute-done((bf16[1,128,1024]{2,1,0:T(8,128)(2,1)S(1)}, bf16[1,128,1024]{2,1,0:T(8,128)(2,1)S(1)}, u32[]{:S(2)}, u32[]{:S(2)}) %collective-permute-start.23) | collective-permute-done | bytes 262176 | tf_op jit(solution)/shard_map/ppermute | solution.py:681
  132.3 11.7 %collective-permute-done.27.got = bf16[1,136,1024]{2,1,0:T(8,128)(2,1)S(1)} collective-permute-done((bf16[1,136,1024]{2,1,0:T(8,128)(2,1)S(1)}, bf16[1,136,1024]{2,1,0:T(8,128)(2,1)S(1)}, u32[]{:S(2)}, u32[]{:S(2)}) %collective-permute-start.27) | collective-permute-done | bytes 278560 | tf_op jit(solution)/shard_map/ppermute | solution.py:681
  146.5 6.5 %collective-permute-done.32.a2 = bf16[128,1024]{1,0:T(8,128)(2,1)S(1)} collective-permute-done((bf16[128,1024]{1,0:T(8,128)(2,1)S(1)}, bf16[128,1024]{1,0:T(8,128)(2,1)S(1)}, u32[]{:S(2)}, u32[]{:S(2)}) %collective-permute-start.32) | collective-permute-done | bytes 262176 | tf_op jit(solution)/shard_map/ppermute | solution.py:681
  157.7 3.9 %collective-permute-done.34.got = bf16[4,72,1024]{2,1,0:T(8,128)(2,1)S(1)} collective-permute-done((bf16[4,72,1024]{2,1,0:T(8,128)(2,1)S(1)}, bf16[4,72,1024]{2,1,0:T(8,128)(2,1)S(1)}, u32[]{:S(2)}, u32[]{:S(2)}) %collective-permute-start.34) | collective-permute-done | bytes 589856 | tf_op jit(solution)/shard_map/ppermute | solution.py:681
  167.3 20.7 %collective-permute-done.38.b = bf16[1,128,1024]{2,1,0:T(8,128)(2,1)S(1)} collective-permute-done((bf16[1,128,1024]{2,1,0:T(8,128)(2,1)S(1)}, bf16[1,128,1024]{2,1,0:T(8,128)(2,1)S(1)}, u32[]{:S(2)}, u32[]{:S(2)}) %collective-permute-start.38) | collective-permute-done | bytes 262176 | tf_op jit(solution)/shard_map/ppermute | solution.py:681
  191.6 8.4 %collective-permute-done.42.b = bf16[2,136,1024]{2,1,0:T(8,128)(2,1)S(1)} collective-permute-done((bf16[2,136,1024]{2,1,0:T(8,128)(2,1)S(1)}, bf16[2,136,1024]{2,1,0:T(8,128)(2,1)S(1)}, u32[]{:S(2)}, u32[]{:S(2)}) %collective-permute-start.42) | collective-permute-done | bytes 557088 | tf_op jit(solution)/shard_map/ppermute | solution.py:681
  200.1 4.9 %collective-permute-done.43.got = bf16[1,72,1024]{2,1,0:T(8,128)(2,1)S(1)} collective-permute-done((bf16[1,72,1024]{2,1,0:T(8,128)(2,1)S(1)}, bf16[1,72,1024]{2,1,0:T(8,128)(2,1)S(1)}, u32[]{:S(2)}, u32[]{:S(2)}) %collective-permute-start.43) | collective-permute-done | bytes 147488 | tf_op jit(solution)/shard_map/ppermute | solution.py:681
  212.2 4.3 %collective-permute-done.46.b = bf16[1,72,1024]{2,1,0:T(8,128)(2,1)S(1)} collective-permute-done((bf16[1,72,1024]{2,1,0:T(8,128)(2,1)S(1)}, bf16[1,72,1024]{2,1,0:T(8,128)(2,1)S(1)}, u32[]{:S(2)}, u32[]{:S(2)}) %collective-permute-start.46) | collective-permute-done | bytes 147488 | tf_op jit(solution)/shard_map/ppermute | solution.py:681
  216.7 3.3 %collective-permute-start.48 = (bf16[2,96,1024]{2,1,0:T(8,128)(2,1)S(1)}, bf16[2,96,1024]{2,1,0:T(8,128)(2,1)S(1)}, u32[]{:S(2)}, u32[]{:S(2)}) collective-permute-start(bf16[2,96,1024]{2,1,0:T(8,128)(2,1)S(1)} %f3_pack.2.a), channel_id=1, source_target_pairs={{0,16},{4,20},{8,24},{12,28},{16,0},{20,4},{24,8},{28,12},{1,17},{... | collective-permute-start | bytes 1179656 | tf_op jit(solution)/shard_map/ppermute | solution.py:681
  221.7 22.6 %collective-permute-done.48.b = bf16[2,96,1024]{2,1,0:T(8,128)(2,1)S(1)} collective-permute-done((bf16[2,96,1024]{2,1,0:T(8,128)(2,1)S(1)}, bf16[2,96,1024]{2,1,0:T(8,128)(2,1)S(1)}, u32[]{:S(2)}, u32[]{:S(2)}) %collective-permute-start.48) | collective-permute-done | bytes 393248 | tf_op jit(solution)/shard_map/ppermute | solution.py:681
  250.4 3.9 %settle_1.1 = (f32[704,1024]{1,0:T(8,128)}, f32[704,1024]{1,0:T(8,128)}) custom-call(s32[1]{0:T(128)} %bitcast.1.first.r_1_.r_0_, bf16[4,128,1024]{2,1,0:T(8,128)(2,1)S(1)} %f1_pack.3.r_1_, bf16[4,128,1024]{2,1,0:T(8,128)(2,1)} %collective-permute-done.50.r_2_, bf16[4,136,1024]{2,1,0:T(8,128)(2,1)S(1)} %f2_pack.3.r_3_.r_1_, ...), custom_call_target="tpu_custom_call" | custom-call | flops 1153500 | bytes 1 | tf_op jit(solution)/shard_map/settle_1/pallas_call | solution.py:78
  256.1 3.1 %collective-permute-done.52.r_2_ = bf16[4,72,1024]{2,1,0:T(8,128)(2,1)} collective-permute-done((bf16[4,72,1024]{2,1,0:T(8,128)(2,1)}, bf16[4,72,1024]{2,1,0:T(8,128)(2,1)}, u32[]{:S(2)}, u32[]{:S(2)}) %collective-permute-start.52) | collective-permute-done | bytes 589856 | tf_op jit(solution)/shard_map/ppermute | solution.py:681
  264.3 3.3 %settle_3.1 = (f32[1024,256]{1,0:T(8,128)}, f32[1024,256]{1,0:T(8,128)}, f32[1024,256]{1,0:T(8,128)}) custom-call(s32[1]{0:T(128)} %bitcast.1.first.r_1_.r_0_, bf16[4,96,1024]{2,1,0:T(8,128)(2,1)} %f3_pack.3.r_1_, bf16[4,96,1024]{2,1,0:T(8,128)(2,1)} %collective-permute-done.53.r_2_), custom_call_target="tpu_custom_call" | custom-call | flops 1153500 | bytes 1 | tf_op jit(solution)/shard_map/settle_3/pallas_call | solution.py:78
  (180 shorter events, 96.1 us)
Async XLA Ops:
  61.8 34.6 %collective-permute-start.18 = (bf16[4,136,1024]{2,1,0:T(8,128)(2,1)S(1)}, bf16[4,136,1024]{2,1,0:T(8,128)(2,1)S(1)}, u32[]{:S(2)}, u32[]{:S(2)}) collective-permute-start(bf16[4,136,1024]{2,1,0:T(8,128)(2,1)S(1)} %get-tuple-element.252), channel_id=1, source_target_pairs={{0,8},{4,12},{8,0},{12,4},{16,24},{20,28},{24,16},{28,20},{1,9},{5... | collective-permute-start | bytes 3342344 | tf_op jit(solution)/shard_map/ppermute | solution.py:681
  63.4 33.2 %collective-permute-start.19 = (bf16[4,128,1024]{2,1,0:T(8,128)(2,1)S(1)}, bf16[4,128,1024]{2,1,0:T(8,128)(2,1)S(1)}, u32[]{:S(2)}, u32[]{:S(2)}) collective-permute-start(bf16[4,128,1024]{2,1,0:T(8,128)(2,1)S(1)} %get-tuple-element.255), channel_id=1, source_target_pairs={{0,4},{4,0},{8,12},{12,8},{16,20},{20,16},{24,28},{28,24},{1,5},{5... | collective-permute-start | bytes 3145736 | tf_op jit(solution)/shard_map/ppermute | solution.py:681
  96.8 14.0 %collective-permute-start.20 = (bf16[2,128,1024]{2,1,0:T(8,128)(2,1)S(1)}, bf16[2,128,1024]{2,1,0:T(8,128)(2,1)S(1)}, u32[]{:S(2)}, u32[]{:S(2)}) collective-permute-start(bf16[2,128,1024]{2,1,0:T(8,128)(2,1)S(1)} %get-tuple-element.266), channel_id=1, source_target_pairs={{0,8},{4,12},{8,0},{12,4},{16,24},{20,28},{24,16},{28,20},{1,9},{5... | collective-permute-start | bytes 1572872 | tf_op jit(solution)/shard_map/ppermute | solution.py:681
  98.3 15.7 %collective-permute-start.21 = (bf16[2,136,1024]{2,1,0:T(8,128)(2,1)S(1)}, bf16[2,136,1024]{2,1,0:T(8,128)(2,1)S(1)}, u32[]{:S(2)}, u32[]{:S(2)}) collective-permute-start(bf16[2,136,1024]{2,1,0:T(8,128)(2,1)S(1)} %get-tuple-element.269), channel_id=1, source_target_pairs={{0,4},{4,0},{8,12},{12,8},{16,20},{20,16},{24,28},{28,24},{1,5},{5... | collective-permute-start | bytes 1671176 | tf_op jit(solution)/shard_map/ppermute | solution.py:681
  99.6 17.5 %collective-permute-start.22 = (bf16[1,128,1024]{2,1,0:T(8,128)(2,1)S(1)}, bf16[1,128,1024]{2,1,0:T(8,128)(2,1)S(1)}, u32[]{:S(2)}, u32[]{:S(2)}) collective-permute-start(bf16[1,128,1024]{2,1,0:T(8,128)(2,1)S(1)} %get-tuple-element.275), channel_id=1, source_target_pairs={{0,2},{1,3},{2,0},{3,1},{4,6},{5,7},{6,4},{7,5},{8,10},{9,11},{10,... | collective-permute-start | bytes 786440 | tf_op jit(solution)/shard_map/ppermute | solution.py:681
  110.9 13.8 %collective-permute-start.23 = (bf16[1,128,1024]{2,1,0:T(8,128)(2,1)S(1)}, bf16[1,128,1024]{2,1,0:T(8,128)(2,1)S(1)}, u32[]{:S(2)}, u32[]{:S(2)}) collective-permute-start(bf16[1,128,1024]{2,1,0:T(8,128)(2,1)S(1)} %get-tuple-element.279), channel_id=1, source_target_pairs={{0,16},{4,20},{8,24},{12,28},{16,0},{20,4},{24,8},{28,12},{1,17},{... | collective-permute-start | bytes 786440 | tf_op jit(solution)/shard_map/ppermute | solution.py:681
  127.8 26.3 %collective-permute-start.30 = (bf16[4,96,1024]{2,1,0:T(8,128)(2,1)S(1)}, bf16[4,96,1024]{2,1,0:T(8,128)(2,1)S(1)}, u32[]{:S(2)}, u32[]{:S(2)}) collective-permute-start(bf16[4,96,1024]{2,1,0:T(8,128)(2,1)S(1)} %get-tuple-element.308), channel_id=1, source_target_pairs={{0,4},{4,0},{8,12},{12,8},{16,20},{20,16},{24,28},{28,24},{1,5},{5... | collective-permute-start | bytes 2359304 | tf_op jit(solution)/shard_map/ppermute | solution.py:681
  128.3 15.6 %collective-permute-start.27 = (bf16[1,136,1024]{2,1,0:T(8,128)(2,1)S(1)}, bf16[1,136,1024]{2,1,0:T(8,128)(2,1)S(1)}, u32[]{:S(2)}, u32[]{:S(2)}) collective-permute-start(bf16[1,136,1024]{2,1,0:T(8,128)(2,1)S(1)} %get-tuple-element.301), channel_id=1, source_target_pairs={{0,16},{4,20},{8,24},{12,28},{16,0},{20,4},{24,8},{28,12},{1,17},{... | collective-permute-start | bytes 835592 | tf_op jit(solution)/shard_map/ppermute | solution.py:681
  128.6 15.5 %collective-permute-start.28 = (bf16[1,128,1024]{2,1,0:T(8,128)(2,1)S(1)}, bf16[1,128,1024]{2,1,0:T(8,128)(2,1)S(1)}, u32[]{:S(2)}, u32[]{:S(2)}) collective-permute-start(bf16[1,128,1024]{2,1,0:T(8,128)(2,1)S(1)} %get-tuple-element.303), channel_id=1, source_target_pairs={{0,2},{1,3},{2,0},{3,1},{4,6},{5,7},{6,4},{7,5},{8,10},{9,11},{10,... | collective-permute-start | bytes 786440 | tf_op jit(solution)/shard_map/ppermute | solution.py:681
  131.2 13.1 %collective-permute-start.29 = (f32[8,1024]{1,0:T(8,128)S(1)}, f32[8,1024]{1,0:T(8,128)S(1)}, u32[]{:S(2)}, u32[]{:S(2)}) collective-permute-start(f32[8,1024]{1,0:T(8,128)S(1)} %plus.2.a), channel_id=1, source_target_pairs={{0,2},{1,3},{2,0},{3,1},{4,6},{5,7},{6,4},{7,5},{8,10},{9,11},{10,... | collective-permute-start | bytes 98312 | tf_op jit(solution)/shard_map/ppermute | solution.py:681
  145.3 16.3 %collective-permute-start.34 = (bf16[4,72,1024]{2,1,0:T(8,128)(2,1)S(1)}, bf16[4,72,1024]{2,1,0:T(8,128)(2,1)S(1)}, u32[]{:S(2)}, u32[]{:S(2)}) collective-permute-start(bf16[4,72,1024]{2,1,0:T(8,128)(2,1)S(1)} %get-tuple-element.312), channel_id=1, source_target_pairs={{0,8},{4,12},{8,0},{12,4},{16,24},{20,28},{24,16},{28,20},{1,9},{5... | collective-permute-start | bytes 1769480 | tf_op jit(solution)/shard_map/ppermute | solution.py:681
  154.5 33.6 %collective-permute-start.40 = (bf16[2,96,1024]{2,1,0:T(8,128)(2,1)S(1)}, bf16[2,96,1024]{2,1,0:T(8,128)(2,1)S(1)}, u32[]{:S(2)}, u32[]{:S(2)}) collective-permute-start(bf16[2,96,1024]{2,1,0:T(8,128)(2,1)S(1)} %get-tuple-element.320), channel_id=1, source_target_pairs={{0,8},{4,12},{8,0},{12,4},{16,24},{20,28},{24,16},{28,20},{1,9},{5... | collective-permute-start | bytes 1179656 | tf_op jit(solution)/shard_map/ppermute | solution.py:681
  161.7 26.3 %collective-permute-start.39 = (bf16[2,72,1024]{2,1,0:T(8,128)(2,1)S(1)}, bf16[2,72,1024]{2,1,0:T(8,128)(2,1)S(1)}, u32[]{:S(2)}, u32[]{:S(2)}) collective-permute-start(bf16[2,72,1024]{2,1,0:T(8,128)(2,1)S(1)} %get-tuple-element.317), channel_id=1, source_target_pairs={{0,4},{4,0},{8,12},{12,8},{16,20},{20,16},{24,28},{28,24},{1,5},{5... | collective-permute-start | bytes 884744 | tf_op jit(solution)/shard_map/ppermute | solution.py:681
  163.3 24.9 %collective-permute-start.41 = (bf16[1,136,1024]{2,1,0:T(8,128)(2,1)S(1)}, bf16[1,136,1024]{2,1,0:T(8,128)(2,1)S(1)}, u32[]{:S(2)}, u32[]{:S(2)}) collective-permute-start(bf16[1,136,1024]{2,1,0:T(8,128)(2,1)S(1)} %f2_last.1.a), channel_id=1, source_target_pairs={{0,16},{4,20},{8,24},{12,28},{16,0},{20,4},{24,8},{28,12},{1,17},{... | collective-permute-start | bytes 835592 | tf_op jit(solution)/shard_map/ppermute | solution.py:681
  163.3 24.7 %collective-permute-start.38 = (bf16[1,128,1024]{2,1,0:T(8,128)(2,1)S(1)}, bf16[1,128,1024]{2,1,0:T(8,128)(2,1)S(1)}, u32[]{:S(2)}, u32[]{:S(2)}) collective-permute-start(bf16[1,128,1024]{2,1,0:T(8,128)(2,1)S(1)} %f1_last.1.a), channel_id=1, source_target_pairs={{0,16},{4,20},{8,24},{12,28},{16,0},{20,4},{24,8},{28,12},{1,17},{... | collective-permute-start | bytes 786440 | tf_op jit(solution)/shard_map/ppermute | solution.py:681
  188.7 21.8 %collective-permute-start.45 = (bf16[2,128,1024]{2,1,0:T(8,128)(2,1)S(1)}, bf16[2,128,1024]{2,1,0:T(8,128)(2,1)S(1)}, u32[]{:S(2)}, u32[]{:S(2)}) collective-permute-start(bf16[2,128,1024]{2,1,0:T(8,128)(2,1)S(1)} %f1_pack.2.a), channel_id=1, source_target_pairs={{0,8},{4,12},{8,0},{12,4},{16,24},{20,28},{24,16},{28,20},{1,9},{5... | collective-permute-start | bytes 1572872 | tf_op jit(solution)/shard_map/ppermute | solution.py:681
  188.7 16.3 %collective-permute-start.44 = (bf16[1,96,1024]{2,1,0:T(8,128)(2,1)S(1)}, bf16[1,96,1024]{2,1,0:T(8,128)(2,1)S(1)}, u32[]{:S(2)}, u32[]{:S(2)}) collective-permute-start(bf16[1,96,1024]{2,1,0:T(8,128)(2,1)S(1)} %get-tuple-element.327), channel_id=1, source_target_pairs={{0,16},{4,20},{8,24},{12,28},{16,0},{20,4},{24,8},{28,12},{1,17},{... | collective-permute-start | bytes 589832 | tf_op jit(solution)/shard_map/ppermute | solution.py:681
  190.6 14.4 %collective-permute-start.43 = (bf16[1,72,1024]{2,1,0:T(8,128)(2,1)S(1)}, bf16[1,72,1024]{2,1,0:T(8,128)(2,1)S(1)}, u32[]{:S(2)}, u32[]{:S(2)}) collective-permute-start(bf16[1,72,1024]{2,1,0:T(8,128)(2,1)S(1)} %get-tuple-element.325), channel_id=1, source_target_pairs={{0,16},{4,20},{8,24},{12,28},{16,0},{20,4},{24,8},{28,12},{1,17},{... | collective-permute-start | bytes 442376 | tf_op jit(solution)/shard_map/ppermute | solution.py:681
  208.6 41.9 %collective-permute-start.51 = (bf16[4,136,1024]{2,1,0:T(8,128)(2,1)S(1)}, bf16[4,136,1024]{2,1,0:T(8,128)(2,1)S(1)}, u32[]{:S(2)}, u32[]{:S(2)}) collective-permute-start(bf16[4,136,1024]{2,1,0:T(8,128)(2,1)S(1)} %f2_pack.3.r_3_.r_1_), channel_id=1, source_target_pairs={{0,8},{4,12},{8,0},{12,4},{16,24},{20,28},{24,16},{28,20},{1,9},{5... | collective-permute-start | bytes 3342344 | tf_op jit(solution)/shard_map/ppermute | solution.py:681
  210.6 39.9 %collective-permute-start.50 = (bf16[4,128,1024]{2,1,0:T(8,128)(2,1)S(1)}, bf16[4,128,1024]{2,1,0:T(8,128)(2,1)}, u32[]{:S(2)}, u32[]{:S(2)}) collective-permute-start(bf16[4,128,1024]{2,1,0:T(8,128)(2,1)S(1)} %f1_pack.3.r_1_), channel_id=1, source_target_pairs={{0,4},{4,0},{8,12},{12,8},{16,20},{20,16},{24,28},{28,24},{1,5},{5... | collective-permute-start | bytes 3145736 | tf_op jit(solution)/shard_map/ppermute | solution.py:681
  216.7 27.6 %collective-permute-start.48 = (bf16[2,96,1024]{2,1,0:T(8,128)(2,1)S(1)}, bf16[2,96,1024]{2,1,0:T(8,128)(2,1)S(1)}, u32[]{:S(2)}, u32[]{:S(2)}) collective-permute-start(bf16[2,96,1024]{2,1,0:T(8,128)(2,1)S(1)} %f3_pack.2.a), channel_id=1, source_target_pairs={{0,16},{4,20},{8,24},{12,28},{16,0},{20,4},{24,8},{28,12},{1,17},{... | collective-permute-start | bytes 1179656 | tf_op jit(solution)/shard_map/ppermute | solution.py:681
  220.0 25.3 %collective-permute-start.49 = (bf16[2,72,1024]{2,1,0:T(8,128)(2,1)S(1)}, bf16[2,72,1024]{2,1,0:T(8,128)(2,1)S(1)}, u32[]{:S(2)}, u32[]{:S(2)}) collective-permute-start(bf16[2,72,1024]{2,1,0:T(8,128)(2,1)S(1)} %f4_pack.2.a), channel_id=1, source_target_pairs={{0,4},{4,0},{8,12},{12,8},{16,20},{20,16},{24,28},{28,24},{1,5},{5... | collective-permute-start | bytes 884744 | tf_op jit(solution)/shard_map/ppermute | solution.py:681
  246.1 13.0 %collective-permute-start.52 = (bf16[4,72,1024]{2,1,0:T(8,128)(2,1)}, bf16[4,72,1024]{2,1,0:T(8,128)(2,1)}, u32[]{:S(2)}, u32[]{:S(2)}) collective-permute-start(bf16[4,72,1024]{2,1,0:T(8,128)(2,1)} %f4_pack.3.r_1_), channel_id=1, source_target_pairs={{0,8},{4,12},{8,0},{12,4},{16,24},{20,28},{24,16},{28,20},{1,9},{5... | collective-permute-start | bytes 1769480 | tf_op jit(solution)/shard_map/ppermute | solution.py:681
  248.7 15.6 %collective-permute-start.53 = (bf16[4,96,1024]{2,1,0:T(8,128)(2,1)}, bf16[4,96,1024]{2,1,0:T(8,128)(2,1)}, u32[]{:S(2)}, u32[]{:S(2)}) collective-permute-start(bf16[4,96,1024]{2,1,0:T(8,128)(2,1)} %f3_pack.3.r_1_), channel_id=1, source_target_pairs={{0,4},{4,0},{8,12},{12,8},{16,20},{20,16},{24,28},{28,24},{1,5},{5... | collective-permute-start | bytes 2359304 | tf_op jit(solution)/shard_map/ppermute | solution.py:681
  (50 other events, 351.9 us)
